TPU v7x, 32 devices: a whole 2x2x4 slice. The times are simulated.
32 devices in a mesh: ctx: 8 (over z, x), wsh: 4 (over y, core).
Axes of the slice: x: 2, y: 2, z: 4, core: 2. Of those that a mesh axis runs over, the one named last changes fastest.
Arguments:
- tokens: bfloat16 [4, 4096, 768], P('wsh', 'ctx'), may hold values from -6 to 6
- cotangent: bfloat16 [4, 4096, 768], P('wsh', 'ctx'), may hold values from -6 to 6
- doc_starts: int32 [4, 8], P('wsh'), may hold values from 0 to 4095, as said below
- query_weight: bfloat16 [768, 768], P('wsh'), may hold values from -0.21875 to 0.21875
- key_weight: bfloat16 [768, 768], P('wsh'), may hold values from -0.21875 to 0.21875
- value_weight: bfloat16 [768, 768], P('wsh'), may hold values from -0.21875 to 0.21875
- out_weight: bfloat16 [768, 768], P('wsh'), may hold values from -3.5 to 3.5
- up_weight: bfloat16 [768, 3072], P('wsh'), may hold values from -0.21875 to 0.21875
- down_weight: bfloat16 [3072, 768], P('wsh'), may hold values from -0.109375 to 0.109375
- query_bias: bfloat16 [768], P('wsh'), may hold values from -3 to 3
- value_bias: bfloat16 [768], P('wsh'), may hold values from -3 to 3
- out_bias: bfloat16 [768], P('wsh'), may hold values from -3 to 3
- attn_gain: bfloat16 [768], P('wsh'), may hold values from 0.5 to 1.5
- attn_shift: bfloat16 [768], P('wsh'), may hold values from -3 to 3
- up_bias: bfloat16 [3072], P('wsh'), may hold values from -3 to 3
- down_bias: bfloat16 [768], P('wsh'), may hold values from -3 to 3
- final_gain: bfloat16 [768], P('wsh'), may hold values from 0.5 to 1.5
- final_shift: bfloat16 [768], P('wsh'), may hold values from -3 to 3
Outputs:
- layer_out: bfloat16 [4, 4096, 768], P('wsh', 'ctx')
- tokens_grad: bfloat16 [4, 4096, 768], P('wsh', 'ctx')
- query_weight_grad: float32 [768, 768], P('wsh')
- key_weight_grad: float32 [768, 768], P('wsh')
- value_weight_grad: float32 [768, 768], P('wsh')
- out_weight_grad: float32 [768, 768], P('wsh')
- up_weight_grad: float32 [768, 3072], P('wsh')
- down_weight_grad: float32 [3072, 768], P('wsh')
- query_bias_grad: float32 [768], P('wsh')
- value_bias_grad: float32 [768], P('wsh')
- out_bias_grad: float32 [768], P('wsh')
- attn_gain_grad: float32 [768], P('wsh')
- attn_shift_grad: float32 [768], P('wsh')
- up_bias_grad: float32 [3072], P('wsh')
- down_bias_grad: float32 [768], P('wsh')
- final_gain_grad: float32 [768], P('wsh')
- final_shift_grad: float32 [768], P('wsh')
Inputs may be any that keep to these rules, and one draw needn't show every extreme that they name: `doc_starts`: each row starts with 0 and rises strictly; each stream holds 8 documents, exactly one of them 2048 tokens long.
All inputs are finite; a program needn't handle non-finite values.
Results may differ from a plain program's by a relative error of at most 0.035.
Values may be sent and summed in bfloat16 or wider, within the bound.
A program may use at most 192 MiB of HBM per device.

v0:
```python
import math

import jax
import jax.numpy as jnp
from jax import lax
from jax.sharding import PartitionSpec as P

D = 768
HEADS = 12
HD = 64


SCALE = 0.125
EPS = 1e-12
NEG = -1e30
ROOT_HALF = 0.7071067811865476


def layer_norm(values, gain_vec, shift_vec):
    average = jnp.mean(values, axis=-1, keepdims=True)
    centred = values - average
    variance = jnp.mean(centred * centred, axis=-1, keepdims=True)
    return centred * lax.rsqrt(variance + EPS) * gain_vec + shift_vec


def gelu_act(values):
    return 0.5 * values * (1.0 + lax.erf(values * ROOT_HALF))


def segment_of(doc_start, positions):
    return jnp.sum((doc_start[None, :] <= positions[:, None]).astype(jnp.int32), axis=1) - 1


def split_rows(row_count):
    block_size = math.gcd(row_count, 512)
    return (row_count // block_size, block_size)


def forward_fold(running, portion, queries, query_seg, doc_start):
    keys_in, values_in = portion
    block_count, block_size = split_rows(keys_in.shape[0])
    key_blocks = keys_in.reshape(block_count, block_size, HEADS, HD)
    value_blocks = values_in.reshape(block_count, block_size, HEADS, HD)
    block_starts = jnp.arange(block_count, dtype=jnp.int32) * block_size

    def forward_one_block(inner, items):
        key_block, value_block, block_first = items
        running_max, running_sum, running_out = inner
        key_seg = segment_of(doc_start, block_first + jnp.arange(block_size, dtype=jnp.int32))
        allowed = (query_seg[:, None] == key_seg[None, :])[None]
        scores = (
            jnp.einsum("qhd,khd->hqk", queries, key_block, preferred_element_type=jnp.float32)
            * SCALE
        )
        scores = jnp.where(allowed, scores, NEG)
        new_max = jnp.maximum(running_max, jnp.max(scores, axis=2))
        exp_terms = jnp.where(allowed, jnp.exp(scores - new_max[:, :, None]), 0.0)
        rescale = jnp.exp(running_max - new_max)
        running_sum = running_sum * rescale + jnp.sum(exp_terms, axis=2)
        mixed = jnp.einsum(
            "hqk,khd->qhd",
            exp_terms.astype(jnp.bfloat16),
            value_block,
            preferred_element_type=jnp.float32,
        )
        running_out = running_out * rescale.T[:, :, None] + mixed
        return ((new_max, running_sum, running_out), None)

    result, unused = lax.scan(forward_one_block, running, (key_blocks, value_blocks, block_starts))
    return result


def key_side_fold(running, portion, queries, query_seg, doc_start, grad_attn, log_rows, delta_rows):
    keys_in, values_in = portion
    block_count, block_size = split_rows(keys_in.shape[0])
    key_blocks = keys_in.reshape(block_count, block_size, HEADS, HD)
    value_blocks = values_in.reshape(block_count, block_size, HEADS, HD)
    block_starts = jnp.arange(block_count, dtype=jnp.int32) * block_size
    log_heads = log_rows.T[:, :, None]
    delta_heads = delta_rows.T[:, :, None]

    def key_one_block(inner, items):
        key_block, value_block, block_first = items
        grad_query, grad_keys, grad_values = inner
        key_seg = segment_of(doc_start, block_first + jnp.arange(block_size, dtype=jnp.int32))
        allowed = (query_seg[:, None] == key_seg[None, :])[None]
        scores = (
            jnp.einsum("qhd,khd->hqk", queries, key_block, preferred_element_type=jnp.float32)
            * SCALE
        )
        weights_f = jnp.where(allowed, jnp.exp(scores - log_heads), 0.0)
        weights_b = weights_f.astype(jnp.bfloat16)
        value_term = jnp.einsum(
            "hqk,qhd->khd", weights_b, grad_attn, preferred_element_type=jnp.float32
        )
        grad_prob = jnp.einsum(
            "qhd,khd->hqk", grad_attn, value_block, preferred_element_type=jnp.float32
        )
        grad_scores = (weights_f * (grad_prob - delta_heads)).astype(jnp.bfloat16)
        grad_query = (
            grad_query
            + jnp.einsum("hqk,khd->qhd", grad_scores, key_block, preferred_element_type=jnp.float32)
            * SCALE
        )
        key_term = (
            jnp.einsum("hqk,qhd->khd", grad_scores, queries, preferred_element_type=jnp.float32)
            * SCALE
        )
        old_keys = lax.dynamic_slice_in_dim(grad_keys, block_first, block_size, 0)
        grad_keys = lax.dynamic_update_slice_in_dim(grad_keys, old_keys + key_term, block_first, 0)
        old_values = lax.dynamic_slice_in_dim(grad_values, block_first, block_size, 0)
        grad_values = lax.dynamic_update_slice_in_dim(
            grad_values, old_values + value_term, block_first, 0
        )
        return ((grad_query, grad_keys, grad_values), None)

    result, unused = lax.scan(key_one_block, running, (key_blocks, value_blocks, block_starts))
    return result


def local(
    tokens,
    cotangent,
    doc_starts,
    query_weight,
    key_weight,
    value_weight,
    out_weight,
    up_weight,
    down_weight,
    query_bias,
    value_bias,
    out_bias,
    attn_gain,
    attn_shift,
    up_bias,
    down_bias,
    final_gain,
    final_shift,
):
    gathered = (
        lax.all_gather(query_weight, "wsh", axis=0, tiled=True),
        lax.all_gather(key_weight, "wsh", axis=0, tiled=True),
        lax.all_gather(value_weight, "wsh", axis=0, tiled=True),
        lax.all_gather(out_weight, "wsh", axis=0, tiled=True),
        lax.all_gather(up_weight, "wsh", axis=0, tiled=True),
        lax.all_gather(down_weight, "wsh", axis=0, tiled=True),
        lax.all_gather(query_bias, "wsh", axis=0, tiled=True),
        lax.all_gather(value_bias, "wsh", axis=0, tiled=True),
        lax.all_gather(out_bias, "wsh", axis=0, tiled=True),
        lax.all_gather(attn_gain, "wsh", axis=0, tiled=True),
        lax.all_gather(attn_shift, "wsh", axis=0, tiled=True),
        lax.all_gather(up_bias, "wsh", axis=0, tiled=True),
        lax.all_gather(down_bias, "wsh", axis=0, tiled=True),
        lax.all_gather(final_gain, "wsh", axis=0, tiled=True),
        lax.all_gather(final_shift, "wsh", axis=0, tiled=True),
    )
    (
        query_w,
        key_w,
        value_w,
        out_w,
        up_w,
        down_w,
        query_b,
        value_b,
        out_b,
        attn_g,
        attn_s,
        up_b,
        down_b,
        final_g,
        final_s,
    ) = gathered
    inputs = tokens[0]
    doc_start = doc_starts[0]
    tok_rows = inputs.shape[0]
    stream_rows = tok_rows * lax.axis_size("ctx")
    first_row = lax.axis_index("ctx") * tok_rows
    local_seg = segment_of(doc_start, first_row + jnp.arange(tok_rows, dtype=jnp.int32))
    query_f = jnp.dot(inputs, query_w, preferred_element_type=jnp.float32) + query_b.astype(
        jnp.float32
    )
    queries = query_f.astype(jnp.bfloat16).reshape(tok_rows, HEADS, HD)
    keys_loc = (
        jnp.dot(inputs, key_w, preferred_element_type=jnp.float32)
        .astype(jnp.bfloat16)
        .reshape(tok_rows, HEADS, HD)
    )
    value_f = jnp.dot(inputs, value_w, preferred_element_type=jnp.float32) + value_b.astype(
        jnp.float32
    )
    values_loc = value_f.astype(jnp.bfloat16).reshape(tok_rows, HEADS, HD)
    start_state = (
        jnp.full((HEADS, tok_rows), NEG, jnp.float32),
        jnp.zeros((HEADS, tok_rows), jnp.float32),
        jnp.zeros((tok_rows, HEADS, HD), jnp.float32),
    )
    run_max, run_sum, run_out = forward_fold(
        start_state,
        (
            lax.all_gather(keys_loc, "ctx", axis=0, tiled=True),
            lax.all_gather(values_loc, "ctx", axis=0, tiled=True),
        ),
        queries,
        local_seg,
        doc_start,
    )
    attn_f = run_out / run_sum.T[:, :, None]
    log_rows = (run_max + jnp.log(run_sum)).T
    attn_b = attn_f.reshape(tok_rows, D).astype(jnp.bfloat16)
    inputs_f = inputs.astype(jnp.float32)
    branch = jnp.dot(attn_b, out_w, preferred_element_type=jnp.float32) + out_b.astype(jnp.float32)
    first_norm, first_pull = jax.vjp(
        layer_norm, inputs_f + branch, attn_g.astype(jnp.float32), attn_s.astype(jnp.float32)
    )
    first_b = first_norm.astype(jnp.bfloat16)
    up_f = jnp.dot(first_b, up_w, preferred_element_type=jnp.float32) + up_b.astype(jnp.float32)
    act_f, act_pull = jax.vjp(gelu_act, up_f)
    act_b = act_f.astype(jnp.bfloat16)
    down_f = jnp.dot(act_b, down_w, preferred_element_type=jnp.float32) + down_b.astype(jnp.float32)
    final_f, final_pull = jax.vjp(
        layer_norm, first_norm + down_f, final_g.astype(jnp.float32), final_s.astype(jnp.float32)
    )
    layer_out = final_f.astype(jnp.bfloat16)
    again = (
        lax.all_gather(query_weight, "wsh", axis=0, tiled=True),
        lax.all_gather(key_weight, "wsh", axis=0, tiled=True),
        lax.all_gather(value_weight, "wsh", axis=0, tiled=True),
        lax.all_gather(out_weight, "wsh", axis=0, tiled=True),
        lax.all_gather(up_weight, "wsh", axis=0, tiled=True),
        lax.all_gather(down_weight, "wsh", axis=0, tiled=True),
        lax.all_gather(query_bias, "wsh", axis=0, tiled=True),
        lax.all_gather(value_bias, "wsh", axis=0, tiled=True),
        lax.all_gather(out_bias, "wsh", axis=0, tiled=True),
        lax.all_gather(attn_gain, "wsh", axis=0, tiled=True),
        lax.all_gather(attn_shift, "wsh", axis=0, tiled=True),
        lax.all_gather(up_bias, "wsh", axis=0, tiled=True),
        lax.all_gather(down_bias, "wsh", axis=0, tiled=True),
        lax.all_gather(final_gain, "wsh", axis=0, tiled=True),
        lax.all_gather(final_shift, "wsh", axis=0, tiled=True),
    )
    query_w2, key_w2, value_w2, out_w2, up_w2, down_w2 = (
        again[0],
        again[1],
        again[2],
        again[3],
        again[4],
        again[5],
    )
    grad_sum2, grad_final_g, grad_final_s = final_pull(cotangent[0].astype(jnp.float32))
    grad_down = grad_sum2.astype(jnp.bfloat16)
    grad_down_w = jnp.einsum("tf,td->fd", act_b, grad_down, preferred_element_type=jnp.float32)
    grad_down_b = jnp.sum(grad_down.astype(jnp.float32), axis=0)
    grad_act = jnp.einsum("td,fd->tf", grad_down, down_w2, preferred_element_type=jnp.float32)
    (grad_up_f,) = act_pull(grad_act)
    grad_up = grad_up_f.astype(jnp.bfloat16)
    grad_up_w = jnp.einsum("td,tf->df", first_b, grad_up, preferred_element_type=jnp.float32)
    grad_up_b = jnp.sum(grad_up.astype(jnp.float32), axis=0)
    grad_first = grad_sum2 + jnp.einsum(
        "tf,df->td", grad_up, up_w2, preferred_element_type=jnp.float32
    )
    grad_sum1, grad_attn_g, grad_attn_s = first_pull(grad_first)
    grad_branch = grad_sum1.astype(jnp.bfloat16)
    grad_out_w = jnp.einsum("td,te->de", attn_b, grad_branch, preferred_element_type=jnp.float32)
    grad_out_b = jnp.sum(grad_branch.astype(jnp.float32), axis=0)
    grad_attn = jnp.einsum("te,de->td", grad_branch, out_w2, preferred_element_type=jnp.float32)
    grad_attn = grad_attn.astype(jnp.bfloat16).reshape(tok_rows, HEADS, HD)
    delta_rows = jnp.sum(grad_attn.astype(jnp.float32) * attn_f, axis=2)
    zero_local = jnp.zeros((tok_rows, HEADS, HD), jnp.float32)
    zero_stream = jnp.zeros((stream_rows, HEADS, HD), jnp.float32)
    grad_query_f, grad_keys_all, grad_values_all = key_side_fold(
        (zero_local, zero_stream, zero_stream),
        (
            lax.all_gather(keys_loc, "ctx", axis=0, tiled=True),
            lax.all_gather(values_loc, "ctx", axis=0, tiled=True),
        ),
        queries,
        local_seg,
        doc_start,
        grad_attn,
        log_rows,
        delta_rows,
    )
    grad_key_f, grad_value_f = (
        lax.psum_scatter(
            grad_keys_all.astype(jnp.bfloat16), "ctx", scatter_dimension=0, tiled=True
        ).astype(jnp.float32),
        lax.psum_scatter(
            grad_values_all.astype(jnp.bfloat16), "ctx", scatter_dimension=0, tiled=True
        ).astype(jnp.float32),
    )
    grad_q = grad_query_f.reshape(tok_rows, D).astype(jnp.bfloat16)
    grad_k = grad_key_f.reshape(tok_rows, D).astype(jnp.bfloat16)
    grad_v = grad_value_f.reshape(tok_rows, D).astype(jnp.bfloat16)
    grad_query_w = jnp.einsum("td,te->de", inputs, grad_q, preferred_element_type=jnp.float32)
    grad_key_w = jnp.einsum("td,te->de", inputs, grad_k, preferred_element_type=jnp.float32)
    grad_value_w = jnp.einsum("td,te->de", inputs, grad_v, preferred_element_type=jnp.float32)
    grad_query_b = jnp.sum(grad_q.astype(jnp.float32), axis=0)
    grad_value_b = jnp.sum(grad_v.astype(jnp.float32), axis=0)
    grad_inputs = grad_sum1 + jnp.einsum(
        "te,de->td", grad_q, query_w2, preferred_element_type=jnp.float32
    )
    grad_inputs = grad_inputs + jnp.einsum(
        "te,de->td", grad_k, key_w2, preferred_element_type=jnp.float32
    )
    grad_inputs = grad_inputs + jnp.einsum(
        "te,de->td", grad_v, value_w2, preferred_element_type=jnp.float32
    )
    shards = (
        lax.psum_scatter(
            grad_query_w.astype(jnp.bfloat16), "wsh", scatter_dimension=0, tiled=True
        ).astype(jnp.float32),
        lax.psum_scatter(
            grad_key_w.astype(jnp.bfloat16), "wsh", scatter_dimension=0, tiled=True
        ).astype(jnp.float32),
        lax.psum_scatter(
            grad_value_w.astype(jnp.bfloat16), "wsh", scatter_dimension=0, tiled=True
        ).astype(jnp.float32),
        lax.psum_scatter(
            grad_out_w.astype(jnp.bfloat16), "wsh", scatter_dimension=0, tiled=True
        ).astype(jnp.float32),
        lax.psum_scatter(
            grad_up_w.astype(jnp.bfloat16), "wsh", scatter_dimension=0, tiled=True
        ).astype(jnp.float32),
        lax.psum_scatter(
            grad_down_w.astype(jnp.bfloat16), "wsh", scatter_dimension=0, tiled=True
        ).astype(jnp.float32),
        lax.psum_scatter(
            grad_query_b.astype(jnp.bfloat16), "wsh", scatter_dimension=0, tiled=True
        ).astype(jnp.float32),
        lax.psum_scatter(
            grad_value_b.astype(jnp.bfloat16), "wsh", scatter_dimension=0, tiled=True
        ).astype(jnp.float32),
        lax.psum_scatter(
            grad_out_b.astype(jnp.bfloat16), "wsh", scatter_dimension=0, tiled=True
        ).astype(jnp.float32),
        lax.psum_scatter(
            grad_attn_g.astype(jnp.bfloat16), "wsh", scatter_dimension=0, tiled=True
        ).astype(jnp.float32),
        lax.psum_scatter(
            grad_attn_s.astype(jnp.bfloat16), "wsh", scatter_dimension=0, tiled=True
        ).astype(jnp.float32),
        lax.psum_scatter(
            grad_up_b.astype(jnp.bfloat16), "wsh", scatter_dimension=0, tiled=True
        ).astype(jnp.float32),
        lax.psum_scatter(
            grad_down_b.astype(jnp.bfloat16), "wsh", scatter_dimension=0, tiled=True
        ).astype(jnp.float32),
        lax.psum_scatter(
            grad_final_g.astype(jnp.bfloat16), "wsh", scatter_dimension=0, tiled=True
        ).astype(jnp.float32),
        lax.psum_scatter(
            grad_final_s.astype(jnp.bfloat16), "wsh", scatter_dimension=0, tiled=True
        ).astype(jnp.float32),
    )
    totals = (
        lax.psum(shards[0].astype(jnp.bfloat16), "ctx").astype(jnp.float32),
        lax.psum(shards[1].astype(jnp.bfloat16), "ctx").astype(jnp.float32),
        lax.psum(shards[2].astype(jnp.bfloat16), "ctx").astype(jnp.float32),
        lax.psum(shards[3].astype(jnp.bfloat16), "ctx").astype(jnp.float32),
        lax.psum(shards[4].astype(jnp.bfloat16), "ctx").astype(jnp.float32),
        lax.psum(shards[5].astype(jnp.bfloat16), "ctx").astype(jnp.float32),
        lax.psum(shards[6].astype(jnp.bfloat16), "ctx").astype(jnp.float32),
        lax.psum(shards[7].astype(jnp.bfloat16), "ctx").astype(jnp.float32),
        lax.psum(shards[8].astype(jnp.bfloat16), "ctx").astype(jnp.float32),
        lax.psum(shards[9].astype(jnp.bfloat16), "ctx").astype(jnp.float32),
        lax.psum(shards[10].astype(jnp.bfloat16), "ctx").astype(jnp.float32),
        lax.psum(shards[11].astype(jnp.bfloat16), "ctx").astype(jnp.float32),
        lax.psum(shards[12].astype(jnp.bfloat16), "ctx").astype(jnp.float32),
        lax.psum(shards[13].astype(jnp.bfloat16), "ctx").astype(jnp.float32),
        lax.psum(shards[14].astype(jnp.bfloat16), "ctx").astype(jnp.float32),
    )
    return (
        layer_out.reshape(1, tok_rows, D),
        grad_inputs.astype(jnp.bfloat16).reshape(1, tok_rows, D),
        totals[0],
        totals[1],
        totals[2],
        totals[3],
        totals[4],
        totals[5],
        totals[6],
        totals[7],
        totals[8],
        totals[9],
        totals[10],
        totals[11],
        totals[12],
        totals[13],
        totals[14],
    )


def solution(mesh):
    return jax.shard_map(
        local,
        mesh=mesh,
        in_specs=(
            P("wsh", "ctx", None),
            P("wsh", "ctx", None),
            P("wsh", None),
            P("wsh", None),
            P("wsh", None),
            P("wsh", None),
            P("wsh", None),
            P("wsh", None),
            P("wsh", None),
            P("wsh"),
            P("wsh"),
            P("wsh"),
            P("wsh"),
            P("wsh"),
            P("wsh"),
            P("wsh"),
            P("wsh"),
            P("wsh"),
        ),
        out_specs=(
            P("wsh", "ctx", None),
            P("wsh", "ctx", None),
            P("wsh", None),
            P("wsh", None),
            P("wsh", None),
            P("wsh", None),
            P("wsh", None),
            P("wsh", None),
            P("wsh"),
            P("wsh"),
            P("wsh"),
            P("wsh"),
            P("wsh"),
            P("wsh"),
            P("wsh"),
            P("wsh"),
            P("wsh"),
        ),
        check_vma=False,
    )
```

profile of v0, /device:TPU:0, one launch (start us, length us, event | category | flops | bytes accessed | tf_op | source)
XLA Modules:
  0.0 1396.5 jit_solution(12322178087028742047)
XLA Ops:
  17.3 13.0 all-reduce.20
  33.8 15.2 %all-gather.10.cloned.1.call-done = bf16[768,768]{1,0:T(8,128)(2,1)} async-done(((bf16[192,768]{1,0:T(8,128)(2,1)}), bf16[768,768]{1,0:T(8,128)(2,1)}) %all-gather.10.cloned.1.call-update) | async-done | bytes 1179664 | tf_op jit(solution)/shard_map/all_gather | solution.py:143
  59.9 8.2 all-gather.14.cloned.1.call-done
  72.5 98.1 %all-gather.18.cloned.1.call-done = bf16[4096,12,64]{0,2,1:T(8,128)(2,1)} async-done(((bf16[512,12,64]{0,2,1:T(8,128)(2,1)}), bf16[4096,12,64]{0,2,1:T(8,128)(2,1)}) %all-gather.18.cloned.1.call-update) | async-done | bytes 6291472 | tf_op jit(solution)/shard_map/all_gather | solution.py:203
  177.0 94.2 %all-gather.12.cloned.1.call-done = bf16[4096,12,64]{0,2,1:T(8,128)(2,1)} async-done(((bf16[512,12,64]{0,2,1:T(8,128)(2,1)}), bf16[4096,12,64]{0,2,1:T(8,128)(2,1)}) %all-gather.12.cloned.1.call-update) | async-done | bytes 6291472 | tf_op jit(solution)/shard_map/all_gather | solution.py:202
  277.6 102.4 %while.34 = (s32[]{:T(128)}, f32[12,512]{1,0:T(8,128)S(1)}, f32[12,512]{1,0:T(8,128)S(1)}, f32[512,12,64]{0,2,1:T(8,128)S(1)}, s32[512]{0:T(512)S(1)}, /*index=5...) while((s32[]{:T(128)}, f32[12,512]{1,0:T(8,128)S(1)}, ...), condition=%wide.region_5.6_spmd.clone, body=%wide.region_1.5_spmd.clone.sunk | while | flops 847692288 | bytes 44710080 | solution.py:69
  385.3 8.4 multiply_convert_fusion
  434.5 331.9 %while.35 = (s32[]{:T(128)}, f32[512,12,64]{0,2,1:T(8,128)}, f32[4096,12,64]{0,2,1:T(8,128)}, f32[4096,12,64]{0,2,1:T(8,128)}, bf16[8,512,12,64]{1,3,2,0:T(8,128...) while((s32[]{:T(128)}, f32[512,12,64]{0,2,1:T(8,128)}, ...), condition=%wide.region_17.18_spmd.clone, body=%wide.region_15.17_spmd.clone.sunk | while | flops 2047357440 | bytes 91314544 | solution.py:117
  459.3 8.2 dynamic_update_slice.16
  467.4 8.5 dynamic_update_slice.17
  509.1 8.5 dynamic_update_slice.17
  550.8 8.5 dynamic_update_slice.17
  584.4 8.1 dynamic_update_slice.16
  592.5 8.5 dynamic_update_slice.17
  626.1 8.2 dynamic_update_slice.16
  634.3 8.5 dynamic_update_slice.17
  667.9 8.2 dynamic_update_slice.16
  676.0 8.5 dynamic_update_slice.17
  709.6 8.2 dynamic_update_slice.16
  717.8 8.6 dynamic_update_slice.17
  766.5 8.2 convert_element_type.290
  774.7 8.1 convert_element_type.288
  788.0 103.6 %reduce-scatter.17.cloned.1.call-done = bf16[512,12,64]{0,2,1:T(8,128)(2,1)} async-done(((bf16[4096,12,64]{0,2,1:T(8,128)(2,1)}), bf16[512,12,64]{0,2,1:T(8,128)(2,1)}) %reduce-scatter.17.cloned.1.call-update) | async-done | bytes 786448 | tf_op jit(solution)/shard_map/reduce_scatter | solution.py:289
  895.0 117.6 %reduce-scatter.15.cloned.1.call-done = bf16[512,12,64]{0,2,1:T(8,128)(2,1)} async-done(((bf16[4096,12,64]{0,2,1:T(8,128)(2,1)}), bf16[512,12,64]{0,2,1:T(8,128)(2,1)}) %reduce-scatter.15.cloned.1.call-update) | async-done | bytes 786448 | tf_op jit(solution)/shard_map/reduce_scatter | solution.py:286
  1042.0 26.5 %reduce-scatter.29.cloned.1.call-done = bf16[192,768]{1,0:T(8,128)(2,1)} async-done(((bf16[768,768]{1,0:T(8,128)(2,1)}), bf16[192,768]{1,0:T(8,128)(2,1)}) %reduce-scatter.29.cloned.1.call-update) | async-done | bytes 294928
  1070.3 26.4 %reduce-scatter.27.cloned.1.call-done = bf16[192,768]{1,0:T(8,128)(2,1)} async-done(((bf16[768,768]{1,0:T(8,128)(2,1)}), bf16[192,768]{1,0:T(8,128)(2,1)}) %reduce-scatter.27.cloned.1.call-update) | async-done | bytes 294928
  1098.6 26.5 %reduce-scatter.19.cloned.1.call-done = bf16[192,768]{1,0:T(8,128)(2,1)} async-done(((bf16[768,768]{1,0:T(8,128)(2,1)}), bf16[192,768]{1,0:T(8,128)(2,1)}) %reduce-scatter.19.cloned.1.call-update) | async-done | bytes 294928 | tf_op jit(solution)/shard_map/reduce_scatter | solution.py:320
  1125.1 50.3 %reduce-scatter.21.cloned.1.call-done = bf16[192,3072]{1,0:T(8,128)(2,1)} async-done(((bf16[768,3072]{1,0:T(8,128)(2,1)}), bf16[192,3072]{1,0:T(8,128)(2,1)}) %reduce-scatter.21.cloned.1.call-update) | async-done | bytes 1179664 | tf_op jit(solution)/shard_map/reduce_scatter | solution.py:323
  1175.4 50.4 %reduce-scatter.23.cloned.1.call-done = bf16[768,768]{1,0:T(8,128)(2,1)} async-done(((bf16[3072,768]{1,0:T(8,128)(2,1)}), bf16[768,768]{1,0:T(8,128)(2,1)}) %reduce-scatter.23.cloned.1.call-update) | async-done | bytes 1179664 | tf_op jit(solution)/shard_map/reduce_scatter | solution.py:326
  1231.5 10.7 all-reduce.19
  1242.9 23.3 %all-reduce.17 = (bf16[192]{0:T(256)(128)(2,1)S(1)}, bf16[192]{0:T(256)(128)(2,1)S(1)}, bf16[192]{0:T(256)(128)(2,1)S(1)}, bf16[192]{0:T(256)(128)(2,1)S(1)}, bf...) all-reduce(bf16[192]{0:T(256)(128)(2,1)S(1)} %dynamic-slice.9, ...), channel_id=1, replica_groups=mesh['ctx'=8,'wsh'=4] {'ctx'}, use_global_device_ids=true, to_apply=%region_34.35 | all-reduce | flops 2304 | bytes 9216 | tf_op jit(solution)/shard_map/psum | solution.py:364
  1276.5 103.7 %all-reduce.23.cloned.1.call-done = (bf16[192,768]{0,1:T(8,128)(2,1)}, bf16[192,768]{0,1:T(8,128)(2,1)}, bf16[192,768]{0,1:T(8,128)(2,1)}, bf16[192,768]{1,0:T(8...) async-done(((bf16[192,768]{0,1:T(8,128)(2,1)}, bf16[192,768]{0,1:T(8,128)(2,1)}, bf16[192,768]{0,1:T(8,128)(2,1)}, bf16[192,768]{1,0:T(8,128)(2,1)}, ...) | async-done | bytes 3538960 | tf_op jit(solution)/shard_map/psum | solution.py:358
  (509 shorter events, 468.9 us)
Async XLA Ops:
  7.2 23.1 %all-gather.16.cloned.1.call-start = ((), (), s32[]{:S(2)}) async-start(), calls=%async_computation.11 | async-start | bytes 1474560 | tf_op jit(solution)/shard_map/all_gather | solution.py:144
  7.9 41.1 %all-gather.10.cloned.1.call-start = ((), (), s32[]{:S(2)}) async-start(), calls=%async_computation.8 | async-start | bytes 1474560 | tf_op jit(solution)/shard_map/all_gather | solution.py:143
  8.7 59.4 %all-gather.14.cloned.1.call-start = ((), (), s32[]{:S(2)}) async-start(), calls=%async_computation.10 | async-start | bytes 1474560 | tf_op jit(solution)/shard_map/all_gather | solution.py:142
  9.4 161.1 %all-gather.18.cloned.1.call-start = ((), (), s32[]{:S(2)}) async-start(), calls=%async_computation.12 | async-start | bytes 7077888 | tf_op jit(solution)/shard_map/all_gather | solution.py:203
  32.6 16.5 %copy-start.55 = (bf16[1,512,768]{2,1,0:T(8,128)(2,1)S(1)}, bf16[1,512,768]{2,1,0:T(8,128)(2,1)}, u32[]{:S(2)}) copy-start(bf16[1,512,768]{2,1,0:T(8,128)(2,1)} %param.22) | copy-start | bytes 2359300
  33.8 237.4 %all-gather.12.cloned.1.call-start = ((), (), s32[]{:S(2)}) async-start(), calls=%async_computation.9 | async-start | bytes 7077888 | tf_op jit(solution)/shard_map/all_gather | solution.py:202
  52.3 15.8 %copy-start.56 = (bf16[1,512,768]{2,1,0:T(8,128)(2,1)S(1)}, bf16[1,512,768]{2,1,0:T(8,128)(2,1)}, u32[]{:S(2)}) copy-start(bf16[1,512,768]{2,1,0:T(8,128)(2,1)} %param.22) | copy-start | bytes 2359300
  52.3 328.8 %all-gather.20.cloned.1.call-start = ((), (), s32[]{:S(2)}) async-start(), calls=%async_computation.13 | async-start | bytes 1474560 | tf_op jit(solution)/shard_map/all_gather | solution.py:145
  52.9 332.4 %all-gather.22.cloned.1.call-start = ((), (), s32[]{:S(2)}) async-start(), calls=%async_computation.14 | async-start | bytes 5898240 | tf_op jit(solution)/shard_map/all_gather | solution.py:146
  53.6 340.0 %all-gather.24.cloned.1.call-start = ((), (), s32[]{:S(2)}) async-start(), calls=%async_computation.15 | async-start | bytes 5898240 | tf_op jit(solution)/shard_map/all_gather | solution.py:147
  54.4 837.2 %reduce-scatter.17.cloned.1.call-start = ((), (), s32[]{:S(2)}) async-start(), calls=%async_computation.17 | async-start | bytes 7077888 | tf_op jit(solution)/shard_map/reduce_scatter | solution.py:289
  54.6 360.8 %copy-start.39 = (f32[768]{0:T(1024)}, f32[768]{0:T(1024)S(1)}, u32[]{:S(2)}) copy-start(f32[768]{0:T(1024)S(1)} %convert_element_type.270) | copy-start | bytes 9220
  54.7 339.0 %copy-start.47 = (f32[768]{0:T(1024)}, f32[768]{0:T(1024)S(1)}, u32[]{:S(2)}) copy-start(f32[768]{0:T(1024)S(1)} %convert_element_type.271) | copy-start | bytes 9220
  54.7 348.6 %copy-start.28 = (f32[768]{0:T(1024)}, f32[768]{0:T(1024)S(1)}, u32[]{:S(2)}) copy-start(f32[768]{0:T(1024)S(1)} %convert_element_type.276) | copy-start | bytes 9220
  383.8 31.7 %copy-start.35 = (f32[512]{0:T(512)}, f32[512]{0:T(512)S(1)}, u32[]{:S(2)}) copy-start(f32[512]{0:T(512)S(1)} %broadcast_multiply_fusion.1) | copy-start | bytes 6148
  385.2 30.3 %copy-start.44 = (f32[512]{0:T(512)}, f32[512]{0:T(512)S(1)}, u32[]{:S(2)}) copy-start(f32[512]{0:T(512)S(1)} %fusion.56) | copy-start | bytes 6148
  393.6 11.2 copy-start.59
  467.4 8.5 copy-start.13
  550.8 8.6 copy-start.13
  717.8 8.6 copy-start.13
  774.7 237.9 %reduce-scatter.15.cloned.1.call-start = ((), (), s32[]{:S(2)}) async-start(), calls=%async_computation.16 | async-start | bytes 7077888 | tf_op jit(solution)/shard_map/reduce_scatter | solution.py:286
  782.9 257.2 %reduce-scatter.25.cloned.1.call-start = ((), (), s32[]{:S(2)}) async-start(), calls=%async_computation.21 | async-start | bytes 1474560
  787.9 280.5 %reduce-scatter.29.cloned.1.call-start = ((), (), s32[]{:S(2)}) async-start(), calls=%async_computation.23 | async-start | bytes 1474560
  895.0 201.8 %reduce-scatter.27.cloned.1.call-start = ((), (), s32[]{:S(2)}) async-start(), calls=%async_computation.22 | async-start | bytes 1474560
  1016.1 109.0 %reduce-scatter.19.cloned.1.call-start = ((), (), s32[]{:S(2)}) async-start(), calls=%async_computation.18 | async-start | bytes 1474560 | tf_op jit(solution)/shard_map/reduce_scatter | solution.py:320
  1018.0 157.3 %reduce-scatter.21.cloned.1.call-start = ((), (), s32[]{:S(2)}) async-start(), calls=%async_computation.19 | async-start | bytes 5898240 | tf_op jit(solution)/shard_map/reduce_scatter | solution.py:323
  1024.8 201.0 %reduce-scatter.23.cloned.1.call-start = ((), (), s32[]{:S(2)}) async-start(), calls=%async_computation.20 | async-start | bytes 5898240 | tf_op jit(solution)/shard_map/reduce_scatter | solution.py:326
  1032.7 347.6 %all-reduce.23.cloned.1.call-start = ((), (), s32[]{:S(2)}) async-start(), calls=%async_computation.24 | async-start | bytes 7667712 | tf_op jit(solution)/shard_map/psum | solution.py:358
  1227.8 43.5 %copy-start.4 = (f32[512,768]{1,0:T(8,128)S(1)}, f32[512,768]{1,0:T(8,128)}, u32[]{:S(2)}) copy-start(f32[512,768]{1,0:T(8,128)} %copy-done.3) | copy-start | bytes 4718596
  1227.8 43.5 %copy-start.29 = (f32[768]{0:T(1024)S(1)}, f32[768]{0:T(1024)}, u32[]{:S(2)}) copy-start(f32[768]{0:T(1024)} %copy-done.28) | copy-start | bytes 9220
  1227.8 43.5 %copy-start.32 = (f32[512]{0:T(512)S(1)}, f32[512]{0:T(512)}, u32[]{:S(2)}) copy-start(f32[512]{0:T(512)} %copy-done.31) | copy-start | bytes 6148
  1227.8 43.4 %copy-start.34 = (f32[512]{0:T(512)S(1)}, f32[512]{0:T(512)}, u32[]{:S(2)}) copy-start(f32[512]{0:T(512)} %copy-done.33) | copy-start | bytes 6148
  (76 other events, 266.5 us)
Sparse Core Ops, SparseCore 0:
  9.6 20.4 all-gather.15
  31.6 17.3 all-gather.9
  50.6 17.4 all-gather.13
  70.6 99.9 all-gather.17
  173.0 98.1 all-gather.11
  272.6 15.6 all-gather.19
  289.8 37.4 all-gather.21
  328.9 37.4 all-gather.23
  774.8 116.7 reduce-scatter.16
  895.0 117.5 reduce-scatter.14
  1015.2 24.8 reduce-scatter.24
  1042.7 25.6 reduce-scatter.28
  1071.0 25.7 reduce-scatter.26
  1099.3 25.7 reduce-scatter.18
  1127.5 47.8 reduce-scatter.20
  1177.9 47.8 reduce-scatter.22
  1230.7 149.5 all-reduce.22
where the time goes:
time: 1410 us; the launch traced here: 1400 us
  waiting for transfers between devices  732 us (52%)
  matrix products  298 us (21%)
  local copies, waits for them, and re-layouts  205 us (15%)
  other arithmetic  74.4 us (5%)
  blocking collectives  52 us (4%)
  loops' own time  17.4 us (1%)
  between operations  17.4 us (1%)
    reduce_scatter x1, waiting for transfers between devices, local(): lax.psum_scatter(grad_keys_all.astype(jnp.bfloat16), 'ctx', scatter_dimen...  118 us
    psum x1, waiting for transfers between devices, local(): lax.psum(shards[0].astype(jnp.bfloat16), 'ctx').astype(jnp.float32)  104 us
    reduce_scatter x1, waiting for transfers between devices, local(): lax.psum_scatter(grad_values_all.astype(jnp.bfloat16), 'ctx', scatter_dim...  104 us
    all_gather x1, waiting for transfers between devices, local(): lax.all_gather(values_loc, 'ctx', axis=0, tiled=True)  98.1 us
    all_gather x1, waiting for transfers between devices, local(): lax.all_gather(keys_loc, 'ctx', axis=0, tiled=True)  94.2 us
    dynamic_update_slice x8, local copies, waits for them, and re-layouts, key_one_block(): lax.dynamic_update_slice_in_dim(grad_values, old_values + value_term, blo...  67.6 us
    unnamed x20, waiting for transfers between devices  64.4 us
    dynamic_update_slice x8, local copies, waits for them, and re-layouts, key_one_block(): lax.dynamic_update_slice_in_dim(grad_keys, old_keys + key_term, block_fir...  64.3 us
  transfers between devices with their start and end apart: 17, of which 13 were waited for; matrix products, arithmetic and copies ran while one was open for 14% of the time, Pallas kernels for 0%

commit v1 on v0

v1 whole, which is shorter than its diff:
```python
import functools

import jax
import jax.numpy as jnp
from jax import lax
from jax.experimental import pallas as pl
from jax.experimental.pallas import tpu as pltpu
from jax.sharding import PartitionSpec as P

D = 768
HEADS = 12
HD = 64
SCALE = 0.125
EPS = 1e-12
ROOT_HALF = 0.7071067811865476
BF = jnp.bfloat16
F32 = jnp.float32
NT = (((1,), (1,)), ((), ()))
NN = (((1,), (0,)), ((), ()))
TN = (((0,), (0,)), ((), ()))


def layer_norm(values, gain_vec, shift_vec):
    average = jnp.mean(values, axis=-1, keepdims=True)
    centred = values - average
    variance = jnp.mean(centred * centred, axis=-1, keepdims=True)
    return centred * lax.rsqrt(variance + EPS) * gain_vec + shift_vec


def gelu_act(values):
    return 0.5 * values * (1.0 + lax.erf(values * ROOT_HALF))


def key_range(doc_start, first_row, rows, stream_rows, tile):
    pos = jnp.arange(rows // tile, dtype=jnp.int32) * tile + first_row
    last = pos + tile - 1
    low = jnp.max(jnp.where(doc_start[None, :] <= pos[:, None], doc_start[None, :], 0), axis=1)
    high = jnp.min(
        jnp.where(doc_start[None, :] > last[:, None], doc_start[None, :], stream_rows), axis=1
    )
    first = low // 128 * 128
    count = (high - first + 255) // 256
    first = jnp.minimum(first, stream_rows - count * 256)
    return jnp.stack([first, count], axis=1).astype(jnp.int32)


def document_lanes(doc_start, first_row, rows, stream_rows):
    far = jnp.full((128 - doc_start.shape[0],), 2**30, jnp.int32)
    starts = jnp.concatenate([doc_start, far])
    ends = jnp.concatenate([doc_start[1:], jnp.full((1,), stream_rows, jnp.int32), far])
    query_pos = first_row + jnp.arange(rows, dtype=jnp.int32)[:, None]
    key_pos = jnp.arange(stream_rows, dtype=jnp.int32)[:, None]
    query_doc = ((query_pos >= starts) & (query_pos < ends)).astype(BF)
    key_doc = jnp.where((key_pos >= starts) & (key_pos < ends), 0.0, -1e30).astype(BF)
    return query_doc, key_doc


def stack_heads(x, extra=None):
    lane = lax.broadcasted_iota(jnp.int32, x.shape, 1)
    zero = jnp.zeros_like(x)
    lo = jnp.where(lane < 64, x, zero)
    hi = jnp.where(lane < 64, zero, x)
    if extra is not None:
        lo = jnp.concatenate([lo, extra], axis=1)
        hi = jnp.concatenate([hi, extra], axis=1)
    return jnp.concatenate([lo, hi], axis=0)

def pick_heads(x, tq):
    return jnp.concatenate([x[:64, :tq], x[64:, tq:]], axis=0)

def two_level(start, count, tk, body, init):
    big = tk // 256
    whole = count // big
    def large(t, c):
        return body(pl.multiple_of(t * tk, 256), pl.multiple_of(start + t * tk, 128), tk, c)
    def small(t, c):
        return body(pl.multiple_of(t * 256, 256), pl.multiple_of(start + t * 256, 128), 256, c)
    c = lax.fori_loop(0, whole, large, init)
    return lax.fori_loop(whole * big, count, small, c)

def fwd_kernel(tk, bounds, q_ref, qaug_ref, k_ref, kaug_ref, v_ref, ot_ref, lse_ref, s_scr, acc):
    qi = pl.program_id(1)
    start, count = bounds[qi, 0], bounds[qi, 1]
    tq = q_ref.shape[0]
    rhs = stack_heads(q_ref[...], qaug_ref[...])

    def scores(loc, off, size, m):
        lhs = jnp.concatenate([k_ref[pl.ds(off, size), :], kaug_ref[pl.ds(off, size), :]], axis=1)
        s = lax.dot_general(lhs, rhs, NT, preferred_element_type=F32)
        s_scr[pl.ds(loc, size), :] = s
        return jnp.maximum(m, jnp.max(s.reshape(size // 8, 8, 2 * tq), axis=0))

    m8 = two_level(start, count, tk, scores, jnp.full((8, 2 * tq), -3e38, F32))
    m = jnp.max(m8, axis=0, keepdims=True)
    acc[...] = jnp.zeros_like(acc)

    def mix(loc, off, size, l8):
        p = jnp.exp(s_scr[pl.ds(loc, size), :] - m)
        acc[...] += lax.dot_general(v_ref[pl.ds(off, size), :], p.astype(BF), TN, preferred_element_type=F32)
        return l8 + jnp.sum(p.reshape(size // 8, 8, 2 * tq), axis=0)

    l8 = two_level(start, count, tk, mix, jnp.zeros((8, 2 * tq), F32))
    l = jnp.sum(l8, axis=0, keepdims=True)
    ot_ref[...] = pick_heads(acc[...] / l, tq)
    lse = m + jnp.log(l)
    lse_ref[0] = jnp.concatenate([lse[:, :tq], lse[:, tq:]], axis=0)

def attn_fwd(bounds, q, qaug, k, kaug, v, *, tq=512, tk=768):
    T, D = q.shape
    S = k.shape[0]
    pairs = D // 128
    return pl.pallas_call(
        functools.partial(fwd_kernel, tk),
        out_shape=(jax.ShapeDtypeStruct((D, T), F32), jax.ShapeDtypeStruct((pairs, 2, T), F32)),
        grid_spec=pltpu.PrefetchScalarGridSpec(
            num_scalar_prefetch=1, grid=(pairs, T // tq),
            in_specs=[pl.BlockSpec((tq, 128), lambda h, i, b: (i, h)),
                      pl.BlockSpec((tq, 128), lambda h, i, b: (i, 0)),
                      pl.BlockSpec((S, 128), lambda h, i, b: (0, h)),
                      pl.BlockSpec((S, 128), lambda h, i, b: (0, 0)),
                      pl.BlockSpec((S, 128), lambda h, i, b: (0, h))],
            out_specs=(pl.BlockSpec((128, tq), lambda h, i, b: (h, i)),
                       pl.BlockSpec((1, 2, tq), lambda h, i, b: (h, 0, i))),
            scratch_shapes=[pltpu.VMEM((S, 2 * tq), F32), pltpu.VMEM((128, 2 * tq), F32)]),
        name="attend",
    )(bounds, q, qaug, k, kaug, v)

def bwd_kernel(tk, bounds, q_ref, qaug_ref, do_ref, lse_ref, ot_ref, k_ref, kaug_ref, v_ref,
               dqt_ref, dk_ref, dv_ref, dk_acc, dv_acc, dq_acc):
    qi = pl.program_id(1)
    start, count = bounds[qi, 0], bounds[qi, 1]
    tq = q_ref.shape[0]

    @pl.when(qi == 0)
    def _():
        dk_acc[...] = jnp.zeros_like(dk_acc)
        dv_acc[...] = jnp.zeros_like(dv_acc)

    qs = stack_heads(q_ref[...])
    qrhs = stack_heads(q_ref[...], qaug_ref[...])
    dos = stack_heads(do_ref[...])
    lse = jnp.concatenate([lse_ref[0, 0:1, :], lse_ref[0, 1:2, :]], axis=1)
    mixed = ot_ref[...] * do_ref[...].astype(F32).T
    delta = jnp.concatenate(
        [jnp.sum(mixed[:64], axis=0, keepdims=True), jnp.sum(mixed[64:], axis=0, keepdims=True)], axis=1
    )
    dq_acc[...] = jnp.zeros_like(dq_acc)

    def step(loc, off, size, carry):
        rows = pl.ds(off, size)
        lhs = jnp.concatenate([k_ref[rows, :], kaug_ref[rows, :]], axis=1)
        x = lax.dot_general(lhs, qrhs, NT, preferred_element_type=F32)
        y = lax.dot_general(v_ref[rows, :], dos, NT, preferred_element_type=F32)
        p = jnp.exp(x - lse)
        ds = (p * (y - delta)).astype(BF)
        pb = p.astype(BF)
        dv_acc[rows, :] += lax.dot_general(pb, dos, NN, preferred_element_type=F32)
        dk_acc[rows, :] += lax.dot_general(ds, qs, NN, preferred_element_type=F32)
        dq_acc[...] += lax.dot_general(k_ref[rows, :], ds, TN, preferred_element_type=F32)
        return carry

    two_level(start, count, tk, step, 0)
    dqt_ref[...] = (pick_heads(dq_acc[...], tq) * 0.125).astype(BF)

    @pl.when(qi == pl.num_programs(1) - 1)
    def _():
        dk_ref[...] = dk_acc[...].astype(BF)
        dv_ref[...] = dv_acc[...].astype(BF)

def attn_bwd(bounds, q, qaug, do, lse, ot, k, kaug, v, *, tq=512, tk=768):
    T, D = q.shape
    S = k.shape[0]
    pairs = D // 128
    row = lambda h, i, b: (h, 0, i)
    return pl.pallas_call(
        functools.partial(bwd_kernel, tk),
        out_shape=(jax.ShapeDtypeStruct((D, T), BF), jax.ShapeDtypeStruct((S, D), BF), jax.ShapeDtypeStruct((S, D), BF)),
        grid_spec=pltpu.PrefetchScalarGridSpec(
            num_scalar_prefetch=1, grid=(pairs, T // tq),
            in_specs=[pl.BlockSpec((tq, 128), lambda h, i, b: (i, h)),
                      pl.BlockSpec((tq, 128), lambda h, i, b: (i, 0)),
                      pl.BlockSpec((tq, 128), lambda h, i, b: (i, h)),
                      pl.BlockSpec((1, 2, tq), row),
                      pl.BlockSpec((128, tq), lambda h, i, b: (h, i)),
                      pl.BlockSpec((S, 128), lambda h, i, b: (0, h)),
                      pl.BlockSpec((S, 128), lambda h, i, b: (0, 0)),
                      pl.BlockSpec((S, 128), lambda h, i, b: (0, h))],
            out_specs=(pl.BlockSpec((128, tq), lambda h, i, b: (h, i)),
                       pl.BlockSpec((S, 128), lambda h, i, b: (0, h)),
                       pl.BlockSpec((S, 128), lambda h, i, b: (0, h))),
            scratch_shapes=[pltpu.VMEM((S, 128), F32), pltpu.VMEM((S, 128), F32), pltpu.VMEM((128, 2 * tq), F32)]),
        name="attend_back",
    )(bounds, q, qaug, do, lse, ot, k, kaug, v)


def local(
    tokens,
    cotangent,
    doc_starts,
    query_weight,
    key_weight,
    value_weight,
    out_weight,
    up_weight,
    down_weight,
    query_bias,
    value_bias,
    out_bias,
    attn_gain,
    attn_shift,
    up_bias,
    down_bias,
    final_gain,
    final_shift,
):
    inputs = tokens[0]
    doc_start = doc_starts[0]
    tok_rows = inputs.shape[0]
    stream_rows = tok_rows * lax.axis_size("ctx")
    first_row = lax.axis_index("ctx") * tok_rows
    tile = min(tok_rows, 512)
    bounds = key_range(doc_start, first_row, tok_rows, stream_rows, tile)
    query_doc, key_doc = document_lanes(doc_start, first_row, tok_rows, stream_rows)

    def gather(x):
        return lax.all_gather(x, "wsh", axis=0, tiled=True)

    all_tokens = lax.all_gather(inputs, "ctx", axis=0, tiled=True)
    qkv_w = gather(jnp.concatenate([query_weight, key_weight, value_weight], axis=1))
    query_w, key_w, value_w = qkv_w[:, :D], qkv_w[:, D : 2 * D], qkv_w[:, 2 * D :]
    small = gather(
        jnp.stack([query_bias, value_bias, out_bias, attn_gain, attn_shift, down_bias, final_gain, final_shift], axis=1)
    ).astype(F32)
    query_b, value_b, out_b, attn_g, attn_s, down_b, final_g, final_s = [small[:, i] for i in range(8)]
    up_b = gather(up_bias).astype(F32)
    out_w = gather(out_weight)
    up_w = gather(up_weight)
    down_w = gather(down_weight)

    queries = (jnp.dot(inputs, query_w, preferred_element_type=F32) + query_b).astype(BF) * jnp.asarray(SCALE, BF)
    keys = jnp.dot(all_tokens, key_w, preferred_element_type=F32).astype(BF)
    values = (jnp.dot(all_tokens, value_w, preferred_element_type=F32) + value_b).astype(BF)
    mixed_t, log_rows = attn_fwd(bounds, queries, query_doc, keys, key_doc, values, tq=tile)
    attn_t = mixed_t.astype(BF)
    inputs_f = inputs.astype(F32)
    branch = lax.dot_general(attn_t, out_w, TN, preferred_element_type=F32) + out_b
    first_norm, first_pull = jax.vjp(layer_norm, inputs_f + branch, attn_g, attn_s)
    first_b = first_norm.astype(BF)
    up_f = jnp.dot(first_b, up_w, preferred_element_type=F32) + up_b
    act_f, act_pull = jax.vjp(gelu_act, up_f)
    act_b = act_f.astype(BF)
    down_f = jnp.dot(act_b, down_w, preferred_element_type=F32) + down_b
    final_f, final_pull = jax.vjp(layer_norm, first_norm + down_f, final_g, final_s)
    layer_out = final_f.astype(BF)

    grad_sum2, grad_final_g, grad_final_s = final_pull(cotangent[0].astype(F32))
    grad_down = grad_sum2.astype(BF)
    grad_down_w = jnp.einsum("tf,td->fd", act_b, grad_down, preferred_element_type=F32)
    grad_down_b = jnp.sum(grad_down.astype(F32), axis=0)
    grad_act = jnp.einsum("td,fd->tf", grad_down, down_w, preferred_element_type=F32)
    (grad_up_f,) = act_pull(grad_act)
    grad_up = grad_up_f.astype(BF)
    grad_up_w = jnp.einsum("td,tf->df", first_b, grad_up, preferred_element_type=F32)
    grad_up_b = jnp.sum(grad_up.astype(F32), axis=0)
    grad_first = grad_sum2 + jnp.einsum("tf,df->td", grad_up, up_w, preferred_element_type=F32)
    grad_sum1, grad_attn_g, grad_attn_s = first_pull(grad_first)
    grad_branch = grad_sum1.astype(BF)
    grad_out_w = jnp.dot(attn_t, grad_branch, preferred_element_type=F32)
    grad_out_b = jnp.sum(grad_branch.astype(F32), axis=0)
    grad_attn = jnp.einsum("te,de->td", grad_branch, out_w, preferred_element_type=F32).astype(BF)
    grad_q_t, grad_k, grad_v = attn_bwd(
        bounds, queries, query_doc, grad_attn, log_rows, mixed_t, keys, key_doc, values, tq=tile
    )
    grad_all = jnp.einsum("te,de->td", grad_k, key_w, preferred_element_type=F32)
    grad_all = grad_all + jnp.einsum("te,de->td", grad_v, value_w, preferred_element_type=F32)
    grad_own = lax.psum_scatter(grad_all.astype(BF), "ctx", scatter_dimension=0, tiled=True)
    grad_query_w = jnp.einsum("td,et->de", inputs, grad_q_t, preferred_element_type=F32)
    grad_key_w = jnp.einsum("td,te->de", all_tokens, grad_k, preferred_element_type=F32)
    grad_value_w = jnp.einsum("td,te->de", all_tokens, grad_v, preferred_element_type=F32)
    grad_query_b = jnp.sum(grad_q_t.astype(F32), axis=1)
    grad_value_b = jnp.sum(grad_v.astype(F32), axis=0)
    grad_inputs = grad_sum1 + lax.dot_general(
        grad_q_t, query_w, (((0,), (1,)), ((), ())), preferred_element_type=F32
    )
    grad_inputs = grad_inputs + grad_own.astype(F32)

    def total(g):
        part = lax.psum_scatter(g.astype(BF), "wsh", scatter_dimension=0, tiled=True)
        return lax.psum(part, "ctx").astype(F32)

    grads = [
        grad_query_w, grad_key_w, grad_value_w, grad_out_w, grad_up_w, grad_down_w,
        grad_query_b, grad_value_b, grad_out_b, grad_attn_g, grad_attn_s, grad_up_b,
        grad_down_b, grad_final_g, grad_final_s,
    ]
    return (
        layer_out.reshape(1, tok_rows, D),
        grad_inputs.astype(BF).reshape(1, tok_rows, D),
        *[total(g) for g in grads],
    )


def solution(mesh):
    rows, mat, vec = P("wsh", "ctx", None), P("wsh", None), P("wsh")
    return jax.shard_map(
        local,
        mesh=mesh,
        in_specs=(rows, rows, mat) + (mat,) * 6 + (vec,) * 9,
        out_specs=(rows, rows) + (mat,) * 6 + (vec,) * 9,
        check_vma=False,
    )
```

time: 1410 us -> 845 us (0.60)
  matrix products: 298 us -> 109 us
  local copies, waits for them, and re-layouts: 205 us -> 21.6 us
  waiting for transfers between devices: 732 us -> 580 us
  other arithmetic: 74.4 us -> 25.7 us
  Pallas kernels: 0 us -> 35.5 us
  loops' own time: 17.4 us -> 0 us
    dot_general x74 -> x18, matrix products: 298 us -> 109 us  [the longest x1 9.88 us: local(): jnp.einsum('td,te->de', all_tokens, grad_v, preferred_element_type=F32)]
    reduce_scatter x5 -> x4, waiting for transfers between devices: 348 us -> 203 us  [the longest x3 127 us: total(): lax.psum_scatter(g.astype(BF), 'wsh', scatter_dimension=0, tiled=True)]
    dynamic_update_slice x16 -> x0, local copies, waits for them, and re-layouts: 132 us -> none  [the longest x8 67.6 us: key_one_block(): lax.dynamic_update_slice_in_dim(grad_values, old_values + value_term, blo...]
    all_gather x8 -> x5, waiting for transfers between devices: 216 us -> 163 us  [the longest x1 98.3 us: local(): all_tokens = lax.all_gather(inputs, 'ctx', axis=0, tiled=True)]
    psum x1, waiting for transfers between devices: 104 us -> 150 us  [total(): return lax.psum(part, 'ctx').astype(F32)]
    pallas_call x0 -> x2, Pallas kernels: none -> 35.5 us  [the longest x1 21.7 us: attn_bwd(): pl.pallas_call(functools.partial(bwd_kernel, tk), out_shape=(jax.ShapeDty...]
    reduce_sum x30 -> x4, other arithmetic: 28.8 us -> 4.32 us  [the longest x1 3.71 us: local(): grad_value_b = jnp.sum(grad_v.astype(F32), axis=0)]
    another operation x2 -> x0, loops' own time: 17.4 us -> none  [the longest x1 16.2 us: key_side_fold(): lax.scan(key_one_block, running, (key_blocks, value_blocks, block_starts))]
  transfers between devices with their start and end apart: 17 -> 13, of which waited for: 13 -> 12; matrix products, arithmetic and copies ran while one was open for 14% -> 13% of each run, Pallas kernels for 0% -> 2%
where the time goes in v1:
time: 845 us; the launch traced here: 837 us
  waiting for transfers between devices  580 us (69%)
  matrix products  109 us (13%)
  blocking collectives  45.6 us (5%)
  Pallas kernels  35.5 us (4%)
  other arithmetic  25.7 us (3%)
  local copies, waits for them, and re-layouts  21.6 us (3%)
  between operations  19.2 us (2%)
    psum x1, waiting for transfers between devices, total(): return lax.psum(part, 'ctx').astype(F32)  150 us
    reduce_scatter x3, waiting for transfers between devices, total(): lax.psum_scatter(g.astype(BF), 'wsh', scatter_dimension=0, tiled=True)  127 us
    all_gather x1, waiting for transfers between devices, local(): all_tokens = lax.all_gather(inputs, 'ctx', axis=0, tiled=True)  98.3 us
    reduce_scatter x1, waiting for transfers between devices, local(): lax.psum_scatter(grad_all.astype(BF), 'ctx', scatter_dimension=0, tiled=T...  75.8 us
    all_gather x4, waiting for transfers between devices, gather(): return lax.all_gather(x, 'wsh', axis=0, tiled=True)  64.7 us
    unnamed x16, waiting for transfers between devices  63.6 us
    psum x1, blocking collectives, total(): return lax.psum(part, 'ctx').astype(F32)  23.4 us
    pallas_call x1, Pallas kernels, attn_bwd(): pl.pallas_call(functools.partial(bwd_kernel, tk), out_shape=(jax.ShapeDty...  21.7 us
  transfers between devices with their start and end apart: 13, of which 12 were waited for; matrix products, arithmetic and copies ran while one was open for 13% of the time, Pallas kernels for 2%

profile of v1, /device:TPU:0, one launch (start us, length us, event | category | flops | bytes accessed | tf_op | source)
XLA Modules:
  0.0 837.4 jit_solution(7813891210407396098)
XLA Ops:
  16.4 6.2 all-gather.1
  22.7 5.4 all-gather.2
  31.1 12.7 %all-gather.9.cloned.1.call-done = bf16[768,2304]{1,0:T(8,128)(2,1)} async-done(((bf16[192,2304]{1,0:T(8,128)(2,1)}), bf16[768,2304]{1,0:T(8,128)(2,1)}) %all-gather.9.cloned.1.call-update) | async-done | bytes 3538960 | tf_op jit(solution)/shard_map/all_gather | solution.py:226
  46.7 98.3 %all-gather.17.cloned.1.call-done = bf16[1,4096,768]{2,1,0:T(8,128)(2,1)} async-done(((bf16[1,512,768]{2,1,0:T(8,128)(2,1)}), bf16[1,4096,768]{2,1,0:T(8,128)(2,1)}) %all-gather.17.cloned.1.call-update) | async-done | bytes 6291472 | tf_op jit(solution)/shard_map/all_gather | solution.py:228
  145.0 9.5 %fusion.8.k_ref = bf16[4096,768]{1,0:T(8,128)(2,1)} fusion(bf16[1,4096,768]{2,1,0:T(8,128)(2,1)} %all-gather.17.cloned.1.call-done, bf16[768,2304]{1,0:T(8,128)(2,1)} %all-gather.9.cloned.1.call-done), kind=kOutput, calls=%fused_computation.14 | convolution fusion | flops 4834983936 | bytes 13762560 | tf_op jit(solution)/shard_map/dot_general | solution.py:241
  154.4 8.4 %fusion.v_ref = bf16[4096,768]{1,0:T(8,128)(2,1)} fusion(f32[768]{0:T(1024)S(1)} %get-tuple-element.106, bf16[1,4096,768]{2,1,0:T(8,128)(2,1)S(1)} %copy-done.13, bf16[768,2304]{1,0:T(8,128)(2,1)} %all-gather.9.cloned.1.call-done), kind=kOutput, calls=%fused_computation.3 | convolution fusion | flops 4838129664 | bytes 13765632 | tf_op jit(solution)/shard_map/dot_general | solution.py:242
  162.9 13.7 %attend.1 = (f32[768,512]{1,0:T(8,128)}, f32[6,2,512]{2,1,0:T(2,128)}) custom-call(s32[1,2]{1,0:T(1,128)} %pad_add_fusion.bounds, bf16[512,768]{1,0:T(8,128)(2,1)} %fusion.33.q_ref, bf16[512,128]{1,0:T(8,128)(2,1)} %and_convert_fusion.qaug_ref, bf16[4096,768]{1,0:T(8,128)(2,1)} %fusion.8.k_ref, bf16[4096,128]{1,0:T(8,128)(2,1)} %select_convert_fusion.kaug_ref, ...), custom_call_target="tpu_custom_call" | custom-call | tf_op jit(solution)/shard_map/attend/pallas_call | solution.py:112
  179.6 21.6 %all-gather.13.cloned.1.call-done = bf16[768,3072]{1,0:T(8,128)(2,1)} async-done(((bf16[192,3072]{1,0:T(8,128)(2,1)}), bf16[768,3072]{1,0:T(8,128)(2,1)}) %all-gather.13.cloned.1.call-update) | async-done | bytes 4718608 | tf_op jit(solution)/shard_map/all_gather | solution.py:226
  201.2 8.4 %multiply_convert_fusion = (bf16[512,3072]{1,0:T(8,128)(2,1)}, f32[512,3072]{1,0:T(8,128)}) fusion(f32[3072]{0:T(1024)S(1)} %bitcast.85, bf16[768,3072]{1,0:T(8,128)(2,1)} %all-gather.13.cloned.1.call-done, f32[512,768]{1,0:T(8,128)S(1)} %get-tuple-element.146, f32[768]{0:T(1024)S(1)} %get-tuple-element.103, f32[768]{0:T(1024)S(1)} %get-tuple-element.104, ...), kind=kOutput, calls=%fused_computation.12 | convolution fusion | flops 2427322368 | bytes 15751168 | tf_op jit(solution)/shard_map/dot_general | solution.py:249
  209.6 30.4 %all-gather.15.cloned.1.call-done = bf16[3072,768]{1,0:T(8,128)(2,1)} async-done(((bf16[768,768]{1,0:T(8,128)(2,1)}), bf16[3072,768]{1,0:T(8,128)(2,1)}) %all-gather.15.cloned.1.call-update) | async-done | bytes 4718608 | tf_op jit(solution)/shard_map/all_gather | solution.py:226
  240.1 6.2 fusion.60
  250.8 5.3 fusion.55
  264.3 21.7 %attend_back.1 = (bf16[768,512]{1,0:T(8,128)(2,1)}, bf16[4096,768]{1,0:T(8,128)(2,1)}, bf16[4096,768]{1,0:T(8,128)(2,1)}) custom-call(s32[1,2]{1,0:T(1,128)} %pad_add_fusion.bounds, bf16[512,768]{1,0:T(8,128)(2,1)} %fusion.33.q_ref, bf16[512,128]{1,0:T(8,128)(2,1)} %and_convert_fusion.qaug_ref, bf16[512,768]{1,0:T(8,128)(2,1)} %convolution_convert_fusion.5.do_ref, ...), custom_call_target="tpu_custom_call" | custom-call | tf_op jit(solution)/shard_map/attend_back/pallas_call | solution.py:175
  286.1 9.9 %fusion.28 = bf16[768,768]{0,1:T(8,128)(2,1)} fusion(bf16[4096,768]{1,0:T(8,128)(2,1)} %get-tuple-element.25, bf16[1,4096,768]{2,1,0:T(8,128)(2,1)} %all-gather.17.cloned.1.call-done), kind=kOutput, calls=%fused_computation.49 | convolution fusion | flops 4832428032 | bytes 13762560 | tf_op jit(solution)/shard_map/td,te->de/dot_general | solution.py:278
  298.4 9.9 %fusion.25 = bf16[768,768]{0,1:T(8,128)(2,1)} fusion(bf16[4096,768]{1,0:T(8,128)(2,1)} %get-tuple-element.26, bf16[1,4096,768]{2,1,0:T(8,128)(2,1)} %all-gather.17.cloned.1.call-done), kind=kOutput, calls=%fused_computation.48 | convolution fusion | flops 4832428032 | bytes 13762560 | tf_op jit(solution)/shard_map/td,te->de/dot_general | solution.py:279
  316.4 3.2 convolution_convert_fusion.3
  319.9 7.3 convolution_convert_fusion.2
  328.4 6.7 convolution_convert_fusion.1
  335.2 7.8 fusion.37
  343.0 9.7 %add_convert_fusion = bf16[4096,768]{1,0:T(8,128)(2,1)} fusion(f32[4096,768]{1,0:T(8,128)S(1)} %fusion.37, bf16[4096,768]{1,0:T(8,128)(2,1)} %get-tuple-element.26, bf16[768,2304]{1,0:T(8,128)(2,1)} %all-gather.9.cloned.1.call-done), kind=kOutput, calls=%fused_computation | convolution fusion | flops 4838129664 | bytes 26345472 | tf_op jit(solution)/shard_map/te,de->td/dot_general | solution.py:275
  352.9 8.0 reduce-scatter.24.cloned.1.call-done
  362.8 26.6 %reduce-scatter.26.cloned.1.call-done = bf16[192,768]{1,0:T(8,128)(2,1)} async-done(((bf16[768,768]{1,0:T(8,128)(2,1)}), bf16[192,768]{1,0:T(8,128)(2,1)}) %reduce-scatter.26.cloned.1.call-update) | async-done | bytes 294928
  391.3 26.4 %reduce-scatter.22.cloned.1.call-done = bf16[192,768]{1,0:T(8,128)(2,1)} async-done(((bf16[768,768]{1,0:T(8,128)(2,1)}), bf16[192,768]{1,0:T(8,128)(2,1)}) %reduce-scatter.22.cloned.1.call-update) | async-done | bytes 294928
  419.6 26.6 %reduce-scatter.16.cloned.1.call-done = bf16[192,768]{1,0:T(8,128)(2,1)} async-done(((bf16[768,768]{1,0:T(8,128)(2,1)}), bf16[192,768]{1,0:T(8,128)(2,1)}) %reduce-scatter.16.cloned.1.call-update) | async-done | bytes 294928 | tf_op jit(solution)/shard_map/reduce_scatter | solution.py:288
  446.2 50.3 %reduce-scatter.18.cloned.1.call-done = bf16[192,3072]{1,0:T(8,128)(2,1)} async-done(((bf16[768,3072]{1,0:T(8,128)(2,1)}), bf16[192,3072]{1,0:T(8,128)(2,1)}) %reduce-scatter.18.cloned.1.call-update) | async-done | bytes 1179664 | tf_op jit(solution)/shard_map/reduce_scatter | solution.py:288
  496.5 50.6 %reduce-scatter.20.cloned.1.call-done = bf16[768,768]{1,0:T(8,128)(2,1)} async-done(((bf16[3072,768]{1,0:T(8,128)(2,1)}), bf16[768,768]{1,0:T(8,128)(2,1)}) %reduce-scatter.20.cloned.1.call-update) | async-done | bytes 1179664 | tf_op jit(solution)/shard_map/reduce_scatter | solution.py:288
  549.8 3.7 reduce_sum.212
  553.5 10.6 %all-reduce.12 = (bf16[768]{0:T(1024)(128)(2,1)S(1)}, bf16[768]{0:T(1024)(128)(2,1)S(1)}, bf16[768]{0:T(1024)(128)(2,1)S(1)}, bf16[768]{0:T(1024)(128)(2,1)S(1)}...) all-reduce(bf16[768]{0:T(1024)(128)(2,1)S(1)} %reduce_sum.211, ...), channel_id=10, replica_groups=mesh['ctx'=8,'wsh'=4] {'wsh'}, use_global_device_ids=true, to_apply=%region_24.25.clone | all-reduce | flops 9216 | bytes 36864
  564.8 23.4 %all-reduce.10 = (bf16[192]{0:T(256)(128)(2,1)S(1)}, bf16[192]{0:T(256)(128)(2,1)S(1)}, bf16[192]{0:T(256)(128)(2,1)S(1)}, bf16[192]{0:T(256)(128)(2,1)S(1)}, bf...) all-reduce(bf16[192]{0:T(256)(128)(2,1)S(1)} %dynamic-slice.1, ...), channel_id=1, replica_groups=mesh['ctx'=8,'wsh'=4] {'ctx'}, use_global_device_ids=true, to_apply=%region_25.26 | all-reduce | flops 2304 | bytes 9216 | tf_op jit(solution)/shard_map/psum | solution.py:289
  593.3 75.8 %reduce-scatter.14.cloned.1.call-done = bf16[512,768]{1,0:T(8,128)(2,1)} async-done(((bf16[4096,768]{1,0:T(8,128)(2,1)}), bf16[512,768]{1,0:T(8,128)(2,1)}) %reduce-scatter.14.cloned.1.call-update) | async-done | bytes 786448 | tf_op jit(solution)/shard_map/reduce_scatter | solution.py:276
  669.1 3.3 fusion.31
  672.5 149.8 %all-reduce.15.cloned.1.call-done = (bf16[192,768]{0,1:T(8,128)(2,1)}, bf16[192,768]{0,1:T(8,128)(2,1)}, bf16[192,768]{0,1:T(8,128)(2,1)}, bf16[192,768]{1,0:T(8...) async-done(((bf16[192,768]{0,1:T(8,128)(2,1)}, bf16[192,768]{0,1:T(8,128)(2,1)}, bf16[192,768]{0,1:T(8,128)(2,1)}, bf16[192,768]{1,0:T(8,128)(2,1)}, ...) | async-done | bytes 3538960 | tf_op jit(solution)/shard_map/psum | solution.py:289
  (163 shorter events, 60.7 us)
Async XLA Ops:
  7.2 36.5 %all-gather.9.cloned.1.call-start = ((), (), s32[]{:S(2)}) async-start(), calls=%async_computation.7 | async-start | bytes 4423680 | tf_op jit(solution)/shard_map/all_gather | solution.py:226
  9.4 2.8 copy-start.12
  9.4 6.8 copy-start.16
  9.4 135.6 %all-gather.17.cloned.1.call-start = ((), (), s32[]{:S(2)}) async-start(), calls=%async_computation.15 | async-start | bytes 7077888 | tf_op jit(solution)/shard_map/all_gather | solution.py:228
  10.1 6.1 copy-start.17
  10.2 6.1 copy-start.18
  10.2 6.1 copy-start.19
  10.2 6.1 copy-start.20
  10.2 6.1 copy-start.21
  10.2 6.1 copy-start.22
  10.2 6.1 copy-start.23
  10.2 12.5 %copy-start.11 = (bf16[768]{0:T(1024)(128)(2,1)S(1)}, bf16[768]{0:T(1024)(128)(2,1)}, u32[]{:S(2)}) copy-start(bf16[768]{0:T(1024)(128)(2,1)} %param.32) | copy-start | bytes 4612
  10.2 166.3 %all-gather.11.cloned.1.call-start = ((), (), s32[]{:S(2)}) async-start(), calls=%async_computation.8 | async-start | bytes 1474560 | tf_op jit(solution)/shard_map/all_gather | solution.py:226
  11.0 190.2 %all-gather.13.cloned.1.call-start = ((), (), s32[]{:S(2)}) async-start(), calls=%async_computation.9 | async-start | bytes 5898240 | tf_op jit(solution)/shard_map/all_gather | solution.py:226
  11.6 32.2 %copy-start.3 = (bf16[1,512,768]{2,1,0:T(8,128)(2,1)S(1)}, bf16[1,512,768]{2,1,0:T(8,128)(2,1)}, u32[]{:S(2)}) copy-start(bf16[1,512,768]{2,1,0:T(8,128)(2,1)} %param.18) | copy-start | bytes 2359300
  11.6 228.5 %all-gather.15.cloned.1.call-start = ((), (), s32[]{:S(2)}) async-start(), calls=%async_computation.10 | async-start | bytes 5898240 | tf_op jit(solution)/shard_map/all_gather | solution.py:226
  12.2 348.8 %reduce-scatter.24.cloned.1.call-start = ((), (), s32[]{:S(2)}) async-start(), calls=%async_computation.17 | async-start | bytes 1474560
  145.0 9.5 %copy-start.13 = (bf16[1,4096,768]{2,1,0:T(8,128)(2,1)S(1)}, bf16[1,4096,768]{2,1,0:T(8,128)(2,1)}, u32[]{:S(2)}) copy-start(bf16[1,4096,768]{2,1,0:T(8,128)(2,1)} %all-gather.17.cloned.1.call-done) | copy-start | bytes 18874372
  179.3 76.9 %copy-start.1 = (f32[512,768]{1,0:T(8,128)}, f32[512,768]{1,0:T(8,128)S(1)}, u32[]{:S(2)}) copy-start(f32[512,768]{1,0:T(8,128)S(1)} %get-tuple-element.146) | copy-start | bytes 4718596
  240.1 9.9 %copy-start.25 = (f32[512,3072]{1,0:T(8,128)S(1)}, f32[512,3072]{1,0:T(8,128)}, u32[]{:S(2)}) copy-start(f32[512,3072]{1,0:T(8,128)} %get-tuple-element.148) | copy-start | bytes 18874372
  249.7 6.4 slice-start
  249.9 6.2 copy-start.5
  250.8 5.4 slice-start.1
  256.1 3.2 copy-start.26
  298.3 91.1 %reduce-scatter.26.cloned.1.call-start = ((), (), s32[]{:S(2)}) async-start(), calls=%async_computation.18 | async-start | bytes 1474560
  310.7 107.0 %reduce-scatter.22.cloned.1.call-start = ((), (), s32[]{:S(2)}) async-start(), calls=%async_computation.16 | async-start | bytes 1474560
  316.4 129.8 %reduce-scatter.16.cloned.1.call-start = ((), (), s32[]{:S(2)}) async-start(), calls=%async_computation.12 | async-start | bytes 1474560 | tf_op jit(solution)/shard_map/reduce_scatter | solution.py:288
  319.7 176.8 %reduce-scatter.18.cloned.1.call-start = ((), (), s32[]{:S(2)}) async-start(), calls=%async_computation.13 | async-start | bytes 5898240 | tf_op jit(solution)/shard_map/reduce_scatter | solution.py:288
  327.3 219.8 %reduce-scatter.20.cloned.1.call-start = ((), (), s32[]{:S(2)}) async-start(), calls=%async_computation.14 | async-start | bytes 5898240 | tf_op jit(solution)/shard_map/reduce_scatter | solution.py:288
  335.1 334.0 %reduce-scatter.14.cloned.1.call-start = ((), (), s32[]{:S(2)}) async-start(), calls=%async_computation.11 | async-start | bytes 7077888 | tf_op jit(solution)/shard_map/reduce_scatter | solution.py:276
  352.7 469.6 %all-reduce.15.cloned.1.call-start = ((), (), s32[]{:S(2)}) async-start(), calls=%async_computation.19 | async-start | bytes 7667712 | tf_op jit(solution)/shard_map/psum | solution.py:289
  822.3 3.0 copy-start.2
  (10 other events, 18.0 us)
Sparse Core Ops, SparseCore 0:
  10.2 33.5 all-gather.8
  45.9 99.0 all-gather.16
  146.6 15.6 all-gather.10
  163.7 37.4 all-gather.12
  202.6 37.4 all-gather.14
  298.5 62.4 reduce-scatter.23
  363.7 25.7 reduce-scatter.25
  392.0 25.7 reduce-scatter.21
  420.5 25.7 reduce-scatter.15
  448.6 47.8 reduce-scatter.17
  499.2 47.8 reduce-scatter.19
  550.5 118.6 reduce-scatter.13
  674.2 148.0 all-reduce.14

commit v2 on v1

--- a/solution.py
+++ b/solution.py
@@ -191,6 +191,324 @@
             scratch_shapes=[pltpu.VMEM((S, 128), F32), pltpu.VMEM((S, 128), F32), pltpu.VMEM((128, 2 * tq), F32)]),
         name="attend_back",
     )(bounds, q, qaug, do, lse, ot, k, kaug, v)
+
+
+def reach(n_ctx):
+    return n_ctx // 2
+
+
+def reduce_kernel(chunks, n_parts, *refs):
+    parts = refs[:n_parts]
+    vec_ref, rows_ref, out_ref, vec_out, own_ref = refs[n_parts : n_parts + 5]
+    (mine, buf_a, buf_h, buf_b, buf_s, keep, buf_c, buf_u, buf_d, buf_f,
+     vmine, vbuf_a, vbuf_h, vbuf_b, vbuf_s, vbuf_c, vbuf_u, vbuf_d,
+     rmine, rbuf_x, rbuf_s, rbuf_z, rkeep,
+     sem_l, sem_a, sem_b, sem_c, sem_d, sem_e, sem_f, sem_v, sem_rl, sem_rx, sem_rz) = refs[n_parts + 5 :]
+    n_chunks = len(chunks)
+    n_ctx, n_wsh = lax.axis_size("ctx"), lax.axis_size("wsh")
+    zs = n_ctx // 2
+    a, w = lax.axis_index("ctx"), lax.axis_index("wsh")
+    z, x = a // 2, lax.rem(a, 2)
+    y, c = w // 2, lax.rem(w, 2)
+    core_peer = (a, y * 2 + (1 - c))
+    y_peer = (a, (1 - y) * 2 + c)
+    x_peer = (z * 2 + (1 - x), w)
+
+    def z_peer(d):
+        other = lax.rem(z + d, zs)
+        return other, (other * 2 + x, w)
+
+    def slot(dest, src):
+        return lax.rem(src - dest + zs, zs) - 1
+
+    rows = out_ref.shape[1]
+    half = out_ref.shape[2] // 2
+    piece = rows // zs
+    MESH = pl.DeviceIdType.MESH
+    barrier = pltpu.get_barrier_semaphore()
+    for dev in [core_peer, y_peer, x_peer] + [z_peer(d)[1] for d in range(1, zs)]:
+        pl.semaphore_signal(barrier, inc=1, device_id=dev, device_id_type=MESH)
+    pl.semaphore_wait(barrier, zs + 2)
+
+    def send(src, dst, sems, idx, dev):
+        return pltpu.make_async_remote_copy(
+            src_ref=src, dst_ref=dst, send_sem=sems.at[(0,) + idx], recv_sem=sems.at[(1,) + idx],
+            device_id=dev, device_id_type=MESH)
+
+    def wait_in(ref, sems, idx):
+        send(ref, ref, sems, idx, core_peer).wait_recv()
+
+    def wait_out(ref, sems, idx):
+        send(ref, ref, sems, idx, core_peer).wait_send()
+
+    for yy in range(2):
+        pltpu.make_async_copy(vec_ref.at[yy * 2 + c], vmine.at[yy], sem_v.at[0, 0]).start()
+        send(vec_ref.at[yy * 2 + (1 - c)], vbuf_a.at[yy], sem_v, (1,), core_peer).start()
+    for k, (p, row0, col0) in enumerate(chunks):
+        for yy in range(2):
+            where = (pl.ds(row0, rows), pl.ds(col0, 2 * half))
+            pltpu.make_async_copy(parts[p].at[(yy * 2 + c,) + where], mine.at[k, yy], sem_l.at[k]).start()
+            send(parts[p].at[(yy * 2 + (1 - c),) + where], buf_a.at[k, yy], sem_a, (k,), core_peer).start()
+
+    n_slices = sem_rl.shape[0]
+    tall = own_ref.shape[0] // n_slices
+    near = reach(n_ctx)
+
+    def runs_start(t):
+        rs = pl.ds(pl.multiple_of(t * tall, tall), tall)
+        for zz in range(zs):
+            run = zz * 2 + (1 - x)
+
+            @pl.when(jnp.abs(run - a) <= near)
+            def _():
+                send(rows_ref.at[run, rs, :], rbuf_x.at[zz, rs, :], sem_rx, (t, zz), x_peer).start()
+
+            @pl.when(jnp.abs(2 * (zz - z)) <= near)
+            def _():
+                pltpu.make_async_copy(rows_ref.at[zz * 2 + x, rs, :], rmine.at[zz, rs, :], sem_rl.at[t, zz]).start()
+
+    def runs_pass(t):
+        rs = pl.ds(pl.multiple_of(t * tall, tall), tall)
+        for zz in range(zs):
+            @pl.when(jnp.abs(2 * (zz - z)) <= near)
+            def _():
+                pltpu.make_async_copy(rmine.at[zz, rs, :], rmine.at[zz, rs, :], sem_rl.at[t, zz]).wait()
+                rkeep[...] = rmine[zz, rs, :].astype(F32)
+
+                @pl.when(jnp.abs(zz * 2 + x - (z * 2 + 1 - x)) <= near)
+                def _():
+                    wait_in(rbuf_x.at[zz, rs, :], sem_rx, (t, zz))
+                    rkeep[...] += rbuf_x[zz, rs, :].astype(F32)
+
+                @pl.when(zz == z)
+                def _():
+                    own_ref[rs, :] = rkeep[...]
+
+                @pl.when(zz != z)
+                def _():
+                    rbuf_s[zz, rs, :] = rkeep[...].astype(BF)
+                    send(rbuf_s.at[zz, rs, :], rbuf_z.at[slot(zz, z), rs, :], sem_rz, (t, slot(zz, z)),
+                         (zz * 2 + x, w)).start()
+
+    def runs_end(t):
+        rs = pl.ds(pl.multiple_of(t * tall, tall), tall)
+        for d in range(1, zs):
+            other, _unused = z_peer(d)
+
+            @pl.when(jnp.abs(2 * (other - z)) <= near)
+            def _():
+                wait_in(rbuf_z.at[d - 1, rs, :], sem_rz, (t, d - 1))
+                own_ref[rs, :] += rbuf_z[d - 1, rs, :].astype(F32)
+
+    def stage_b(k):
+        pltpu.make_async_copy(mine.at[k], mine.at[k], sem_l.at[k]).wait()
+        wait_in(buf_a.at[k], sem_a, (k,))
+        buf_h[k] = (mine[k, 1 - y].astype(F32) + buf_a[k, 1 - y].astype(F32)).astype(BF)
+        send(buf_h.at[k], buf_b.at[k], sem_b, (k,), y_peer).start()
+
+    def column(side):
+        return pl.ds(pl.multiple_of(side * half, 128), half)
+
+    def stage_c(k):
+        wait_in(buf_b.at[k], sem_b, (k,))
+        def total(side):
+            cols = column(side)
+            return (mine[k, y, :, cols].astype(F32) + buf_a[k, y, :, cols].astype(F32)
+                    + buf_b[k, :, cols].astype(F32))
+        buf_s[k] = total(1 - x).astype(BF)
+        send(buf_s.at[k], buf_c.at[k], sem_c, (k,), x_peer).start()
+        keep[k] = total(x)
+
+    def stage_d(k):
+        wait_in(buf_c.at[k], sem_c, (k,))
+        s = keep[k] + buf_c[k].astype(F32)
+        keep[k] = s
+        buf_u[k] = s.astype(BF)
+        for d in range(1, zs):
+            other, dev = z_peer(d)
+            send(buf_u.at[k, pl.ds(pl.multiple_of(other * piece, 16), piece), :], buf_d.at[k, slot(other, z)],
+                 sem_d, (k, ), dev).start()
+
+    def stage_e(k):
+        wait_in(buf_d.at[k], sem_d, (k,))
+        my = pl.ds(pl.multiple_of(z * piece, 16), piece)
+        s = keep[k, my, :]
+        for d in range(zs - 1):
+            s = s + buf_d[k, d].astype(F32)
+        buf_f[k] = s.astype(BF)
+        out_ref[k, my, column(x)] = s.astype(BF)
+        for d in range(1, zs):
+            other, dev = z_peer(d)
+            send(buf_f.at[k], out_ref.at[k, my, column(x)], sem_e, (k,), dev).start()
+
+    def stage_f(k):
+        wait_in(buf_d.at[k], sem_e, (k,))
+        send(out_ref.at[k, :, column(x)], out_ref.at[k, :, column(x)], sem_f, (k,), x_peer).start()
+
+    def stage_g(k):
+        wait_in(out_ref.at[k, :, column(1 - x)], sem_f, (k,))
+
+    def vec_b():
+        pltpu.make_async_copy(vmine, vmine, sem_v.at[0, 0]).wait()
+        wait_in(vbuf_a, sem_v, (1,))
+        vbuf_h[...] = (vmine[1 - y].astype(F32) + vbuf_a[1 - y].astype(F32)).astype(BF)
+        send(vbuf_h, vbuf_b, sem_v, (2,), y_peer).start()
+
+    def vec_c():
+        wait_in(vbuf_b, sem_v, (2,))
+        vbuf_s[...] = (vmine[y].astype(F32) + vbuf_a[y].astype(F32) + vbuf_b[...].astype(F32)).astype(BF)
+        send(vbuf_s, vbuf_c, sem_v, (3,), x_peer).start()
+
+    def vec_d():
+        wait_in(vbuf_c, sem_v, (3,))
+        s = (vbuf_s[...].astype(F32) + vbuf_c[...].astype(F32)).astype(BF)
+        vbuf_u[...] = s
+        vbuf_d[z] = s
+        for d in range(1, zs):
+            _unused, dev = z_peer(d)
+            send(vbuf_u, vbuf_d.at[z], sem_v, (4,), dev).start()
+
+    def vec_e():
+        wait_in(vbuf_d.at[pl.ds(0, zs - 1)], sem_v, (4,))
+        s = vbuf_d[0].astype(F32)
+        for d in range(1, zs):
+            s = s + vbuf_d[d].astype(F32)
+        vec_out[...] = s
+
+    def guarded(fn, k, n):
+        @pl.when((k >= 0) & (k < n))
+        def _():
+            fn(k)
+
+    vec_b()
+
+    def step(t, carry):
+        guarded(runs_start, t, n_slices)
+        guarded(stage_b, t, n_chunks)
+        guarded(runs_pass, t - 1, n_slices)
+        guarded(stage_c, t - 2, n_chunks)
+        guarded(runs_end, t - 2, n_slices)
+        guarded(stage_d, t - 3, n_chunks)
+        guarded(stage_e, t - 4, n_chunks)
+        guarded(stage_f, t - 5, n_chunks)
+        guarded(stage_g, t - 6, n_chunks)
+        guarded(lambda k: vec_c(), t - 1, 1)
+        guarded(lambda k: vec_d(), t - 2, 1)
+        guarded(lambda k: vec_e(), t - 3, 1)
+        return carry
+
+    lax.fori_loop(0, max(n_chunks + 6, n_slices + 3, 5), step, 0)
+
+    wait_out(vbuf_a, sem_v, (1,))
+    wait_out(vbuf_h, sem_v, (2,))
+    wait_out(vbuf_s, sem_v, (3,))
+    wait_out(vbuf_d.at[pl.ds(0, zs - 1)], sem_v, (4,))
+
+    def drain(k, carry):
+        wait_out(buf_a.at[k], sem_a, (k,))
+        wait_out(buf_b.at[k], sem_b, (k,))
+        wait_out(buf_c.at[k], sem_c, (k,))
+        wait_out(buf_d.at[k], sem_d, (k,))
+        wait_out(buf_d.at[k], sem_e, (k,))
+        wait_out(out_ref.at[k, :, column(x)], sem_f, (k,))
+        return carry
+
+    lax.fori_loop(0, n_chunks, drain, 0)
+
+    def drain_runs(t, carry):
+        rs = pl.ds(pl.multiple_of(t * tall, tall), tall)
+        for zz in range(zs):
+            @pl.when(jnp.abs(zz * 2 + (1 - x) - a) <= near)
+            def _():
+                wait_out(rbuf_x.at[zz, rs, :], sem_rx, (t, zz))
+
+            @pl.when((zz != z) & (jnp.abs(2 * (zz - z)) <= near))
+            def _():
+                wait_out(rbuf_s.at[zz, rs, :], sem_rz, (t, slot(zz, z)))
+        return carry
+
+    lax.fori_loop(0, n_slices, drain_runs, 0)
+
+
+def reduce_grads(parts, chunks, vec, runs):
+    n_ctx, n_wsh = lax.axis_size("ctx"), lax.axis_size("wsh")
+    zs = n_ctx // 2
+    rows = chunks[0][1]
+    chunk_list = [(p, r, col) for p, _rows, r, col in chunks]
+    n = len(chunks)
+    half, piece = D // 2, rows // zs
+    tall = runs.shape[1]
+    n_slices = 8
+    vm = pltpu.VMEM
+    dma = pltpu.SemaphoreType.DMA
+    vrows = vec.shape[1]
+    any_spec = pl.BlockSpec(memory_space=pl.ANY)
+    vm_spec = pl.BlockSpec(memory_space=pltpu.VMEM)
+    return pl.pallas_call(
+        functools.partial(reduce_kernel, chunk_list, len(parts)),
+        out_shape=(
+            jax.ShapeDtypeStruct((n, rows, D), BF),
+            jax.ShapeDtypeStruct((vrows, D), F32),
+            jax.ShapeDtypeStruct((tall, D), F32),
+        ),
+        in_specs=[any_spec] * (len(parts) + 2),
+        out_specs=(vm_spec,) * 3,
+        scratch_shapes=[
+            vm((n, 2, rows, D), BF), vm((n, 2, rows, D), BF), vm((n, rows, D), BF), vm((n, rows, D), BF),
+            vm((n, rows, half), BF), vm((n, rows, half), F32), vm((n, rows, half), BF), vm((n, rows, half), BF),
+            vm((n, zs - 1, piece, half), BF), vm((n, piece, half), BF),
+            vm((2, vrows, D), BF), vm((2, vrows, D), BF), vm((vrows, D), BF), vm((vrows, D), BF),
+            vm((vrows, D), BF), vm((vrows, D), BF), vm((vrows, D), BF), vm((zs, vrows, D), BF),
+            vm((zs, tall, D), BF), vm((zs, tall, D), BF), vm((zs, tall, D), BF), vm((zs - 1, tall, D), BF),
+            vm((tall // n_slices, D), F32),
+            dma((n,)), dma((2, n)), dma((2, n)), dma((2, n)), dma((2, n)), dma((2, n)), dma((2, n)), dma((2, 5)),
+            dma((n_slices, zs)), dma((2, n_slices, zs)), dma((2, n_slices, zs)),
+        ],
+        compiler_params=pltpu.CompilerParams(collective_id=2, has_side_effects=True, vmem_limit_bytes=62 * 2**20),
+        name="reduce_grads",
+    )(*parts, vec, runs)
+
+
+def reduce_all(matrices, vectors, grad_all):
+    n_ctx, n_wsh = lax.axis_size("ctx"), lax.axis_size("wsh")
+    zs = max(n_ctx // 2, 1)
+    own = D // n_wsh
+    if n_wsh != 4 or n_ctx % 2 or own % (zs * 16) or (grad_all.shape[0] // n_ctx) % 128:
+
+        def total(g):
+            part = lax.psum_scatter(g.astype(BF), "wsh", scatter_dimension=0, tiled=True)
+            return lax.psum(part, "ctx").astype(F32)
+
+        grad_own = lax.psum_scatter(grad_all, "ctx", scatter_dimension=0, tiled=True)
+        return [total(g) for g in matrices + vectors], grad_own.astype(F32)
+
+    parts, chunks, spans = [], [], []
+    for p, g in enumerate(matrices):
+        tall, wide = g.shape[0] // n_wsh, g.shape[1]
+        parts.append(g.astype(BF).reshape(n_wsh, tall, wide))
+        spans.append((len(chunks), tall // own, wide // D))
+        for r in range(tall // own):
+            for col in range(wide // D):
+                chunks.append((p, own, r * own, col * D))
+    vec = jnp.concatenate([v.reshape(n_wsh, -1) for v in vectors], axis=1)
+    width = vec.shape[1]
+    tall = -(-width // (16 * D)) * 16
+    vec = jnp.pad(vec, ((0, 0), (0, tall * D - width))).astype(BF).reshape(n_wsh, tall, D)
+    summed, vec_sum, grad_own = reduce_grads(
+        parts, chunks, vec, grad_all.reshape(n_ctx, grad_all.shape[0] // n_ctx, D)
+    )
+    sums = []
+    for first, down, across in spans:
+        block = summed[first : first + down * across]
+        if across > 1:
+            block = jnp.concatenate([block[i] for i in range(across)], axis=1)
+        sums.append(block.reshape(down * own, across * D).astype(F32))
+    flat, place = vec_sum.reshape(-1), 0
+    for v in vectors:
+        size = v.shape[0] // n_wsh
+        sums.append(flat[place : place + size])
+        place += size
+    return sums, grad_own
 
 
 def local(
@@ -273,7 +591,6 @@
     )
     grad_all = jnp.einsum("te,de->td", grad_k, key_w, preferred_element_type=F32)
     grad_all = grad_all + jnp.einsum("te,de->td", grad_v, value_w, preferred_element_type=F32)
-    grad_own = lax.psum_scatter(grad_all.astype(BF), "ctx", scatter_dimension=0, tiled=True)
     grad_query_w = jnp.einsum("td,et->de", inputs, grad_q_t, preferred_element_type=F32)
     grad_key_w = jnp.einsum("td,te->de", all_tokens, grad_k, preferred_element_type=F32)
     grad_value_w = jnp.einsum("td,te->de", all_tokens, grad_v, preferred_element_type=F32)
@@ -282,21 +599,17 @@
     grad_inputs = grad_sum1 + lax.dot_general(
         grad_q_t, query_w, (((0,), (1,)), ((), ())), preferred_element_type=F32
     )
-    grad_inputs = grad_inputs + grad_own.astype(F32)
-
-    def total(g):
-        part = lax.psum_scatter(g.astype(BF), "wsh", scatter_dimension=0, tiled=True)
-        return lax.psum(part, "ctx").astype(F32)
-
-    grads = [
-        grad_query_w, grad_key_w, grad_value_w, grad_out_w, grad_up_w, grad_down_w,
-        grad_query_b, grad_value_b, grad_out_b, grad_attn_g, grad_attn_s, grad_up_b,
-        grad_down_b, grad_final_g, grad_final_s,
-    ]
+    matrices = (grad_query_w, grad_key_w, grad_value_w, grad_out_w, grad_up_w, grad_down_w)
+    vectors = (
+        grad_query_b, grad_value_b, grad_out_b, grad_attn_g, grad_attn_s,
+        grad_up_b, grad_down_b, grad_final_g, grad_final_s,
+    )
+    sums, grad_own = reduce_all(matrices, vectors, grad_all.astype(BF))
+    grad_inputs = grad_inputs + grad_own
     return (
         layer_out.reshape(1, tok_rows, D),
         grad_inputs.astype(BF).reshape(1, tok_rows, D),
-        *[total(g) for g in grads],
+        *sums,
     )
 
 

time: 845 us -> 561 us (0.66)
  waiting for transfers between devices: 580 us -> 165 us
  Pallas kernels: 35.5 us -> 226 us
  blocking collectives: 45.6 us -> 11.6 us
  local copies, waits for them, and re-layouts: 21.6 us -> 7.77 us
    reduce_scatter x4 -> x0, waiting for transfers between devices: 203 us -> none  [the longest x3 127 us: total(): lax.psum_scatter(g.astype(BF), 'wsh', scatter_dimension=0, tiled=True)]
    pallas_call x0 -> x1, Pallas kernels: none -> 190 us  [reduce_grads(): pl.pallas_call(functools.partial(reduce_kernel, chunk_list, len(parts)),...]
    psum x1 -> x0, waiting for transfers between devices: 150 us -> none  [total(): return lax.psum(part, 'ctx').astype(F32)]
    unnamed x16 -> x5, waiting for transfers between devices: 63.6 us -> 2.45 us
    psum x1 -> x0, blocking collectives: 23.4 us -> none  [total(): return lax.psum(part, 'ctx').astype(F32)]
    unnamed x78 -> x68, local copies, waits for them, and re-layouts: 21.3 us -> 3.96 us
    unnamed x1 -> x0, blocking collectives: 10.6 us -> none
  transfers between devices with their start and end apart: 13 -> 5, of which waited for: 12 -> 4; matrix products, arithmetic and copies ran while one was open for 13% -> 7% of each run, Pallas kernels for 2% -> 3%
where the time goes in v2:
time: 561 us; the launch traced here: 552 us
  Pallas kernels  226 us (40%)
  waiting for transfers between devices  165 us (29%)
  matrix products  104 us (19%)
  other arithmetic  20.1 us (4%)
  between operations  17.8 us (3%)
  blocking collectives  11.6 us (2%)
  local copies, waits for them, and re-layouts  7.77 us (1%)
    pallas_call x1, Pallas kernels, reduce_grads(): pl.pallas_call(functools.partial(reduce_kernel, chunk_list, len(parts)),...  190 us
    all_gather x1, waiting for transfers between devices, local(): all_tokens = lax.all_gather(inputs, 'ctx', axis=0, tiled=True)  98.3 us
    all_gather x4, waiting for transfers between devices, gather(): return lax.all_gather(x, 'wsh', axis=0, tiled=True)  64.5 us
    pallas_call x1, Pallas kernels, attn_bwd(): pl.pallas_call(functools.partial(bwd_kernel, tk), out_shape=(jax.ShapeDty...  21.4 us
    pallas_call x1, Pallas kernels, attn_fwd(): pl.pallas_call(functools.partial(fwd_kernel, tk), out_shape=(jax.ShapeDty...  13.9 us
    all_gather x2, blocking collectives, gather(): return lax.all_gather(x, 'wsh', axis=0, tiled=True)  11.6 us
  transfers between devices with their start and end apart: 5, of which 4 were waited for; matrix products, arithmetic and copies ran while one was open for 7% of the time, Pallas kernels for 3%

profile of v2, /device:TPU:0, one launch (start us, length us, event | category | flops | bytes accessed | tf_op | source)
XLA Modules:
  0.0 552.3 jit_solution(1844105490664373437)
XLA Ops:
  7.2 2.1 pad_maximum_fusion
  16.4 6.2 %all-gather.1 = bf16[4,192,8]{1,2,0:T(8,128)(2,1)S(1)} all-gather(bf16[1,192,8]{1,2,0:T(8,128)(2,1)S(1)} %bitcast.121), channel_id=1, replica_groups=mesh['ctx'=8,'wsh'=4] {'wsh'}, dimensions={0}, use_global_device_ids=true | all-gather | bytes 15360 | tf_op jit(solution)/shard_map/all_gather | solution.py:544
  22.7 5.4 all-gather.2
  31.3 12.4 %all-gather.9.cloned.1.call-done = bf16[768,2304]{1,0:T(8,128)(2,1)} async-done(((bf16[192,2304]{1,0:T(8,128)(2,1)}), bf16[768,2304]{1,0:T(8,128)(2,1)}) %all-gather.9.cloned.1.call-update) | async-done | bytes 3538960 | tf_op jit(solution)/shard_map/all_gather | solution.py:544
  43.7 2.9 fusion.25.q_ref
  46.7 98.3 %all-gather.17.cloned.1.call-done = bf16[1,4096,768]{2,1,0:T(8,128)(2,1)} async-done(((bf16[1,512,768]{2,1,0:T(8,128)(2,1)}), bf16[1,4096,768]{2,1,0:T(8,128)(2,1)}) %all-gather.17.cloned.1.call-update) | async-done | bytes 6291472 | tf_op jit(solution)/shard_map/all_gather | solution.py:546
  145.0 9.3 %fusion.8.k_ref = bf16[4096,768]{1,0:T(8,128)(2,1)} fusion(bf16[1,4096,768]{2,1,0:T(8,128)(2,1)} %all-gather.17.cloned.1.call-done, bf16[768,2304]{1,0:T(8,128)(2,1)} %all-gather.9.cloned.1.call-done), kind=kOutput, calls=%fused_computation.14 | convolution fusion | flops 4834983936 | bytes 13762560 | tf_op jit(solution)/shard_map/dot_general | solution.py:559
  154.3 8.3 %fusion.v_ref = bf16[4096,768]{1,0:T(8,128)(2,1)} fusion(f32[768]{0:T(1024)S(1)} %get-tuple-element.44, bf16[1,4096,768]{2,1,0:T(8,128)(2,1)S(1)} %copy-done.10, bf16[768,2304]{1,0:T(8,128)(2,1)} %all-gather.9.cloned.1.call-done), kind=kOutput, calls=%fused_computation.3 | convolution fusion | flops 4838129664 | bytes 13765632 | tf_op jit(solution)/shard_map/dot_general | solution.py:560
  162.6 13.9 %attend.1 = (f32[768,512]{1,0:T(8,128)}, f32[6,2,512]{2,1,0:T(2,128)}) custom-call(s32[1,2]{1,0:T(1,128)} %pad_add_fusion.bounds, bf16[512,768]{1,0:T(8,128)(2,1)} %fusion.25.q_ref, bf16[512,128]{1,0:T(8,128)(2,1)} %and_convert_fusion.qaug_ref, bf16[4096,768]{1,0:T(8,128)(2,1)} %fusion.8.k_ref, bf16[4096,128]{1,0:T(8,128)(2,1)} %select_convert_fusion.kaug_ref, ...), custom_call_target="tpu_custom_call" | custom-call | tf_op jit(solution)/shard_map/attend/pallas_call | solution.py:112
  176.6 2.7 fusion.53
  179.6 21.6 %all-gather.13.cloned.1.call-done = bf16[768,3072]{1,0:T(8,128)(2,1)} async-done(((bf16[192,3072]{1,0:T(8,128)(2,1)}), bf16[768,3072]{1,0:T(8,128)(2,1)}) %all-gather.13.cloned.1.call-update) | async-done | bytes 4718608 | tf_op jit(solution)/shard_map/all_gather | solution.py:544
  201.2 8.4 %multiply_convert_fusion = (bf16[512,3072]{1,0:T(8,128)(2,1)}, f32[512,3072]{1,0:T(8,128)}) fusion(f32[3072]{0:T(1024)S(1)} %bitcast.122, bf16[768,3072]{1,0:T(8,128)(2,1)} %all-gather.13.cloned.1.call-done, f32[512,768]{1,0:T(8,128)S(1)} %get-tuple-element.76, f32[768]{0:T(1024)S(1)} %get-tuple-element.41, f32[768]{0:T(1024)S(1)} %get-tuple-element.42, ...), kind=kOutput, calls=%fused_computation.12 | convolution fusion | flops 2427322368 | bytes 15751168 | tf_op jit(solution)/shard_map/dot_general | solution.py:567
  209.5 30.5 %all-gather.15.cloned.1.call-done = bf16[3072,768]{1,0:T(8,128)(2,1)} async-done(((bf16[768,768]{1,0:T(8,128)(2,1)}), bf16[3072,768]{1,0:T(8,128)(2,1)}) %all-gather.15.cloned.1.call-update) | async-done | bytes 4718608 | tf_op jit(solution)/shard_map/all_gather | solution.py:544
  240.1 6.1 %fusion.54 = (f32[512]{0:T(512)S(1)}, f32[512,768]{1,0:T(8,128)S(1)}) fusion(f32[768]{0:T(1024)S(1)} %get-tuple-element.40, bf16[512,3072]{1,0:T(8,128)(2,1)} %get-tuple-element.77, bf16[3072,768]{1,0:T(8,128)(2,1)} %all-gather.15.cloned.1.call-done, f32[768]{0:T(1024)S(1)} %get-tuple-element.41, f32[768]{0:T(1024)S(1)} %get-tuple-element.42, ...), kind=kOutput, calls=%fused_computation.110 | convolution fusion | flops 2418671104 | bytes 11025408 | tf_op jit(solution)/shard_map/dot_general | solution.py:570
  249.4 4.3 convolution_convert_fusion.1
  253.9 5.3 fusion.48
  259.3 5.2 convolution_convert_fusion.2
  264.5 3.2 multiply_reduce_fusion
  268.6 1.7 copy-done.3
  270.4 1.8 convolution_convert_fusion.3
  272.2 1.7 convolution_convert_fusion.5.do_ref
  273.9 21.4 %attend_back.1 = (bf16[768,512]{1,0:T(8,128)(2,1)}, bf16[4096,768]{1,0:T(8,128)(2,1)}, bf16[4096,768]{1,0:T(8,128)(2,1)}) custom-call(s32[1,2]{1,0:T(1,128)} %pad_add_fusion.bounds, bf16[512,768]{1,0:T(8,128)(2,1)} %fusion.25.q_ref, bf16[512,128]{1,0:T(8,128)(2,1)} %and_convert_fusion.qaug_ref, bf16[512,768]{1,0:T(8,128)(2,1)} %convolution_convert_fusion.5.do_ref, ...), custom_call_target="tpu_custom_call" | custom-call | tf_op jit(solution)/shard_map/attend_back/pallas_call | solution.py:175
  295.3 3.0 convolution_convert_fusion.4
  298.6 3.7 reduce.4
  303.6 10.2 %fusion.21 = bf16[768,768]{0,1:T(8,128)(2,1)} fusion(bf16[4096,768]{1,0:T(8,128)(2,1)} %get-tuple-element.29, bf16[1,4096,768]{2,1,0:T(8,128)(2,1)} %all-gather.17.cloned.1.call-done), kind=kOutput, calls=%fused_computation.40 | convolution fusion | flops 4832428032 | bytes 13762560 | tf_op jit(solution)/shard_map/td,te->de/dot_general | solution.py:596
  313.8 10.0 %fusion.18 = bf16[768,768]{0,1:T(8,128)(2,1)} fusion(bf16[4096,768]{1,0:T(8,128)(2,1)} %get-tuple-element.28, bf16[1,4096,768]{2,1,0:T(8,128)(2,1)} %all-gather.17.cloned.1.call-done), kind=kOutput, calls=%fused_computation.39 | convolution fusion | flops 4832428032 | bytes 13762560 | tf_op jit(solution)/shard_map/td,te->de/dot_general | solution.py:595
  323.9 8.3 %fusion.30 = f32[4096,768]{1,0:T(8,128)} fusion(bf16[4096,768]{1,0:T(8,128)(2,1)S(1)} %bitcast.126, bf16[768,2304]{1,0:T(8,128)(2,1)S(1)} %copy-done.11), kind=kOutput, calls=%fused_computation.55 | convolution fusion | flops 4831838208 | bytes 20054016 | tf_op jit(solution)/shard_map/te,de->td/dot_general | solution.py:592
  332.1 10.0 %add_convert_fusion = bf16[4096,768]{1,0:T(8,128)(2,1)} fusion(f32[4096,768]{1,0:T(8,128)} %fusion.30, bf16[4096,768]{1,0:T(8,128)(2,1)S(1)} %bitcast.111, bf16[768,2304]{1,0:T(8,128)(2,1)S(1)} %copy-done.11), kind=kOutput, calls=%fused_computation | convolution fusion | flops 4838129664 | bytes 26345472 | tf_op jit(solution)/shard_map/te,de->td/dot_general | solution.py:593
  342.2 190.3 %reduce_grads.1 = (bf16[12,192,768]{2,1,0:T(8,128)(2,1)}, f32[16,768]{1,0:T(8,128)}, f32[512,768]{1,0:T(8,128)}) custom-call(bf16[4,192,768]{2,1,0:T(8,128)(2,1)} %bitcast.116, bf16[4,192,768]{2,1,0:T(8,128)(2,1)} %bitcast.118, bf16[4,192,768]{2,1,0:T(8,128)(2,1)} %bitcast.117, bf16[4,192,768]{2,1,0:T(8,128)(2,1)} %bitcast.113, ...), custom_call_target="tpu_custom_call" | custom-call | tf_op jit(solution)/shard_map/reduce_grads/pallas_call | solution.py:447
  532.5 3.1 slice_bitcast_fusion.3
  539.9 1.7 maximum_convert_fusion
  542.5 3.1 fusion.26
  (138 shorter events, 18.3 us)
Async XLA Ops:
  7.2 36.5 %all-gather.9.cloned.1.call-start = ((), (), s32[]{:S(2)}) async-start(), calls=%async_computation | async-start | bytes 4423680 | tf_op jit(solution)/shard_map/all_gather | solution.py:544
  9.4 2.8 copy-start.9
  9.4 6.8 %copy-start.14 = (bf16[192]{0:T(256)(128)(2,1)S(1)}, bf16[192]{0:T(256)(128)(2,1)}, u32[]{:S(2)}) copy-start(bf16[192]{0:T(256)(128)(2,1)} %param.27) | copy-start | bytes 1156
  9.4 6.8 %copy-start.15 = (bf16[192]{0:T(256)(128)(2,1)S(1)}, bf16[192]{0:T(256)(128)(2,1)}, u32[]{:S(2)}) copy-start(bf16[192]{0:T(256)(128)(2,1)} %param.28) | copy-start | bytes 1156
  9.4 6.8 %copy-start.16 = (bf16[192]{0:T(256)(128)(2,1)S(1)}, bf16[192]{0:T(256)(128)(2,1)}, u32[]{:S(2)}) copy-start(bf16[192]{0:T(256)(128)(2,1)} %param.29) | copy-start | bytes 1156
  9.4 6.8 %copy-start.17 = (bf16[192]{0:T(256)(128)(2,1)S(1)}, bf16[192]{0:T(256)(128)(2,1)}, u32[]{:S(2)}) copy-start(bf16[192]{0:T(256)(128)(2,1)} %param.30) | copy-start | bytes 1156
  9.4 6.8 %copy-start.18 = (bf16[192]{0:T(256)(128)(2,1)S(1)}, bf16[192]{0:T(256)(128)(2,1)}, u32[]{:S(2)}) copy-start(bf16[192]{0:T(256)(128)(2,1)} %param.31) | copy-start | bytes 1156
  9.4 6.8 %copy-start.19 = (bf16[192]{0:T(256)(128)(2,1)S(1)}, bf16[192]{0:T(256)(128)(2,1)}, u32[]{:S(2)}) copy-start(bf16[192]{0:T(256)(128)(2,1)} %param.33) | copy-start | bytes 1156
  9.5 6.8 %copy-start.20 = (bf16[192]{0:T(256)(128)(2,1)S(1)}, bf16[192]{0:T(256)(128)(2,1)}, u32[]{:S(2)}) copy-start(bf16[192]{0:T(256)(128)(2,1)} %param.34) | copy-start | bytes 1156
  9.5 6.8 %copy-start.21 = (bf16[192]{0:T(256)(128)(2,1)S(1)}, bf16[192]{0:T(256)(128)(2,1)}, u32[]{:S(2)}) copy-start(bf16[192]{0:T(256)(128)(2,1)} %param.35) | copy-start | bytes 1156
  9.5 135.5 %all-gather.17.cloned.1.call-start = ((), (), s32[]{:S(2)}) async-start(), calls=%async_computation.4 | async-start | bytes 7077888 | tf_op jit(solution)/shard_map/all_gather | solution.py:546
  10.2 12.4 %copy-start.8 = (bf16[768]{0:T(1024)(128)(2,1)S(1)}, bf16[768]{0:T(1024)(128)(2,1)}, u32[]{:S(2)}) copy-start(bf16[768]{0:T(1024)(128)(2,1)} %param.32) | copy-start | bytes 4612
  10.2 17.9 %copy-start = (bf16[1,512,768]{2,1,0:T(8,128)(2,1)S(1)}, bf16[1,512,768]{2,1,0:T(8,128)(2,1)}, u32[]{:S(2)}) copy-start(bf16[1,512,768]{2,1,0:T(8,128)(2,1)} %param.19) | copy-start | bytes 2359300
  10.3 166.3 %all-gather.11.cloned.1.call-start = ((), (), s32[]{:S(2)}) async-start(), calls=%async_computation.1 | async-start | bytes 1474560 | tf_op jit(solution)/shard_map/all_gather | solution.py:544
  11.0 190.2 %all-gather.13.cloned.1.call-start = ((), (), s32[]{:S(2)}) async-start(), calls=%async_computation.2 | async-start | bytes 5898240 | tf_op jit(solution)/shard_map/all_gather | solution.py:544
  11.6 32.2 %copy-start.4 = (bf16[1,512,768]{2,1,0:T(8,128)(2,1)S(1)}, bf16[1,512,768]{2,1,0:T(8,128)(2,1)}, u32[]{:S(2)}) copy-start(bf16[1,512,768]{2,1,0:T(8,128)(2,1)} %param.18) | copy-start | bytes 2359300
  11.6 228.5 %all-gather.15.cloned.1.call-start = ((), (), s32[]{:S(2)}) async-start(), calls=%async_computation.3 | async-start | bytes 5898240 | tf_op jit(solution)/shard_map/all_gather | solution.py:544
  145.0 9.3 %copy-start.10 = (bf16[1,4096,768]{2,1,0:T(8,128)(2,1)S(1)}, bf16[1,4096,768]{2,1,0:T(8,128)(2,1)}, u32[]{:S(2)}) copy-start(bf16[1,4096,768]{2,1,0:T(8,128)(2,1)} %all-gather.17.cloned.1.call-done) | copy-start | bytes 18874372
  247.2 6.5 %slice-start.8 = ((s8[6291456]{0:T(1024)(128)(4,1)}), s8[4194304]{0:T(1024)(128)(4,1)S(1)}, s32[]{:S(2)}) async-start(s8[6291456]{0:T(1024)(128)(4,1)} %bitcast.131), calls=%async_computation.13 | async-start | bytes 8388608
  248.8 4.8 slice-start.6
  249.4 4.3 slice-start.7
  249.4 4.5 slice-start.9
  249.4 15.1 %slice-start.4 = ((s8[4718592]{0:T(1024)(128)(4,1)}), s8[4194304]{0:T(1024)(128)(4,1)S(1)}, s32[]{:S(2)}) async-start(s8[4718592]{0:T(1024)(128)(4,1)} %bitcast.127), calls=%async_computation.9 | async-start | bytes 8388608
  253.9 10.6 %slice-start.5 = ((s8[4718592]{0:T(1024)(128)(4,1)}), s8[524288]{0:T(1024)(128)(4,1)S(1)}, s32[]{:S(2)}) async-start(s8[4718592]{0:T(1024)(128)(4,1)} %bitcast.127), calls=%async_computation.10 | async-start | bytes 1048576
  268.4 3.8 copy-start.1
  295.3 3.1 copy-start.5
  303.6 20.2 %slice-start.2 = ((s8[6291456]{0:T(1024)(128)(4,1)}), s8[4194304]{0:T(1024)(128)(4,1)S(1)}, s32[]{:S(2)}) async-start(s8[6291456]{0:T(1024)(128)(4,1)} %bitcast.125), calls=%async_computation.7 | async-start | bytes 8388608
  303.6 28.5 %slice-start = ((s8[6291456]{0:T(1024)(128)(4,1)}), s8[4194304]{0:T(1024)(128)(4,1)S(1)}, s32[]{:S(2)}) async-start(s8[6291456]{0:T(1024)(128)(4,1)} %bitcast.110), calls=%async_computation.5 | async-start | bytes 8388608
  313.8 10.0 %slice-start.3 = ((s8[6291456]{0:T(1024)(128)(4,1)}), s8[2097152]{0:T(1024)(128)(4,1)S(1)}, s32[]{:S(2)}) async-start(s8[6291456]{0:T(1024)(128)(4,1)} %bitcast.125), calls=%async_computation.8 | async-start | bytes 4194304
  313.8 10.0 %copy-start.11 = (bf16[768,2304]{1,0:T(8,128)(2,1)S(1)}, bf16[768,2304]{1,0:T(8,128)(2,1)}, u32[]{:S(2)}) copy-start(bf16[768,2304]{1,0:T(8,128)(2,1)} %all-gather.9.cloned.1.call-done) | copy-start | bytes 10616836
  313.8 18.3 %slice-start.1 = ((s8[6291456]{0:T(1024)(128)(4,1)}), s8[2097152]{0:T(1024)(128)(4,1)S(1)}, s32[]{:S(2)}) async-start(s8[6291456]{0:T(1024)(128)(4,1)} %bitcast.110), calls=%async_computation.6 | async-start | bytes 4194304
  538.3 3.3 copy-start.12
  (6 other events, 11.8 us)
Sparse Core Ops, SparseCore 0:
  10.2 33.5 all-gather.8
  45.9 99.0 all-gather.16
  146.6 15.6 all-gather.10
  163.7 37.4 all-gather.12
  202.6 37.4 all-gather.14

commit v3 on v2

--- a/solution.py
+++ b/solution.py
@@ -469,6 +469,240 @@
     )(*parts, vec, runs)
 
 
+def gather_kernel(cut, tok_ref, vec_ref, wk_ref, wv_ref, wq_ref,
+                  tok_out, k_out, v_out, q_out, w_out, vec_out,
+                  tok, kbuf, vbuf, qbuf, wbuf, vecs,
+                  sem_in, sem_out, sem_w, sem_l, sem_o):
+    n_ctx = lax.axis_size("ctx")
+    zs = n_ctx // 2
+    a, w = lax.axis_index("ctx"), lax.axis_index("wsh")
+    z, x = a // 2, lax.rem(a, 2)
+    y, c = w // 2, lax.rem(w, 2)
+    core_peer = (a, y * 2 + (1 - c))
+    y_peer = (a, (1 - y) * 2 + c)
+    x_peer = (z * 2 + (1 - x), w)
+    up, down = (a + 2, w), (a - 2, w)
+    near = reach(n_ctx)
+    MESH = pl.DeviceIdType.MESH
+    n_slices = sem_in.shape[1]
+    tall = tok.shape[1] // n_slices
+    own = wk_ref.shape[0]
+    far = 4 * (near // 2 + 1)
+
+    barrier = pltpu.get_barrier_semaphore()
+    around = [(lax.rem(z + d, zs) * 2 + x, w) for d in (1, zs - 1)]
+    for dev in [core_peer, y_peer, x_peer] + around:
+        pl.semaphore_signal(barrier, inc=1, device_id=dev, device_id_type=MESH)
+    pl.semaphore_wait(barrier, 5)
+
+    def relative(u):
+        dz = (u // 4) * (1 - 2 * lax.rem(u, 2))
+        other = lax.rem(u // 2, 2)
+        run = 2 * (z + dz) + (x + other - 2 * x * other)
+        there = (z + dz >= 0) & (z + dz < zs) & (jnp.abs(run - a) <= near) & ((u >= 4) | (lax.rem(u, 2) == 0))
+        return run, dz, other, there
+
+    def rows(s):
+        return pl.ds(pl.multiple_of(s * tall, tall), tall)
+
+    def remote(src, dst, send_sem, recv_sem, dev):
+        return pltpu.make_async_remote_copy(
+            src_ref=src, dst_ref=dst, send_sem=send_sem, recv_sem=recv_sem, device_id=dev, device_id_type=MESH)
+
+    def routes(u, s):
+        run, dz, other, there = relative(u)
+        z_first = s < cut
+        to_x = there & (z_first | (dz == 0)) & (other == 0) & (jnp.abs(run - x_peer[0]) <= near)
+        along = there & ((other == 0) | jnp.logical_not(z_first))
+        to_up = along & (dz <= 0) & (z + 1 < zs) & (jnp.abs(run - (a + 2)) <= near)
+        to_down = along & (dz >= 0) & (z > 0) & (jnp.abs(run - (a - 2)) <= near)
+        return run, ((0, x_peer, to_x), (1, up, to_up), (2, down, to_down))
+
+    def pass_on(u, s):
+        run, where = routes(u, s)
+        for d, dev, ok in where:
+            @pl.when(ok)
+            def _():
+                source = tok_ref if isinstance(u, int) and u == 0 else tok.at[run]
+                remote(source.at[rows(s), :], tok.at[run, rows(s), :], sem_out.at[d, u, s], sem_in.at[run, s], dev).start()
+
+    def await_slice(u, s):
+        run, _dz, _other, there = relative(u)
+
+        @pl.when(there)
+        def _():
+            remote(tok.at[run, rows(s), :], tok.at[run, rows(s), :], sem_out.at[0, 0, 0], sem_in.at[run, s], x_peer).wait_recv()
+
+    def start_own(s, carry):
+        pass_on(0, s)
+        return carry
+
+    def weight_rows(owner):
+        return pl.ds(pl.multiple_of(owner * own, 16), own)
+
+    vec_own = vecs.at[w]
+    remote(vec_ref, vec_own, sem_w.at[0, 0, 3], sem_w.at[1, 0, 3], core_peer).start()
+    remote(vec_ref, vec_own, sem_w.at[0, 1, 3], sem_w.at[1, 1, 3], y_peer).start()
+    pltpu.make_async_copy(vec_ref, vec_own, sem_l.at[3]).start()
+    for m, ref in enumerate((wk_ref, wv_ref, wq_ref)):
+        there = wbuf.at[m, weight_rows(w), :]
+        remote(ref, there, sem_w.at[0, 1, m], sem_w.at[1, 1, m], y_peer).start()
+        remote(ref, there, sem_w.at[0, 0, m], sem_w.at[1, 0, m], core_peer).start()
+        pltpu.make_async_copy(ref, there, sem_l.at[m]).start()
+    lax.fori_loop(0, n_slices, start_own, 0)
+    pltpu.make_async_copy(tok_ref, tok.at[a], sem_l.at[4]).start()
+
+    for j in range(n_ctx):
+        @pl.when(jnp.abs(j - a) > near)
+        def _():
+            tok[j] = jnp.zeros_like(tok[j])
+
+    def shard(m, owner):
+        return vecs.at[owner] if m == 3 else wbuf.at[m, weight_rows(owner), :]
+
+    def weight_arrival(m, kind):
+        part = shard(m, w)
+        return remote(part, part, sem_w.at[0, kind, m], sem_w.at[1, kind, m], core_peer)
+
+    across = (1 - y) * 2 + c
+
+    def weight_forward(m):
+        weight_arrival(m, 1).wait_recv()
+        remote(shard(m, across), shard(m, across), sem_w.at[0, 2, m], sem_w.at[1, 2, m], core_peer).start()
+
+    def weight_end(m):
+        weight_arrival(m, 0).wait_recv()
+        weight_arrival(m, 2).wait_recv()
+        pltpu.make_async_copy(shard(m, w), shard(m, w), sem_l.at[m]).wait()
+
+    weight_forward(3)
+    weight_forward(0)
+    weight_forward(1)
+    weight_end(3)
+    total = vecs[0].astype(F32)
+    for owner in range(1, 4):
+        total = total + vecs[owner].astype(F32)
+    vec_out[...] = total
+    pltpu.make_async_copy(tok_ref, tok.at[a], sem_l.at[4]).wait()
+    weight_end(0)
+    weight_end(1)
+
+    def relay(first, last):
+        def one(i, carry):
+            s = i // (last - first)
+            u = first + lax.rem(i, last - first)
+            await_slice(u, s)
+            pass_on(u, s)
+            return carry
+
+        lax.fori_loop(0, n_slices * (last - first), one, 0)
+
+    step_rows = 128
+    steps = tok.shape[1] // step_rows
+
+    def project(u, carry):
+        run, _dz, _other, there = relative(u)
+
+        @pl.when(u == 1)
+        def _():
+            relay(2, 6)
+
+        @pl.when(u == 6)
+        def _():
+            weight_forward(2)
+            weight_end(2)
+            relay(6, 10)
+
+        @pl.when(there)
+        def _():
+            @pl.when(u >= 10)
+            def _():
+                def one(s, carry):
+                    await_slice(u, s)
+                    return carry
+
+                lax.fori_loop(0, n_slices, one, 0)
+
+            def part(i, carry):
+                r = pl.ds(pl.multiple_of(i * step_rows, step_rows), step_rows)
+                t = tok[run, r, :]
+                kbuf[run, r, :] = jnp.dot(t, wbuf[0], preferred_element_type=F32).astype(BF)
+                vbuf[run, r, :] = (jnp.dot(t, wbuf[1], preferred_element_type=F32) + vec_out[1:2, :]).astype(BF)
+                return carry
+
+            lax.fori_loop(0, steps, part, 0)
+            for i, (src, dst) in enumerate(((kbuf, k_out), (vbuf, v_out), (tok, tok_out))):
+                pltpu.make_async_copy(src.at[run], dst.at[run], sem_o.at[i, run]).start()
+
+        return carry
+
+    for j in range(n_ctx):
+        @pl.when(jnp.abs(j - a) > near)
+        def _():
+            kbuf[j] = jnp.zeros_like(kbuf[j])
+            vbuf[j] = jnp.zeros_like(vbuf[j])
+            for i, (src, dst) in enumerate(((kbuf, k_out), (vbuf, v_out), (tok, tok_out))):
+                pltpu.make_async_copy(src.at[j], dst.at[j], sem_o.at[i, j]).start()
+
+    lax.fori_loop(0, far, project, 0)
+
+    def query_part(i, carry):
+        r = pl.ds(pl.multiple_of(i * step_rows, step_rows), step_rows)
+        q = (jnp.dot(tok[a, r, :], wbuf[2], preferred_element_type=F32) + vec_out[0:1, :]).astype(BF)
+        qbuf[r, :] = q * jnp.asarray(SCALE, BF)
+        return carry
+
+    lax.fori_loop(0, steps, query_part, 0)
+    pltpu.make_async_copy(qbuf, q_out, sem_l.at[5]).start()
+    pltpu.make_async_copy(wbuf, w_out, sem_l.at[6]).start()
+
+    for m in range(4):
+        for kind in range(3):
+            weight_arrival(m, kind).wait_send()
+
+    def drain(i, carry):
+        s = i // far
+        u = lax.rem(i, far)
+        run, where = routes(u, s)
+        for d, dev, ok in where:
+            @pl.when(ok & (u < 10))
+            def _():
+                remote(tok.at[run, rows(s), :], tok.at[run, rows(s), :], sem_out.at[d, u, s], sem_in.at[run, s], dev).wait_send()
+        return carry
+
+    lax.fori_loop(0, n_slices * far, drain, 0)
+    for j in range(n_ctx):
+        for i, (src, dst) in enumerate(((kbuf, k_out), (vbuf, v_out), (tok, tok_out))):
+            pltpu.make_async_copy(src.at[j], dst.at[j], sem_o.at[i, j]).wait()
+    pltpu.make_async_copy(qbuf, q_out, sem_l.at[5]).wait()
+    pltpu.make_async_copy(wbuf, w_out, sem_l.at[6]).wait()
+
+
+def gather_project(inputs, vec, key_weight, value_weight, query_weight):
+    n_ctx, n_wsh = lax.axis_size("ctx"), lax.axis_size("wsh")
+    tall = inputs.shape[0]
+    n_slices = 8
+    far = 4 * (reach(n_ctx) // 2 + 1)
+    vm, dma = pltpu.VMEM, pltpu.SemaphoreType.DMA
+    any_spec = pl.BlockSpec(memory_space=pl.ANY)
+    vm_spec = pl.BlockSpec(memory_space=pltpu.VMEM)
+    runs = (n_ctx, tall, D)
+    shape = jax.ShapeDtypeStruct
+    return pl.pallas_call(
+        functools.partial(gather_kernel, 5),
+        out_shape=(shape(runs, BF), shape(runs, BF), shape(runs, BF), shape((tall, D), BF), shape((3, D, D), BF),
+                   shape(vec.shape, F32)),
+        in_specs=[any_spec] * 5,
+        out_specs=(any_spec,) * 5 + (vm_spec,),
+        scratch_shapes=[
+            vm(runs, BF), vm(runs, BF), vm(runs, BF), vm((tall, D), BF), vm((3, D, D), BF), vm((n_wsh,) + vec.shape, BF),
+            dma((n_ctx, n_slices)), dma((3, far, n_slices)), dma((2, 3, 4)), dma((7,)), dma((3, n_ctx)),
+        ],
+        compiler_params=pltpu.CompilerParams(collective_id=1, has_side_effects=True, vmem_limit_bytes=48 * 2**20),
+        name="gather_project",
+    )(inputs, vec, key_weight, value_weight, query_weight)
+
+
 def reduce_all(matrices, vectors, grad_all):
     n_ctx, n_wsh = lax.axis_size("ctx"), lax.axis_size("wsh")
     zs = max(n_ctx // 2, 1)
@@ -540,24 +774,42 @@
     bounds = key_range(doc_start, first_row, tok_rows, stream_rows, tile)
     query_doc, key_doc = document_lanes(doc_start, first_row, tok_rows, stream_rows)
 
+    n_ctx, n_wsh = lax.axis_size("ctx"), lax.axis_size("wsh")
+    own = D // n_wsh
+
     def gather(x):
         return lax.all_gather(x, "wsh", axis=0, tiled=True)
 
-    all_tokens = lax.all_gather(inputs, "ctx", axis=0, tiled=True)
-    qkv_w = gather(jnp.concatenate([query_weight, key_weight, value_weight], axis=1))
-    query_w, key_w, value_w = qkv_w[:, :D], qkv_w[:, D : 2 * D], qkv_w[:, 2 * D :]
-    small = gather(
-        jnp.stack([query_bias, value_bias, out_bias, attn_gain, attn_shift, down_bias, final_gain, final_shift], axis=1)
-    ).astype(F32)
-    query_b, value_b, out_b, attn_g, attn_s, down_b, final_g, final_s = [small[:, i] for i in range(8)]
-    up_b = gather(up_bias).astype(F32)
+    small = jnp.stack(
+        [query_bias, value_bias, out_bias, attn_gain, attn_shift, down_bias, final_gain, final_shift]
+    )
+    if n_wsh == 4 and n_ctx % 4 == 0 and own % 16 == 0 and tok_rows % 512 == 0:
+        w = lax.axis_index("wsh")
+        at = lax.broadcasted_iota(jnp.int32, (8, D), 1) // own == w
+        vec = jnp.where(at, jnp.tile(small, (1, n_wsh)), jnp.zeros((), BF))
+        at = lax.broadcasted_iota(jnp.int32, (8, D), 0) == w
+        vec = jnp.concatenate([vec, jnp.where(at, up_bias[None, :], jnp.zeros((), BF))], axis=0)
+        all_tokens, keys, values, queries, kvq_w, vec = gather_project(
+            inputs, vec, key_weight, value_weight, query_weight
+        )
+        all_tokens, keys, values = [r.reshape(stream_rows, D) for r in (all_tokens, keys, values)]
+        key_w, value_w, query_w = kvq_w[0], kvq_w[1], kvq_w[2]
+        query_b, value_b, out_b, attn_g, attn_s, down_b, final_g, final_s = [vec[i] for i in range(8)]
+        up_b = vec[8 : 8 + n_wsh].reshape(-1)
+    else:
+        all_tokens = lax.all_gather(inputs, "ctx", axis=0, tiled=True)
+        query_w, key_w, value_w = gather(query_weight), gather(key_weight), gather(value_weight)
+        small = gather(small.T).astype(F32)
+        query_b, value_b, out_b, attn_g, attn_s, down_b, final_g, final_s = [small[:, i] for i in range(8)]
+        up_b = gather(up_bias).astype(F32)
+        queries = jnp.dot(inputs, query_w, preferred_element_type=F32) + query_b
+        queries = queries.astype(BF) * jnp.asarray(SCALE, BF)
+        keys = jnp.dot(all_tokens, key_w, preferred_element_type=F32).astype(BF)
+        values = (jnp.dot(all_tokens, value_w, preferred_element_type=F32) + value_b).astype(BF)
     out_w = gather(out_weight)
     up_w = gather(up_weight)
     down_w = gather(down_weight)
 
-    queries = (jnp.dot(inputs, query_w, preferred_element_type=F32) + query_b).astype(BF) * jnp.asarray(SCALE, BF)
-    keys = jnp.dot(all_tokens, key_w, preferred_element_type=F32).astype(BF)
-    values = (jnp.dot(all_tokens, value_w, preferred_element_type=F32) + value_b).astype(BF)
     mixed_t, log_rows = attn_fwd(bounds, queries, query_doc, keys, key_doc, values, tq=tile)
     attn_t = mixed_t.astype(BF)
     inputs_f = inputs.astype(F32)

time: 561 us -> 483 us (0.86); the launches traced: 552 us -> 489 us
  waiting for transfers between devices: 165 us -> 2.1 us
  Pallas kernels: 226 us -> 339 us
  matrix products: 104 us -> 88.4 us
  blocking collectives: 11.6 us -> 0 us
  local copies, waits for them, and re-layouts: 7.77 us -> 19.3 us
    all_gather x1 -> x0, waiting for transfers between devices: 98.3 us -> none  [local(): all_tokens = lax.all_gather(inputs, 'ctx', axis=0, tiled=True)]
    pallas_call x0 -> x1, Pallas kernels: none -> 67.9 us  [gather_project(): pl.pallas_call(functools.partial(gather_kernel, 5), out_shape=(shape(runs...]
    all_gather x4 -> x3, waiting for transfers between devices: 64.5 us -> 0.04 us  [gather(): return lax.all_gather(x, 'wsh', axis=0, tiled=True)]
    pallas_call x1, Pallas kernels: 190 us -> 228 us  [reduce_grads(): pl.pallas_call(functools.partial(reduce_kernel, chunk_list, len(parts)),...]
    dot_general x3 -> x0, matrix products: 20.6 us -> none  [the longest x1 9.33 us: local(): keys = jnp.dot(all_tokens, key_w, preferred_element_type=F32).astype(BF)]
    all_gather x2 -> x0, blocking collectives: 11.6 us -> none  [gather(): return lax.all_gather(x, 'wsh', axis=0, tiled=True)]
    reshape x9, local copies, waits for them, and re-layouts: 0.7 us -> 8.74 us  [reduce_all(): vec = jnp.concatenate([v.reshape(n_wsh, -1) for v in vectors], axis=1)]
  transfers between devices with their start and end apart: 5 -> 3, of which waited for: 4 -> 0; matrix products, arithmetic and copies ran while one was open for 7% -> 4% of each run, Pallas kernels for 3% -> 17%
where the time goes in v3:
time: 483 us; the launch traced here: 489 us
  Pallas kernels  339 us (70%)
  matrix products  88.4 us (18%)
  other arithmetic  22.2 us (5%)
  local copies, waits for them, and re-layouts  19.3 us (4%)
  between operations  17.9 us (4%)
    pallas_call x1, Pallas kernels, reduce_grads(): pl.pallas_call(functools.partial(reduce_kernel, chunk_list, len(parts)),...  228 us
    pallas_call x1, Pallas kernels, gather_project(): pl.pallas_call(functools.partial(gather_kernel, 5), out_shape=(shape(runs...  67.9 us
    pallas_call x1, Pallas kernels, attn_bwd(): pl.pallas_call(functools.partial(bwd_kernel, tk), out_shape=(jax.ShapeDty...  26.5 us
    pallas_call x1, Pallas kernels, attn_fwd(): pl.pallas_call(functools.partial(fwd_kernel, tk), out_shape=(jax.ShapeDty...  16.6 us
    dot_general x1, matrix products, local(): jnp.einsum('te,de->td', grad_v, value_w, preferred_element_type=F32)  10.1 us
    dot_general x1, matrix products, local(): jnp.einsum('td,te->de', all_tokens, grad_k, preferred_element_type=F32)  10 us
    dot_general x1, matrix products, local(): jnp.einsum('td,te->de', all_tokens, grad_v, preferred_element_type=F32)  9.89 us
  transfers between devices with their start and end apart: 3, of which 0 were waited for; matrix products, arithmetic and copies ran while one was open for 4% of the time, Pallas kernels for 17%

profile of v3, /device:TPU:0, one launch (start us, length us, event | category | flops | bytes accessed | tf_op | source)
XLA Modules:
  0.0 488.8 jit_solution(17726996675196308157)
XLA Ops:
  14.0 67.9 %gather_project.1 = (bf16[8,512,768]{2,1,0:T(8,128)(2,1)}, bf16[8,512,768]{2,1,0:T(8,128)(2,1)}, bf16[8,512,768]{2,1,0:T(8,128)(2,1)}, bf16[512,768]{1,0:T(8,128...) custom-call(bf16[512,768]{1,0:T(8,128)(2,1)S(1)} %bitcast.91, ...), custom_call_target="tpu_custom_call" | custom-call | tf_op jit(solution)/shard_map/gather_project/pallas_call | solution.py:691
  82.7 1.8 copy-done.5
  87.0 1.4 select_convert_fusion.kaug_ref
  88.4 16.6 %attend.1 = (f32[768,512]{1,0:T(8,128)}, f32[6,2,512]{2,1,0:T(2,128)}) custom-call(s32[1,2]{1,0:T(1,128)} %pad_add_fusion.bounds, bf16[512,768]{1,0:T(8,128)(2,1)} %copy-done, bf16[512,128]{1,0:T(8,128)(2,1)} %and_convert_fusion.qaug_ref, bf16[4096,768]{1,0:T(8,128)(2,1)} %bitcast.92, bf16[4096,128]{1,0:T(8,128)(2,1)} %select_convert_fusion.kaug_ref, ...), custom_call_target="tpu_custom_call" | custom-call | tf_op jit(solution)/shard_map/attend/pallas_call | solution.py:112
  105.1 3.7 fusion.35
  108.8 1.7 multiply_reduce_fusion.3
  110.6 8.4 %multiply_convert_fusion = (bf16[512,3072]{1,0:T(8,128)(2,1)}, f32[512,3072]{1,0:T(8,128)}) fusion(f32[3072]{0:T(1024)S(1)} %add.133, bf16[768,3072]{1,0:T(8,128)(2,1)} %all-gather.6.cloned.1.call-done, f32[512,768]{1,0:T(8,128)} %get-tuple-element.86, f32[768]{0:T(1024)S(1)} %get-tuple-element.53, f32[768]{0:T(1024)S(1)} %get-tuple-element.54, ...), kind=kOutput, calls=%fused_computation.2 | convolution fusion | flops 2427322368 | bytes 15751168 | tf_op jit(solution)/shard_map/dot_general | solution.py:819
  119.0 6.5 %fusion.36 = (f32[512]{0:T(512)S(1)}, f32[512,768]{1,0:T(8,128)S(1)}) fusion(f32[768]{0:T(1024)S(1)} %get-tuple-element.52, bf16[512,3072]{1,0:T(8,128)(2,1)} %get-tuple-element.87, bf16[3072,768]{1,0:T(8,128)(2,1)} %all-gather.8.cloned.1.call-done, f32[768]{0:T(1024)S(1)} %get-tuple-element.53, f32[768]{0:T(1024)S(1)} %get-tuple-element.54, ...), kind=kOutput, calls=%fused_computation.104 | convolution fusion | flops 2418671104 | bytes 11025408 | tf_op jit(solution)/shard_map/dot_general | solution.py:822
  126.5 1.6 fusion.33
  128.9 4.5 convolution_convert_fusion
  133.5 6.0 %fusion.30 = (bf16[3072]{0:T(1024)(128)(2,1)}, bf16[512,3072]{1,0:T(8,128)(2,1)S(1)}) fusion(f32[512,3072]{1,0:T(8,128)S(1)} %bitcast.113, f32[3072]{0:T(1024)S(1)} %add.133, bf16[512,768]{1,0:T(8,128)(2,1)S(1)} %get-tuple-element.59, bf16[3072,768]{1,0:T(8,128)(2,1)S(1)} %bitcast.111), kind=kOutput, calls=%fused_computation.98 | convolution fusion | flops 2439508992 | bytes 14960640 | tf_op jit(solution)/shard_map/td,fd->tf/dot_general | solution.py:830
  139.4 6.2 %convolution_convert_fusion.1 = bf16[768,3072]{1,0:T(8,128)(2,1)} fusion(bf16[512,3072]{1,0:T(8,128)(2,1)S(1)} %get-tuple-element.61, f32[512,768]{1,0:T(8,128)} %get-tuple-element.86, f32[768]{0:T(1024)S(1)} %get-tuple-element.53, f32[768]{0:T(1024)S(1)} %get-tuple-element.54, f32[512]{0:T(512)S(1)} %fusion.21, f32[512]{0:T(512)S(1)} %broadcast_multiply_fusion.1), kind=kOutput, calls=%fused_computation.5 | convolution fusion | flops 2420244480 | bytes 9447424 | tf_op jit(solution)/shard_map/td,tf->df/dot_general | solution.py:833
  145.6 5.1 %multiply_reduce_fusion = (bf16[768]{0:T(1024)(128)(2,1)}, f32[512]{0:T(512)S(1)}, bf16[768]{0:T(1024)(128)(2,1)}, f32[512,768]{1,0:T(8,128)S(1)}) fusion(f32[512,768]{1,0:T(8,128)} %get-tuple-element.86, f32[512]{0:T(512)S(1)} %fusion.21, f32[512]{0:T(512)S(1)} %broadcast_multiply_fusion.1, f32[768]{0:T(1024)S(1)} %get-tuple-element.54, ...), kind=kOutput, calls=%fused_computation.19 | convolution fusion | flops 2419849216 | bytes 12597248 | tf_op jit(solution)/shard_map/tf,df->td/dot_general | solution.py:835
  150.8 2.0 fusion.32
  153.1 1.7 copy-done.10
  154.8 1.8 convolution_convert_fusion.2
  156.6 1.7 convolution_convert_fusion.6.do_ref
  158.3 26.5 %attend_back.1 = (bf16[768,512]{1,0:T(8,128)(2,1)}, bf16[4096,768]{1,0:T(8,128)(2,1)}, bf16[4096,768]{1,0:T(8,128)(2,1)}) custom-call(s32[1,2]{1,0:T(1,128)} %pad_add_fusion.bounds, bf16[512,768]{1,0:T(8,128)(2,1)} %copy-done, bf16[512,128]{1,0:T(8,128)(2,1)} %and_convert_fusion.qaug_ref, bf16[512,768]{1,0:T(8,128)(2,1)} %convolution_convert_fusion.6.do_ref, ...), custom_call_target="tpu_custom_call" | custom-call | tf_op jit(solution)/shard_map/attend_back/pallas_call | solution.py:175
  184.8 3.0 convolution_convert_fusion.5
  188.6 3.7 reduce.4
  192.3 9.9 %convolution_convert_fusion.3 = bf16[768,768]{1,0:T(8,128)(2,1)} fusion(bf16[4096,768]{1,0:T(8,128)(2,1)} %bitcast.106, bf16[4096,768]{1,0:T(8,128)(2,1)} %get-tuple-element.41), kind=kOutput, calls=%fused_computation.28 | convolution fusion | flops 4832428032 | bytes 13762560 | tf_op jit(solution)/shard_map/td,te->de/dot_general | solution.py:848
  202.2 10.0 %convolution_convert_fusion.4 = bf16[768,768]{1,0:T(8,128)(2,1)} fusion(bf16[4096,768]{1,0:T(8,128)(2,1)} %bitcast.107, bf16[4096,768]{1,0:T(8,128)(2,1)} %get-tuple-element.40), kind=kOutput, calls=%fused_computation.29 | convolution fusion | flops 4832428032 | bytes 13762560 | tf_op jit(solution)/shard_map/td,te->de/dot_general | solution.py:847
  214.9 1.4 reshape.238
  220.3 1.5 concatenate.19
  223.2 7.7 %fusion.8 = f32[4096,768]{1,0:T(8,128)S(1)} fusion(bf16[4096,768]{1,0:T(8,128)(2,1)} %get-tuple-element.40, bf16[3,768,768]{2,1,0:T(8,128)(2,1)S(1)} %copy-done.6), kind=kOutput, calls=%fused_computation.40 | convolution fusion | flops 4831838208 | bytes 20054016 | tf_op jit(solution)/shard_map/te,de->td/dot_general | solution.py:844
  230.9 10.1 %add_convert_fusion = bf16[4096,768]{1,0:T(8,128)(2,1)} fusion(f32[4096,768]{1,0:T(8,128)S(1)} %fusion.8, bf16[4096,768]{1,0:T(8,128)(2,1)} %get-tuple-element.41, bf16[3,768,768]{2,1,0:T(8,128)(2,1)S(1)} %copy-done.6), kind=kOutput, calls=%fused_computation | convolution fusion | flops 4838129664 | bytes 26345472 | tf_op jit(solution)/shard_map/te,de->td/dot_general | solution.py:845
  241.0 227.9 %reduce_grads.1 = (bf16[12,192,768]{2,1,0:T(8,128)(2,1)}, f32[16,768]{1,0:T(8,128)}, f32[512,768]{1,0:T(8,128)}) custom-call(bf16[4,192,768]{2,1,0:T(8,128)(2,1)} %bitcast.100, bf16[4,192,768]{2,1,0:T(8,128)(2,1)} %bitcast.102, bf16[4,192,768]{2,1,0:T(8,128)(2,1)} %bitcast.101, bf16[4,192,768]{2,1,0:T(8,128)(2,1)} %bitcast.97, ...), custom_call_target="tpu_custom_call" | custom-call | tf_op jit(solution)/shard_map/reduce_grads/pallas_call | solution.py:447
  468.9 3.2 slice_bitcast_fusion.3
  472.1 1.5 slice.115
  474.9 3.8 fusion.5
  478.7 1.7 bitcast_convert_fusion
  480.4 1.7 maximum_convert_fusion
  (131 shorter events, 18.9 us)
Async XLA Ops:
  7.2 2.4 copy-start.16
  7.2 6.3 %copy-start.18 = (bf16[192]{0:T(256)(128)(2,1)S(1)}, bf16[192]{0:T(256)(128)(2,1)}, u32[]{:S(2)}) copy-start(bf16[192]{0:T(256)(128)(2,1)} %param.27) | copy-start | bytes 1156
  7.2 6.3 %copy-start.19 = (bf16[192]{0:T(256)(128)(2,1)S(1)}, bf16[192]{0:T(256)(128)(2,1)}, u32[]{:S(2)}) copy-start(bf16[192]{0:T(256)(128)(2,1)} %param.28) | copy-start | bytes 1156
  7.2 6.3 %copy-start.20 = (bf16[192]{0:T(256)(128)(2,1)S(1)}, bf16[192]{0:T(256)(128)(2,1)}, u32[]{:S(2)}) copy-start(bf16[192]{0:T(256)(128)(2,1)} %param.29) | copy-start | bytes 1156
  7.2 6.3 %copy-start.21 = (bf16[192]{0:T(256)(128)(2,1)S(1)}, bf16[192]{0:T(256)(128)(2,1)}, u32[]{:S(2)}) copy-start(bf16[192]{0:T(256)(128)(2,1)} %param.30) | copy-start | bytes 1156
  7.2 6.3 %copy-start.22 = (bf16[192]{0:T(256)(128)(2,1)S(1)}, bf16[192]{0:T(256)(128)(2,1)}, u32[]{:S(2)}) copy-start(bf16[192]{0:T(256)(128)(2,1)} %param.31) | copy-start | bytes 1156
  7.3 6.3 %copy-start.23 = (bf16[192]{0:T(256)(128)(2,1)S(1)}, bf16[192]{0:T(256)(128)(2,1)}, u32[]{:S(2)}) copy-start(bf16[192]{0:T(256)(128)(2,1)} %param.33) | copy-start | bytes 1156
  7.3 6.3 %copy-start.24 = (bf16[192]{0:T(256)(128)(2,1)S(1)}, bf16[192]{0:T(256)(128)(2,1)}, u32[]{:S(2)}) copy-start(bf16[192]{0:T(256)(128)(2,1)} %param.34) | copy-start | bytes 1156
  7.3 6.4 %copy-start.25 = (bf16[192]{0:T(256)(128)(2,1)S(1)}, bf16[192]{0:T(256)(128)(2,1)}, u32[]{:S(2)}) copy-start(bf16[192]{0:T(256)(128)(2,1)} %param.35) | copy-start | bytes 1156
  7.3 6.5 %copy-start.15 = (bf16[768]{0:T(1024)(128)(2,1)S(1)}, bf16[768]{0:T(1024)(128)(2,1)}, u32[]{:S(2)}) copy-start(bf16[768]{0:T(1024)(128)(2,1)} %param.32) | copy-start | bytes 4612
  7.3 6.6 %copy-start.1 = (bf16[1,512,768]{2,1,0:T(8,128)(2,1)S(1)}, bf16[1,512,768]{2,1,0:T(8,128)(2,1)}, u32[]{:S(2)}) copy-start(bf16[1,512,768]{2,1,0:T(8,128)(2,1)} %param.18) | copy-start | bytes 2359300
  7.3 6.6 %copy-start.2 = (bf16[192,768]{1,0:T(8,128)(2,1)S(1)}, bf16[192,768]{1,0:T(8,128)(2,1)}, u32[]{:S(2)}) copy-start(bf16[192,768]{1,0:T(8,128)(2,1)} %wk_ref.1) | copy-start | bytes 884740
  7.3 6.6 %copy-start.3 = (bf16[192,768]{1,0:T(8,128)(2,1)S(1)}, bf16[192,768]{1,0:T(8,128)(2,1)}, u32[]{:S(2)}) copy-start(bf16[192,768]{1,0:T(8,128)(2,1)} %wv_ref.1) | copy-start | bytes 884740
  7.3 6.6 %copy-start.4 = (bf16[192,768]{1,0:T(8,128)(2,1)S(1)}, bf16[192,768]{1,0:T(8,128)(2,1)}, u32[]{:S(2)}) copy-start(bf16[192,768]{1,0:T(8,128)(2,1)} %wq_ref.1) | copy-start | bytes 884740
  7.3 97.7 %all-gather.4.cloned.1.call-start = ((), (), s32[]{:S(2)}) async-start(), calls=%async_computation | async-start | bytes 1474560 | tf_op jit(solution)/shard_map/all_gather | solution.py:781
  8.1 102.5 %all-gather.6.cloned.1.call-start = ((), (), s32[]{:S(2)}) async-start(), calls=%async_computation.1 | async-start | bytes 5898240 | tf_op jit(solution)/shard_map/all_gather | solution.py:781
  8.8 75.8 %copy-start.7 = (bf16[1,512,768]{2,1,0:T(8,128)(2,1)S(1)}, bf16[1,512,768]{2,1,0:T(8,128)(2,1)}, u32[]{:S(2)}) copy-start(bf16[1,512,768]{2,1,0:T(8,128)(2,1)} %param.19) | copy-start | bytes 2359300
  8.8 110.1 %all-gather.8.cloned.1.call-start = ((), (), s32[]{:S(2)}) async-start(), calls=%async_computation.2 | async-start | bytes 5898240 | tf_op jit(solution)/shard_map/all_gather | solution.py:781
  82.7 1.8 copy-start.5
  126.5 2.4 copy-start.26
  126.5 6.9 %slice-start.4 = ((s8[6291456]{0:T(1024)(128)(4,1)}), s8[4194304]{0:T(1024)(128)(4,1)S(1)}, s32[]{:S(2)}) async-start(s8[6291456]{0:T(1024)(128)(4,1)} %bitcast.112), calls=%async_computation.7 | async-start | bytes 8388608
  128.1 5.3 %slice-start.2 = ((s8[4718592]{0:T(1024)(128)(4,1)}), s8[4194304]{0:T(1024)(128)(4,1)S(1)}, s32[]{:S(2)}) async-start(s8[4718592]{0:T(1024)(128)(4,1)} %bitcast.110), calls=%async_computation.5 | async-start | bytes 8388608
  128.9 4.5 slice-start.3
  128.9 4.5 slice-start.5
  128.9 16.7 %slice-start = ((s8[4718592]{0:T(1024)(128)(4,1)}), s8[4194304]{0:T(1024)(128)(4,1)S(1)}, s32[]{:S(2)}) async-start(s8[4718592]{0:T(1024)(128)(4,1)} %bitcast.108), calls=%async_computation.3 | async-start | bytes 8388608
  133.5 12.2 %slice-start.1 = ((s8[4718592]{0:T(1024)(128)(4,1)}), s8[524288]{0:T(1024)(128)(4,1)S(1)}, s32[]{:S(2)}) async-start(s8[4718592]{0:T(1024)(128)(4,1)} %bitcast.108), calls=%async_computation.4 | async-start | bytes 1048576
  152.8 3.8 copy-start.8
  152.8 2.0 copy-start.10
  154.8 1.8 copy-start.17
  184.8 3.1 copy-start.13
  202.2 21.0 %copy-start.6 = (bf16[3,768,768]{2,1,0:T(8,128)(2,1)S(1)}, bf16[3,768,768]{2,1,0:T(8,128)(2,1)}, u32[]{:S(2)}) copy-start(bf16[3,768,768]{2,1,0:T(8,128)(2,1)} %copy-done.5) | copy-start | bytes 10616836
  472.1 2.8 copy-start.9
  (4 other events, 5.7 us)
Sparse Core Ops, SparseCore 0:
  9.7 26.4 all-gather.3
  37.8 37.5 all-gather.5
  77.0 37.4 all-gather.7

commit v4 on v3

--- a/solution.py
+++ b/solution.py
@@ -126,7 +126,7 @@
     )(bounds, q, qaug, k, kaug, v)
 
 def bwd_kernel(tk, bounds, q_ref, qaug_ref, do_ref, lse_ref, ot_ref, k_ref, kaug_ref, v_ref,
-               dqt_ref, dk_ref, dv_ref, dk_acc, dv_acc, dq_acc):
+               dq_ref, dk_ref, dv_ref, dk_acc, dv_acc, dq_acc):
     qi = pl.program_id(1)
     start, count = bounds[qi, 0], bounds[qi, 1]
     tq = q_ref.shape[0]
@@ -160,7 +160,7 @@
         return carry
 
     two_level(start, count, tk, step, 0)
-    dqt_ref[...] = (pick_heads(dq_acc[...], tq) * 0.125).astype(BF)
+    dq_ref[...] = (pick_heads(dq_acc[...], tq) * SCALE).T.astype(BF)
 
     @pl.when(qi == pl.num_programs(1) - 1)
     def _():
@@ -174,7 +174,7 @@
     row = lambda h, i, b: (h, 0, i)
     return pl.pallas_call(
         functools.partial(bwd_kernel, tk),
-        out_shape=(jax.ShapeDtypeStruct((D, T), BF), jax.ShapeDtypeStruct((S, D), BF), jax.ShapeDtypeStruct((S, D), BF)),
+        out_shape=(jax.ShapeDtypeStruct((T, D), BF), jax.ShapeDtypeStruct((S, D), BF), jax.ShapeDtypeStruct((S, D), BF)),
         grid_spec=pltpu.PrefetchScalarGridSpec(
             num_scalar_prefetch=1, grid=(pairs, T // tq),
             in_specs=[pl.BlockSpec((tq, 128), lambda h, i, b: (i, h)),
@@ -185,7 +185,7 @@
                       pl.BlockSpec((S, 128), lambda h, i, b: (0, h)),
                       pl.BlockSpec((S, 128), lambda h, i, b: (0, 0)),
                       pl.BlockSpec((S, 128), lambda h, i, b: (0, h))],
-            out_specs=(pl.BlockSpec((128, tq), lambda h, i, b: (h, i)),
+            out_specs=(pl.BlockSpec((tq, 128), lambda h, i, b: (i, h)),
                        pl.BlockSpec((S, 128), lambda h, i, b: (0, h)),
                        pl.BlockSpec((S, 128), lambda h, i, b: (0, h))),
             scratch_shapes=[pltpu.VMEM((S, 128), F32), pltpu.VMEM((S, 128), F32), pltpu.VMEM((128, 2 * tq), F32)]),
@@ -197,14 +197,14 @@
     return n_ctx // 2
 
 
-def reduce_kernel(chunks, n_parts, *refs):
-    parts = refs[:n_parts]
-    vec_ref, rows_ref, out_ref, vec_out, own_ref = refs[n_parts : n_parts + 5]
-    (mine, buf_a, buf_h, buf_b, buf_s, keep, buf_c, buf_u, buf_d, buf_f,
-     vmine, vbuf_a, vbuf_h, vbuf_b, vbuf_s, vbuf_c, vbuf_u, vbuf_d,
-     rmine, rbuf_x, rbuf_s, rbuf_z, rkeep,
-     sem_l, sem_a, sem_b, sem_c, sem_d, sem_e, sem_f, sem_v, sem_rl, sem_rx, sem_rz) = refs[n_parts + 5 :]
-    n_chunks = len(chunks)
+def finish_kernel(n_up, up_ref, vec_ref, dk_ref, dv_ref, tok_ref, dq_ref, w_ref, own_in_ref, mine_tok_ref,
+                  out_ref, vec_out, wide_out, grad_ref,
+                  mine, buf_a, buf_h, buf_b, buf_s, keep, buf_c, buf_u, buf_d, buf_f, gbf,
+                  sums, heard, line,
+                  loads, weights, acc, dq, own, bias,
+                  rsend, rmine, rbuf_x, rbuf_z,
+                  sem_l, sem_a, sem_b, sem_c, sem_d, sem_e, sem_f, sem_v, sem_rx, sem_rz, sem_load, sem_in):
+    n_chunks = out_ref.shape[0]
     n_ctx, n_wsh = lax.axis_size("ctx"), lax.axis_size("wsh")
     zs = n_ctx // 2
     a, w = lax.axis_index("ctx"), lax.axis_index("wsh")
@@ -213,6 +213,9 @@
     core_peer = (a, y * 2 + (1 - c))
     y_peer = (a, (1 - y) * 2 + c)
     x_peer = (z * 2 + (1 - x), w)
+    near = reach(n_ctx)
+    hops = near // 2
+    MESH = pl.DeviceIdType.MESH
 
     def z_peer(d):
         other = lax.rem(z + d, zs)
@@ -224,7 +227,10 @@
     rows = out_ref.shape[1]
     half = out_ref.shape[2] // 2
     piece = rows // zs
-    MESH = pl.DeviceIdType.MESH
+    tall = own.shape[0]
+    n_slices = sem_rx.shape[2]
+    part = tall // n_slices
+
     barrier = pltpu.get_barrier_semaphore()
     for dev in [core_peer, y_peer, x_peer] + [z_peer(d)[1] for d in range(1, zs)]:
         pl.semaphore_signal(barrier, inc=1, device_id=dev, device_id_type=MESH)
@@ -241,64 +247,127 @@
     def wait_out(ref, sems, idx):
         send(ref, ref, sems, idx, core_peer).wait_send()
 
-    for yy in range(2):
-        pltpu.make_async_copy(vec_ref.at[yy * 2 + c], vmine.at[yy], sem_v.at[0, 0]).start()
-        send(vec_ref.at[yy * 2 + (1 - c)], vbuf_a.at[yy], sem_v, (1,), core_peer).start()
-    for k, (p, row0, col0) in enumerate(chunks):
+    def distance(i):
+        return (hops - i // 4) * (1 - 2 * lax.rem(i // 2, 2))
+
+    def position(i):
+        dz = distance(i)
+        mine_too = lax.rem(i, 2)
+        run = 2 * (z + dz) + (1 - x) * (1 - mine_too) + x * mine_too
+        there = (z + dz >= 0) & (z + dz < zs) & (jnp.abs(run - a) <= near)
+        return run, mine_too, i // 2, there
+
+    n_pos = 4 * hops + 2
+
+    def load(i):
+        run, _mine_too, _turn, there = position(i)
+        return there, [
+            pltpu.make_async_copy(src.at[run], loads.at[lax.rem(i, 2), j], sem_load.at[lax.rem(i, 2), j])
+            for j, src in enumerate((dk_ref, dv_ref, tok_ref))
+        ]
+
+    def load_start(i):
+        there, copies = load(i)
+
+        @pl.when(there & (i < n_pos))
+        def _():
+            for copy in copies:
+                copy.start()
+
+    load_start(0)
+    fetch = [pltpu.make_async_copy(w_ref, weights, sem_in.at[0]), pltpu.make_async_copy(dq_ref, dq, sem_in.at[1]),
+             pltpu.make_async_copy(own_in_ref, own, sem_in.at[2])]
+    for copy in fetch:
+        copy.start()
+    for k in range(n_up):
         for yy in range(2):
-            where = (pl.ds(row0, rows), pl.ds(col0, 2 * half))
-            pltpu.make_async_copy(parts[p].at[(yy * 2 + c,) + where], mine.at[k, yy], sem_l.at[k]).start()
-            send(parts[p].at[(yy * 2 + (1 - c),) + where], buf_a.at[k, yy], sem_a, (k,), core_peer).start()
-
-    n_slices = sem_rl.shape[0]
-    tall = own_ref.shape[0] // n_slices
-    near = reach(n_ctx)
-
-    def runs_start(t):
-        rs = pl.ds(pl.multiple_of(t * tall, tall), tall)
-        for zz in range(zs):
-            run = zz * 2 + (1 - x)
-
-            @pl.when(jnp.abs(run - a) <= near)
+            where = (slice(None), pl.ds(k * 2 * half, 2 * half))
+            pltpu.make_async_copy(up_ref.at[(yy * 2 + c,) + where], mine.at[k, yy], sem_l.at[k]).start()
+            send(up_ref.at[(yy * 2 + (1 - c),) + where], buf_a.at[k, yy], sem_a, (k,), core_peer).start()
+    acc[...] = jnp.zeros_like(acc)
+    bias[...] = jnp.zeros_like(bias)
+    fetch[0].wait()
+
+    def unit(i):
+        run, mine_too, turn, there = position(i)
+        at = lax.rem(i, 2)
+        load_start(i + 1)
+
+        @pl.when(there)
+        def _():
+            for copy in load(i)[1]:
+                copy.wait()
+
+            def tokens_part(r, carry):
+                rs = pl.ds(pl.multiple_of(r * 128, 128), 128)
+                g = lax.dot_general(loads[at, 0, rs, :], weights[0], NT, preferred_element_type=F32)
+                g = g + lax.dot_general(loads[at, 1, rs, :], weights[1], NT, preferred_element_type=F32)
+
+                @pl.when(mine_too == 1)
+                def _():
+                    rmine[turn, rs, :] = g.astype(BF)
+
+                @pl.when(mine_too == 0)
+                def _():
+                    rsend[turn, rs, :] = g.astype(BF)
+
+                bias[0:8, :] += jnp.sum(loads[at, 1, rs, :].astype(F32).reshape(16, 8, 2 * half), axis=0)
+                return carry
+
+            lax.fori_loop(0, tall // 128, tokens_part, 0)
+
+            @pl.when(mine_too == 0)
             def _():
-                send(rows_ref.at[run, rs, :], rbuf_x.at[zz, rs, :], sem_rx, (t, zz), x_peer).start()
-
-            @pl.when(jnp.abs(2 * (zz - z)) <= near)
+                for s in range(n_slices):
+                    rs = pl.ds(s * part, part)
+                    send(rsend.at[turn, rs, :], rbuf_x.at[turn, rs, :], sem_rx, (turn, s), x_peer).start()
+
+            def weights_part(r, carry):
+                fs = pl.ds(pl.multiple_of(r * 256, 256), 256)
+                flipped = loads[at, 2, :, fs].T
+                for j in range(2):
+                    acc[j, fs, :] += lax.dot_general(flipped, loads[at, j], NN, preferred_element_type=F32)
+                return carry
+
+            lax.fori_loop(0, 2 * half // 256, weights_part, 0)
+
+    def runs(e):
+        turn, s = e // n_slices, lax.rem(e, n_slices)
+        rs = pl.ds(pl.multiple_of(s * part, part), part)
+        dz = distance(2 * turn)
+        other = z + dz
+
+        @pl.when((other >= 0) & (other < zs))
+        def _():
+            joined = jnp.abs(2 * dz + 2 * x - 1) <= near
+
+            @pl.when(joined)
             def _():
-                pltpu.make_async_copy(rows_ref.at[zz * 2 + x, rs, :], rmine.at[zz, rs, :], sem_rl.at[t, zz]).start()
-
-    def runs_pass(t):
-        rs = pl.ds(pl.multiple_of(t * tall, tall), tall)
-        for zz in range(zs):
-            @pl.when(jnp.abs(2 * (zz - z)) <= near)
+                wait_in(rbuf_x.at[turn, rs, :], sem_rx, (turn, s))
+                sum_ = rmine[turn, rs, :].astype(F32) + rbuf_x[turn, rs, :].astype(F32)
+
+                @pl.when(dz == 0)
+                def _():
+                    own[rs, :] += sum_
+
+                @pl.when(dz != 0)
+                def _():
+                    rmine[turn, rs, :] = sum_.astype(BF)
+
+            @pl.when(dz != 0)
             def _():
-                pltpu.make_async_copy(rmine.at[zz, rs, :], rmine.at[zz, rs, :], sem_rl.at[t, zz]).wait()
-                rkeep[...] = rmine[zz, rs, :].astype(F32)
-
-                @pl.when(jnp.abs(zz * 2 + x - (z * 2 + 1 - x)) <= near)
-                def _():
-                    wait_in(rbuf_x.at[zz, rs, :], sem_rx, (t, zz))
-                    rkeep[...] += rbuf_x[zz, rs, :].astype(F32)
-
-                @pl.when(zz == z)
-                def _():
-                    own_ref[rs, :] = rkeep[...]
-
-                @pl.when(zz != z)
-                def _():
-                    rbuf_s[zz, rs, :] = rkeep[...].astype(BF)
-                    send(rbuf_s.at[zz, rs, :], rbuf_z.at[slot(zz, z), rs, :], sem_rz, (t, slot(zz, z)),
-                         (zz * 2 + x, w)).start()
-
-    def runs_end(t):
-        rs = pl.ds(pl.multiple_of(t * tall, tall), tall)
-        for d in range(1, zs):
-            other, _unused = z_peer(d)
-
-            @pl.when(jnp.abs(2 * (other - z)) <= near)
-            def _():
-                wait_in(rbuf_z.at[d - 1, rs, :], sem_rz, (t, d - 1))
-                own_ref[rs, :] += rbuf_z[d - 1, rs, :].astype(F32)
+                send(rmine.at[turn, rs, :], rbuf_z.at[slot(other, z), rs, :], sem_rz, (slot(other, z), s),
+                     (other * 2 + x, w)).start()
+
+    def runs_end(e):
+        d, s = 1 + e // n_slices, lax.rem(e, n_slices)
+        rs = pl.ds(pl.multiple_of(s * part, part), part)
+        other = lax.rem(z + d, zs)
+
+        @pl.when(jnp.abs(2 * (other - z)) <= near)
+        def _():
+            wait_in(rbuf_z.at[d - 1, rs, :], sem_rz, (d - 1, s))
+            own[rs, :] += rbuf_z[d - 1, rs, :].astype(F32)
 
     def stage_b(k):
         pltpu.make_async_copy(mine.at[k], mine.at[k], sem_l.at[k]).wait()
@@ -311,10 +380,12 @@
 
     def stage_c(k):
         wait_in(buf_b.at[k], sem_b, (k,))
+
         def total(side):
             cols = column(side)
             return (mine[k, y, :, cols].astype(F32) + buf_a[k, y, :, cols].astype(F32)
                     + buf_b[k, :, cols].astype(F32))
+
         buf_s[k] = total(1 - x).astype(BF)
         send(buf_s.at[k], buf_c.at[k], sem_c, (k,), x_peer).start()
         keep[k] = total(x)
@@ -327,7 +398,7 @@
         for d in range(1, zs):
             other, dev = z_peer(d)
             send(buf_u.at[k, pl.ds(pl.multiple_of(other * piece, 16), piece), :], buf_d.at[k, slot(other, z)],
-                 sem_d, (k, ), dev).start()
+                 sem_d, (k,), dev).start()
 
     def stage_e(k):
         wait_in(buf_d.at[k], sem_d, (k,))
@@ -338,7 +409,7 @@
         buf_f[k] = s.astype(BF)
         out_ref[k, my, column(x)] = s.astype(BF)
         for d in range(1, zs):
-            other, dev = z_peer(d)
+            _other, dev = z_peer(d)
             send(buf_f.at[k], out_ref.at[k, my, column(x)], sem_e, (k,), dev).start()
 
     def stage_f(k):
@@ -348,63 +419,117 @@
     def stage_g(k):
         wait_in(out_ref.at[k, :, column(1 - x)], sem_f, (k,))
 
-    def vec_b():
-        pltpu.make_async_copy(vmine, vmine, sem_v.at[0, 0]).wait()
-        wait_in(vbuf_a, sem_v, (1,))
-        vbuf_h[...] = (vmine[1 - y].astype(F32) + vbuf_a[1 - y].astype(F32)).astype(BF)
-        send(vbuf_h, vbuf_b, sem_v, (2,), y_peer).start()
-
-    def vec_c():
-        wait_in(vbuf_b, sem_v, (2,))
-        vbuf_s[...] = (vmine[y].astype(F32) + vbuf_a[y].astype(F32) + vbuf_b[...].astype(F32)).astype(BF)
-        send(vbuf_s, vbuf_c, sem_v, (3,), x_peer).start()
-
-    def vec_d():
-        wait_in(vbuf_c, sem_v, (3,))
-        s = (vbuf_s[...].astype(F32) + vbuf_c[...].astype(F32)).astype(BF)
-        vbuf_u[...] = s
-        vbuf_d[z] = s
+    def guarded(fn, k, low, high):
+        @pl.when((k >= low) & (k < high))
+        def _():
+            fn(k)
+
+    def first_step(t, carry):
+        guarded(unit, t, 0, n_pos)
+        guarded(stage_b, t, 0, n_up)
+        guarded(stage_c, t - 2, 0, n_up)
+        guarded(runs, t - 5, 0, n_slices)
+        guarded(stage_d, t - 5, 0, n_up)
+        guarded(stage_e, t - 7, 0, n_up)
+        return carry
+
+    lax.fori_loop(0, n_up + 7, first_step, 0)
+
+    fetch[1].wait()
+    fetch[2].wait()
+    own_tok = pltpu.make_async_copy(mine_tok_ref, loads.at[0, 2], sem_load.at[0, 2])
+    own_tok.start()
+
+    def to_bf(j, target):
+        for owner in range(n_wsh):
+            gbf[target, owner] = acc[j, owner * rows : (owner + 1) * rows, :].astype(BF)
+
+    def chunk_start(k, j):
+        for yy in range(2):
+            pltpu.make_async_copy(gbf.at[j, yy * 2 + c], mine.at[k, yy], sem_l.at[k]).start()
+            send(gbf.at[j, yy * 2 + (1 - c)], buf_a.at[k, yy], sem_a, (k,), core_peer).start()
+
+    for j in range(2):
+        to_bf(j, j)
+        chunk_start(n_up + j, j)
+    own_tok.wait()
+
+    def query_part(r, carry):
+        fs = pl.ds(pl.multiple_of(r * 256, 256), 256)
+        acc[0, fs, :] = lax.dot_general(loads[0, 2, :, fs].T, dq[...], NN, preferred_element_type=F32)
+        return carry
+
+    lax.fori_loop(0, 2 * half // 256, query_part, 0)
+    to_bf(0, 2)
+    chunk_start(n_up + 2, 2)
+
+    def query_tokens(r, carry):
+        rs = pl.ds(pl.multiple_of(r * 128, 128), 128)
+        own[rs, :] += lax.dot_general(dq[rs, :], weights[2], NT, preferred_element_type=F32)
+        bias[8:16, :] += jnp.sum(dq[rs, :].astype(F32).reshape(16, 8, 2 * half), axis=0)
+        return carry
+
+    lax.fori_loop(0, tall // 128, query_tokens, 0)
+
+    sums[0] = vec_ref[...]
+    sums[0, 0:1, :] = jnp.sum(bias[8:16, :], axis=0, keepdims=True)
+    sums[0, 1:2, :] = jnp.sum(bias[0:8, :], axis=0, keepdims=True)
+    pair = (core_peer, y_peer, x_peer)
+
+    def vec_send(stage):
+        send(sums.at[stage], heard.at[stage], sem_v, (stage,), pair[stage]).start()
+
+    def vec_stage(stage):
+        wait_in(heard.at[stage], sem_v, (stage,))
+        total = sums[stage] + heard[stage]
+        sums[stage + 1] = total
+        if stage < 2:
+            vec_send(stage + 1)
+        else:
+            line[z] = total
+            for d in range(1, zs):
+                _other, dev = z_peer(d)
+                send(sums.at[3], line.at[z], sem_v, (3,), dev).start()
+
+    def vec_last():
+        wait_in(line.at[pl.ds(0, zs - 1)], sem_v, (3,))
+        total = line[0]
         for d in range(1, zs):
-            _unused, dev = z_peer(d)
-            send(vbuf_u, vbuf_d.at[z], sem_v, (4,), dev).start()
-
-    def vec_e():
-        wait_in(vbuf_d.at[pl.ds(0, zs - 1)], sem_v, (4,))
-        s = vbuf_d[0].astype(F32)
-        for d in range(1, zs):
-            s = s + vbuf_d[d].astype(F32)
-        vec_out[...] = s
-
-    def guarded(fn, k, n):
-        @pl.when((k >= 0) & (k < n))
-        def _():
-            fn(k)
-
-    vec_b()
-
-    def step(t, carry):
-        guarded(runs_start, t, n_slices)
-        guarded(stage_b, t, n_chunks)
-        guarded(runs_pass, t - 1, n_slices)
-        guarded(stage_c, t - 2, n_chunks)
-        guarded(runs_end, t - 2, n_slices)
-        guarded(stage_d, t - 3, n_chunks)
-        guarded(stage_e, t - 4, n_chunks)
-        guarded(stage_f, t - 5, n_chunks)
-        guarded(stage_g, t - 6, n_chunks)
-        guarded(lambda k: vec_c(), t - 1, 1)
-        guarded(lambda k: vec_d(), t - 2, 1)
-        guarded(lambda k: vec_e(), t - 3, 1)
-        return carry
-
-    lax.fori_loop(0, max(n_chunks + 6, n_slices + 3, 5), step, 0)
-
-    wait_out(vbuf_a, sem_v, (1,))
-    wait_out(vbuf_h, sem_v, (2,))
-    wait_out(vbuf_s, sem_v, (3,))
-    wait_out(vbuf_d.at[pl.ds(0, zs - 1)], sem_v, (4,))
+            total = total + line[d]
+        small, wide = total[0:8, 0:rows], total[8:9, :]
+        for owner in range(1, n_wsh):
+            small = jnp.where(w == owner, total[0:8, owner * rows : (owner + 1) * rows], small)
+            wide = jnp.where(w == owner, total[8 + owner : 9 + owner, :], wide)
+        vec_out[...] = small
+        wide_out[...] = wide
+
+    vec_send(0)
+
+    def second_step(t, carry):
+        guarded(stage_b, n_up + t, n_up, n_chunks)
+        for stage in range(3):
+            guarded(lambda k: vec_stage(stage), t - 1 - stage, 0, 1)
+        for j in range(2):
+            guarded(runs, n_slices + 2 * t + j, n_slices, (2 * hops + 1) * n_slices)
+        guarded(stage_f, t, 0, n_up)
+        guarded(stage_c, n_up + t - 2, n_up, n_chunks)
+        guarded(stage_d, n_up + t - 5, n_up, n_chunks)
+        guarded(stage_e, n_up + t - 8, n_up, n_chunks)
+        guarded(stage_f, n_up + t - 11, n_up, n_chunks)
+        guarded(lambda k: vec_last(), t - 6, 0, 1)
+        return carry
+
+    lax.fori_loop(0, n_chunks - n_up + 11, second_step, 0)
+
+    def each_end(e, carry):
+        runs_end(e)
+        return carry
+
+    lax.fori_loop(0, (zs - 1) * n_slices, each_end, 0)
+    grad_ref[...] = own[...].astype(BF)
 
     def drain(k, carry):
+        stage_g(k)
         wait_out(buf_a.at[k], sem_a, (k,))
         wait_out(buf_b.at[k], sem_b, (k,))
         wait_out(buf_c.at[k], sem_c, (k,))
@@ -414,59 +539,59 @@
         return carry
 
     lax.fori_loop(0, n_chunks, drain, 0)
-
-    def drain_runs(t, carry):
-        rs = pl.ds(pl.multiple_of(t * tall, tall), tall)
-        for zz in range(zs):
-            @pl.when(jnp.abs(zz * 2 + (1 - x) - a) <= near)
-            def _():
-                wait_out(rbuf_x.at[zz, rs, :], sem_rx, (t, zz))
-
-            @pl.when((zz != z) & (jnp.abs(2 * (zz - z)) <= near))
-            def _():
-                wait_out(rbuf_s.at[zz, rs, :], sem_rz, (t, slot(zz, z)))
-        return carry
-
-    lax.fori_loop(0, n_slices, drain_runs, 0)
-
-
-def reduce_grads(parts, chunks, vec, runs):
+    for stage in range(3):
+        wait_out(heard.at[stage], sem_v, (stage,))
+    wait_out(line.at[pl.ds(0, zs - 1)], sem_v, (3,))
+
+    def drain_runs(e, carry):
+        turn, s = e // n_slices, lax.rem(e, n_slices)
+        rs = pl.ds(pl.multiple_of(s * part, part), part)
+        _run, _mine_too, _turn, there = position(2 * turn)
+
+        @pl.when(there)
+        def _():
+            wait_out(rbuf_x.at[turn, rs, :], sem_rx, (turn, s))
+
+        dz = distance(2 * turn)
+
+        @pl.when((dz != 0) & (z + dz >= 0) & (z + dz < zs))
+        def _():
+            wait_out(rmine.at[turn, rs, :], sem_rz, (slot(z + dz, z), s))
+
+        return carry
+
+    lax.fori_loop(0, (2 * hops + 1) * n_slices, drain_runs, 0)
+
+
+def finish(up_parts, vec, grad_k, grad_v, all_tokens, grad_q, kvq_w, own_grad, inputs):
     n_ctx, n_wsh = lax.axis_size("ctx"), lax.axis_size("wsh")
-    zs = n_ctx // 2
-    rows = chunks[0][1]
-    chunk_list = [(p, r, col) for p, _rows, r, col in chunks]
-    n = len(chunks)
-    half, piece = D // 2, rows // zs
-    tall = runs.shape[1]
-    n_slices = 8
-    vm = pltpu.VMEM
-    dma = pltpu.SemaphoreType.DMA
-    vrows = vec.shape[1]
+    zs, hops = n_ctx // 2, reach(n_ctx) // 2
+    rows, n_up = up_parts.shape[1], up_parts.shape[2] // D
+    n = n_up + 3
+    half, piece, tall = D // 2, rows // zs, inputs.shape[0]
+    turns, n_slices = 2 * hops + 1, 4
+    vm, dma, shape = pltpu.VMEM, pltpu.SemaphoreType.DMA, jax.ShapeDtypeStruct
     any_spec = pl.BlockSpec(memory_space=pl.ANY)
     vm_spec = pl.BlockSpec(memory_space=pltpu.VMEM)
     return pl.pallas_call(
-        functools.partial(reduce_kernel, chunk_list, len(parts)),
-        out_shape=(
-            jax.ShapeDtypeStruct((n, rows, D), BF),
-            jax.ShapeDtypeStruct((vrows, D), F32),
-            jax.ShapeDtypeStruct((tall, D), F32),
-        ),
-        in_specs=[any_spec] * (len(parts) + 2),
-        out_specs=(vm_spec,) * 3,
+        functools.partial(finish_kernel, n_up),
+        out_shape=(shape((n, rows, D), BF), shape((8, rows), F32), shape((1, D), F32), shape((tall, D), BF)),
+        in_specs=[any_spec, vm_spec] + [any_spec] * 7,
+        out_specs=(vm_spec,) * 4,
         scratch_shapes=[
             vm((n, 2, rows, D), BF), vm((n, 2, rows, D), BF), vm((n, rows, D), BF), vm((n, rows, D), BF),
             vm((n, rows, half), BF), vm((n, rows, half), F32), vm((n, rows, half), BF), vm((n, rows, half), BF),
-            vm((n, zs - 1, piece, half), BF), vm((n, piece, half), BF),
-            vm((2, vrows, D), BF), vm((2, vrows, D), BF), vm((vrows, D), BF), vm((vrows, D), BF),
-            vm((vrows, D), BF), vm((vrows, D), BF), vm((vrows, D), BF), vm((zs, vrows, D), BF),
-            vm((zs, tall, D), BF), vm((zs, tall, D), BF), vm((zs, tall, D), BF), vm((zs - 1, tall, D), BF),
-            vm((tall // n_slices, D), F32),
-            dma((n,)), dma((2, n)), dma((2, n)), dma((2, n)), dma((2, n)), dma((2, n)), dma((2, n)), dma((2, 5)),
-            dma((n_slices, zs)), dma((2, n_slices, zs)), dma((2, n_slices, zs)),
+            vm((n, zs - 1, piece, half), BF), vm((n, piece, half), BF), vm((3, n_wsh, rows, D), BF),
+            vm((4,) + vec.shape, F32), vm((3,) + vec.shape, F32), vm((zs,) + vec.shape, F32),
+            vm((2, 3, tall, D), BF), vm((3, D, D), BF), vm((2, D, D), F32), vm((tall, D), BF), vm((tall, D), F32),
+            vm((16, D), F32),
+            vm((turns, tall, D), BF), vm((turns, tall, D), BF), vm((turns, tall, D), BF), vm((zs - 1, tall, D), BF),
+            dma((n,)), dma((2, n)), dma((2, n)), dma((2, n)), dma((2, n)), dma((2, n)), dma((2, n)), dma((2, 4)),
+            dma((2, turns, n_slices)), dma((2, zs - 1, n_slices)), dma((2, 3)), dma((3,)),
         ],
-        compiler_params=pltpu.CompilerParams(collective_id=2, has_side_effects=True, vmem_limit_bytes=62 * 2**20),
-        name="reduce_grads",
-    )(*parts, vec, runs)
+        compiler_params=pltpu.CompilerParams(collective_id=2, has_side_effects=True, vmem_limit_bytes=63 * 2**20),
+        name="finish",
+    )(up_parts, vec, grad_k, grad_v, all_tokens, grad_q, kvq_w, own_grad, inputs)
 
 
 def gather_kernel(cut, tok_ref, vec_ref, wk_ref, wv_ref, wq_ref,
@@ -701,48 +826,6 @@
         compiler_params=pltpu.CompilerParams(collective_id=1, has_side_effects=True, vmem_limit_bytes=48 * 2**20),
         name="gather_project",
     )(inputs, vec, key_weight, value_weight, query_weight)
-
-
-def reduce_all(matrices, vectors, grad_all):
-    n_ctx, n_wsh = lax.axis_size("ctx"), lax.axis_size("wsh")
-    zs = max(n_ctx // 2, 1)
-    own = D // n_wsh
-    if n_wsh != 4 or n_ctx % 2 or own % (zs * 16) or (grad_all.shape[0] // n_ctx) % 128:
-
-        def total(g):
-            part = lax.psum_scatter(g.astype(BF), "wsh", scatter_dimension=0, tiled=True)
-            return lax.psum(part, "ctx").astype(F32)
-
-        grad_own = lax.psum_scatter(grad_all, "ctx", scatter_dimension=0, tiled=True)
-        return [total(g) for g in matrices + vectors], grad_own.astype(F32)
-
-    parts, chunks, spans = [], [], []
-    for p, g in enumerate(matrices):
-        tall, wide = g.shape[0] // n_wsh, g.shape[1]
-        parts.append(g.astype(BF).reshape(n_wsh, tall, wide))
-        spans.append((len(chunks), tall // own, wide // D))
-        for r in range(tall // own):
-            for col in range(wide // D):
-                chunks.append((p, own, r * own, col * D))
-    vec = jnp.concatenate([v.reshape(n_wsh, -1) for v in vectors], axis=1)
-    width = vec.shape[1]
-    tall = -(-width // (16 * D)) * 16
-    vec = jnp.pad(vec, ((0, 0), (0, tall * D - width))).astype(BF).reshape(n_wsh, tall, D)
-    summed, vec_sum, grad_own = reduce_grads(
-        parts, chunks, vec, grad_all.reshape(n_ctx, grad_all.shape[0] // n_ctx, D)
-    )
-    sums = []
-    for first, down, across in spans:
-        block = summed[first : first + down * across]
-        if across > 1:
-            block = jnp.concatenate([block[i] for i in range(across)], axis=1)
-        sums.append(block.reshape(down * own, across * D).astype(F32))
-    flat, place = vec_sum.reshape(-1), 0
-    for v in vectors:
-        size = v.shape[0] // n_wsh
-        sums.append(flat[place : place + size])
-        place += size
-    return sums, grad_own
 
 
 def local(
@@ -783,7 +866,8 @@
     small = jnp.stack(
         [query_bias, value_bias, out_bias, attn_gain, attn_shift, down_bias, final_gain, final_shift]
     )
-    if n_wsh == 4 and n_ctx % 4 == 0 and own % 16 == 0 and tok_rows % 512 == 0:
+    fast = n_wsh == 4 and n_ctx % 4 == 0 and own % (n_ctx // 2 * 16) == 0 and tok_rows % 512 == 0
+    if fast:
         w = lax.axis_index("wsh")
         at = lax.broadcasted_iota(jnp.int32, (8, D), 1) // own == w
         vec = jnp.where(at, jnp.tile(small, (1, n_wsh)), jnp.zeros((), BF))
@@ -838,26 +922,47 @@
     grad_out_w = jnp.dot(attn_t, grad_branch, preferred_element_type=F32)
     grad_out_b = jnp.sum(grad_branch.astype(F32), axis=0)
     grad_attn = jnp.einsum("te,de->td", grad_branch, out_w, preferred_element_type=F32).astype(BF)
-    grad_q_t, grad_k, grad_v = attn_bwd(
+    grad_q, grad_k, grad_v = attn_bwd(
         bounds, queries, query_doc, grad_attn, log_rows, mixed_t, keys, key_doc, values, tq=tile
     )
-    grad_all = jnp.einsum("te,de->td", grad_k, key_w, preferred_element_type=F32)
-    grad_all = grad_all + jnp.einsum("te,de->td", grad_v, value_w, preferred_element_type=F32)
-    grad_query_w = jnp.einsum("td,et->de", inputs, grad_q_t, preferred_element_type=F32)
-    grad_key_w = jnp.einsum("td,te->de", all_tokens, grad_k, preferred_element_type=F32)
-    grad_value_w = jnp.einsum("td,te->de", all_tokens, grad_v, preferred_element_type=F32)
-    grad_query_b = jnp.sum(grad_q_t.astype(F32), axis=1)
-    grad_value_b = jnp.sum(grad_v.astype(F32), axis=0)
-    grad_inputs = grad_sum1 + lax.dot_general(
-        grad_q_t, query_w, (((0,), (1,)), ((), ())), preferred_element_type=F32
-    )
-    matrices = (grad_query_w, grad_key_w, grad_value_w, grad_out_w, grad_up_w, grad_down_w)
-    vectors = (
-        grad_query_b, grad_value_b, grad_out_b, grad_attn_g, grad_attn_s,
-        grad_up_b, grad_down_b, grad_final_g, grad_final_s,
-    )
-    sums, grad_own = reduce_all(matrices, vectors, grad_all.astype(BF))
-    grad_inputs = grad_inputs + grad_own
+    def total(g):
+        part = lax.psum_scatter(g.astype(BF), "wsh", scatter_dimension=0, tiled=True)
+        return lax.psum(part, "ctx").astype(F32)
+
+    if fast:
+        none = jnp.zeros((D,), F32)
+        vec = jnp.stack([none, none, grad_out_b, grad_attn_g, grad_attn_s, grad_down_b, grad_final_g, grad_final_s])
+        vec = jnp.concatenate([vec, grad_up_b.reshape(n_wsh, -1), jnp.zeros((8 - n_wsh, D), F32)], axis=0)
+        summed, small, wide, grad_inputs = finish(
+            grad_up_w.astype(BF).reshape(n_wsh, own, -1), vec, grad_k.reshape(n_ctx, tok_rows, D),
+            grad_v.reshape(n_ctx, tok_rows, D), all_tokens.reshape(n_ctx, tok_rows, D), grad_q, kvq_w, grad_sum1, inputs,
+        )
+        n_up = summed.shape[0] - 3
+        up_sum = jnp.concatenate([summed[i] for i in range(n_up)], axis=1)
+        sums = [
+            summed[n_up + 2].astype(F32), summed[n_up].astype(F32), summed[n_up + 1].astype(F32), total(grad_out_w),
+            up_sum.astype(F32), total(grad_down_w), small[0], small[1], small[2], small[3], small[4], wide[0],
+            small[5], small[6], small[7],
+        ]
+    else:
+        grad_all = jnp.einsum("te,de->td", grad_k, key_w, preferred_element_type=F32)
+        grad_all = grad_all + jnp.einsum("te,de->td", grad_v, value_w, preferred_element_type=F32)
+        grad_own = lax.psum_scatter(grad_all.astype(BF), "ctx", scatter_dimension=0, tiled=True)
+        grad_query_w = jnp.einsum("td,te->de", inputs, grad_q, preferred_element_type=F32)
+        grad_key_w = jnp.einsum("td,te->de", all_tokens, grad_k, preferred_element_type=F32)
+        grad_value_w = jnp.einsum("td,te->de", all_tokens, grad_v, preferred_element_type=F32)
+        grad_query_b = jnp.sum(grad_q.astype(F32), axis=0)
+        grad_value_b = jnp.sum(grad_v.astype(F32), axis=0)
+        grad_inputs = grad_sum1 + jnp.einsum("te,de->td", grad_q, query_w, preferred_element_type=F32)
+        grad_inputs = grad_inputs + grad_own.astype(F32)
+        sums = [
+            total(g)
+            for g in (
+                grad_query_w, grad_key_w, grad_value_w, grad_out_w, grad_up_w, grad_down_w,
+                grad_query_b, grad_value_b, grad_out_b, grad_attn_g, grad_attn_s, grad_up_b,
+                grad_down_b, grad_final_g, grad_final_s,
+            )
+        ]
     return (
         layer_out.reshape(1, tok_rows, D),
         grad_inputs.astype(BF).reshape(1, tok_rows, D),

time: 483 us -> 473 us (0.979); the launches traced: 489 us -> 472 us
  matrix products: 88.4 us -> 43.5 us
  waiting for transfers between devices: 2.1 us -> 33.1 us
  Pallas kernels: 339 us -> 349 us
  local copies, waits for them, and re-layouts: 19.3 us -> 10.2 us
    dot_general x6 -> x0, matrix products: 44.6 us -> none  [the longest x1 10.1 us: local(): jnp.einsum('te,de->td', grad_v, value_w, preferred_element_type=F32)]
    reduce_scatter x0 -> x2, waiting for transfers between devices: none -> 30.9 us  [total(): lax.psum_scatter(g.astype(BF), 'wsh', scatter_dimension=0, tiled=True)]
    pallas_call x1, Pallas kernels: 228 us -> 206 us  [finish(): pl.pallas_call(functools.partial(finish_kernel, n_up), out_shape=(shape((...]
    pallas_call x1, Pallas kernels: 26.5 us -> 46.7 us  [attn_bwd(): pl.pallas_call(functools.partial(bwd_kernel, tk), out_shape=(jax.ShapeDty...]
    pallas_call x1, Pallas kernels: 16.6 us -> 28.6 us  [attn_fwd(): pl.pallas_call(functools.partial(fwd_kernel, tk), out_shape=(jax.ShapeDty...]
    reshape x10 -> x5, local copies, waits for them, and re-layouts: 8.75 us -> 0.03 us  [the longest x4 0.02 us: layer_norm(): return centred * lax.rsqrt(variance + EPS) * gain_vec + shift_vec]
  transfers between devices with their start and end apart: 3 -> 6, of which waited for: 0 -> 1; matrix products, arithmetic and copies ran while one was open for 4% -> 9% of each run, Pallas kernels for 17% -> 74%
where the time goes in v4:
time: 473 us; the launch traced here: 472 us
  Pallas kernels  349 us (74%)
  matrix products  43.5 us (9%)
  waiting for transfers between devices  33.1 us (7%)
  other arithmetic  18.2 us (4%)
  between operations  18 us (4%)
  local copies, waits for them, and re-layouts  10.2 us (2%)
    pallas_call x1, Pallas kernels, finish(): pl.pallas_call(functools.partial(finish_kernel, n_up), out_shape=(shape((...  206 us
    pallas_call x1, Pallas kernels, gather_project(): pl.pallas_call(functools.partial(gather_kernel, 5), out_shape=(shape(runs...  67.5 us
    pallas_call x1, Pallas kernels, attn_bwd(): pl.pallas_call(functools.partial(bwd_kernel, tk), out_shape=(jax.ShapeDty...  46.7 us
    reduce_scatter x2, waiting for transfers between devices, total(): lax.psum_scatter(g.astype(BF), 'wsh', scatter_dimension=0, tiled=True)  30.9 us
    pallas_call x1, Pallas kernels, attn_fwd(): pl.pallas_call(functools.partial(fwd_kernel, tk), out_shape=(jax.ShapeDty...  28.6 us
  transfers between devices with their start and end apart: 6, of which 1 were waited for; matrix products, arithmetic and copies ran while one was open for 9% of the time, Pallas kernels for 74%

profile of v4, /device:TPU:0, one launch (start us, length us, event | category | flops | bytes accessed | tf_op | source)
XLA Modules:
  0.0 471.8 jit_solution(2583021163312973290)
XLA Ops:
  8.1 0.7 all-gather.6.cloned.1.call-update
  14.0 67.5 %gather_project.1 = (bf16[8,512,768]{2,1,0:T(8,128)(2,1)}, bf16[8,512,768]{2,1,0:T(8,128)(2,1)}, bf16[8,512,768]{2,1,0:T(8,128)(2,1)}, bf16[512,768]{1,0:T(8,128...) custom-call(bf16[512,768]{1,0:T(8,128)(2,1)S(1)} %bitcast.72, ...), custom_call_target="tpu_custom_call" | custom-call | tf_op jit(solution)/shard_map/gather_project/pallas_call | solution.py:816
  81.5 1.7 copy-done
  83.3 0.9 copy-done.1
  85.0 0.8 and_convert_fusion.qaug_ref
  85.8 1.4 select_convert_fusion.kaug_ref
  87.2 28.6 %attend.1 = (f32[768,512]{1,0:T(8,128)}, f32[6,2,512]{2,1,0:T(2,128)}) custom-call(s32[1,2]{1,0:T(1,128)} %pad_add_fusion.bounds, bf16[512,768]{1,0:T(8,128)(2,1)} %copy-done.1, bf16[512,128]{1,0:T(8,128)(2,1)} %and_convert_fusion.qaug_ref, bf16[4096,768]{1,0:T(8,128)(2,1)} %bitcast.73, bf16[4096,128]{1,0:T(8,128)(2,1)} %select_convert_fusion.kaug_ref, ...), custom_call_target="tpu_custom_call" | custom-call | tf_op jit(solution)/shard_map/attend/pallas_call | solution.py:112
  115.9 2.7 fusion.27
  118.9 8.3 %multiply_convert_fusion = (bf16[512,3072]{1,0:T(8,128)(2,1)}, f32[512,3072]{1,0:T(8,128)}) fusion(f32[3072]{0:T(1024)S(1)} %add.130, bf16[768,3072]{1,0:T(8,128)(2,1)} %all-gather.6.cloned.1.call-done, f32[512,768]{1,0:T(8,128)S(1)} %get-tuple-element.89, f32[768]{0:T(1024)S(1)} %get-tuple-element.55, f32[768]{0:T(1024)S(1)} %get-tuple-element.56, ...), kind=kOutput, calls=%fused_computation.2 | convolution fusion | flops 2427322368 | bytes 15751168 | tf_op jit(solution)/shard_map/dot_general | solution.py:903
  127.2 6.2 %fusion.28 = (f32[512]{0:T(512)S(1)}, f32[512,768]{1,0:T(8,128)S(1)}) fusion(f32[768]{0:T(1024)S(1)} %get-tuple-element.54, bf16[512,3072]{1,0:T(8,128)(2,1)} %get-tuple-element.90, bf16[3072,768]{1,0:T(8,128)(2,1)} %all-gather.8.cloned.1.call-done, f32[768]{0:T(1024)S(1)} %get-tuple-element.55, f32[768]{0:T(1024)S(1)} %get-tuple-element.56, ...), kind=kOutput, calls=%fused_computation.91 | convolution fusion | flops 2418671104 | bytes 11025408 | tf_op jit(solution)/shard_map/dot_general | solution.py:906
  133.7 0.8 copy-done.7
  134.5 0.8 fusion.6
  135.3 1.6 fusion.25
  137.1 0.8 copy-done.14
  137.9 5.2 %convert_reduce_fusion = (f32[3072]{0:T(1024)S(1)}, bf16[512,3072]{1,0:T(8,128)(2,1)S(1)}) fusion(f32[512,3072]{1,0:T(8,128)S(1)} %copy-done.23, f32[3072]{0:T(1024)S(1)} %add.130, bf16[512,768]{1,0:T(8,128)(2,1)S(1)} %get-tuple-element.65, bf16[3072,768]{1,0:T(8,128)(2,1)S(1)} %copy-done.14), kind=kOutput, calls=%fused_computation | convolution fusion | flops 2441081856 | bytes 14966784 | tf_op jit(solution)/shard_map/td,fd->tf/dot_general | solution.py:914
  143.2 3.1 multiply_reduce_fusion
  147.2 1.7 copy-done.10
  149.0 1.8 convolution_convert_fusion.2
  150.9 6.7 %convolution_convert_fusion = bf16[3072,768]{1,0:T(8,128)(2,1)} fusion(bf16[512,3072]{1,0:T(8,128)(2,1)} %get-tuple-element.90, bf16[512,768]{1,0:T(8,128)(2,1)S(1)} %get-tuple-element.65), kind=kOutput, calls=%fused_computation.4 | convolution fusion | flops 2418278400 | bytes 8650752 | tf_op jit(solution)/shard_map/tf,td->fd/dot_general | solution.py:912
  157.8 3.0 convolution_convert_fusion.3.do_ref
  160.8 46.7 %attend_back.1 = (bf16[512,768]{1,0:T(8,128)(2,1)}, bf16[4096,768]{1,0:T(8,128)(2,1)}, bf16[4096,768]{1,0:T(8,128)(2,1)}) custom-call(s32[1,2]{1,0:T(1,128)} %pad_add_fusion.bounds, bf16[512,768]{1,0:T(8,128)(2,1)} %copy-done.1, bf16[512,128]{1,0:T(8,128)(2,1)} %and_convert_fusion.qaug_ref, bf16[512,768]{1,0:T(8,128)(2,1)} %convolution_convert_fusion.3.do_ref, ...), custom_call_target="tpu_custom_call" | custom-call | tf_op jit(solution)/shard_map/attend_back/pallas_call | solution.py:175
  207.6 1.3 concatenate.22.vec_ref
  208.8 30.9 %reduce-scatter.5.cloned.1.call-done = bf16[768,768]{1,0:T(8,128)(2,1)} async-done(((bf16[3072,768]{1,0:T(8,128)(2,1)}), bf16[768,768]{1,0:T(8,128)(2,1)}) %reduce-scatter.5.cloned.1.call-update) | async-done | bytes 1179664 | tf_op jit(solution)/shard_map/reduce_scatter | solution.py:929
  239.8 6.5 %convolution_convert_fusion.1 = bf16[768,3072]{1,0:T(8,128)(2,1)} fusion(bf16[512,3072]{1,0:T(8,128)(2,1)} %copy-done.24, f32[512,768]{1,0:T(8,128)S(1)} %copy-done.9, f32[768]{0:T(1024)S(1)} %get-tuple-element.55, f32[768]{0:T(1024)S(1)} %get-tuple-element.56, f32[512]{0:T(512)S(1)} %fusion.15, f32[512]{0:T(512)S(1)} %broadcast_multiply_fusion.1), kind=kOutput, calls=%fused_computation.5 | convolution fusion | flops 2420244480 | bytes 9447424 | tf_op jit(solution)/shard_map/td,tf->df/dot_general | solution.py:917
  246.3 205.8 %finish.1 = (bf16[7,192,768]{2,1,0:T(8,128)(2,1)}, f32[8,192]{1,0:T(8,128)}, f32[1,768]{1,0:T(1,128)}, bf16[512,768]{1,0:T(8,128)(2,1)}) custom-call(bf16[4,192,3072]{2,1,0:T(8,128)(2,1)} %bitcast.79, f32[16,768]{1,0:T(8,128)} %concatenate.22.vec_ref, bf16[8,512,768]{2,1,0:T(8,128)(2,1)} %bitcast.77, bf16[8,512,768]{2,1,0:T(8,128)(2,1)} %bitcast.78, ...), custom_call_target="tpu_custom_call" | custom-call | tf_op jit(solution)/shard_map/finish/pallas_call | solution.py:576
  452.1 1.3 reduce.9
  453.4 1.6 fusion.26
  455.0 2.7 slice_bitcast_fusion.3
  457.7 1.7 maximum_convert_fusion
  459.4 1.8 convert_element_type.108
  461.2 2.9 convert_element_type.111
  464.1 0.9 copy.38
  (116 shorter events, 5.4 us)
Async XLA Ops:
  7.2 2.4 copy-start.13
  7.2 6.3 %copy-start.15 = (bf16[192]{0:T(256)(128)(2,1)S(1)}, bf16[192]{0:T(256)(128)(2,1)}, u32[]{:S(2)}) copy-start(bf16[192]{0:T(256)(128)(2,1)} %param.27) | copy-start | bytes 1156
  7.2 6.3 %copy-start.16 = (bf16[192]{0:T(256)(128)(2,1)S(1)}, bf16[192]{0:T(256)(128)(2,1)}, u32[]{:S(2)}) copy-start(bf16[192]{0:T(256)(128)(2,1)} %param.28) | copy-start | bytes 1156
  7.2 6.3 %copy-start.17 = (bf16[192]{0:T(256)(128)(2,1)S(1)}, bf16[192]{0:T(256)(128)(2,1)}, u32[]{:S(2)}) copy-start(bf16[192]{0:T(256)(128)(2,1)} %param.29) | copy-start | bytes 1156
  7.2 6.4 %copy-start.18 = (bf16[192]{0:T(256)(128)(2,1)S(1)}, bf16[192]{0:T(256)(128)(2,1)}, u32[]{:S(2)}) copy-start(bf16[192]{0:T(256)(128)(2,1)} %param.30) | copy-start | bytes 1156
  7.2 6.4 %copy-start.19 = (bf16[192]{0:T(256)(128)(2,1)S(1)}, bf16[192]{0:T(256)(128)(2,1)}, u32[]{:S(2)}) copy-start(bf16[192]{0:T(256)(128)(2,1)} %param.31) | copy-start | bytes 1156
  7.3 6.4 %copy-start.20 = (bf16[192]{0:T(256)(128)(2,1)S(1)}, bf16[192]{0:T(256)(128)(2,1)}, u32[]{:S(2)}) copy-start(bf16[192]{0:T(256)(128)(2,1)} %param.33) | copy-start | bytes 1156
  7.3 6.4 %copy-start.21 = (bf16[192]{0:T(256)(128)(2,1)S(1)}, bf16[192]{0:T(256)(128)(2,1)}, u32[]{:S(2)}) copy-start(bf16[192]{0:T(256)(128)(2,1)} %param.34) | copy-start | bytes 1156
  7.3 6.4 %copy-start.22 = (bf16[192]{0:T(256)(128)(2,1)S(1)}, bf16[192]{0:T(256)(128)(2,1)}, u32[]{:S(2)}) copy-start(bf16[192]{0:T(256)(128)(2,1)} %param.35) | copy-start | bytes 1156
  7.3 6.6 %copy-start.12 = (bf16[768]{0:T(1024)(128)(2,1)S(1)}, bf16[768]{0:T(1024)(128)(2,1)}, u32[]{:S(2)}) copy-start(bf16[768]{0:T(1024)(128)(2,1)} %param.32) | copy-start | bytes 4612
  7.3 6.7 %copy-start.2 = (bf16[1,512,768]{2,1,0:T(8,128)(2,1)S(1)}, bf16[1,512,768]{2,1,0:T(8,128)(2,1)}, u32[]{:S(2)}) copy-start(bf16[1,512,768]{2,1,0:T(8,128)(2,1)} %param.18) | copy-start | bytes 2359300
  7.3 6.7 %copy-start.3 = (bf16[192,768]{1,0:T(8,128)(2,1)S(1)}, bf16[192,768]{1,0:T(8,128)(2,1)}, u32[]{:S(2)}) copy-start(bf16[192,768]{1,0:T(8,128)(2,1)} %wk_ref.1) | copy-start | bytes 884740
  7.3 6.7 %copy-start.4 = (bf16[192,768]{1,0:T(8,128)(2,1)S(1)}, bf16[192,768]{1,0:T(8,128)(2,1)}, u32[]{:S(2)}) copy-start(bf16[192,768]{1,0:T(8,128)(2,1)} %wv_ref.1) | copy-start | bytes 884740
  7.3 6.7 %copy-start.5 = (bf16[192,768]{1,0:T(8,128)(2,1)S(1)}, bf16[192,768]{1,0:T(8,128)(2,1)}, u32[]{:S(2)}) copy-start(bf16[192,768]{1,0:T(8,128)(2,1)} %wq_ref.1) | copy-start | bytes 884740
  7.3 108.5 %all-gather.4.cloned.1.call-start = ((), (), s32[]{:S(2)}) async-start(), calls=%async_computation.2 | async-start | bytes 1474560 | tf_op jit(solution)/shard_map/all_gather | solution.py:864
  8.1 110.8 %all-gather.6.cloned.1.call-start = ((), (), s32[]{:S(2)}) async-start(), calls=%async_computation.3 | async-start | bytes 5898240 | tf_op jit(solution)/shard_map/all_gather | solution.py:864
  8.8 118.4 %all-gather.8.cloned.1.call-start = ((), (), s32[]{:S(2)}) async-start(), calls=%async_computation.4 | async-start | bytes 5898240 | tf_op jit(solution)/shard_map/all_gather | solution.py:864
  9.6 199.3 %reduce-scatter.3.cloned.1.call-start = ((), (), s32[]{:S(2)}) async-start(), calls=%async_computation.5 | async-start | bytes 1474560 | tf_op jit(solution)/shard_map/reduce_scatter | solution.py:929
  81.5 1.7 copy-start
  118.5 27.8 %copy-start.8 = (f32[512,768]{1,0:T(8,128)}, f32[512,768]{1,0:T(8,128)S(1)}, u32[]{:S(2)}) copy-start(f32[512,768]{1,0:T(8,128)S(1)} %get-tuple-element.89) | copy-start | bytes 4718596
  127.2 9.9 %copy-start.23 = (f32[512,3072]{1,0:T(8,128)S(1)}, f32[512,3072]{1,0:T(8,128)}, u32[]{:S(2)}) copy-start(f32[512,3072]{1,0:T(8,128)} %get-tuple-element.91) | copy-start | bytes 18874372
  133.4 1.1 copy-start.7
  135.3 2.6 copy-start.14
  136.9 6.3 %slice-start = ((s8[4718592]{0:T(1024)(128)(4,1)}), s8[4194304]{0:T(1024)(128)(4,1)S(1)}, s32[]{:S(2)}) async-start(s8[4718592]{0:T(1024)(128)(4,1)} %bitcast.90), calls=%async_computation.8 | async-start | bytes 8388608
  137.9 5.3 %slice-start.1 = ((s8[4718592]{0:T(1024)(128)(4,1)}), s8[524288]{0:T(1024)(128)(4,1)S(1)}, s32[]{:S(2)}) async-start(s8[4718592]{0:T(1024)(128)(4,1)} %bitcast.90), calls=%async_computation.9 | async-start | bytes 1048576
  143.2 3.2 copy-start.24
  147.0 2.0 copy-start.10
  147.2 10.6 %copy-start.6 = (f32[512,768]{1,0:T(8,128)}, f32[512,768]{1,0:T(8,128)S(1)}, u32[]{:S(2)}) copy-start(f32[512,768]{1,0:T(8,128)S(1)} %get-tuple-element.67.own_in_ref) | copy-start | bytes 4718596
  150.8 88.9 %reduce-scatter.5.cloned.1.call-start = ((), (), s32[]{:S(2)}) async-start(), calls=%async_computation.6 | async-start | bytes 5898240 | tf_op jit(solution)/shard_map/reduce_scatter | solution.py:929
  157.5 301.8 %all-reduce.4.cloned.1.call-start = ((), (), s32[]{:S(2)}) async-start(), calls=%async_computation.7 | async-start | bytes 2949120 | tf_op jit(solution)/shard_map/psum | solution.py:930
  207.5 32.2 %copy-start.9 = (f32[512,768]{1,0:T(8,128)S(1)}, f32[512,768]{1,0:T(8,128)}, u32[]{:S(2)}) copy-start(f32[512,768]{1,0:T(8,128)} %copy-done.8) | copy-start | bytes 4718596
  461.2 2.9 copy-start.11
  (1 other events, 0.9 us)
Sparse Core Ops, SparseCore 0:
  9.7 26.4 all-gather.3
  37.8 37.5 all-gather.5
  77.0 37.4 all-gather.7
  150.9 38.3 reduce-scatter.2
  191.9 47.8 reduce-scatter.4
  243.4 107.6 all-reduce.3

commit v5 on v4

--- a/solution.py
+++ b/solution.py
@@ -197,13 +197,16 @@
     return n_ctx // 2
 
 
-def finish_kernel(n_up, up_ref, vec_ref, dk_ref, dv_ref, tok_ref, dq_ref, w_ref, own_in_ref, mine_tok_ref,
-                  out_ref, vec_out, wide_out, grad_ref,
-                  mine, buf_a, buf_h, buf_b, buf_s, keep, buf_c, buf_u, buf_d, buf_f, gbf,
-                  sums, heard, line,
-                  loads, weights, acc, dq, own, bias,
-                  rsend, rmine, rbuf_x, rbuf_z,
-                  sem_l, sem_a, sem_b, sem_c, sem_d, sem_e, sem_f, sem_v, sem_rx, sem_rz, sem_load, sem_in):
+def finish_kernel(sources, n_parts, *refs):
+    parts = refs[:n_parts]
+    (vec_ref, dk_ref, dv_ref, tok_ref, dq_ref, w_ref, own_in_ref, mine_tok_ref,
+     out_ref, vec_out, wide_out, grad_ref,
+     mine, buf_a, buf_h, buf_b, buf_s, buf_c, buf_d, buf_e, gbf,
+     sums, heard, line,
+     loads, weights, acc, dq, own, bias,
+     run_part, from_x, from_z, far_z, last_x,
+     sem_l, sem_a, sem_b, sem_c, sem_d, sem_v, sem_x, sem_z, sem_far, sem_load, sem_in) = refs[n_parts:]
+    n_ready = len(sources)
     n_chunks = out_ref.shape[0]
     n_ctx, n_wsh = lax.axis_size("ctx"), lax.axis_size("wsh")
     zs = n_ctx // 2
@@ -213,26 +216,25 @@
     core_peer = (a, y * 2 + (1 - c))
     y_peer = (a, (1 - y) * 2 + c)
     x_peer = (z * 2 + (1 - x), w)
+    low, high = lax.rem(z, 2), z // 2
+    pair_peer = ((z + 1 - 2 * low) * 2 + x, w)
+    skip_peer = (lax.rem(z + 2, zs) * 2 + x, w)
+    up_peer, down_peer = (a + 2, w), (a - 2, w)
     near = reach(n_ctx)
     hops = near // 2
     MESH = pl.DeviceIdType.MESH
-
-    def z_peer(d):
-        other = lax.rem(z + d, zs)
-        return other, (other * 2 + x, w)
-
-    def slot(dest, src):
-        return lax.rem(src - dest + zs, zs) - 1
 
     rows = out_ref.shape[1]
     half = out_ref.shape[2] // 2
     piece = rows // zs
     tall = own.shape[0]
-    n_slices = sem_rx.shape[2]
-    part = tall // n_slices
+    cut = from_x.shape[1]
+
+    def z_peer(d):
+        return (lax.rem(z + d, zs) * 2 + x, w)
 
     barrier = pltpu.get_barrier_semaphore()
-    for dev in [core_peer, y_peer, x_peer] + [z_peer(d)[1] for d in range(1, zs)]:
+    for dev in [core_peer, y_peer, x_peer] + [z_peer(d) for d in range(1, zs)]:
         pl.semaphore_signal(barrier, inc=1, device_id=dev, device_id_type=MESH)
     pl.semaphore_wait(barrier, zs + 2)
 
@@ -254,13 +256,12 @@
         dz = distance(i)
         mine_too = lax.rem(i, 2)
         run = 2 * (z + dz) + (1 - x) * (1 - mine_too) + x * mine_too
-        there = (z + dz >= 0) & (z + dz < zs) & (jnp.abs(run - a) <= near)
-        return run, mine_too, i // 2, there
+        return run, mine_too, (z + dz >= 0) & (z + dz < zs) & (jnp.abs(run - a) <= near)
 
     n_pos = 4 * hops + 2
 
     def load(i):
-        run, _mine_too, _turn, there = position(i)
+        run, _mine_too, there = position(i)
         return there, [
             pltpu.make_async_copy(src.at[run], loads.at[lax.rem(i, 2), j], sem_load.at[lax.rem(i, 2), j])
             for j, src in enumerate((dk_ref, dv_ref, tok_ref))
@@ -273,23 +274,38 @@
         def _():
             for copy in copies:
                 copy.start()
+
+    def share(k, owner):
+        if k < n_ready:
+            p, row0, col0 = sources[k]
+            return parts[p].at[owner, pl.ds(row0, rows), pl.ds(col0, 2 * half)]
+        return gbf.at[k - n_ready, owner]
+
+    def share_load(k):
+        for yy in range(2):
+            pltpu.make_async_copy(share(k, yy * 2 + c), mine.at[k % 4, yy], sem_l.at[k]).start()
+
+    def share_send(k):
+        for yy in range(2):
+            send(share(k, yy * 2 + (1 - c)), buf_a.at[k, yy], sem_a, (k,), core_peer).start()
 
     load_start(0)
     fetch = [pltpu.make_async_copy(w_ref, weights, sem_in.at[0]), pltpu.make_async_copy(dq_ref, dq, sem_in.at[1]),
              pltpu.make_async_copy(own_in_ref, own, sem_in.at[2])]
     for copy in fetch:
         copy.start()
-    for k in range(n_up):
-        for yy in range(2):
-            where = (slice(None), pl.ds(k * 2 * half, 2 * half))
-            pltpu.make_async_copy(up_ref.at[(yy * 2 + c,) + where], mine.at[k, yy], sem_l.at[k]).start()
-            send(up_ref.at[(yy * 2 + (1 - c),) + where], buf_a.at[k, yy], sem_a, (k,), core_peer).start()
+    for k in range(n_ready):
+        share_send(k)
+        if k < 4:
+            share_load(k)
     acc[...] = jnp.zeros_like(acc)
     bias[...] = jnp.zeros_like(bias)
     fetch[0].wait()
 
+    near_rows, far_rows = pl.ds(0, cut), pl.ds(cut, tall - cut)
+
     def unit(i):
-        run, mine_too, turn, there = position(i)
+        run, mine_too, there = position(i)
         at = lax.rem(i, 2)
         load_start(i + 1)
 
@@ -302,15 +318,7 @@
                 rs = pl.ds(pl.multiple_of(r * 128, 128), 128)
                 g = lax.dot_general(loads[at, 0, rs, :], weights[0], NT, preferred_element_type=F32)
                 g = g + lax.dot_general(loads[at, 1, rs, :], weights[1], NT, preferred_element_type=F32)
-
-                @pl.when(mine_too == 1)
-                def _():
-                    rmine[turn, rs, :] = g.astype(BF)
-
-                @pl.when(mine_too == 0)
-                def _():
-                    rsend[turn, rs, :] = g.astype(BF)
-
+                run_part[i, rs, :] = g.astype(BF)
                 bias[0:8, :] += jnp.sum(loads[at, 1, rs, :].astype(F32).reshape(16, 8, 2 * half), axis=0)
                 return carry
 
@@ -318,9 +326,11 @@
 
             @pl.when(mine_too == 0)
             def _():
-                for s in range(n_slices):
-                    rs = pl.ds(s * part, part)
-                    send(rsend.at[turn, rs, :], rbuf_x.at[turn, rs, :], sem_rx, (turn, s), x_peer).start()
+                send(run_part.at[i, near_rows, :], from_x.at[i // 2], sem_x, (i // 2,), x_peer).start()
+
+            @pl.when(i < 4)
+            def _():
+                far_send(i)
 
             def weights_part(r, carry):
                 fs = pl.ds(pl.multiple_of(r * 256, 256), 256)
@@ -331,109 +341,171 @@
 
             lax.fori_loop(0, 2 * half // 256, weights_part, 0)
 
-    def runs(e):
-        turn, s = e // n_slices, lax.rem(e, n_slices)
-        rs = pl.ds(pl.multiple_of(s * part, part), part)
-        dz = distance(2 * turn)
-        other = z + dz
-
-        @pl.when((other >= 0) & (other < zs))
-        def _():
-            joined = jnp.abs(2 * dz + 2 * x - 1) <= near
-
-            @pl.when(joined)
+    def from_below(i):
+        dz = distance(i)
+        step = 1 - 2 * lax.rem(i // 2, 2)
+        sender, target = z - step, z - step + dz
+        side = jnp.abs(2 * dz + (1 - 2 * x) * (1 - lax.rem(i, 2))) <= near
+        return (sender >= 0) & (sender < zs) & (target >= 0) & (target < zs) & side
+
+    def toward(i, copy_of):
+        step = 1 - 2 * lax.rem(i // 2, 2)
+
+        @pl.when(step == 1)
+        def _():
+            copy_of(up_peer).start()
+
+        @pl.when(step == -1)
+        def _():
+            copy_of(down_peer).start()
+
+    def far_send(i):
+        toward(i, lambda dev: send(run_part.at[i, far_rows, :], far_z.at[i], sem_far, (i,), dev))
+
+    def far_pass(i):
+        _run, _mine_too, there = position(i)
+
+        @pl.when(there)
+        def _():
+            @pl.when(from_below(i - 4))
             def _():
-                wait_in(rbuf_x.at[turn, rs, :], sem_rx, (turn, s))
-                sum_ = rmine[turn, rs, :].astype(F32) + rbuf_x[turn, rs, :].astype(F32)
-
-                @pl.when(dz == 0)
+                wait_in(far_z.at[i - 4], sem_far, (i - 4,))
+                run_part[i, far_rows, :] = (
+                    run_part[i, far_rows, :].astype(F32) + far_z[i - 4].astype(F32)).astype(BF)
+
+            far_send(i)
+
+    def far_end():
+        for col in range(2):
+            total = n_pos - 2 + col
+            for src in (4 + col, 6 + col):
+                @pl.when(from_below(src))
                 def _():
-                    own[rs, :] += sum_
-
-                @pl.when(dz != 0)
-                def _():
-                    rmine[turn, rs, :] = sum_.astype(BF)
-
-            @pl.when(dz != 0)
+                    wait_in(far_z.at[src], sem_far, (src,))
+                    run_part[total, far_rows, :] = (
+                        run_part[total, far_rows, :].astype(F32) + far_z[src].astype(F32)).astype(BF)
+            if col == 0:
+                send(run_part.at[total, far_rows, :], last_x, sem_x, (n_pos // 2,), x_peer).start()
+        own[far_rows, :] += run_part[n_pos - 1, far_rows, :].astype(F32)
+
+    def near_pass(n):
+        dz = distance(2 * n)
+        i = 2 * n + 1
+
+        @pl.when((z + dz >= 0) & (z + dz < zs))
+        def _():
+            @pl.when(jnp.abs(2 * dz + 2 * x - 1) <= near)
             def _():
-                send(rmine.at[turn, rs, :], rbuf_z.at[slot(other, z), rs, :], sem_rz, (slot(other, z), s),
-                     (other * 2 + x, w)).start()
-
-    def runs_end(e):
-        d, s = 1 + e // n_slices, lax.rem(e, n_slices)
-        rs = pl.ds(pl.multiple_of(s * part, part), part)
-        other = lax.rem(z + d, zs)
-
-        @pl.when(jnp.abs(2 * (other - z)) <= near)
-        def _():
-            wait_in(rbuf_z.at[d - 1, rs, :], sem_rz, (d - 1, s))
-            own[rs, :] += rbuf_z[d - 1, rs, :].astype(F32)
-
-    def stage_b(k):
-        pltpu.make_async_copy(mine.at[k], mine.at[k], sem_l.at[k]).wait()
-        wait_in(buf_a.at[k], sem_a, (k,))
-        buf_h[k] = (mine[k, 1 - y].astype(F32) + buf_a[k, 1 - y].astype(F32)).astype(BF)
-        send(buf_h.at[k], buf_b.at[k], sem_b, (k,), y_peer).start()
+                wait_in(from_x.at[n], sem_x, (n,))
+                run_part[i, near_rows, :] = (
+                    run_part[i, near_rows, :].astype(F32) + from_x[n].astype(F32)).astype(BF)
+
+            @pl.when((n >= 2) & from_below(i - 4))
+            def _():
+                wait_in(from_z.at[n - 2], sem_z, (n - 2,))
+                run_part[i, near_rows, :] = (
+                    run_part[i, near_rows, :].astype(F32) + from_z[n - 2].astype(F32)).astype(BF)
+
+            toward(i, lambda dev: send(run_part.at[i, near_rows, :], from_z.at[n], sem_z, (n,), dev))
+
+    def near_own():
+        n = n_pos // 2 - 1
+        wait_in(from_x.at[n], sem_x, (n,))
+        own[near_rows, :] += run_part[n_pos - 1, near_rows, :].astype(F32) + from_x[n].astype(F32)
+
+    def near_end():
+        for n in (2, 3):
+            @pl.when(from_below(2 * n + 1))
+            def _():
+                wait_in(from_z.at[n], sem_z, (n,))
+                own[near_rows, :] += from_z[n].astype(F32)
+
+    def add(p, q):
+        return (p.astype(F32) + q.astype(F32)).astype(BF)
 
     def column(side):
         return pl.ds(pl.multiple_of(side * half, 128), half)
 
+    def band(start, size):
+        return pl.ds(pl.multiple_of(start, 16), size)
+
+    def stage_b(k):
+        at = lax.rem(k, 4)
+        pltpu.make_async_copy(mine.at[at], mine.at[at], sem_l.at[k]).wait()
+        wait_in(buf_a.at[k], sem_a, (k,))
+        buf_h[k] = add(mine[at, 1 - y], buf_a[k, 1 - y])
+        send(buf_h.at[k], buf_b.at[k], sem_b, (k,), y_peer).start()
+        buf_a[k, y] = add(mine[at, y], buf_a[k, y])
+
     def stage_c(k):
         wait_in(buf_b.at[k], sem_b, (k,))
-
-        def total(side):
-            cols = column(side)
-            return (mine[k, y, :, cols].astype(F32) + buf_a[k, y, :, cols].astype(F32)
-                    + buf_b[k, :, cols].astype(F32))
-
-        buf_s[k] = total(1 - x).astype(BF)
-        send(buf_s.at[k], buf_c.at[k], sem_c, (k,), x_peer).start()
-        keep[k] = total(x)
+        buf_s[k] = add(buf_a[k, y, :, column(1 - x)], buf_b[k, :, column(1 - x)])
+        send(buf_s.at[k], buf_c.at[k], sem_c, (0, k), x_peer).start()
+
+    my_two, other_two = band(low * 2 * piece, 2 * piece), band((1 - low) * 2 * piece, 2 * piece)
+    my_one, other_one = band(high * piece, piece), band((1 - high) * piece, piece)
+    my_rows = band(low * 2 * piece + high * piece, piece)
 
     def stage_d(k):
-        wait_in(buf_c.at[k], sem_c, (k,))
-        s = keep[k] + buf_c[k].astype(F32)
-        keep[k] = s
-        buf_u[k] = s.astype(BF)
-        for d in range(1, zs):
-            other, dev = z_peer(d)
-            send(buf_u.at[k, pl.ds(pl.multiple_of(other * piece, 16), piece), :], buf_d.at[k, slot(other, z)],
-                 sem_d, (k,), dev).start()
+        wait_in(buf_c.at[k], sem_c, (0, k))
+        cols = column(x)
+        joined = buf_a[k, y, :, cols].astype(F32) + buf_b[k, :, cols].astype(F32) + buf_c[k].astype(F32)
+        buf_c[k] = joined.astype(BF)
+        send(buf_c.at[k, other_two, :], buf_d.at[k], sem_d, (0, k), pair_peer).start()
+
+    def stage_d2(k):
+        wait_in(buf_d.at[k], sem_d, (0, k))
+        buf_d[k] = add(buf_d[k], buf_c[k, my_two, :])
+        send(buf_d.at[k, other_one, :], buf_e.at[k], sem_d, (1, k), skip_peer).start()
 
     def stage_e(k):
-        wait_in(buf_d.at[k], sem_d, (k,))
-        my = pl.ds(pl.multiple_of(z * piece, 16), piece)
-        s = keep[k, my, :]
-        for d in range(zs - 1):
-            s = s + buf_d[k, d].astype(F32)
-        buf_f[k] = s.astype(BF)
-        out_ref[k, my, column(x)] = s.astype(BF)
-        for d in range(1, zs):
-            _other, dev = z_peer(d)
-            send(buf_f.at[k], out_ref.at[k, my, column(x)], sem_e, (k,), dev).start()
+        wait_in(buf_e.at[k], sem_d, (1, k))
+        buf_e[k] = add(buf_e[k], buf_d[k, my_one, :])
+        out_ref[k, my_rows, column(x)] = buf_e[k]
+        send(buf_e.at[k], out_ref.at[k, my_rows, column(x)], sem_d, (2, k), skip_peer).start()
+
+    def stage_e2(k):
+        wait_in(buf_e.at[k], sem_d, (2, k))
+        there = out_ref.at[k, my_two, column(x)]
+        send(there, there, sem_d, (3, k), pair_peer).start()
 
     def stage_f(k):
-        wait_in(buf_d.at[k], sem_e, (k,))
-        send(out_ref.at[k, :, column(x)], out_ref.at[k, :, column(x)], sem_f, (k,), x_peer).start()
-
-    def stage_g(k):
-        wait_in(out_ref.at[k, :, column(1 - x)], sem_f, (k,))
-
-    def guarded(fn, k, low, high):
-        @pl.when((k >= low) & (k < high))
+        wait_in(buf_d.at[k], sem_d, (3, k))
+        there = out_ref.at[k, :, column(x)]
+        send(there, there, sem_c, (1, k), x_peer).start()
+
+    def guarded(fn, k, first, last):
+        @pl.when((k >= first) & (k < last))
         def _():
             fn(k)
+
+    def chunk_step(m):
+        for lag, stage in enumerate((stage_c, stage_d, stage_d2, stage_e, stage_e2, stage_f)):
+            guarded(stage, m - (lag and lag + 5), 0, n_chunks)
 
     def first_step(t, carry):
         guarded(unit, t, 0, n_pos)
-        guarded(stage_b, t, 0, n_up)
-        guarded(stage_c, t - 2, 0, n_up)
-        guarded(runs, t - 5, 0, n_slices)
-        guarded(stage_d, t - 5, 0, n_up)
-        guarded(stage_e, t - 7, 0, n_up)
-        return carry
-
-    lax.fori_loop(0, n_up + 7, first_step, 0)
+        for j in range(2):
+            guarded(stage_b, 2 * t + j, 0, n_ready)
+        for k in range(4, n_ready):
+            @pl.when(t == (k - 4) // 2)
+            def _():
+                share_load(k)
+
+        @pl.when(lax.rem(t, 2) == 1)
+        def _():
+            guarded(near_pass, t // 2 - 1, 0, 4)
+
+        guarded(far_pass, t - 2, 4, 8)
+
+        @pl.when((lax.rem(t, 2) == 0) & (t >= 2))
+        def _():
+            chunk_step(t // 2 - 1)
+
+        return carry
+
+    lax.fori_loop(0, n_pos, first_step, 0)
+    done = n_pos // 2 - 1
 
     fetch[1].wait()
     fetch[2].wait()
@@ -443,15 +515,11 @@
     def to_bf(j, target):
         for owner in range(n_wsh):
             gbf[target, owner] = acc[j, owner * rows : (owner + 1) * rows, :].astype(BF)
-
-    def chunk_start(k, j):
-        for yy in range(2):
-            pltpu.make_async_copy(gbf.at[j, yy * 2 + c], mine.at[k, yy], sem_l.at[k]).start()
-            send(gbf.at[j, yy * 2 + (1 - c)], buf_a.at[k, yy], sem_a, (k,), core_peer).start()
-
-    for j in range(2):
-        to_bf(j, j)
-        chunk_start(n_up + j, j)
+        share_load(n_ready + target)
+        share_send(n_ready + target)
+
+    to_bf(0, 0)
+    to_bf(1, 1)
     own_tok.wait()
 
     def query_part(r, carry):
@@ -461,7 +529,6 @@
 
     lax.fori_loop(0, 2 * half // 256, query_part, 0)
     to_bf(0, 2)
-    chunk_start(n_up + 2, 2)
 
     def query_tokens(r, carry):
         rs = pl.ds(pl.multiple_of(r * 128, 128), 128)
@@ -488,8 +555,7 @@
         else:
             line[z] = total
             for d in range(1, zs):
-                _other, dev = z_peer(d)
-                send(sums.at[3], line.at[z], sem_v, (3,), dev).start()
+                send(sums.at[3], line.at[z], sem_v, (3,), z_peer(d)).start()
 
     def vec_last():
         wait_in(line.at[pl.ds(0, zs - 1)], sem_v, (3,))
@@ -505,93 +571,111 @@
 
     vec_send(0)
 
-    def second_step(t, carry):
-        guarded(stage_b, n_up + t, n_up, n_chunks)
+    def second_step(m, carry):
+        guarded(stage_b, m - done + n_ready, n_ready, n_chunks)
+        chunk_step(m)
+        guarded(lambda k: near_own(), m - done, 0, 1)
         for stage in range(3):
-            guarded(lambda k: vec_stage(stage), t - 1 - stage, 0, 1)
-        for j in range(2):
-            guarded(runs, n_slices + 2 * t + j, n_slices, (2 * hops + 1) * n_slices)
-        guarded(stage_f, t, 0, n_up)
-        guarded(stage_c, n_up + t - 2, n_up, n_chunks)
-        guarded(stage_d, n_up + t - 5, n_up, n_chunks)
-        guarded(stage_e, n_up + t - 8, n_up, n_chunks)
-        guarded(stage_f, n_up + t - 11, n_up, n_chunks)
-        guarded(lambda k: vec_last(), t - 6, 0, 1)
-        return carry
-
-    lax.fori_loop(0, n_chunks - n_up + 11, second_step, 0)
-
-    def each_end(e, carry):
-        runs_end(e)
-        return carry
-
-    lax.fori_loop(0, (zs - 1) * n_slices, each_end, 0)
+            guarded(lambda k: vec_stage(stage), m - done - 1 - stage, 0, 1)
+        guarded(lambda k: near_end(), m - done - 3, 0, 1)
+        guarded(lambda k: far_end(), m - done - 4, 0, 1)
+        guarded(lambda k: vec_last(), m - done - 5, 0, 1)
+        return carry
+
+    lax.fori_loop(done, n_chunks + 10, second_step, 0)
+    wait_in(last_x, sem_x, (n_pos // 2,))
+    own[far_rows, :] += last_x[...].astype(F32)
     grad_ref[...] = own[...].astype(BF)
 
     def drain(k, carry):
-        stage_g(k)
+        wait_in(buf_s.at[k], sem_c, (1, k))
         wait_out(buf_a.at[k], sem_a, (k,))
         wait_out(buf_b.at[k], sem_b, (k,))
-        wait_out(buf_c.at[k], sem_c, (k,))
-        wait_out(buf_d.at[k], sem_d, (k,))
-        wait_out(buf_d.at[k], sem_e, (k,))
-        wait_out(out_ref.at[k, :, column(x)], sem_f, (k,))
+        wait_out(buf_s.at[k], sem_c, (0, k))
+        wait_out(buf_s.at[k], sem_c, (1, k))
+        wait_out(buf_d.at[k], sem_d, (0, k))
+        wait_out(buf_e.at[k], sem_d, (1, k))
+        wait_out(buf_e.at[k], sem_d, (2, k))
+        wait_out(buf_d.at[k], sem_d, (3, k))
         return carry
 
     lax.fori_loop(0, n_chunks, drain, 0)
     for stage in range(3):
         wait_out(heard.at[stage], sem_v, (stage,))
     wait_out(line.at[pl.ds(0, zs - 1)], sem_v, (3,))
-
-    def drain_runs(e, carry):
-        turn, s = e // n_slices, lax.rem(e, n_slices)
-        rs = pl.ds(pl.multiple_of(s * part, part), part)
-        _run, _mine_too, _turn, there = position(2 * turn)
+    wait_out(last_x, sem_x, (n_pos // 2,))
+
+    def drain_runs(i, carry):
+        _run, mine_too, there = position(i)
 
         @pl.when(there)
         def _():
-            wait_out(rbuf_x.at[turn, rs, :], sem_rx, (turn, s))
-
-        dz = distance(2 * turn)
-
-        @pl.when((dz != 0) & (z + dz >= 0) & (z + dz < zs))
-        def _():
-            wait_out(rmine.at[turn, rs, :], sem_rz, (slot(z + dz, z), s))
-
-        return carry
-
-    lax.fori_loop(0, (2 * hops + 1) * n_slices, drain_runs, 0)
-
-
-def finish(up_parts, vec, grad_k, grad_v, all_tokens, grad_q, kvq_w, own_grad, inputs):
+            wait_out(far_z.at[i], sem_far, (i,))
+
+            @pl.when(mine_too == 1)
+            def _():
+                wait_out(from_z.at[i // 2], sem_z, (i // 2,))
+
+        return carry
+
+    lax.fori_loop(0, n_pos - 2, drain_runs, 0)
+
+    def drain_x(n, carry):
+        _run, _mine_too, there = position(2 * n)
+
+        @pl.when(there)
+        def _():
+            wait_out(from_x.at[n], sem_x, (n,))
+
+        return carry
+
+    lax.fori_loop(0, n_pos // 2, drain_x, 0)
+
+
+def finish(matrices, vec, grad_k, grad_v, all_tokens, grad_q, kvq_w, own_grad, inputs):
     n_ctx, n_wsh = lax.axis_size("ctx"), lax.axis_size("wsh")
     zs, hops = n_ctx // 2, reach(n_ctx) // 2
-    rows, n_up = up_parts.shape[1], up_parts.shape[2] // D
-    n = n_up + 3
+    rows = D // n_wsh
+    parts, sources, spans = [], [], []
+    for p, g in enumerate(matrices):
+        down, across = g.shape[0] // D, g.shape[1] // D
+        parts.append(g.astype(BF).reshape(n_wsh, down * rows, across * D))
+        spans.append((len(sources), down, across))
+        sources += [(p, r * rows, col * D) for r in range(down) for col in range(across)]
+    n = len(sources) + 3
+    spans += [(len(sources) + j, 1, 1) for j in range(3)]
     half, piece, tall = D // 2, rows // zs, inputs.shape[0]
-    turns, n_slices = 2 * hops + 1, 4
+    n_pos, cut = 4 * hops + 2, tall // 2
     vm, dma, shape = pltpu.VMEM, pltpu.SemaphoreType.DMA, jax.ShapeDtypeStruct
     any_spec = pl.BlockSpec(memory_space=pl.ANY)
     vm_spec = pl.BlockSpec(memory_space=pltpu.VMEM)
-    return pl.pallas_call(
-        functools.partial(finish_kernel, n_up),
+    summed, small, wide, grad_own = pl.pallas_call(
+        functools.partial(finish_kernel, sources, len(parts)),
         out_shape=(shape((n, rows, D), BF), shape((8, rows), F32), shape((1, D), F32), shape((tall, D), BF)),
-        in_specs=[any_spec, vm_spec] + [any_spec] * 7,
+        in_specs=[any_spec] * len(parts) + [vm_spec] + [any_spec] * 7,
         out_specs=(vm_spec,) * 4,
         scratch_shapes=[
-            vm((n, 2, rows, D), BF), vm((n, 2, rows, D), BF), vm((n, rows, D), BF), vm((n, rows, D), BF),
-            vm((n, rows, half), BF), vm((n, rows, half), F32), vm((n, rows, half), BF), vm((n, rows, half), BF),
-            vm((n, zs - 1, piece, half), BF), vm((n, piece, half), BF), vm((3, n_wsh, rows, D), BF),
+            vm((4, 2, rows, D), BF), vm((n, 2, rows, D), BF), vm((n, rows, D), BF), vm((n, rows, D), BF),
+            vm((n, rows, half), BF), vm((n, rows, half), BF), vm((n, 2 * piece, half), BF), vm((n, piece, half), BF),
+            vm((3, n_wsh, rows, D), BF),
             vm((4,) + vec.shape, F32), vm((3,) + vec.shape, F32), vm((zs,) + vec.shape, F32),
             vm((2, 3, tall, D), BF), vm((3, D, D), BF), vm((2, D, D), F32), vm((tall, D), BF), vm((tall, D), F32),
             vm((16, D), F32),
-            vm((turns, tall, D), BF), vm((turns, tall, D), BF), vm((turns, tall, D), BF), vm((zs - 1, tall, D), BF),
-            dma((n,)), dma((2, n)), dma((2, n)), dma((2, n)), dma((2, n)), dma((2, n)), dma((2, n)), dma((2, 4)),
-            dma((2, turns, n_slices)), dma((2, zs - 1, n_slices)), dma((2, 3)), dma((3,)),
+            vm((n_pos, tall, D), BF), vm((n_pos // 2, cut, D), BF), vm((4, cut, D), BF),
+            vm((n_pos - 2, tall - cut, D), BF), vm((tall - cut, D), BF),
+            dma((n,)), dma((2, n)), dma((2, n)), dma((2, 2, n)), dma((2, 4, n)), dma((2, 4)),
+            dma((2, n_pos // 2 + 1)), dma((2, 4)), dma((2, n_pos - 2)), dma((2, 3)), dma((3,)),
         ],
         compiler_params=pltpu.CompilerParams(collective_id=2, has_side_effects=True, vmem_limit_bytes=63 * 2**20),
         name="finish",
-    )(up_parts, vec, grad_k, grad_v, all_tokens, grad_q, kvq_w, own_grad, inputs)
+    )(*parts, vec, grad_k, grad_v, all_tokens, grad_q, kvq_w, own_grad, inputs)
+    sums = []
+    for first, down, across in spans:
+        block = summed[first : first + down * across]
+        if across > 1:
+            block = jnp.concatenate([block[i] for i in range(across)], axis=1)
+        sums.append(block.reshape(down * rows, across * D).astype(F32))
+    return sums, small, wide, grad_own
 
 
 def gather_kernel(cut, tok_ref, vec_ref, wk_ref, wv_ref, wq_ref,
@@ -700,6 +784,17 @@
         weight_arrival(m, 2).wait_recv()
         pltpu.make_async_copy(shard(m, w), shard(m, w), sem_l.at[m]).wait()
 
+    def relay(first, last):
+        def one(i, carry):
+            s = i // (last - first)
+            u = first + lax.rem(i, last - first)
+            await_slice(u, s)
+            pass_on(u, s)
+            return carry
+
+        lax.fori_loop(0, n_slices * (last - first), one, 0)
+
+    relay(2, 6)
     weight_forward(3)
     weight_forward(0)
     weight_forward(1)
@@ -712,30 +807,24 @@
     weight_end(0)
     weight_end(1)
 
-    def relay(first, last):
-        def one(i, carry):
-            s = i // (last - first)
-            u = first + lax.rem(i, last - first)
-            await_slice(u, s)
-            pass_on(u, s)
-            return carry
-
-        lax.fori_loop(0, n_slices * (last - first), one, 0)
-
     step_rows = 128
     steps = tok.shape[1] // step_rows
 
+    def query_part(i, carry):
+        r = pl.ds(pl.multiple_of(i * step_rows, step_rows), step_rows)
+        q = (jnp.dot(tok[a, r, :], wbuf[2], preferred_element_type=F32) + vec_out[0:1, :]).astype(BF)
+        qbuf[r, :] = q * jnp.asarray(SCALE, BF)
+        return carry
+
     def project(u, carry):
         run, _dz, _other, there = relative(u)
 
-        @pl.when(u == 1)
-        def _():
-            relay(2, 6)
-
         @pl.when(u == 6)
         def _():
             weight_forward(2)
             weight_end(2)
+            lax.fori_loop(0, steps, query_part, 0)
+            pltpu.make_async_copy(qbuf, q_out, sem_l.at[5]).start()
             relay(6, 10)
 
         @pl.when(there)
@@ -771,14 +860,6 @@
 
     lax.fori_loop(0, far, project, 0)
 
-    def query_part(i, carry):
-        r = pl.ds(pl.multiple_of(i * step_rows, step_rows), step_rows)
-        q = (jnp.dot(tok[a, r, :], wbuf[2], preferred_element_type=F32) + vec_out[0:1, :]).astype(BF)
-        qbuf[r, :] = q * jnp.asarray(SCALE, BF)
-        return carry
-
-    lax.fori_loop(0, steps, query_part, 0)
-    pltpu.make_async_copy(qbuf, q_out, sem_l.at[5]).start()
     pltpu.make_async_copy(wbuf, w_out, sem_l.at[6]).start()
 
     for m in range(4):
@@ -866,7 +947,7 @@
     small = jnp.stack(
         [query_bias, value_bias, out_bias, attn_gain, attn_shift, down_bias, final_gain, final_shift]
     )
-    fast = n_wsh == 4 and n_ctx % 4 == 0 and own % (n_ctx // 2 * 16) == 0 and tok_rows % 512 == 0
+    fast = n_wsh == 4 and n_ctx == 8 and own % (n_ctx // 2 * 16) == 0 and tok_rows % 512 == 0
     if fast:
         w = lax.axis_index("wsh")
         at = lax.broadcasted_iota(jnp.int32, (8, D), 1) // own == w
@@ -933,16 +1014,14 @@
         none = jnp.zeros((D,), F32)
         vec = jnp.stack([none, none, grad_out_b, grad_attn_g, grad_attn_s, grad_down_b, grad_final_g, grad_final_s])
         vec = jnp.concatenate([vec, grad_up_b.reshape(n_wsh, -1), jnp.zeros((8 - n_wsh, D), F32)], axis=0)
-        summed, small, wide, grad_inputs = finish(
-            grad_up_w.astype(BF).reshape(n_wsh, own, -1), vec, grad_k.reshape(n_ctx, tok_rows, D),
+        mats, small, wide, grad_inputs = finish(
+            (grad_up_w, grad_out_w, grad_down_w), vec, grad_k.reshape(n_ctx, tok_rows, D),
             grad_v.reshape(n_ctx, tok_rows, D), all_tokens.reshape(n_ctx, tok_rows, D), grad_q, kvq_w, grad_sum1, inputs,
         )
-        n_up = summed.shape[0] - 3
-        up_sum = jnp.concatenate([summed[i] for i in range(n_up)], axis=1)
+        up_sum, out_sum, down_sum, key_sum, value_sum, query_sum = mats
         sums = [
-            summed[n_up + 2].astype(F32), summed[n_up].astype(F32), summed[n_up + 1].astype(F32), total(grad_out_w),
-            up_sum.astype(F32), total(grad_down_w), small[0], small[1], small[2], small[3], small[4], wide[0],
-            small[5], small[6], small[7],
+            query_sum, key_sum, value_sum, out_sum, up_sum, down_sum, small[0], small[1], small[2], small[3], small[4],
+            wide[0], small[5], small[6], small[7],
         ]
     else:
         grad_all = jnp.einsum("te,de->td", grad_k, key_w, preferred_element_type=F32)

time: 473 us -> 398 us (0.84)
  Pallas kernels: 349 us -> 301 us
  waiting for transfers between devices: 33.1 us -> 11 us
    reduce_scatter x2 -> x0, waiting for transfers between devices: 30.9 us -> none  [total(): lax.psum_scatter(g.astype(BF), 'wsh', scatter_dimension=0, tiled=True)]
    pallas_call x1, Pallas kernels: 46.7 us -> 26.6 us  [attn_bwd(): pl.pallas_call(functools.partial(bwd_kernel, tk), out_shape=(jax.ShapeDty...]
    pallas_call x1, Pallas kernels: 28.6 us -> 16.6 us  [attn_fwd(): pl.pallas_call(functools.partial(fwd_kernel, tk), out_shape=(jax.ShapeDty...]
    pallas_call x1, Pallas kernels: 67.5 us -> 57.9 us  [gather_project(): pl.pallas_call(functools.partial(gather_kernel, 5), out_shape=(shape(runs...]
    all_gather x3, waiting for transfers between devices: 0.04 us -> 8.95 us  [gather(): return lax.all_gather(x, 'wsh', axis=0, tiled=True)]
    pallas_call x1, Pallas kernels: 206 us -> 200 us  [finish(): pl.pallas_call(functools.partial(finish_kernel, sources, len(parts)), out...]
  transfers between devices with their start and end apart: 6 -> 3, of which waited for: 1 -> 1; matrix products, arithmetic and copies ran while one was open for 9% -> 4% of each run, Pallas kernels for 74% -> 19%
where the time goes in v5:
time: 398 us; the launch traced here: 394 us
  Pallas kernels  301 us (76%)
  matrix products  39.6 us (10%)
  between operations  17.6 us (4%)
  other arithmetic  14.9 us (4%)
  waiting for transfers between devices  11 us (3%)
  local copies, waits for them, and re-layouts  9.33 us (2%)
    pallas_call x1, Pallas kernels, finish(): pl.pallas_call(functools.partial(finish_kernel, sources, len(parts)), out...  200 us
    pallas_call x1, Pallas kernels, gather_project(): pl.pallas_call(functools.partial(gather_kernel, 5), out_shape=(shape(runs...  57.9 us
    pallas_call x1, Pallas kernels, attn_bwd(): pl.pallas_call(functools.partial(bwd_kernel, tk), out_shape=(jax.ShapeDty...  26.6 us
    pallas_call x1, Pallas kernels, attn_fwd(): pl.pallas_call(functools.partial(fwd_kernel, tk), out_shape=(jax.ShapeDty...  16.6 us
    all_gather x3, waiting for transfers between devices, gather(): return lax.all_gather(x, 'wsh', axis=0, tiled=True)  8.95 us
    dot_general x1, matrix products, local(): up_f = jnp.dot(first_b, up_w, preferred_element_type=F32) + up_b  8.25 us
  transfers between devices with their start and end apart: 3, of which 1 were waited for; matrix products, arithmetic and copies ran while one was open for 4% of the time, Pallas kernels for 19%

profile of v5, /device:TPU:0, one launch (start us, length us, event | category | flops | bytes accessed | tf_op | source)
XLA Modules:
  0.0 393.8 jit_solution(12974776662324827414)
XLA Ops:
  7.4 0.7 all-gather.4.cloned.1.call-update
  8.1 0.7 all-gather.6.cloned.1.call-update
  8.9 0.7 all-gather.8.cloned.1.call-update
  9.6 0.6 fusion.17
  14.0 57.9 %gather_project.1 = (bf16[8,512,768]{2,1,0:T(8,128)(2,1)}, bf16[8,512,768]{2,1,0:T(8,128)(2,1)}, bf16[8,512,768]{2,1,0:T(8,128)(2,1)}, bf16[512,768]{1,0:T(8,128...) custom-call(bf16[512,768]{1,0:T(8,128)(2,1)S(1)} %bitcast.80, ...), custom_call_target="tpu_custom_call" | custom-call | tf_op jit(solution)/shard_map/gather_project/pallas_call | solution.py:897
  71.9 1.8 copy-done
  73.7 0.9 copy-done.1
  75.5 0.8 and_convert_fusion.qaug_ref
  76.3 1.4 select_convert_fusion.kaug_ref
  77.7 16.6 %attend.1 = (f32[768,512]{1,0:T(8,128)}, f32[6,2,512]{2,1,0:T(2,128)}) custom-call(s32[1,2]{1,0:T(1,128)} %pad_add_fusion.bounds, bf16[512,768]{1,0:T(8,128)(2,1)} %copy-done.1, bf16[512,128]{1,0:T(8,128)(2,1)} %and_convert_fusion.qaug_ref, bf16[4096,768]{1,0:T(8,128)(2,1)} %bitcast.81, bf16[4096,128]{1,0:T(8,128)(2,1)} %select_convert_fusion.kaug_ref, ...), custom_call_target="tpu_custom_call" | custom-call | tf_op jit(solution)/shard_map/attend/pallas_call | solution.py:112
  94.4 2.7 fusion.27
  97.5 8.3 %multiply_convert_fusion = (bf16[512,3072]{1,0:T(8,128)(2,1)}, f32[512,3072]{1,0:T(8,128)}) fusion(f32[3072]{0:T(1024)S(1)} %add.122, bf16[768,3072]{1,0:T(8,128)(2,1)} %all-gather.6.cloned.1.call-done, f32[512,768]{1,0:T(8,128)S(1)} %get-tuple-element.88, f32[768]{0:T(1024)S(1)} %get-tuple-element.55, f32[768]{0:T(1024)S(1)} %get-tuple-element.56, ...), kind=kOutput, calls=%fused_computation.2 | convolution fusion | flops 2427322368 | bytes 15751168 | tf_op jit(solution)/shard_map/dot_general | solution.py:984
  105.8 8.9 %all-gather.8.cloned.1.call-done = bf16[3072,768]{1,0:T(8,128)(2,1)} async-done(((bf16[768,768]{1,0:T(8,128)(2,1)}), bf16[3072,768]{1,0:T(8,128)(2,1)}) %all-gather.8.cloned.1.call-update) | async-done | bytes 4718608 | tf_op jit(solution)/shard_map/all_gather | solution.py:945
  114.7 6.1 %fusion.28 = (f32[512]{0:T(512)S(1)}, f32[512,768]{1,0:T(8,128)S(1)}) fusion(f32[768]{0:T(1024)S(1)} %get-tuple-element.54, bf16[512,3072]{1,0:T(8,128)(2,1)} %get-tuple-element.89, bf16[3072,768]{1,0:T(8,128)(2,1)} %all-gather.8.cloned.1.call-done, f32[768]{0:T(1024)S(1)} %get-tuple-element.55, f32[768]{0:T(1024)S(1)} %get-tuple-element.56, ...), kind=kOutput, calls=%fused_computation.93 | convolution fusion | flops 2418671104 | bytes 11025408 | tf_op jit(solution)/shard_map/dot_general | solution.py:987
  121.1 0.8 fusion.6
  121.9 1.6 fusion.25
  124.0 4.4 %convolution_convert_fusion = bf16[3072,768]{1,0:T(8,128)(2,1)} fusion(bf16[512,3072]{1,0:T(8,128)(2,1)S(1)} %copy-done.22, bf16[512,768]{1,0:T(8,128)(2,1)S(1)} %get-tuple-element.63), kind=kOutput, calls=%fused_computation.4 | convolution fusion | flops 2418278400 | bytes 8650752 | tf_op jit(solution)/shard_map/tf,td->fd/dot_general | solution.py:993
  128.5 5.3 %convert_reduce_fusion = (f32[3072]{0:T(1024)S(1)}, bf16[512,3072]{1,0:T(8,128)(2,1)S(1)}) fusion(f32[512,3072]{1,0:T(8,128)S(1)} %bitcast.105, f32[3072]{0:T(1024)S(1)} %add.122, bf16[512,768]{1,0:T(8,128)(2,1)S(1)} %get-tuple-element.63, bf16[3072,768]{1,0:T(8,128)(2,1)S(1)} %bitcast.103), kind=kOutput, calls=%fused_computation | convolution fusion | flops 2441081856 | bytes 14966784 | tf_op jit(solution)/shard_map/td,fd->tf/dot_general | solution.py:995
  133.8 4.9 %convolution_convert_fusion.1 = bf16[768,3072]{1,0:T(8,128)(2,1)} fusion(bf16[512,3072]{1,0:T(8,128)(2,1)S(1)} %get-tuple-element.61, f32[512,768]{1,0:T(8,128)S(1)} %get-tuple-element.88, f32[768]{0:T(1024)S(1)} %get-tuple-element.55, f32[768]{0:T(1024)S(1)} %get-tuple-element.56, f32[512]{0:T(512)S(1)} %fusion.15, f32[512]{0:T(512)S(1)} %broadcast_multiply_fusion.1), kind=kOutput, calls=%fused_computation.5 | convolution fusion | flops 2420244480 | bytes 9447424 | tf_op jit(solution)/shard_map/td,tf->df/dot_general | solution.py:998
  138.7 3.2 multiply_reduce_fusion
  141.9 0.7 fusion.24
  142.8 1.7 copy-done.8
  144.5 1.8 convolution_convert_fusion.2
  146.4 3.0 convolution_convert_fusion.3.do_ref
  149.4 26.6 %attend_back.1 = (bf16[512,768]{1,0:T(8,128)(2,1)}, bf16[4096,768]{1,0:T(8,128)(2,1)}, bf16[4096,768]{1,0:T(8,128)(2,1)}) custom-call(s32[1,2]{1,0:T(1,128)} %pad_add_fusion.bounds, bf16[512,768]{1,0:T(8,128)(2,1)} %copy-done.1, bf16[512,128]{1,0:T(8,128)(2,1)} %and_convert_fusion.qaug_ref, bf16[512,768]{1,0:T(8,128)(2,1)} %convolution_convert_fusion.3.do_ref, ...), custom_call_target="tpu_custom_call" | custom-call | tf_op jit(solution)/shard_map/attend_back/pallas_call | solution.py:175
  176.0 1.3 concatenate.22.refs_3_
  177.3 200.1 %finish.1 = (bf16[12,192,768]{2,1,0:T(8,128)(2,1)}, f32[8,192]{1,0:T(8,128)}, f32[1,768]{1,0:T(1,128)}, bf16[512,768]{1,0:T(8,128)(2,1)}) custom-call(bf16[4,192,3072]{2,1,0:T(8,128)(2,1)} %bitcast.88, bf16[4,192,768]{2,1,0:T(8,128)(2,1)} %bitcast.89, bf16[4,768,768]{2,1,0:T(8,128)(2,1)} %bitcast.87, f32[16,768]{1,0:T(8,128)} %concatenate.22.refs_3_, ...), custom_call_target="tpu_custom_call" | custom-call | tf_op jit(solution)/shard_map/finish/pallas_call | solution.py:652
  377.4 3.1 slice_bitcast_fusion.3
  380.4 1.3 slice.100
  381.8 1.7 bitcast_convert_fusion
  384.7 1.7 maximum_convert_fusion
  386.4 0.9 copy.36
  (113 shorter events, 4.2 us)
Async XLA Ops:
  7.2 2.4 copy-start.13
  7.2 6.3 %copy-start.14 = (bf16[192]{0:T(256)(128)(2,1)S(1)}, bf16[192]{0:T(256)(128)(2,1)}, u32[]{:S(2)}) copy-start(bf16[192]{0:T(256)(128)(2,1)} %param.27) | copy-start | bytes 1156
  7.2 6.3 %copy-start.15 = (bf16[192]{0:T(256)(128)(2,1)S(1)}, bf16[192]{0:T(256)(128)(2,1)}, u32[]{:S(2)}) copy-start(bf16[192]{0:T(256)(128)(2,1)} %param.28) | copy-start | bytes 1156
  7.2 6.3 %copy-start.16 = (bf16[192]{0:T(256)(128)(2,1)S(1)}, bf16[192]{0:T(256)(128)(2,1)}, u32[]{:S(2)}) copy-start(bf16[192]{0:T(256)(128)(2,1)} %param.29) | copy-start | bytes 1156
  7.2 6.3 %copy-start.17 = (bf16[192]{0:T(256)(128)(2,1)S(1)}, bf16[192]{0:T(256)(128)(2,1)}, u32[]{:S(2)}) copy-start(bf16[192]{0:T(256)(128)(2,1)} %param.30) | copy-start | bytes 1156
  7.2 6.3 %copy-start.18 = (bf16[192]{0:T(256)(128)(2,1)S(1)}, bf16[192]{0:T(256)(128)(2,1)}, u32[]{:S(2)}) copy-start(bf16[192]{0:T(256)(128)(2,1)} %param.31) | copy-start | bytes 1156
  7.3 6.3 %copy-start.19 = (bf16[192]{0:T(256)(128)(2,1)S(1)}, bf16[192]{0:T(256)(128)(2,1)}, u32[]{:S(2)}) copy-start(bf16[192]{0:T(256)(128)(2,1)} %param.33) | copy-start | bytes 1156
  7.3 6.3 %copy-start.20 = (bf16[192]{0:T(256)(128)(2,1)S(1)}, bf16[192]{0:T(256)(128)(2,1)}, u32[]{:S(2)}) copy-start(bf16[192]{0:T(256)(128)(2,1)} %param.34) | copy-start | bytes 1156
  7.3 6.4 %copy-start.21 = (bf16[192]{0:T(256)(128)(2,1)S(1)}, bf16[192]{0:T(256)(128)(2,1)}, u32[]{:S(2)}) copy-start(bf16[192]{0:T(256)(128)(2,1)} %param.35) | copy-start | bytes 1156
  7.3 6.5 %copy-start.12 = (bf16[768]{0:T(1024)(128)(2,1)S(1)}, bf16[768]{0:T(1024)(128)(2,1)}, u32[]{:S(2)}) copy-start(bf16[768]{0:T(1024)(128)(2,1)} %param.32) | copy-start | bytes 4612
  7.3 6.6 %copy-start.2 = (bf16[1,512,768]{2,1,0:T(8,128)(2,1)S(1)}, bf16[1,512,768]{2,1,0:T(8,128)(2,1)}, u32[]{:S(2)}) copy-start(bf16[1,512,768]{2,1,0:T(8,128)(2,1)} %param.18) | copy-start | bytes 2359300
  7.3 6.6 %copy-start.3 = (bf16[192,768]{1,0:T(8,128)(2,1)S(1)}, bf16[192,768]{1,0:T(8,128)(2,1)}, u32[]{:S(2)}) copy-start(bf16[192,768]{1,0:T(8,128)(2,1)} %wk_ref.1) | copy-start | bytes 884740
  7.3 6.6 %copy-start.4 = (bf16[192,768]{1,0:T(8,128)(2,1)S(1)}, bf16[192,768]{1,0:T(8,128)(2,1)}, u32[]{:S(2)}) copy-start(bf16[192,768]{1,0:T(8,128)(2,1)} %wv_ref.1) | copy-start | bytes 884740
  7.3 6.6 %copy-start.5 = (bf16[192,768]{1,0:T(8,128)(2,1)S(1)}, bf16[192,768]{1,0:T(8,128)(2,1)}, u32[]{:S(2)}) copy-start(bf16[192,768]{1,0:T(8,128)(2,1)} %wq_ref.1) | copy-start | bytes 884740
  7.3 87.1 %all-gather.4.cloned.1.call-start = ((), (), s32[]{:S(2)}) async-start(), calls=%async_computation | async-start | bytes 1474560 | tf_op jit(solution)/shard_map/all_gather | solution.py:945
  8.1 89.4 %all-gather.6.cloned.1.call-start = ((), (), s32[]{:S(2)}) async-start(), calls=%async_computation.1 | async-start | bytes 5898240 | tf_op jit(solution)/shard_map/all_gather | solution.py:945
  8.8 65.8 %copy-start.7 = (bf16[1,512,768]{2,1,0:T(8,128)(2,1)S(1)}, bf16[1,512,768]{2,1,0:T(8,128)(2,1)}, u32[]{:S(2)}) copy-start(bf16[1,512,768]{2,1,0:T(8,128)(2,1)} %param.19) | copy-start | bytes 2359300
  8.8 105.8 %all-gather.8.cloned.1.call-start = ((), (), s32[]{:S(2)}) async-start(), calls=%async_computation.2 | async-start | bytes 5898240 | tf_op jit(solution)/shard_map/all_gather | solution.py:945
  71.8 1.8 copy-start
  73.7 0.9 copy-start.1
  121.8 2.2 copy-start.22
  121.9 6.6 %slice-start.4 = ((s8[6291456]{0:T(1024)(128)(4,1)}), s8[4194304]{0:T(1024)(128)(4,1)S(1)}, s32[]{:S(2)}) async-start(s8[6291456]{0:T(1024)(128)(4,1)} %bitcast.104), calls=%async_computation.7 | async-start | bytes 8388608
  123.5 5.0 %slice-start.2 = ((s8[4718592]{0:T(1024)(128)(4,1)}), s8[4194304]{0:T(1024)(128)(4,1)S(1)}, s32[]{:S(2)}) async-start(s8[4718592]{0:T(1024)(128)(4,1)} %bitcast.102), calls=%async_computation.5 | async-start | bytes 8388608
  124.0 4.4 %slice-start.3 = ((s8[4718592]{0:T(1024)(128)(4,1)}), s8[524288]{0:T(1024)(128)(4,1)S(1)}, s32[]{:S(2)}) async-start(s8[4718592]{0:T(1024)(128)(4,1)} %bitcast.102), calls=%async_computation.6 | async-start | bytes 1048576
  124.0 4.4 %slice-start.5 = ((s8[6291456]{0:T(1024)(128)(4,1)}), s8[2097152]{0:T(1024)(128)(4,1)S(1)}, s32[]{:S(2)}) async-start(s8[6291456]{0:T(1024)(128)(4,1)} %bitcast.104), calls=%async_computation.8 | async-start | bytes 4194304
  124.0 14.7 %slice-start = ((s8[4718592]{0:T(1024)(128)(4,1)}), s8[4194304]{0:T(1024)(128)(4,1)S(1)}, s32[]{:S(2)}) async-start(s8[4718592]{0:T(1024)(128)(4,1)} %bitcast.100), calls=%async_computation.3 | async-start | bytes 8388608
  128.5 10.2 %slice-start.1 = ((s8[4718592]{0:T(1024)(128)(4,1)}), s8[524288]{0:T(1024)(128)(4,1)S(1)}, s32[]{:S(2)}) async-start(s8[4718592]{0:T(1024)(128)(4,1)} %bitcast.100), calls=%async_computation.4 | async-start | bytes 1048576
  142.6 2.0 copy-start.8
  142.8 3.6 copy-start.6
  381.8 1.7 copy-start.10
  381.8 2.3 copy-start.11
  384.7 1.7 copy-start.9
Sparse Core Ops, SparseCore 0:
  9.7 26.4 all-gather.3
  37.8 37.7 all-gather.5
  77.2 37.4 all-gather.7

commit v6 on v5

--- a/solution.py
+++ b/solution.py
@@ -191,6 +191,181 @@
             scratch_shapes=[pltpu.VMEM((S, 128), F32), pltpu.VMEM((S, 128), F32), pltpu.VMEM((128, 2 * tq), F32)]),
         name="attend_back",
     )(bounds, q, qaug, do, lse, ot, k, kaug, v)
+
+
+def middle_kernel(attn_ref, in_ref, cot_ref, vec_ref, wo_ref, wu_ref, down_own, down_far,
+                  out_ref, sum1_ref, do_ref, grads_ref, up_out, down_out, attn_out,
+                  wo, wu, wd, attn_b, first, hat1, scale1, first_b, act, slope, sum2, down_b, up_b, first_b2, first_t,
+                  g_up, g_down, g_out, sem_w, sem_d, sem_o):
+    rows, wide = in_ref.shape[0], wu.shape[1]
+    a, w = lax.axis_index("ctx"), lax.axis_index("wsh")
+    y, c = w // 2, lax.rem(w, 2)
+    core_peer = (a, y * 2 + (1 - c))
+    tall = down_own.shape[0]
+    MESH = pl.DeviceIdType.MESH
+    barrier = pltpu.get_barrier_semaphore()
+    pl.semaphore_signal(barrier, inc=1, device_id=core_peer, device_id_type=MESH)
+    pl.semaphore_wait(barrier, 1)
+    passed = []
+    for s, (ref, owner) in enumerate(((down_own, w), (down_far, (1 - y) * 2 + c))):
+        there = wd.at[pl.ds(pl.multiple_of(owner * tall, 16), tall), :]
+        passed.append(pltpu.make_async_remote_copy(
+            src_ref=ref, dst_ref=there, send_sem=sem_d.at[0, s], recv_sem=sem_d.at[1, s],
+            device_id=core_peer, device_id_type=MESH))
+        passed[-1].start()
+        pltpu.make_async_copy(ref, there, sem_w.at[2 + s]).start()
+    loading = [pltpu.make_async_copy(wo_ref, wo, sem_w.at[0]), pltpu.make_async_copy(wu_ref, wu, sem_w.at[1])]
+    for copy in loading:
+        copy.start()
+
+    def arrived(j):
+        if j < 2:
+            loading[j].wait()
+        else:
+            for s, owner in enumerate((w, (1 - y) * 2 + c)):
+                there = wd.at[pl.ds(pl.multiple_of(owner * tall, 16), tall), :]
+                pltpu.make_async_copy(there, there, sem_w.at[2 + s]).wait()
+                passed[s].wait_recv()
+
+    grads_ref[...] = jnp.zeros_like(grads_ref)
+    attn_b[...] = attn_ref[...].astype(BF)
+    out_b, attn_g, attn_s, down_bias, final_g, final_s = [vec_ref[i : i + 1, :] for i in range(2, 8)]
+    arrived(0)
+    block = 128
+
+    def over_rows(fn):
+        def one(i, carry):
+            fn(pl.ds(pl.multiple_of(i * block, block), block))
+            return carry
+
+        lax.fori_loop(0, rows // block, one, 0)
+
+    def norm(values):
+        average = jnp.mean(values, axis=-1, keepdims=True)
+        centred = values - average
+        scale = lax.rsqrt(jnp.mean(centred * centred, axis=-1, keepdims=True) + EPS)
+        return centred * scale, scale
+
+    def norm_back(grad, hat, scale, gain):
+        g = grad * gain
+        return scale * (g - jnp.mean(g, axis=-1, keepdims=True) - hat * jnp.mean(g * hat, axis=-1, keepdims=True))
+
+    def note(row, values):
+        grads_ref[row : row + 1, :] += jnp.sum(values, axis=0, keepdims=True)
+
+    def branch_part(r):
+        a = attn_b[:, r].T
+        v = lax.dot_general(a, wo[...], NN, preferred_element_type=F32) + out_b + in_ref[r, :].astype(F32)
+        hat, scale = norm(v)
+        hat1[r, :] = hat
+        scale1[r, :] = scale
+        f = hat * attn_g + attn_s
+        first[r, :] = f
+        first_b[r, :] = f.astype(BF)
+
+    over_rows(branch_part)
+    arrived(1)
+    cols = vec_ref.shape[1]
+
+    def over_wide(fn):
+        def one(i, carry):
+            fn(pl.ds(pl.multiple_of(i * cols, cols), cols), i)
+            return carry
+
+        lax.fori_loop(0, wide // cols, one, 0)
+
+    def up_part(n, i):
+        u = lax.dot_general(first_b[...], wu[:, n], NN, preferred_element_type=F32) + vec_ref[pl.ds(8 + i, 1), :]
+        half = 0.5 * (1.0 + lax.erf(u * ROOT_HALF))
+        act[:, n] = (u * half).astype(BF)
+        slope[:, n] = half + u * (0.3989422804014327 * jnp.exp(-0.5 * u * u))
+
+    over_wide(up_part)
+    arrived(2)
+
+    def down_part(r):
+        v = lax.dot_general(act[r, :], wd[...], NN, preferred_element_type=F32) + down_bias + first[r, :]
+        hat, scale = norm(v)
+        out_ref[r, :] = (hat * final_g + final_s).astype(BF)
+        cot = cot_ref[r, :].astype(F32)
+        note(6, cot * hat)
+        note(7, cot)
+        g = norm_back(cot, hat, scale, final_g)
+        sum2[r, :] = g
+        rounded = g.astype(BF)
+        down_b[r, :] = rounded
+        note(5, rounded.astype(F32))
+
+    over_rows(down_part)
+
+    def up_back(n, i):
+        g = lax.dot_general(down_b[...], wd[n, :], NT, preferred_element_type=F32) * slope[:, n]
+        rounded = g.astype(BF)
+        up_b[:, n] = rounded
+        grads_ref[pl.ds(8 + i, 1), :] = jnp.sum(rounded.astype(F32), axis=0, keepdims=True)
+
+    over_wide(up_back)
+
+    def first_part(r):
+        g = sum2[r, :] + lax.dot_general(up_b[r, :], wu[...], NT, preferred_element_type=F32)
+        hat = hat1[r, :]
+        note(3, g * hat)
+        note(4, g)
+        s1 = norm_back(g, hat, scale1[r, :], attn_g)
+        sum1_ref[r, :] = s1
+        rounded = s1.astype(BF)
+        note(2, rounded.astype(F32))
+        first_b2[r, :] = rounded
+
+    over_rows(first_part)
+
+    def do_part(r):
+        do_ref[r, :] = lax.dot_general(first_b2[r, :], wo[...], NT, preferred_element_type=F32).astype(BF)
+
+    over_rows(do_part)
+
+    def wide_grads(n, i):
+        g_down[n, :] = lax.dot_general(act[:, n].T, down_b[...], NN, preferred_element_type=F32).astype(BF)
+        pltpu.make_async_copy(g_down.at[n, :], down_out.at[n, :], sem_o.at[0, i]).start()
+        g_up[:, n] = lax.dot_general(first_t[...], up_b[:, n], NN, preferred_element_type=F32).astype(BF)
+        pltpu.make_async_copy(g_up.at[:, n], up_out.at[:, n], sem_o.at[1, i]).start()
+
+    first_t[...] = first_b[...].T
+    over_wide(wide_grads)
+    g_out[...] = lax.dot_general(attn_b[...], first_b2[...], NN, preferred_element_type=F32).astype(BF)
+    pltpu.make_async_copy(g_out, attn_out, sem_o.at[2, 0]).start()
+
+    def wide_end(n, i):
+        pltpu.make_async_copy(g_down.at[n, :], down_out.at[n, :], sem_o.at[0, i]).wait()
+        pltpu.make_async_copy(g_up.at[:, n], up_out.at[:, n], sem_o.at[1, i]).wait()
+
+    over_wide(wide_end)
+    pltpu.make_async_copy(g_out, attn_out, sem_o.at[2, 0]).wait()
+    for copy in passed:
+        copy.wait_send()
+
+
+def middle(attn_t, inputs, cotangent, vec, out_w, up_w, down_own, down_far):
+    rows = inputs.shape[0]
+    wide = up_w.shape[1]
+    vm, dma, shape = pltpu.VMEM, pltpu.SemaphoreType.DMA, jax.ShapeDtypeStruct
+    any_spec = pl.BlockSpec(memory_space=pl.ANY)
+    vm_spec = pl.BlockSpec(memory_space=pltpu.VMEM)
+    return pl.pallas_call(
+        middle_kernel,
+        out_shape=(shape((rows, D), BF), shape((rows, D), F32), shape((rows, D), BF), shape((16, D), F32),
+                   shape((D, wide), BF), shape((wide, D), BF), shape((D, D), BF)),
+        in_specs=[vm_spec] * 4 + [any_spec] * 4,
+        out_specs=(vm_spec,) * 4 + (any_spec,) * 3,
+        scratch_shapes=[
+            vm((D, D), BF), vm((D, wide), BF), vm((wide, D), BF), vm((D, rows), BF), vm((rows, D), F32),
+            vm((rows, D), F32), vm((rows, 1), F32), vm((rows, D), BF), vm((rows, wide), BF), vm((rows, wide), F32),
+            vm((rows, D), F32), vm((rows, D), BF), vm((rows, wide), BF), vm((rows, D), BF), vm((D, rows), BF),
+            vm((D, wide), BF), vm((wide, D), BF), vm((D, D), BF), dma((4,)), dma((2, 2)), dma((3, wide // D)),
+        ],
+        compiler_params=pltpu.CompilerParams(collective_id=3, has_side_effects=True, vmem_limit_bytes=56 * 2**20),
+        name="middle",
+    )(attn_t, inputs, cotangent, vec, out_w, up_w, down_own, down_far)
 
 
 def reach(n_ctx):
@@ -678,9 +853,9 @@
     return sums, small, wide, grad_own
 
 
-def gather_kernel(cut, tok_ref, vec_ref, wk_ref, wv_ref, wq_ref,
-                  tok_out, k_out, v_out, q_out, w_out, vec_out,
-                  tok, kbuf, vbuf, qbuf, wbuf, vecs,
+def gather_kernel(cut, tok_ref, vec_ref, wk_ref, wv_ref, wq_ref, wo_ref, wu_ref,
+                  tok_out, k_out, v_out, q_out, w_out, vec_out, wo_out, wu_out,
+                  tok, kbuf, vbuf, qbuf, wbuf, vecs, wo, wu,
                   sem_in, sem_out, sem_w, sem_l, sem_o):
     n_ctx = lax.axis_size("ctx")
     zs = n_ctx // 2
@@ -749,15 +924,16 @@
     def weight_rows(owner):
         return pl.ds(pl.multiple_of(owner * own, 16), own)
 
-    vec_own = vecs.at[w]
-    remote(vec_ref, vec_own, sem_w.at[0, 0, 3], sem_w.at[1, 0, 3], core_peer).start()
-    remote(vec_ref, vec_own, sem_w.at[0, 1, 3], sem_w.at[1, 1, 3], y_peer).start()
-    pltpu.make_async_copy(vec_ref, vec_own, sem_l.at[3]).start()
-    for m, ref in enumerate((wk_ref, wv_ref, wq_ref)):
-        there = wbuf.at[m, weight_rows(w), :]
-        remote(ref, there, sem_w.at[0, 1, m], sem_w.at[1, 1, m], y_peer).start()
-        remote(ref, there, sem_w.at[0, 0, m], sem_w.at[1, 0, m], core_peer).start()
-        pltpu.make_async_copy(ref, there, sem_l.at[m]).start()
+    def shard(m, owner):
+        if m == 3:
+            return vecs.at[owner]
+        return (wbuf.at[0], wbuf.at[1], wbuf.at[2], None, wo, wu)[m].at[weight_rows(owner), :]
+
+    shards = (wk_ref, wv_ref, wq_ref, vec_ref, wo_ref, wu_ref)
+    for m in (3, 0, 1, 2, 4, 5):
+        remote(shards[m], shard(m, w), sem_w.at[0, 1, m], sem_w.at[1, 1, m], y_peer).start()
+        remote(shards[m], shard(m, w), sem_w.at[0, 0, m], sem_w.at[1, 0, m], core_peer).start()
+        pltpu.make_async_copy(shards[m], shard(m, w), sem_w.at[0, 3, m]).start()
     lax.fori_loop(0, n_slices, start_own, 0)
     pltpu.make_async_copy(tok_ref, tok.at[a], sem_l.at[4]).start()
 
@@ -765,9 +941,6 @@
         @pl.when(jnp.abs(j - a) > near)
         def _():
             tok[j] = jnp.zeros_like(tok[j])
-
-    def shard(m, owner):
-        return vecs.at[owner] if m == 3 else wbuf.at[m, weight_rows(owner), :]
 
     def weight_arrival(m, kind):
         part = shard(m, w)
@@ -782,7 +955,7 @@
     def weight_end(m):
         weight_arrival(m, 0).wait_recv()
         weight_arrival(m, 2).wait_recv()
-        pltpu.make_async_copy(shard(m, w), shard(m, w), sem_l.at[m]).wait()
+        pltpu.make_async_copy(shard(m, w), shard(m, w), sem_w.at[0, 3, m]).wait()
 
     def relay(first, last):
         def one(i, carry):
@@ -862,7 +1035,12 @@
 
     pltpu.make_async_copy(wbuf, w_out, sem_l.at[6]).start()
 
-    for m in range(4):
+    for m in (4, 5):
+        weight_forward(m)
+    for m, full, target in ((4, wo, wo_out), (5, wu, wu_out)):
+        weight_end(m)
+        pltpu.make_async_copy(full, target, sem_l.at[m - 4]).start()
+    for m in range(6):
         for kind in range(3):
             weight_arrival(m, kind).wait_send()
 
@@ -882,9 +1060,11 @@
             pltpu.make_async_copy(src.at[j], dst.at[j], sem_o.at[i, j]).wait()
     pltpu.make_async_copy(qbuf, q_out, sem_l.at[5]).wait()
     pltpu.make_async_copy(wbuf, w_out, sem_l.at[6]).wait()
-
-
-def gather_project(inputs, vec, key_weight, value_weight, query_weight):
+    pltpu.make_async_copy(wo, wo_out, sem_l.at[0]).wait()
+    pltpu.make_async_copy(wu, wu_out, sem_l.at[1]).wait()
+
+
+def gather_project(inputs, vec, key_weight, value_weight, query_weight, out_weight, up_weight):
     n_ctx, n_wsh = lax.axis_size("ctx"), lax.axis_size("wsh")
     tall = inputs.shape[0]
     n_slices = 8
@@ -897,16 +1077,17 @@
     return pl.pallas_call(
         functools.partial(gather_kernel, 5),
         out_shape=(shape(runs, BF), shape(runs, BF), shape(runs, BF), shape((tall, D), BF), shape((3, D, D), BF),
-                   shape(vec.shape, F32)),
-        in_specs=[any_spec] * 5,
-        out_specs=(any_spec,) * 5 + (vm_spec,),
+                   shape(vec.shape, F32), shape((D, D), BF), shape((D, up_weight.shape[1]), BF)),
+        in_specs=[any_spec] * 7,
+        out_specs=(any_spec,) * 5 + (vm_spec,) + (any_spec,) * 2,
         scratch_shapes=[
             vm(runs, BF), vm(runs, BF), vm(runs, BF), vm((tall, D), BF), vm((3, D, D), BF), vm((n_wsh,) + vec.shape, BF),
-            dma((n_ctx, n_slices)), dma((3, far, n_slices)), dma((2, 3, 4)), dma((7,)), dma((3, n_ctx)),
+            vm((D, D), BF), vm((D, up_weight.shape[1]), BF),
+            dma((n_ctx, n_slices)), dma((3, far, n_slices)), dma((2, 4, 6)), dma((7,)), dma((3, n_ctx)),
         ],
         compiler_params=pltpu.CompilerParams(collective_id=1, has_side_effects=True, vmem_limit_bytes=48 * 2**20),
         name="gather_project",
-    )(inputs, vec, key_weight, value_weight, query_weight)
+    )(inputs, vec, key_weight, value_weight, query_weight, out_weight, up_weight)
 
 
 def local(
@@ -954,9 +1135,11 @@
         vec = jnp.where(at, jnp.tile(small, (1, n_wsh)), jnp.zeros((), BF))
         at = lax.broadcasted_iota(jnp.int32, (8, D), 0) == w
         vec = jnp.concatenate([vec, jnp.where(at, up_bias[None, :], jnp.zeros((), BF))], axis=0)
-        all_tokens, keys, values, queries, kvq_w, vec = gather_project(
-            inputs, vec, key_weight, value_weight, query_weight
+        all_tokens, keys, values, queries, kvq_w, vec, out_w, up_w = gather_project(
+            inputs, vec, key_weight, value_weight, query_weight, out_weight, up_weight
         )
+        down_own, _unused = lax.optimization_barrier((down_weight, vec))
+        down_far = lax.ppermute(down_own, "wsh", [(i, i ^ 2) for i in range(n_wsh)])
         all_tokens, keys, values = [r.reshape(stream_rows, D) for r in (all_tokens, keys, values)]
         key_w, value_w, query_w = kvq_w[0], kvq_w[1], kvq_w[2]
         query_b, value_b, out_b, attn_g, attn_s, down_b, final_g, final_s = [vec[i] for i in range(8)]
@@ -971,11 +1154,28 @@
         queries = queries.astype(BF) * jnp.asarray(SCALE, BF)
         keys = jnp.dot(all_tokens, key_w, preferred_element_type=F32).astype(BF)
         values = (jnp.dot(all_tokens, value_w, preferred_element_type=F32) + value_b).astype(BF)
+    mixed_t, log_rows = attn_fwd(bounds, queries, query_doc, keys, key_doc, values, tq=tile)
+    if fast:
+        layer_out, grad_sum1, grad_attn, vec_grads, grad_up_w, grad_down_w, grad_out_w = middle(
+            mixed_t, inputs, cotangent[0], vec, out_w, up_w, down_own, down_far
+        )
+        grad_q, grad_k, grad_v = attn_bwd(
+            bounds, queries, query_doc, grad_attn, log_rows, mixed_t, keys, key_doc, values, tq=tile
+        )
+        mats, small, wide, grad_inputs = finish(
+            (grad_up_w, grad_out_w, grad_down_w), vec_grads, grad_k.reshape(n_ctx, tok_rows, D),
+            grad_v.reshape(n_ctx, tok_rows, D), all_tokens.reshape(n_ctx, tok_rows, D), grad_q, kvq_w, grad_sum1, inputs,
+        )
+        up_sum, out_sum, down_sum, key_sum, value_sum, query_sum = mats
+        return (
+            layer_out.reshape(1, tok_rows, D), grad_inputs.reshape(1, tok_rows, D), query_sum, key_sum, value_sum,
+            out_sum, up_sum, down_sum, small[0], small[1], small[2], small[3], small[4], wide[0],
+            small[5], small[6], small[7],
+        )
+
     out_w = gather(out_weight)
     up_w = gather(up_weight)
     down_w = gather(down_weight)
-
-    mixed_t, log_rows = attn_fwd(bounds, queries, query_doc, keys, key_doc, values, tq=tile)
     attn_t = mixed_t.astype(BF)
     inputs_f = inputs.astype(F32)
     branch = lax.dot_general(attn_t, out_w, TN, preferred_element_type=F32) + out_b
@@ -1010,38 +1210,24 @@
         part = lax.psum_scatter(g.astype(BF), "wsh", scatter_dimension=0, tiled=True)
         return lax.psum(part, "ctx").astype(F32)
 
-    if fast:
-        none = jnp.zeros((D,), F32)
-        vec = jnp.stack([none, none, grad_out_b, grad_attn_g, grad_attn_s, grad_down_b, grad_final_g, grad_final_s])
-        vec = jnp.concatenate([vec, grad_up_b.reshape(n_wsh, -1), jnp.zeros((8 - n_wsh, D), F32)], axis=0)
-        mats, small, wide, grad_inputs = finish(
-            (grad_up_w, grad_out_w, grad_down_w), vec, grad_k.reshape(n_ctx, tok_rows, D),
-            grad_v.reshape(n_ctx, tok_rows, D), all_tokens.reshape(n_ctx, tok_rows, D), grad_q, kvq_w, grad_sum1, inputs,
+    grad_all = jnp.einsum("te,de->td", grad_k, key_w, preferred_element_type=F32)
+    grad_all = grad_all + jnp.einsum("te,de->td", grad_v, value_w, preferred_element_type=F32)
+    grad_own = lax.psum_scatter(grad_all.astype(BF), "ctx", scatter_dimension=0, tiled=True)
+    grad_query_w = jnp.einsum("td,te->de", inputs, grad_q, preferred_element_type=F32)
+    grad_key_w = jnp.einsum("td,te->de", all_tokens, grad_k, preferred_element_type=F32)
+    grad_value_w = jnp.einsum("td,te->de", all_tokens, grad_v, preferred_element_type=F32)
+    grad_query_b = jnp.sum(grad_q.astype(F32), axis=0)
+    grad_value_b = jnp.sum(grad_v.astype(F32), axis=0)
+    grad_inputs = grad_sum1 + jnp.einsum("te,de->td", grad_q, query_w, preferred_element_type=F32)
+    grad_inputs = grad_inputs + grad_own.astype(F32)
+    sums = [
+        total(g)
+        for g in (
+            grad_query_w, grad_key_w, grad_value_w, grad_out_w, grad_up_w, grad_down_w,
+            grad_query_b, grad_value_b, grad_out_b, grad_attn_g, grad_attn_s, grad_up_b,
+            grad_down_b, grad_final_g, grad_final_s,
         )
-        up_sum, out_sum, down_sum, key_sum, value_sum, query_sum = mats
-        sums = [
-            query_sum, key_sum, value_sum, out_sum, up_sum, down_sum, small[0], small[1], small[2], small[3], small[4],
-            wide[0], small[5], small[6], small[7],
-        ]
-    else:
-        grad_all = jnp.einsum("te,de->td", grad_k, key_w, preferred_element_type=F32)
-        grad_all = grad_all + jnp.einsum("te,de->td", grad_v, value_w, preferred_element_type=F32)
-        grad_own = lax.psum_scatter(grad_all.astype(BF), "ctx", scatter_dimension=0, tiled=True)
-        grad_query_w = jnp.einsum("td,te->de", inputs, grad_q, preferred_element_type=F32)
-        grad_key_w = jnp.einsum("td,te->de", all_tokens, grad_k, preferred_element_type=F32)
-        grad_value_w = jnp.einsum("td,te->de", all_tokens, grad_v, preferred_element_type=F32)
-        grad_query_b = jnp.sum(grad_q.astype(F32), axis=0)
-        grad_value_b = jnp.sum(grad_v.astype(F32), axis=0)
-        grad_inputs = grad_sum1 + jnp.einsum("te,de->td", grad_q, query_w, preferred_element_type=F32)
-        grad_inputs = grad_inputs + grad_own.astype(F32)
-        sums = [
-            total(g)
-            for g in (
-                grad_query_w, grad_key_w, grad_value_w, grad_out_w, grad_up_w, grad_down_w,
-                grad_query_b, grad_value_b, grad_out_b, grad_attn_g, grad_attn_s, grad_up_b,
-                grad_down_b, grad_final_g, grad_final_s,
-            )
-        ]
+    ]
     return (
         layer_out.reshape(1, tok_rows, D),
         grad_inputs.astype(BF).reshape(1, tok_rows, D),

time: 398 us -> 388 us (0.975)
  Pallas kernels: 301 us -> 351 us
  matrix products: 39.6 us -> 0 us
  between operations: 17.6 us -> 4.1 us
  waiting for transfers between devices: 11 us -> 0.01 us
  local copies, waits for them, and re-layouts: 9.33 us -> 19 us
    dot_general x9 -> x0, matrix products: 39.6 us -> none  [the longest x1 8.25 us: local(): up_f = jnp.dot(first_b, up_w, preferred_element_type=F32) + up_b]
    pallas_call x1, Pallas kernels: 200 us -> 161 us  [finish(): pl.pallas_call(functools.partial(finish_kernel, sources, len(parts)), out...]
    pallas_call x0 -> x1, Pallas kernels: none -> 38.3 us  [middle(): pl.pallas_call(middle_kernel, out_shape=(shape((rows, D), BF), shape((row...]
    pallas_call x1, Pallas kernels: 26.6 us -> 51.6 us  [attn_bwd(): pl.pallas_call(functools.partial(bwd_kernel, tk), out_shape=(jax.ShapeDty...]
    pallas_call x1, Pallas kernels: 16.6 us -> 32.6 us  [attn_fwd(): pl.pallas_call(functools.partial(fwd_kernel, tk), out_shape=(jax.ShapeDty...]
    pallas_call x1, Pallas kernels: 57.9 us -> 67.8 us  [gather_project(): pl.pallas_call(functools.partial(gather_kernel, 5), out_shape=(shape(runs...]
    all_gather x3 -> x0, waiting for transfers between devices: 8.95 us -> none  [gather(): return lax.all_gather(x, 'wsh', axis=0, tiled=True)]
    unnamed x59 -> x34, local copies, waits for them, and re-layouts: 5.76 us -> 11.5 us
  transfers between devices with their start and end apart: 3 -> 1, of which waited for: 1 -> 0; matrix products, arithmetic and copies ran while one was open for 4% -> 1% of each run, Pallas kernels for 19% -> 8%
where the time goes in v6:
time: 388 us; the launch traced here: 386 us
  Pallas kernels  351 us (90%)
  local copies, waits for them, and re-layouts  19 us (5%)
  other arithmetic  11.3 us (3%)
  between operations  4.1 us (1%)
    pallas_call x1, Pallas kernels, finish(): pl.pallas_call(functools.partial(finish_kernel, sources, len(parts)), out...  161 us
    pallas_call x1, Pallas kernels, gather_project(): pl.pallas_call(functools.partial(gather_kernel, 5), out_shape=(shape(runs...  67.8 us
    pallas_call x1, Pallas kernels, attn_bwd(): pl.pallas_call(functools.partial(bwd_kernel, tk), out_shape=(jax.ShapeDty...  51.6 us
    pallas_call x1, Pallas kernels, middle(): pl.pallas_call(middle_kernel, out_shape=(shape((rows, D), BF), shape((row...  38.3 us
    pallas_call x1, Pallas kernels, attn_fwd(): pl.pallas_call(functools.partial(fwd_kernel, tk), out_shape=(jax.ShapeDty...  32.6 us
    unnamed x34, local copies, waits for them, and re-layouts  11.5 us
  transfers between devices with their start and end apart: 1, of which 0 were waited for; matrix products, arithmetic and copies ran while one was open for 1% of the time, Pallas kernels for 8%

profile of v6, /device:TPU:0, one launch (start us, length us, event | category | flops | bytes accessed | tf_op | source)
XLA Modules:
  0.0 386.1 jit_solution(2931833577647559908)
XLA Ops:
  0.7 0.7 stack.39
  1.4 0.7 stack.40
  2.0 0.7 stack.41
  2.7 0.7 stack.42
  3.3 0.7 stack.43
  4.0 0.7 stack.44
  4.7 0.7 stack.45
  5.3 0.7 stack.46
  6.1 0.8 broadcast_select_fusion
  6.9 1.1 copy-done
  8.0 1.3 copy-done.2
  9.3 1.0 copy-done.4
  10.3 1.0 copy-done.5
  11.2 1.0 copy-done.6
  12.2 1.0 copy-done.7
  13.2 67.8 %gather_project.1 = (bf16[8,512,768]{2,1,0:T(8,128)(2,1)}, bf16[8,512,768]{2,1,0:T(8,128)(2,1)}, bf16[8,512,768]{2,1,0:T(8,128)(2,1)}, bf16[512,768]{1,0:T(8,128...) custom-call(bf16[512,768]{1,0:T(8,128)(2,1)S(1)} %bitcast.51, ...), custom_call_target="tpu_custom_call" | custom-call | tf_op jit(solution)/shard_map/gather_project/pallas_call | solution.py:1077
  80.9 0.9 copy-done.1
  81.8 1.0 copy-done.3
  84.0 0.6 fusion.5
  88.6 0.8 and_convert_fusion.qaug_ref
  89.4 1.4 select_convert_fusion.kaug_ref
  90.8 32.6 %attend.1 = (f32[768,512]{1,0:T(8,128)}, f32[6,2,512]{2,1,0:T(2,128)}) custom-call(s32[1,2]{1,0:T(1,128)} %pad_add_fusion.bounds, bf16[512,768]{1,0:T(8,128)(2,1)} %copy-done.1, bf16[512,128]{1,0:T(8,128)(2,1)} %and_convert_fusion.qaug_ref, bf16[4096,768]{1,0:T(8,128)(2,1)} %bitcast.52, bf16[4096,128]{1,0:T(8,128)(2,1)} %select_convert_fusion.kaug_ref, ...), custom_call_target="tpu_custom_call" | custom-call | tf_op jit(solution)/shard_map/attend/pallas_call | solution.py:112
  123.5 1.0 copy-done.10
  124.5 38.3 %middle.1 = (bf16[512,768]{1,0:T(8,128)(2,1)}, f32[512,768]{1,0:T(8,128)}, bf16[512,768]{1,0:T(8,128)(2,1)}, f32[16,768]{1,0:T(8,128)}, bf16[768,3072]{1,0:T(8,1...) custom-call(f32[768,512]{1,0:T(8,128)} %get-tuple-element.45.attn_ref.ot_ref, bf16[512,768]{1,0:T(8,128)(2,1)} %bitcast.49, ...), custom_call_target="tpu_custom_call" | custom-call | tf_op jit(solution)/shard_map/middle/pallas_call | solution.py:354
  162.8 51.6 %attend_back.1 = (bf16[512,768]{1,0:T(8,128)(2,1)}, bf16[4096,768]{1,0:T(8,128)(2,1)}, bf16[4096,768]{1,0:T(8,128)(2,1)}) custom-call(s32[1,2]{1,0:T(1,128)} %pad_add_fusion.bounds, bf16[512,768]{1,0:T(8,128)(2,1)} %copy-done.1, bf16[512,128]{1,0:T(8,128)(2,1)} %and_convert_fusion.qaug_ref, bf16[512,768]{1,0:T(8,128)(2,1)} %get-tuple-element.55.do_ref, ...), custom_call_target="tpu_custom_call" | custom-call | tf_op jit(solution)/shard_map/attend_back/pallas_call | solution.py:175
  214.4 161.0 %finish.1 = (bf16[12,192,768]{2,1,0:T(8,128)(2,1)}, f32[8,192]{1,0:T(8,128)}, f32[1,768]{1,0:T(1,128)}, bf16[512,768]{1,0:T(8,128)(2,1)}) custom-call(bf16[4,192,3072]{2,1,0:T(8,128)(2,1)} %bitcast.58, bf16[4,192,768]{2,1,0:T(8,128)(2,1)} %bitcast.60, bf16[4,768,768]{2,1,0:T(8,128)(2,1)} %bitcast.59, f32[16,768]{1,0:T(8,128)} %get-tuple-element.54.refs_3_, ...), custom_call_target="tpu_custom_call" | custom-call | tf_op jit(solution)/shard_map/finish/pallas_call | solution.py:827
  375.4 1.3 slice.72
  376.8 3.1 slice_bitcast_fusion.3
  380.4 1.7 bitcast_convert_fusion
  382.7 1.7 maximum_convert_fusion
  384.4 0.9 copy.37
  385.3 0.9 copy.38
  (41 shorter events, 3.3 us)
Async XLA Ops:
  0.7 83.3 %copy-start.15 = (s32[1,8]{1,0:T(1,128)S(1)}, s32[1,8]{1,0:T(1,128)}, u32[]{:S(2)}) copy-start(s32[1,8]{1,0:T(1,128)} %param.20) | copy-start | bytes 100
  6.9 1.1 copy-start
  8.0 1.3 copy-start.2
  9.3 1.0 copy-start.4
  10.3 1.0 copy-start.5
  11.2 1.0 copy-start.6
  12.2 1.0 copy-start.7
  13.2 70.3 %copy-start.9 = (bf16[768,768]{1,0:T(8,128)(2,1)S(1)}, bf16[768,768]{1,0:T(8,128)(2,1)}, u32[]{:S(2)}) copy-start(bf16[768,768]{1,0:T(8,128)(2,1)} %down_own) | copy-start | bytes 3538948
  80.9 0.9 copy-start.1
  81.8 1.0 copy-start.3
  82.8 0.6 copy-start.8
  83.4 40.0 %collective-permute-start = (bf16[768,768]{1,0:T(8,128)(2,1)S(1)}, bf16[768,768]{1,0:T(8,128)(2,1)S(1)}, u32[]{:S(2)}, u32[]{:S(2)}) collective-permute-start(bf16[768,768]{1,0:T(8,128)(2,1)S(1)} %copy-done.9), channel_id=1, source_target_pairs={{0,2},{1,3},{2,0},{3,1},{4,6},{5,7},{6,4},{7,5},{8,10},{9,11},{10,... | collective-permute-start | bytes 3538952 | tf_op jit(solution)/shard_map/ppermute | solution.py:1142
  123.5 1.0 copy-start.10
  376.8 3.1 copy-start.13
  379.8 2.3 copy-start.14
  382.1 2.3 copy-start.11
  382.7 2.6 copy-start.12

commit v7 on v6

--- a/solution.py
+++ b/solution.py
@@ -31,17 +31,16 @@
     return 0.5 * values * (1.0 + lax.erf(values * ROOT_HALF))
 
 
-def key_range(doc_start, first_row, rows, stream_rows, tile):
-    pos = jnp.arange(rows // tile, dtype=jnp.int32) * tile + first_row
-    last = pos + tile - 1
-    low = jnp.max(jnp.where(doc_start[None, :] <= pos[:, None], doc_start[None, :], 0), axis=1)
-    high = jnp.min(
-        jnp.where(doc_start[None, :] > last[:, None], doc_start[None, :], stream_rows), axis=1
-    )
+def key_range(docs, first_row, tile, stream_rows):
+    last = first_row + tile - 1
+    low, high = 0, stream_rows
+    for d in range(1, docs.shape[0]):
+        low = jnp.where(docs[d] <= first_row, docs[d], low)
+    for d in range(docs.shape[0] - 1, 0, -1):
+        high = jnp.where(docs[d] > last, docs[d], high)
     first = low // 128 * 128
     count = (high - first + 255) // 256
-    first = jnp.minimum(first, stream_rows - count * 256)
-    return jnp.stack([first, count], axis=1).astype(jnp.int32)
+    return jnp.minimum(first, stream_rows - count * 256), count
 
 
 def document_lanes(doc_start, first_row, rows, stream_rows):
@@ -78,10 +77,11 @@
     c = lax.fori_loop(0, whole, large, init)
     return lax.fori_loop(whole * big, count, small, c)
 
-def fwd_kernel(tk, bounds, q_ref, qaug_ref, k_ref, kaug_ref, v_ref, ot_ref, lse_ref, s_scr, acc):
+def fwd_kernel(tk, docs, q_ref, qaug_ref, k_ref, kaug_ref, v_ref, ot_ref, lse_ref, s_scr, acc):
     qi = pl.program_id(1)
-    start, count = bounds[qi, 0], bounds[qi, 1]
     tq = q_ref.shape[0]
+    first_row = lax.axis_index("ctx") * (tq * pl.num_programs(1)) + qi * tq
+    start, count = key_range(docs, first_row, tq, k_ref.shape[0])
     rhs = stack_heads(q_ref[...], qaug_ref[...])
 
     def scores(loc, off, size, m):
@@ -105,7 +105,7 @@
     lse = m + jnp.log(l)
     lse_ref[0] = jnp.concatenate([lse[:, :tq], lse[:, tq:]], axis=0)
 
-def attn_fwd(bounds, q, qaug, k, kaug, v, *, tq=512, tk=768):
+def attn_fwd(docs, q, qaug, k, kaug, v, *, tq=512, tk=768):
     T, D = q.shape
     S = k.shape[0]
     pairs = D // 128
@@ -123,13 +123,14 @@
                        pl.BlockSpec((1, 2, tq), lambda h, i, b: (h, 0, i))),
             scratch_shapes=[pltpu.VMEM((S, 2 * tq), F32), pltpu.VMEM((128, 2 * tq), F32)]),
         name="attend",
-    )(bounds, q, qaug, k, kaug, v)
-
-def bwd_kernel(tk, bounds, q_ref, qaug_ref, do_ref, lse_ref, ot_ref, k_ref, kaug_ref, v_ref,
+    )(docs, q, qaug, k, kaug, v)
+
+def bwd_kernel(tk, docs, q_ref, qaug_ref, do_ref, lse_ref, ot_ref, k_ref, kaug_ref, v_ref,
                dq_ref, dk_ref, dv_ref, dk_acc, dv_acc, dq_acc):
     qi = pl.program_id(1)
-    start, count = bounds[qi, 0], bounds[qi, 1]
     tq = q_ref.shape[0]
+    first_row = lax.axis_index("ctx") * (tq * pl.num_programs(1)) + qi * tq
+    start, count = key_range(docs, first_row, tq, k_ref.shape[0])
 
     @pl.when(qi == 0)
     def _():
@@ -167,7 +168,7 @@
         dk_ref[...] = dk_acc[...].astype(BF)
         dv_ref[...] = dv_acc[...].astype(BF)
 
-def attn_bwd(bounds, q, qaug, do, lse, ot, k, kaug, v, *, tq=512, tk=768):
+def attn_bwd(docs, q, qaug, do, lse, ot, k, kaug, v, *, tq=512, tk=768):
     T, D = q.shape
     S = k.shape[0]
     pairs = D // 128
@@ -190,7 +191,7 @@
                        pl.BlockSpec((S, 128), lambda h, i, b: (0, h))),
             scratch_shapes=[pltpu.VMEM((S, 128), F32), pltpu.VMEM((S, 128), F32), pltpu.VMEM((128, 2 * tq), F32)]),
         name="attend_back",
-    )(bounds, q, qaug, do, lse, ot, k, kaug, v)
+    )(docs, q, qaug, do, lse, ot, k, kaug, v)
 
 
 def middle_kernel(attn_ref, in_ref, cot_ref, vec_ref, wo_ref, wu_ref, down_own, down_far,
@@ -349,7 +350,7 @@
     rows = inputs.shape[0]
     wide = up_w.shape[1]
     vm, dma, shape = pltpu.VMEM, pltpu.SemaphoreType.DMA, jax.ShapeDtypeStruct
-    any_spec = pl.BlockSpec(memory_space=pl.ANY)
+    any_spec = pl.BlockSpec(memory_space=pltpu.HBM)
     vm_spec = pl.BlockSpec(memory_space=pltpu.VMEM)
     return pl.pallas_call(
         middle_kernel,
@@ -363,7 +364,7 @@
             vm((rows, D), F32), vm((rows, D), BF), vm((rows, wide), BF), vm((rows, D), BF), vm((D, rows), BF),
             vm((D, wide), BF), vm((wide, D), BF), vm((D, D), BF), dma((4,)), dma((2, 2)), dma((3, wide // D)),
         ],
-        compiler_params=pltpu.CompilerParams(collective_id=3, has_side_effects=True, vmem_limit_bytes=56 * 2**20),
+        compiler_params=pltpu.CompilerParams(collective_id=3, has_side_effects=True, vmem_limit_bytes=63 * 2**20),
         name="middle",
     )(attn_t, inputs, cotangent, vec, out_w, up_w, down_own, down_far)
 
@@ -807,6 +808,27 @@
     lax.fori_loop(0, n_pos // 2, drain_x, 0)
 
 
+def widen_kernel(spans, in_ref, *outs):
+    for (first, down, across), out in zip(spans, outs):
+        for r in range(down):
+            for col in range(across):
+                out[r, :, col * D : (col + 1) * D] = in_ref[first + r * across + col].astype(F32)
+
+
+def widen(summed, spans):
+    n, rows, _width = summed.shape
+    part = rows // 4
+    outs = pl.pallas_call(
+        functools.partial(widen_kernel, spans),
+        grid=(4,),
+        out_shape=[jax.ShapeDtypeStruct((down, rows, across * D), F32) for _first, down, across in spans],
+        in_specs=[pl.BlockSpec((n, part, D), lambda i: (0, i, 0))],
+        out_specs=[pl.BlockSpec((down, part, across * D), lambda i: (0, i, 0)) for _first, down, across in spans],
+        name="widen",
+    )(summed)
+    return [o.reshape(-1, o.shape[2]) for o in outs]
+
+
 def finish(matrices, vec, grad_k, grad_v, all_tokens, grad_q, kvq_w, own_grad, inputs):
     n_ctx, n_wsh = lax.axis_size("ctx"), lax.axis_size("wsh")
     zs, hops = n_ctx // 2, reach(n_ctx) // 2
@@ -822,7 +844,7 @@
     half, piece, tall = D // 2, rows // zs, inputs.shape[0]
     n_pos, cut = 4 * hops + 2, tall // 2
     vm, dma, shape = pltpu.VMEM, pltpu.SemaphoreType.DMA, jax.ShapeDtypeStruct
-    any_spec = pl.BlockSpec(memory_space=pl.ANY)
+    any_spec = pl.BlockSpec(memory_space=pltpu.HBM)
     vm_spec = pl.BlockSpec(memory_space=pltpu.VMEM)
     summed, small, wide, grad_own = pl.pallas_call(
         functools.partial(finish_kernel, sources, len(parts)),
@@ -844,18 +866,12 @@
         compiler_params=pltpu.CompilerParams(collective_id=2, has_side_effects=True, vmem_limit_bytes=63 * 2**20),
         name="finish",
     )(*parts, vec, grad_k, grad_v, all_tokens, grad_q, kvq_w, own_grad, inputs)
-    sums = []
-    for first, down, across in spans:
-        block = summed[first : first + down * across]
-        if across > 1:
-            block = jnp.concatenate([block[i] for i in range(across)], axis=1)
-        sums.append(block.reshape(down * rows, across * D).astype(F32))
-    return sums, small, wide, grad_own
-
-
-def gather_kernel(cut, tok_ref, vec_ref, wk_ref, wv_ref, wq_ref, wo_ref, wu_ref,
-                  tok_out, k_out, v_out, q_out, w_out, vec_out, wo_out, wu_out,
-                  tok, kbuf, vbuf, qbuf, wbuf, vecs, wo, wu,
+    return widen(summed, spans), small, wide, grad_own
+
+
+def gather_kernel(cut, tok_ref, docs_ref, wk_ref, wv_ref, wq_ref, wo_ref, wu_ref, vec_ref,
+                  tok_out, k_out, v_out, q_out, w_out, vec_out, wo_out, wu_out, query_doc, key_doc,
+                  tok, kbuf, vbuf, qbuf, wbuf, vecs, wo, wu, kdoc,
                   sem_in, sem_out, sem_w, sem_l, sem_o):
     n_ctx = lax.axis_size("ctx")
     zs = n_ctx // 2
@@ -929,11 +945,13 @@
             return vecs.at[owner]
         return (wbuf.at[0], wbuf.at[1], wbuf.at[2], None, wo, wu)[m].at[weight_rows(owner), :]
 
-    shards = (wk_ref, wv_ref, wq_ref, vec_ref, wo_ref, wu_ref)
+    vecs[w, 0 : vec_ref.shape[0], :] = vec_ref[...]
+    shards = (wk_ref, wv_ref, wq_ref, vecs.at[w], wo_ref, wu_ref)
     for m in (3, 0, 1, 2, 4, 5):
         remote(shards[m], shard(m, w), sem_w.at[0, 1, m], sem_w.at[1, 1, m], y_peer).start()
         remote(shards[m], shard(m, w), sem_w.at[0, 0, m], sem_w.at[1, 0, m], core_peer).start()
-        pltpu.make_async_copy(shards[m], shard(m, w), sem_w.at[0, 3, m]).start()
+        if m != 3:
+            pltpu.make_async_copy(shards[m], shard(m, w), sem_w.at[0, 3, m]).start()
     lax.fori_loop(0, n_slices, start_own, 0)
     pltpu.make_async_copy(tok_ref, tok.at[a], sem_l.at[4]).start()
 
@@ -941,6 +959,24 @@
         @pl.when(jnp.abs(j - a) > near)
         def _():
             tok[j] = jnp.zeros_like(tok[j])
+
+    n_rows = tok.shape[1]
+
+    def is_own_lane(first):
+        pos = first + lax.broadcasted_iota(jnp.int32, (n_rows, 128), 0)
+        doc = jnp.full((n_rows, 128), -1, jnp.int32)
+        for d in range(docs_ref.shape[1]):
+            doc = doc + jnp.where(pos >= docs_ref[0, d], 1, 0)
+        return lax.broadcasted_iota(jnp.int32, (n_rows, 128), 1) == doc
+
+    def key_lanes(j, carry):
+        kdoc[pl.ds(pl.multiple_of(j * n_rows, n_rows), n_rows), :] = jnp.where(
+            is_own_lane(j * n_rows), 0.0, -1e30).astype(BF)
+        return carry
+
+    lax.fori_loop(0, n_ctx, key_lanes, 0)
+    pltpu.make_async_copy(kdoc, key_doc, sem_l.at[3]).start()
+    query_doc[...] = jnp.where(is_own_lane(a * n_rows), 1.0, 0.0).astype(BF)
 
     def weight_arrival(m, kind):
         part = shard(m, w)
@@ -955,7 +991,8 @@
     def weight_end(m):
         weight_arrival(m, 0).wait_recv()
         weight_arrival(m, 2).wait_recv()
-        pltpu.make_async_copy(shard(m, w), shard(m, w), sem_w.at[0, 3, m]).wait()
+        if m != 3:
+            pltpu.make_async_copy(shard(m, w), shard(m, w), sem_w.at[0, 3, m]).wait()
 
     def relay(first, last):
         def one(i, carry):
@@ -972,10 +1009,9 @@
     weight_forward(0)
     weight_forward(1)
     weight_end(3)
-    total = vecs[0].astype(F32)
-    for owner in range(1, 4):
-        total = total + vecs[owner].astype(F32)
-    vec_out[...] = total
+    vec_out[0:8, :] = jnp.concatenate([vecs[o, 0:8, :] for o in range(4)], axis=1)
+    for o in range(4):
+        vec_out[8 + o : 9 + o, :] = jnp.concatenate([vecs[o, 8 + i : 9 + i, :] for i in range(4)], axis=1)
     pltpu.make_async_copy(tok_ref, tok.at[a], sem_l.at[4]).wait()
     weight_end(0)
     weight_end(1)
@@ -1062,32 +1098,34 @@
     pltpu.make_async_copy(wbuf, w_out, sem_l.at[6]).wait()
     pltpu.make_async_copy(wo, wo_out, sem_l.at[0]).wait()
     pltpu.make_async_copy(wu, wu_out, sem_l.at[1]).wait()
-
-
-def gather_project(inputs, vec, key_weight, value_weight, query_weight, out_weight, up_weight):
+    pltpu.make_async_copy(kdoc, key_doc, sem_l.at[3]).wait()
+
+
+def gather_project(inputs, doc_starts, vectors, key_weight, value_weight, query_weight, out_weight, up_weight):
     n_ctx, n_wsh = lax.axis_size("ctx"), lax.axis_size("wsh")
     tall = inputs.shape[0]
     n_slices = 8
     far = 4 * (reach(n_ctx) // 2 + 1)
     vm, dma = pltpu.VMEM, pltpu.SemaphoreType.DMA
-    any_spec = pl.BlockSpec(memory_space=pl.ANY)
+    any_spec = pl.BlockSpec(memory_space=pltpu.HBM)
     vm_spec = pl.BlockSpec(memory_space=pltpu.VMEM)
     runs = (n_ctx, tall, D)
     shape = jax.ShapeDtypeStruct
     return pl.pallas_call(
         functools.partial(gather_kernel, 5),
         out_shape=(shape(runs, BF), shape(runs, BF), shape(runs, BF), shape((tall, D), BF), shape((3, D, D), BF),
-                   shape(vec.shape, F32), shape((D, D), BF), shape((D, up_weight.shape[1]), BF)),
-        in_specs=[any_spec] * 7,
-        out_specs=(any_spec,) * 5 + (vm_spec,) + (any_spec,) * 2,
+                   shape((16, D), F32), shape((D, D), BF), shape((D, up_weight.shape[1]), BF), shape((tall, 128), BF),
+                   shape((n_ctx * tall, 128), BF)),
+        in_specs=[any_spec, pl.BlockSpec(memory_space=pltpu.SMEM)] + [any_spec] * 5 + [vm_spec],
+        out_specs=(any_spec,) * 5 + (vm_spec,) + (any_spec,) * 2 + (vm_spec, any_spec),
         scratch_shapes=[
-            vm(runs, BF), vm(runs, BF), vm(runs, BF), vm((tall, D), BF), vm((3, D, D), BF), vm((n_wsh,) + vec.shape, BF),
-            vm((D, D), BF), vm((D, up_weight.shape[1]), BF),
+            vm(runs, BF), vm(runs, BF), vm(runs, BF), vm((tall, D), BF), vm((3, D, D), BF), vm((n_wsh, 16, D // n_wsh), F32),
+            vm((D, D), BF), vm((D, up_weight.shape[1]), BF), vm((n_ctx * tall, 128), BF),
             dma((n_ctx, n_slices)), dma((3, far, n_slices)), dma((2, 4, 6)), dma((7,)), dma((3, n_ctx)),
         ],
-        compiler_params=pltpu.CompilerParams(collective_id=1, has_side_effects=True, vmem_limit_bytes=48 * 2**20),
+        compiler_params=pltpu.CompilerParams(collective_id=1, has_side_effects=True, vmem_limit_bytes=63 * 2**20),
         name="gather_project",
-    )(inputs, vec, key_weight, value_weight, query_weight, out_weight, up_weight)
+    )(inputs, doc_starts, key_weight, value_weight, query_weight, out_weight, up_weight, vectors)
 
 
 def local(
@@ -1114,37 +1152,29 @@
     doc_start = doc_starts[0]
     tok_rows = inputs.shape[0]
     stream_rows = tok_rows * lax.axis_size("ctx")
-    first_row = lax.axis_index("ctx") * tok_rows
     tile = min(tok_rows, 512)
-    bounds = key_range(doc_start, first_row, tok_rows, stream_rows, tile)
-    query_doc, key_doc = document_lanes(doc_start, first_row, tok_rows, stream_rows)
-
     n_ctx, n_wsh = lax.axis_size("ctx"), lax.axis_size("wsh")
     own = D // n_wsh
 
     def gather(x):
         return lax.all_gather(x, "wsh", axis=0, tiled=True)
 
-    small = jnp.stack(
-        [query_bias, value_bias, out_bias, attn_gain, attn_shift, down_bias, final_gain, final_shift]
-    )
     fast = n_wsh == 4 and n_ctx == 8 and own % (n_ctx // 2 * 16) == 0 and tok_rows % 512 == 0
     if fast:
-        w = lax.axis_index("wsh")
-        at = lax.broadcasted_iota(jnp.int32, (8, D), 1) // own == w
-        vec = jnp.where(at, jnp.tile(small, (1, n_wsh)), jnp.zeros((), BF))
-        at = lax.broadcasted_iota(jnp.int32, (8, D), 0) == w
-        vec = jnp.concatenate([vec, jnp.where(at, up_bias[None, :], jnp.zeros((), BF))], axis=0)
-        all_tokens, keys, values, queries, kvq_w, vec, out_w, up_w = gather_project(
-            inputs, vec, key_weight, value_weight, query_weight, out_weight, up_weight
+        small = (query_bias, value_bias, out_bias, attn_gain, attn_shift, down_bias, final_gain, final_shift)
+        vectors = jnp.concatenate(small + (up_bias,)).astype(F32).reshape(8 + n_wsh, own)
+        all_tokens, keys, values, queries, kvq_w, vec, out_w, up_w, query_doc, key_doc = gather_project(
+            inputs, doc_starts, vectors, key_weight, value_weight, query_weight, out_weight, up_weight
         )
         down_own, _unused = lax.optimization_barrier((down_weight, vec))
         down_far = lax.ppermute(down_own, "wsh", [(i, i ^ 2) for i in range(n_wsh)])
         all_tokens, keys, values = [r.reshape(stream_rows, D) for r in (all_tokens, keys, values)]
-        key_w, value_w, query_w = kvq_w[0], kvq_w[1], kvq_w[2]
-        query_b, value_b, out_b, attn_g, attn_s, down_b, final_g, final_s = [vec[i] for i in range(8)]
-        up_b = vec[8 : 8 + n_wsh].reshape(-1)
     else:
+        first_row = lax.axis_index("ctx") * tok_rows
+        query_doc, key_doc = document_lanes(doc_start, first_row, tok_rows, stream_rows)
+        small = jnp.stack(
+            [query_bias, value_bias, out_bias, attn_gain, attn_shift, down_bias, final_gain, final_shift]
+        )
         all_tokens = lax.all_gather(inputs, "ctx", axis=0, tiled=True)
         query_w, key_w, value_w = gather(query_weight), gather(key_weight), gather(value_weight)
         small = gather(small.T).astype(F32)
@@ -1154,13 +1184,13 @@
         queries = queries.astype(BF) * jnp.asarray(SCALE, BF)
         keys = jnp.dot(all_tokens, key_w, preferred_element_type=F32).astype(BF)
         values = (jnp.dot(all_tokens, value_w, preferred_element_type=F32) + value_b).astype(BF)
-    mixed_t, log_rows = attn_fwd(bounds, queries, query_doc, keys, key_doc, values, tq=tile)
+    mixed_t, log_rows = attn_fwd(doc_start, queries, query_doc, keys, key_doc, values, tq=tile)
     if fast:
         layer_out, grad_sum1, grad_attn, vec_grads, grad_up_w, grad_down_w, grad_out_w = middle(
             mixed_t, inputs, cotangent[0], vec, out_w, up_w, down_own, down_far
         )
         grad_q, grad_k, grad_v = attn_bwd(
-            bounds, queries, query_doc, grad_attn, log_rows, mixed_t, keys, key_doc, values, tq=tile
+            doc_start, queries, query_doc, grad_attn, log_rows, mixed_t, keys, key_doc, values, tq=tile
         )
         mats, small, wide, grad_inputs = finish(
             (grad_up_w, grad_out_w, grad_down_w), vec_grads, grad_k.reshape(n_ctx, tok_rows, D),
@@ -1204,7 +1234,7 @@
     grad_out_b = jnp.sum(grad_branch.astype(F32), axis=0)
     grad_attn = jnp.einsum("te,de->td", grad_branch, out_w, preferred_element_type=F32).astype(BF)
     grad_q, grad_k, grad_v = attn_bwd(
-        bounds, queries, query_doc, grad_attn, log_rows, mixed_t, keys, key_doc, values, tq=tile
+        doc_start, queries, query_doc, grad_attn, log_rows, mixed_t, keys, key_doc, values, tq=tile
     )
     def total(g):
         part = lax.psum_scatter(g.astype(BF), "wsh", scatter_dimension=0, tiled=True)

time: 388 us -> 388 us (level)
  Pallas kernels: 351 us -> 373 us
  other arithmetic: 11.3 us -> 0.61 us
  local copies, waits for them, and re-layouts: 19 us -> 10.4 us
    pallas_call x1, Pallas kernels: 161 us -> 196 us  [finish(): pl.pallas_call(functools.partial(finish_kernel, sources, len(parts)), out...]
    pallas_call x1, Pallas kernels: 51.6 us -> 39 us  [attn_bwd(): pl.pallas_call(functools.partial(bwd_kernel, tk), out_shape=(jax.ShapeDty...]
    unnamed x34 -> x8, local copies, waits for them, and re-layouts: 11.5 us -> 1.77 us
    pallas_call x1, Pallas kernels: 32.6 us -> 24.7 us  [attn_fwd(): pl.pallas_call(functools.partial(fwd_kernel, tk), out_shape=(jax.ShapeDty...]
    concatenate x1, local copies, waits for them, and re-layouts: 0.01 us -> 6.1 us  [local(): jnp.concatenate(small + (up_bias,)).astype(F32).reshape(8 + n_wsh, own)]
    convert_element_type x4 -> x0, other arithmetic: 5.52 us -> none  [the longest x2 3.32 us: finish(): sums.append(block.reshape(down * rows, across * D).astype(F32))]
    another operation x11 -> x0, local copies, waits for them, and re-layouts: 5.4 us -> none  [the longest x9 5.3 us: local(): jnp.stack([query_bias, value_bias, out_bias, attn_gain, attn_shift, down_...]
    pallas_call x0 -> x1, Pallas kernels: none -> 5.3 us  [widen(): pl.pallas_call(functools.partial(widen_kernel, spans), grid=(4,), out_sha...]
  transfers between devices with their start and end apart: 1 -> 1, of which waited for: 0 -> 1; matrix products, arithmetic and copies ran while one was open for 1% -> 0% of each run, Pallas kernels for 8% -> 6%
where the time goes in v7:
time: 388 us; the launch traced here: 389 us
  Pallas kernels  373 us (96%)
  local copies, waits for them, and re-layouts  10.4 us (3%)
    pallas_call x1, Pallas kernels, finish(): pl.pallas_call(functools.partial(finish_kernel, sources, len(parts)), out...  196 us
    pallas_call x1, Pallas kernels, gather_project(): pl.pallas_call(functools.partial(gather_kernel, 5), out_shape=(shape(runs...  69.2 us
    pallas_call x1, Pallas kernels, attn_bwd(): pl.pallas_call(functools.partial(bwd_kernel, tk), out_shape=(jax.ShapeDty...  39 us
    pallas_call x1, Pallas kernels, middle(): pl.pallas_call(middle_kernel, out_shape=(shape((rows, D), BF), shape((row...  38.4 us
    pallas_call x1, Pallas kernels, attn_fwd(): pl.pallas_call(functools.partial(fwd_kernel, tk), out_shape=(jax.ShapeDty...  24.7 us
  transfers between devices with their start and end apart: 1, of which 1 were waited for; matrix products, arithmetic and copies ran while one was open for 0% of the time, Pallas kernels for 6%

profile of v7, /device:TPU:0, one launch (start us, length us, event | category | flops | bytes accessed | tf_op | source)
XLA Modules:
  0.0 388.6 jit_solution(2118008198711359593)
XLA Ops:
  0.7 6.1 %concatenate.3 = bf16[2304]{0:T(1024)(128)(2,1)S(1)} concatenate(bf16[192]{0:T(256)(128)(2,1)} %param.27, bf16[192]{0:T(256)(128)(2,1)} %param.28, bf16[192]{0:T(256)(128)(2,1)} %param.29, bf16[192]{0:T(256)(128)(2,1)} %param.30, bf16[192]{0:T(256)(128)(2,1)} %param.31, bf16[192]{0:T(256)(128)(2,1)} %param.33, bf16[192]{0:T(256)(128)(2,1)} %param.34, bf16[192]{0:T(256)(128)(2,1)} %param.35, ...), dimensions={0} | concatenate | bytes 9216 | tf_op jit(solution)/shard_map/concatenate | solution.py:1165
  6.8 0.7 reshape.98.vec_ref
  7.5 69.2 %gather_project.1 = (bf16[8,512,768]{2,1,0:T(8,128)(2,1)}, bf16[8,512,768]{2,1,0:T(8,128)(2,1)}, bf16[8,512,768]{2,1,0:T(8,128)(2,1)}, bf16[512,768]{1,0:T(8,128...) custom-call(bf16[512,768]{1,0:T(8,128)(2,1)} %bitcast.30, ...), custom_call_target="tpu_custom_call" | custom-call | tf_op jit(solution)/shard_map/gather_project/pallas_call | solution.py:1114
  76.6 0.6 collective-permute-start
  77.2 24.7 %attend.1 = (f32[768,512]{1,0:T(8,128)}, f32[6,2,512]{2,1,0:T(2,128)}) custom-call(s32[8]{0:T(128)} %bitcast.41, bf16[512,768]{1,0:T(8,128)(2,1)} %get-tuple-element.50.q_ref, bf16[512,128]{1,0:T(8,128)(2,1)} %get-tuple-element.51.qaug_ref, bf16[4096,768]{1,0:T(8,128)(2,1)} %bitcast.26, bf16[4096,128]{1,0:T(8,128)(2,1)} %get-tuple-element.53.kaug_ref, ...), custom_call_target="tpu_custom_call" | custom-call | tf_op jit(solution)/shard_map/attend/pallas_call | solution.py:112
  101.9 3.6 collective-permute-done.down_far
  105.5 38.4 %middle.1 = (bf16[512,768]{1,0:T(8,128)(2,1)}, f32[512,768]{1,0:T(8,128)}, bf16[512,768]{1,0:T(8,128)(2,1)}, f32[16,768]{1,0:T(8,128)}, bf16[768,3072]{1,0:T(8,1...) custom-call(f32[768,512]{1,0:T(8,128)} %get-tuple-element.55.attn_ref.ot_ref, bf16[512,768]{1,0:T(8,128)(2,1)} %bitcast.31, ...), custom_call_target="tpu_custom_call" | custom-call | tf_op jit(solution)/shard_map/middle/pallas_call | solution.py:355
  143.9 39.0 %attend_back.1 = (bf16[512,768]{1,0:T(8,128)(2,1)}, bf16[4096,768]{1,0:T(8,128)(2,1)}, bf16[4096,768]{1,0:T(8,128)(2,1)}) custom-call(s32[8]{0:T(128)} %bitcast.42, bf16[512,768]{1,0:T(8,128)(2,1)} %get-tuple-element.50.q_ref, bf16[512,128]{1,0:T(8,128)(2,1)} %get-tuple-element.51.qaug_ref, bf16[512,768]{1,0:T(8,128)(2,1)} %get-tuple-element.65.do_ref, ...), custom_call_target="tpu_custom_call" | custom-call | tf_op jit(solution)/shard_map/attend_back/pallas_call | solution.py:176
  183.0 196.1 %finish.1 = (bf16[12,192,768]{2,1,0:T(8,128)(2,1)}, f32[8,192]{1,0:T(8,128)}, f32[1,768]{1,0:T(1,128)}, bf16[512,768]{1,0:T(8,128)(2,1)}) custom-call(bf16[4,192,3072]{2,1,0:T(8,128)(2,1)} %bitcast.35, bf16[4,192,768]{2,1,0:T(8,128)(2,1)} %bitcast.37, bf16[4,768,768]{2,1,0:T(8,128)(2,1)} %bitcast.36, f32[16,768]{1,0:T(8,128)} %get-tuple-element.64.refs_3_, ...), custom_call_target="tpu_custom_call" | custom-call | tf_op jit(solution)/shard_map/finish/pallas_call | solution.py:849
  379.1 0.0 copy-start.2
  379.1 0.0 copy-start
  379.1 0.0 copy-start.1
  379.1 1.8 fusion
  380.9 5.3 %widen.1 = (f32[1,192,3072]{2,1,0:T(8,128)}, f32[1,192,768]{2,1,0:T(8,128)}, f32[4,192,768]{2,1,0:T(8,128)}, f32[1,192,768]{2,1,0:T(8,128)}, f32[1,192,768]{2,1,0:T(8,128)}, /*index=5*/f32[1,192,768]{2,1,0:T(8,128)}) custom-call(bf16[12,192,768]{2,1,0:T(8,128)(2,1)} %get-tuple-element.74.in_ref), custom_call_target="tpu_custom_call" | custom-call | tf_op jit(solution)/shard_map/widen/pallas_call | solution.py:821
  386.2 0.0 copy-done.2
  386.2 0.6 reduce
  386.9 0.0 copy-done
  386.9 0.9 copy.37
  387.7 0.0 copy-done.1
  387.7 0.9 copy.38
Async XLA Ops:
  76.6 28.9 %collective-permute-start = (bf16[768,768]{1,0:T(8,128)(2,1)}, bf16[768,768]{1,0:T(8,128)(2,1)}, u32[]{:S(2)}, u32[]{:S(2)}) collective-permute-start(bf16[768,768]{1,0:T(8,128)(2,1)} %down_own), channel_id=1, source_target_pairs={{0,2},{1,3},{2,0},{3,1},{4,6},{5,7},{6,4},{7,5},{8,10},{9,11},{10,... | collective-permute-start | bytes 3538952 | tf_op jit(solution)/shard_map/ppermute | solution.py:1170
  379.1 7.1 %copy-start.2 = (f32[1,768]{1,0:T(1,128)S(1)}, f32[1,768]{1,0:T(1,128)}, u32[]{:S(2)}) copy-start(f32[1,768]{1,0:T(1,128)} %get-tuple-element.82) | copy-start | bytes 9220
  379.1 7.7 %copy-start = (bf16[512,768]{1,0:T(8,128)(2,1)S(1)}, bf16[512,768]{1,0:T(8,128)(2,1)}, u32[]{:S(2)}) copy-start(bf16[512,768]{1,0:T(8,128)(2,1)} %get-tuple-element.60) | copy-start | bytes 2359300
  379.1 8.6 %copy-start.1 = (bf16[512,768]{1,0:T(8,128)(2,1)S(1)}, bf16[512,768]{1,0:T(8,128)(2,1)}, u32[]{:S(2)}) copy-start(bf16[512,768]{1,0:T(8,128)(2,1)} %get-tuple-element.73) | copy-start | bytes 2359300

commit v8 on v7

--- a/solution.py
+++ b/solution.py
@@ -68,14 +68,20 @@
     return jnp.concatenate([x[:64, :tq], x[64:, tq:]], axis=0)
 
 def two_level(start, count, tk, body, init):
-    big = tk // 256
-    whole = count // big
-    def large(t, c):
-        return body(pl.multiple_of(t * tk, 256), pl.multiple_of(start + t * tk, 128), tk, c)
-    def small(t, c):
-        return body(pl.multiple_of(t * 256, 256), pl.multiple_of(start + t * 256, 128), 256, c)
-    c = lax.fori_loop(0, whole, large, init)
-    return lax.fori_loop(whole * big, count, small, c)
+    done, carried = 0, init
+    for n in (6, 3, 1):
+        if n * 256 > tk:
+            continue
+
+        def step(t, c, n=n, done=done):
+            at = done + t * n
+            return body(pl.multiple_of(at * 256, 256), pl.multiple_of(start + at * 256, 128), n * 256, c)
+
+        trips = (count - done) // n
+        carried = lax.fori_loop(0, trips, step, carried)
+        done = done + trips * n
+    return carried
+
 
 def fwd_kernel(tk, docs, q_ref, qaug_ref, k_ref, kaug_ref, v_ref, ot_ref, lse_ref, s_scr, acc):
     qi = pl.program_id(1)
@@ -105,7 +111,7 @@
     lse = m + jnp.log(l)
     lse_ref[0] = jnp.concatenate([lse[:, :tq], lse[:, tq:]], axis=0)
 
-def attn_fwd(docs, q, qaug, k, kaug, v, *, tq=512, tk=768):
+def attn_fwd(docs, q, qaug, k, kaug, v, *, tq=256, tk=1536):
     T, D = q.shape
     S = k.shape[0]
     pairs = D // 128
@@ -168,7 +174,7 @@
         dk_ref[...] = dk_acc[...].astype(BF)
         dv_ref[...] = dv_acc[...].astype(BF)
 
-def attn_bwd(docs, q, qaug, do, lse, ot, k, kaug, v, *, tq=512, tk=768):
+def attn_bwd(docs, q, qaug, do, lse, ot, k, kaug, v, *, tq=256, tk=1536):
     T, D = q.shape
     S = k.shape[0]
     pairs = D // 128
@@ -1152,7 +1158,7 @@
     doc_start = doc_starts[0]
     tok_rows = inputs.shape[0]
     stream_rows = tok_rows * lax.axis_size("ctx")
-    tile = min(tok_rows, 512)
+    tile = min(tok_rows, 256)
     n_ctx, n_wsh = lax.axis_size("ctx"), lax.axis_size("wsh")
     own = D // n_wsh
 
@@ -1162,7 +1168,12 @@
     fast = n_wsh == 4 and n_ctx == 8 and own % (n_ctx // 2 * 16) == 0 and tok_rows % 512 == 0
     if fast:
         small = (query_bias, value_bias, out_bias, attn_gain, attn_shift, down_bias, final_gain, final_shift)
-        vectors = jnp.concatenate(small + (up_bias,)).astype(F32).reshape(8 + n_wsh, own)
+        vectors, place = jnp.zeros(((8 + n_wsh) * own,), F32), 0
+        for v in small + (up_bias,):
+            ends = (place, vectors.shape[0] - place - v.shape[0], 0)
+            vectors = vectors + lax.pad(v.astype(F32), jnp.zeros((), F32), (ends,))
+            place += v.shape[0]
+        vectors = vectors.reshape(8 + n_wsh, own)
         all_tokens, keys, values, queries, kvq_w, vec, out_w, up_w, query_doc, key_doc = gather_project(
             inputs, doc_starts, vectors, key_weight, value_weight, query_weight, out_weight, up_weight
         )

time: 388 us -> 360 us (0.928); the launches traced: 389 us -> 355 us
  Pallas kernels: 373 us -> 340 us
  local copies, waits for them, and re-layouts: 10.4 us -> 4.26 us
  waiting for transfers between devices: 3.59 us -> 8.55 us
    pallas_call x1, Pallas kernels: 39 us -> 23.7 us  [attn_bwd(): pl.pallas_call(functools.partial(bwd_kernel, tk), out_shape=(jax.ShapeDty...]
    pallas_call x1, Pallas kernels: 196 us -> 184 us  [finish(): pl.pallas_call(functools.partial(finish_kernel, sources, len(parts)), out...]
    concatenate x1 -> x0, local copies, waits for them, and re-layouts: 6.1 us -> none  [local(): jnp.concatenate(small + (up_bias,)).astype(F32).reshape(8 + n_wsh, own)]
    pallas_call x1, Pallas kernels: 24.7 us -> 19.7 us  [attn_fwd(): pl.pallas_call(functools.partial(fwd_kernel, tk), out_shape=(jax.ShapeDty...]
    ppermute x1, waiting for transfers between devices: 3.59 us -> 8.55 us  [local(): down_far = lax.ppermute(down_own, 'wsh', [(i, i ^ 2) for i in range(n_wsh)])]
where the time goes in v8:
time: 360 us; the launch traced here: 355 us
  Pallas kernels  340 us (94%)
  waiting for transfers between devices  8.55 us (2%)
  local copies, waits for them, and re-layouts  4.26 us (1%)
    pallas_call x1, Pallas kernels, finish(): pl.pallas_call(functools.partial(finish_kernel, sources, len(parts)), out...  184 us
    pallas_call x1, Pallas kernels, gather_project(): pl.pallas_call(functools.partial(gather_kernel, 5), out_shape=(shape(runs...  69.2 us
    pallas_call x1, Pallas kernels, middle(): pl.pallas_call(middle_kernel, out_shape=(shape((rows, D), BF), shape((row...  38.4 us
    pallas_call x1, Pallas kernels, attn_bwd(): pl.pallas_call(functools.partial(bwd_kernel, tk), out_shape=(jax.ShapeDty...  23.7 us
    pallas_call x1, Pallas kernels, attn_fwd(): pl.pallas_call(functools.partial(fwd_kernel, tk), out_shape=(jax.ShapeDty...  19.7 us
    ppermute x1, waiting for transfers between devices, local(): down_far = lax.ppermute(down_own, 'wsh', [(i, i ^ 2) for i in range(n_wsh)])  8.55 us
  transfers between devices with their start and end apart: 1, of which 1 were waited for; matrix products, arithmetic and copies ran while one was open for 0% of the time, Pallas kernels for 6%

profile of v8, /device:TPU:0, one launch (start us, length us, event | category | flops | bytes accessed | tf_op | source)
XLA Modules:
  0.0 355.4 jit_solution(684534263051312854)
XLA Ops:
  0.7 0.9 convert_add_fusion
  1.5 0.7 reshape.82.vec_ref
  2.2 69.2 %gather_project.1 = (bf16[8,512,768]{2,1,0:T(8,128)(2,1)}, bf16[8,512,768]{2,1,0:T(8,128)(2,1)}, bf16[8,512,768]{2,1,0:T(8,128)(2,1)}, bf16[512,768]{1,0:T(8,128...) custom-call(bf16[512,768]{1,0:T(8,128)(2,1)} %bitcast.30, ...), custom_call_target="tpu_custom_call" | custom-call | tf_op jit(solution)/shard_map/gather_project/pallas_call | solution.py:1120
  71.4 0.6 collective-permute-start
  72.0 19.7 %attend.1 = (f32[768,512]{1,0:T(8,128)}, f32[6,2,512]{2,1,0:T(2,128)}) custom-call(s32[8]{0:T(128)} %bitcast.41, bf16[512,768]{1,0:T(8,128)(2,1)} %get-tuple-element.50.q_ref, bf16[512,128]{1,0:T(8,128)(2,1)} %get-tuple-element.51.qaug_ref, bf16[4096,768]{1,0:T(8,128)(2,1)} %bitcast.26, bf16[4096,128]{1,0:T(8,128)(2,1)} %get-tuple-element.53.kaug_ref, ...), custom_call_target="tpu_custom_call" | custom-call | tf_op jit(solution)/shard_map/attend/pallas_call | solution.py:118
  91.7 8.6 %collective-permute-done.down_far = bf16[768,768]{1,0:T(8,128)(2,1)} collective-permute-done((bf16[768,768]{1,0:T(8,128)(2,1)}, bf16[768,768]{1,0:T(8,128)(2,1)}, u32[]{:S(2)}, u32[]{:S(2)}) %collective-permute-start) | collective-permute-done | bytes 1179680 | tf_op jit(solution)/shard_map/ppermute | solution.py:1181
  100.3 38.4 %middle.1 = (bf16[512,768]{1,0:T(8,128)(2,1)}, f32[512,768]{1,0:T(8,128)}, bf16[512,768]{1,0:T(8,128)(2,1)}, f32[16,768]{1,0:T(8,128)}, bf16[768,3072]{1,0:T(8,1...) custom-call(f32[768,512]{1,0:T(8,128)} %get-tuple-element.55.attn_ref.ot_ref, bf16[512,768]{1,0:T(8,128)(2,1)} %bitcast.31, ...), custom_call_target="tpu_custom_call" | custom-call | tf_op jit(solution)/shard_map/middle/pallas_call | solution.py:361
  138.7 23.7 %attend_back.1 = (bf16[512,768]{1,0:T(8,128)(2,1)}, bf16[4096,768]{1,0:T(8,128)(2,1)}, bf16[4096,768]{1,0:T(8,128)(2,1)}) custom-call(s32[8]{0:T(128)} %bitcast.42, bf16[512,768]{1,0:T(8,128)(2,1)} %get-tuple-element.50.q_ref, bf16[512,128]{1,0:T(8,128)(2,1)} %get-tuple-element.51.qaug_ref, bf16[512,768]{1,0:T(8,128)(2,1)} %get-tuple-element.65.do_ref, ...), custom_call_target="tpu_custom_call" | custom-call | tf_op jit(solution)/shard_map/attend_back/pallas_call | solution.py:182
  162.4 183.5 %finish.1 = (bf16[12,192,768]{2,1,0:T(8,128)(2,1)}, f32[8,192]{1,0:T(8,128)}, f32[1,768]{1,0:T(1,128)}, bf16[512,768]{1,0:T(8,128)(2,1)}) custom-call(bf16[4,192,3072]{2,1,0:T(8,128)(2,1)} %bitcast.35, bf16[4,192,768]{2,1,0:T(8,128)(2,1)} %bitcast.37, bf16[4,768,768]{2,1,0:T(8,128)(2,1)} %bitcast.36, f32[16,768]{1,0:T(8,128)} %get-tuple-element.64.refs_3_, ...), custom_call_target="tpu_custom_call" | custom-call | tf_op jit(solution)/shard_map/finish/pallas_call | solution.py:855
  345.9 0.0 copy-start.2
  345.9 0.0 copy-start
  345.9 0.0 copy-start.1
  345.9 1.8 fusion
  347.8 5.3 %widen.1 = (f32[1,192,3072]{2,1,0:T(8,128)}, f32[1,192,768]{2,1,0:T(8,128)}, f32[4,192,768]{2,1,0:T(8,128)}, f32[1,192,768]{2,1,0:T(8,128)}, f32[1,192,768]{2,1,0:T(8,128)}, /*index=5*/f32[1,192,768]{2,1,0:T(8,128)}) custom-call(bf16[12,192,768]{2,1,0:T(8,128)(2,1)} %get-tuple-element.74.in_ref), custom_call_target="tpu_custom_call" | custom-call | tf_op jit(solution)/shard_map/widen/pallas_call | solution.py:827
  353.1 0.0 copy-done.2
  353.1 0.6 reduce
  353.7 0.0 copy-done
  353.7 0.9 copy.37
  354.5 0.0 copy-done.1
  354.6 0.9 copy.38
Async XLA Ops:
  71.4 28.9 %collective-permute-start = (bf16[768,768]{1,0:T(8,128)(2,1)}, bf16[768,768]{1,0:T(8,128)(2,1)}, u32[]{:S(2)}, u32[]{:S(2)}) collective-permute-start(bf16[768,768]{1,0:T(8,128)(2,1)} %down_own), channel_id=1, source_target_pairs={{0,2},{1,3},{2,0},{3,1},{4,6},{5,7},{6,4},{7,5},{8,10},{9,11},{10,... | collective-permute-start | bytes 3538952 | tf_op jit(solution)/shard_map/ppermute | solution.py:1181
  345.9 7.1 %copy-start.2 = (f32[1,768]{1,0:T(1,128)S(1)}, f32[1,768]{1,0:T(1,128)}, u32[]{:S(2)}) copy-start(f32[1,768]{1,0:T(1,128)} %get-tuple-element.82) | copy-start | bytes 9220
  345.9 7.7 %copy-start = (bf16[512,768]{1,0:T(8,128)(2,1)S(1)}, bf16[512,768]{1,0:T(8,128)(2,1)}, u32[]{:S(2)}) copy-start(bf16[512,768]{1,0:T(8,128)(2,1)} %get-tuple-element.60) | copy-start | bytes 2359300
  345.9 8.6 %copy-start.1 = (bf16[512,768]{1,0:T(8,128)(2,1)S(1)}, bf16[512,768]{1,0:T(8,128)(2,1)}, u32[]{:S(2)}) copy-start(bf16[512,768]{1,0:T(8,128)(2,1)} %get-tuple-element.73) | copy-start | bytes 2359300

commit v9 on v8

--- a/solution.py
+++ b/solution.py
@@ -83,124 +83,149 @@
     return carried
 
 
-def fwd_kernel(tk, docs, q_ref, qaug_ref, k_ref, kaug_ref, v_ref, ot_ref, lse_ref, s_scr, acc):
-    qi = pl.program_id(1)
-    tq = q_ref.shape[0]
-    first_row = lax.axis_index("ctx") * (tq * pl.num_programs(1)) + qi * tq
-    start, count = key_range(docs, first_row, tq, k_ref.shape[0])
-    rhs = stack_heads(q_ref[...], qaug_ref[...])
-
-    def scores(loc, off, size, m):
-        lhs = jnp.concatenate([k_ref[pl.ds(off, size), :], kaug_ref[pl.ds(off, size), :]], axis=1)
-        s = lax.dot_general(lhs, rhs, NT, preferred_element_type=F32)
-        s_scr[pl.ds(loc, size), :] = s
-        return jnp.maximum(m, jnp.max(s.reshape(size // 8, 8, 2 * tq), axis=0))
-
-    m8 = two_level(start, count, tk, scores, jnp.full((8, 2 * tq), -3e38, F32))
-    m = jnp.max(m8, axis=0, keepdims=True)
-    acc[...] = jnp.zeros_like(acc)
-
-    def mix(loc, off, size, l8):
-        p = jnp.exp(s_scr[pl.ds(loc, size), :] - m)
-        acc[...] += lax.dot_general(v_ref[pl.ds(off, size), :], p.astype(BF), TN, preferred_element_type=F32)
-        return l8 + jnp.sum(p.reshape(size // 8, 8, 2 * tq), axis=0)
-
-    l8 = two_level(start, count, tk, mix, jnp.zeros((8, 2 * tq), F32))
-    l = jnp.sum(l8, axis=0, keepdims=True)
-    ot_ref[...] = pick_heads(acc[...] / l, tq)
-    lse = m + jnp.log(l)
-    lse_ref[0] = jnp.concatenate([lse[:, :tq], lse[:, tq:]], axis=0)
+def fwd_kernel(tq, tk, docs, q_ref, qaug_ref, k_ref, kaug_ref, v_ref, ot_ref, lse_ref, s_scr, acc):
+    def part(i, carry):
+        rows = pl.ds(pl.multiple_of(i * tq, tq), tq)
+        start, count = key_range(docs, lax.axis_index("ctx") * q_ref.shape[0] + i * tq, tq, k_ref.shape[0])
+        rhs = stack_heads(q_ref[rows, :], qaug_ref[rows, :])
+
+        def scores(loc, off, size, m):
+            lhs = jnp.concatenate([k_ref[pl.ds(off, size), :], kaug_ref[pl.ds(off, size), :]], axis=1)
+            s = lax.dot_general(lhs, rhs, NT, preferred_element_type=F32)
+            s_scr[pl.ds(loc, size), :] = s
+            return jnp.maximum(m, jnp.max(s.reshape(size // 8, 8, 2 * tq), axis=0))
+
+        m8 = two_level(start, count, tk, scores, jnp.full((8, 2 * tq), -3e38, F32))
+        m = jnp.max(m8, axis=0, keepdims=True)
+        acc[...] = jnp.zeros_like(acc)
+
+        def mix(loc, off, size, l8):
+            p = jnp.exp(s_scr[pl.ds(loc, size), :] - m)
+            acc[...] += lax.dot_general(v_ref[pl.ds(off, size), :], p.astype(BF), TN, preferred_element_type=F32)
+            return l8 + jnp.sum(p.reshape(size // 8, 8, 2 * tq), axis=0)
+
+        l8 = two_level(start, count, tk, mix, jnp.zeros((8, 2 * tq), F32))
+        l = jnp.sum(l8, axis=0, keepdims=True)
+        ot_ref[:, rows] = pick_heads(acc[...] / l, tq)
+        lse = m + jnp.log(l)
+        lse_ref[0, :, rows] = jnp.concatenate([lse[:, :tq], lse[:, tq:]], axis=0)
+        return carry
+
+    lax.fori_loop(0, q_ref.shape[0] // tq, part, 0)
+
 
 def attn_fwd(docs, q, qaug, k, kaug, v, *, tq=256, tk=1536):
     T, D = q.shape
     S = k.shape[0]
     pairs = D // 128
     return pl.pallas_call(
-        functools.partial(fwd_kernel, tk),
+        functools.partial(fwd_kernel, tq, tk),
         out_shape=(jax.ShapeDtypeStruct((D, T), F32), jax.ShapeDtypeStruct((pairs, 2, T), F32)),
         grid_spec=pltpu.PrefetchScalarGridSpec(
-            num_scalar_prefetch=1, grid=(pairs, T // tq),
-            in_specs=[pl.BlockSpec((tq, 128), lambda h, i, b: (i, h)),
-                      pl.BlockSpec((tq, 128), lambda h, i, b: (i, 0)),
-                      pl.BlockSpec((S, 128), lambda h, i, b: (0, h)),
-                      pl.BlockSpec((S, 128), lambda h, i, b: (0, 0)),
-                      pl.BlockSpec((S, 128), lambda h, i, b: (0, h))],
-            out_specs=(pl.BlockSpec((128, tq), lambda h, i, b: (h, i)),
-                       pl.BlockSpec((1, 2, tq), lambda h, i, b: (h, 0, i))),
+            num_scalar_prefetch=1, grid=(pairs,),
+            in_specs=[pl.BlockSpec((T, 128), lambda h, b: (0, h)),
+                      pl.BlockSpec((T, 128), lambda h, b: (0, 0)),
+                      pl.BlockSpec((S, 128), lambda h, b: (0, h)),
+                      pl.BlockSpec((S, 128), lambda h, b: (0, 0)),
+                      pl.BlockSpec((S, 128), lambda h, b: (0, h))],
+            out_specs=(pl.BlockSpec((128, T), lambda h, b: (h, 0)),
+                       pl.BlockSpec((1, 2, T), lambda h, b: (h, 0, 0))),
             scratch_shapes=[pltpu.VMEM((S, 2 * tq), F32), pltpu.VMEM((128, 2 * tq), F32)]),
         name="attend",
     )(docs, q, qaug, k, kaug, v)
 
-def bwd_kernel(tk, docs, q_ref, qaug_ref, do_ref, lse_ref, ot_ref, k_ref, kaug_ref, v_ref,
-               dq_ref, dk_ref, dv_ref, dk_acc, dv_acc, dq_acc):
-    qi = pl.program_id(1)
-    tq = q_ref.shape[0]
-    first_row = lax.axis_index("ctx") * (tq * pl.num_programs(1)) + qi * tq
-    start, count = key_range(docs, first_row, tq, k_ref.shape[0])
-
-    @pl.when(qi == 0)
-    def _():
-        dk_acc[...] = jnp.zeros_like(dk_acc)
-        dv_acc[...] = jnp.zeros_like(dv_acc)
-
-    qs = stack_heads(q_ref[...])
-    qrhs = stack_heads(q_ref[...], qaug_ref[...])
-    dos = stack_heads(do_ref[...])
-    lse = jnp.concatenate([lse_ref[0, 0:1, :], lse_ref[0, 1:2, :]], axis=1)
+
+def bwd_kernel(tq, tk, docs, q_ref, qaug_ref, do_ref, lse_ref, ot_ref, k_ref, kaug_ref, v_ref,
+               dq_ref, dk_ref, dv_ref, dk_acc, dv_acc, dq_acc, delta_scr):
+    n_rows, n_keys = q_ref.shape[0], k_ref.shape[0]
+    first_row = lax.axis_index("ctx") * n_rows
+    low, high = n_keys, 0
+    for i in range(n_rows // tq):
+        start, count = key_range(docs, first_row + i * tq, tq, n_keys)
+        low, high = jnp.minimum(low, start), jnp.maximum(high, start + count * 256)
+
+    def over_seen(fn):
+        def one(t, carry):
+            fn(pl.ds(pl.multiple_of(low + t * 128, 128), 128))
+            return carry
+
+        lax.fori_loop(0, (high - low) // 128, one, 0)
+
+    def clear(rows):
+        dk_acc[rows, :] = jnp.zeros((128, 128), F32)
+        dv_acc[rows, :] = jnp.zeros((128, 128), F32)
+
+    over_seen(clear)
     mixed = ot_ref[...] * do_ref[...].astype(F32).T
-    delta = jnp.concatenate(
-        [jnp.sum(mixed[:64], axis=0, keepdims=True), jnp.sum(mixed[64:], axis=0, keepdims=True)], axis=1
-    )
-    dq_acc[...] = jnp.zeros_like(dq_acc)
-
-    def step(loc, off, size, carry):
-        rows = pl.ds(off, size)
-        lhs = jnp.concatenate([k_ref[rows, :], kaug_ref[rows, :]], axis=1)
-        x = lax.dot_general(lhs, qrhs, NT, preferred_element_type=F32)
-        y = lax.dot_general(v_ref[rows, :], dos, NT, preferred_element_type=F32)
-        p = jnp.exp(x - lse)
-        ds = (p * (y - delta)).astype(BF)
-        pb = p.astype(BF)
-        dv_acc[rows, :] += lax.dot_general(pb, dos, NN, preferred_element_type=F32)
-        dk_acc[rows, :] += lax.dot_general(ds, qs, NN, preferred_element_type=F32)
-        dq_acc[...] += lax.dot_general(k_ref[rows, :], ds, TN, preferred_element_type=F32)
+    deltas = [jnp.sum(mixed[:64], axis=0, keepdims=True), jnp.sum(mixed[64:], axis=0, keepdims=True)]
+    delta_scr[...] = jnp.concatenate(deltas, axis=0)
+
+    def part(i, carry):
+        part_rows = pl.ds(pl.multiple_of(i * tq, tq), tq)
+        start, count = key_range(docs, first_row + i * tq, tq, n_keys)
+        q, do = q_ref[part_rows, :], do_ref[part_rows, :]
+        qs = stack_heads(q)
+        qrhs = stack_heads(q, qaug_ref[part_rows, :])
+        dos = stack_heads(do)
+        lse = jnp.concatenate([lse_ref[0, 0:1, part_rows], lse_ref[0, 1:2, part_rows]], axis=1)
+        delta = jnp.concatenate([delta_scr[0:1, part_rows], delta_scr[1:2, part_rows]], axis=1)
+        dq_acc[...] = jnp.zeros_like(dq_acc)
+
+        def step(loc, off, size, carry):
+            rows = pl.ds(off, size)
+            lhs = jnp.concatenate([k_ref[rows, :], kaug_ref[rows, :]], axis=1)
+            x = lax.dot_general(lhs, qrhs, NT, preferred_element_type=F32)
+            y = lax.dot_general(v_ref[rows, :], dos, NT, preferred_element_type=F32)
+            p = jnp.exp(x - lse)
+            ds = (p * (y - delta)).astype(BF)
+            pb = p.astype(BF)
+            dv_acc[rows, :] += lax.dot_general(pb, dos, NN, preferred_element_type=F32)
+            dk_acc[rows, :] += lax.dot_general(ds, qs, NN, preferred_element_type=F32)
+            dq_acc[...] += lax.dot_general(k_ref[rows, :], ds, TN, preferred_element_type=F32)
+            return carry
+
+        two_level(start, count, tk, step, 0)
+        dq_ref[part_rows, :] = (pick_heads(dq_acc[...], tq) * SCALE).T.astype(BF)
         return carry
 
-    two_level(start, count, tk, step, 0)
-    dq_ref[...] = (pick_heads(dq_acc[...], tq) * SCALE).T.astype(BF)
-
-    @pl.when(qi == pl.num_programs(1) - 1)
-    def _():
-        dk_ref[...] = dk_acc[...].astype(BF)
-        dv_ref[...] = dv_acc[...].astype(BF)
+    lax.fori_loop(0, n_rows // tq, part, 0)
+    dk_ref[...] = jnp.zeros_like(dk_ref)
+    dv_ref[...] = jnp.zeros_like(dv_ref)
+
+    def give(rows):
+        dk_ref[rows, :] = dk_acc[rows, :].astype(BF)
+        dv_ref[rows, :] = dv_acc[rows, :].astype(BF)
+
+    over_seen(give)
+
 
 def attn_bwd(docs, q, qaug, do, lse, ot, k, kaug, v, *, tq=256, tk=1536):
     T, D = q.shape
     S = k.shape[0]
     pairs = D // 128
-    row = lambda h, i, b: (h, 0, i)
     return pl.pallas_call(
-        functools.partial(bwd_kernel, tk),
+        functools.partial(bwd_kernel, tq, tk),
         out_shape=(jax.ShapeDtypeStruct((T, D), BF), jax.ShapeDtypeStruct((S, D), BF), jax.ShapeDtypeStruct((S, D), BF)),
         grid_spec=pltpu.PrefetchScalarGridSpec(
-            num_scalar_prefetch=1, grid=(pairs, T // tq),
-            in_specs=[pl.BlockSpec((tq, 128), lambda h, i, b: (i, h)),
-                      pl.BlockSpec((tq, 128), lambda h, i, b: (i, 0)),
-                      pl.BlockSpec((tq, 128), lambda h, i, b: (i, h)),
-                      pl.BlockSpec((1, 2, tq), row),
-                      pl.BlockSpec((128, tq), lambda h, i, b: (h, i)),
-                      pl.BlockSpec((S, 128), lambda h, i, b: (0, h)),
-                      pl.BlockSpec((S, 128), lambda h, i, b: (0, 0)),
-                      pl.BlockSpec((S, 128), lambda h, i, b: (0, h))],
-            out_specs=(pl.BlockSpec((tq, 128), lambda h, i, b: (i, h)),
-                       pl.BlockSpec((S, 128), lambda h, i, b: (0, h)),
-                       pl.BlockSpec((S, 128), lambda h, i, b: (0, h))),
-            scratch_shapes=[pltpu.VMEM((S, 128), F32), pltpu.VMEM((S, 128), F32), pltpu.VMEM((128, 2 * tq), F32)]),
+            num_scalar_prefetch=1, grid=(pairs,),
+            in_specs=[pl.BlockSpec((T, 128), lambda h, b: (0, h)),
+                      pl.BlockSpec((T, 128), lambda h, b: (0, 0)),
+                      pl.BlockSpec((T, 128), lambda h, b: (0, h)),
+                      pl.BlockSpec((1, 2, T), lambda h, b: (h, 0, 0)),
+                      pl.BlockSpec((128, T), lambda h, b: (h, 0)),
+                      pl.BlockSpec((S, 128), lambda h, b: (0, h)),
+                      pl.BlockSpec((S, 128), lambda h, b: (0, 0)),
+                      pl.BlockSpec((S, 128), lambda h, b: (0, h))],
+            out_specs=(pl.BlockSpec((T, 128), lambda h, b: (0, h)),
+                       pl.BlockSpec((S, 128), lambda h, b: (0, h)),
+                       pl.BlockSpec((S, 128), lambda h, b: (0, h))),
+            scratch_shapes=[pltpu.VMEM((S, 128), F32), pltpu.VMEM((S, 128), F32), pltpu.VMEM((128, 2 * tq), F32),
+                            pltpu.VMEM((2, T), F32)]),
         name="attend_back",
     )(docs, q, qaug, do, lse, ot, k, kaug, v)
 
 
-def middle_kernel(attn_ref, in_ref, cot_ref, vec_ref, wo_ref, wu_ref, down_own, down_far,
+def middle_kernel(attn_ref, in_ref, cot_ref, vec_ref, out_own, out_far, wu_ref, down_own, down_far,
                   out_ref, sum1_ref, do_ref, grads_ref, up_out, down_out, attn_out,
                   wo, wu, wd, attn_b, first, hat1, scale1, first_b, act, slope, sum2, down_b, up_b, first_b2, first_t,
                   g_up, g_down, g_out, sem_w, sem_d, sem_o):
@@ -208,31 +233,38 @@
     a, w = lax.axis_index("ctx"), lax.axis_index("wsh")
     y, c = w // 2, lax.rem(w, 2)
     core_peer = (a, y * 2 + (1 - c))
-    tall = down_own.shape[0]
     MESH = pl.DeviceIdType.MESH
+    owners = (w, (1 - y) * 2 + c)
     barrier = pltpu.get_barrier_semaphore()
     pl.semaphore_signal(barrier, inc=1, device_id=core_peer, device_id_type=MESH)
     pl.semaphore_wait(barrier, 1)
-    passed = []
-    for s, (ref, owner) in enumerate(((down_own, w), (down_far, (1 - y) * 2 + c))):
-        there = wd.at[pl.ds(pl.multiple_of(owner * tall, 16), tall), :]
-        passed.append(pltpu.make_async_remote_copy(
-            src_ref=ref, dst_ref=there, send_sem=sem_d.at[0, s], recv_sem=sem_d.at[1, s],
-            device_id=core_peer, device_id_type=MESH))
-        passed[-1].start()
-        pltpu.make_async_copy(ref, there, sem_w.at[2 + s]).start()
-    loading = [pltpu.make_async_copy(wo_ref, wo, sem_w.at[0]), pltpu.make_async_copy(wu_ref, wu, sem_w.at[1])]
-    for copy in loading:
-        copy.start()
+
+    def share(j, s, full, ref):
+        tall = ref.shape[0]
+        there = full.at[pl.ds(pl.multiple_of(owners[s] * tall, 16), tall), :]
+        return (
+            pltpu.make_async_copy(ref, there, sem_w.at[j, s]),
+            pltpu.make_async_remote_copy(
+                src_ref=ref, dst_ref=there, send_sem=sem_d.at[0, j, s], recv_sem=sem_d.at[1, j, s],
+                device_id=core_peer, device_id_type=MESH),
+        )
+
+    shares = [[share(j, s, full, ref) for s, ref in enumerate(pair)]
+              for j, (full, pair) in enumerate(((wo, (out_own, out_far)), (wd, (down_own, down_far))))]
+    up_load = pltpu.make_async_copy(wu_ref, wu, sem_w.at[2, 0])
+    for pair in shares:
+        for kept, passed in pair:
+            passed.start()
+            kept.start()
+    up_load.start()
 
     def arrived(j):
-        if j < 2:
-            loading[j].wait()
+        if j == 1:
+            up_load.wait()
         else:
-            for s, owner in enumerate((w, (1 - y) * 2 + c)):
-                there = wd.at[pl.ds(pl.multiple_of(owner * tall, 16), tall), :]
-                pltpu.make_async_copy(there, there, sem_w.at[2 + s]).wait()
-                passed[s].wait_recv()
+            for kept, passed in shares[j // 2]:
+                kept.wait()
+                passed.wait_recv()
 
     grads_ref[...] = jnp.zeros_like(grads_ref)
     attn_b[...] = attn_ref[...].astype(BF)
@@ -348,11 +380,12 @@
 
     over_wide(wide_end)
     pltpu.make_async_copy(g_out, attn_out, sem_o.at[2, 0]).wait()
-    for copy in passed:
-        copy.wait_send()
-
-
-def middle(attn_t, inputs, cotangent, vec, out_w, up_w, down_own, down_far):
+    for pair in shares:
+        for _kept, passed in pair:
+            passed.wait_send()
+
+
+def middle(attn_t, inputs, cotangent, vec, out_own, out_far, up_w, down_own, down_far):
     rows = inputs.shape[0]
     wide = up_w.shape[1]
     vm, dma, shape = pltpu.VMEM, pltpu.SemaphoreType.DMA, jax.ShapeDtypeStruct
@@ -362,17 +395,17 @@
         middle_kernel,
         out_shape=(shape((rows, D), BF), shape((rows, D), F32), shape((rows, D), BF), shape((16, D), F32),
                    shape((D, wide), BF), shape((wide, D), BF), shape((D, D), BF)),
-        in_specs=[vm_spec] * 4 + [any_spec] * 4,
+        in_specs=[vm_spec] * 4 + [any_spec] * 5,
         out_specs=(vm_spec,) * 4 + (any_spec,) * 3,
         scratch_shapes=[
             vm((D, D), BF), vm((D, wide), BF), vm((wide, D), BF), vm((D, rows), BF), vm((rows, D), F32),
             vm((rows, D), F32), vm((rows, 1), F32), vm((rows, D), BF), vm((rows, wide), BF), vm((rows, wide), F32),
             vm((rows, D), F32), vm((rows, D), BF), vm((rows, wide), BF), vm((rows, D), BF), vm((D, rows), BF),
-            vm((D, wide), BF), vm((wide, D), BF), vm((D, D), BF), dma((4,)), dma((2, 2)), dma((3, wide // D)),
+            vm((D, wide), BF), vm((wide, D), BF), vm((D, D), BF), dma((3, 2)), dma((2, 2, 2)), dma((3, wide // D)),
         ],
         compiler_params=pltpu.CompilerParams(collective_id=3, has_side_effects=True, vmem_limit_bytes=63 * 2**20),
         name="middle",
-    )(attn_t, inputs, cotangent, vec, out_w, up_w, down_own, down_far)
+    )(attn_t, inputs, cotangent, vec, out_own, out_far, up_w, down_own, down_far)
 
 
 def reach(n_ctx):
@@ -875,9 +908,9 @@
     return widen(summed, spans), small, wide, grad_own
 
 
-def gather_kernel(cut, tok_ref, docs_ref, wk_ref, wv_ref, wq_ref, wo_ref, wu_ref, vec_ref,
-                  tok_out, k_out, v_out, q_out, w_out, vec_out, wo_out, wu_out, query_doc, key_doc,
-                  tok, kbuf, vbuf, qbuf, wbuf, vecs, wo, wu, kdoc,
+def gather_kernel(cut, tok_ref, docs_ref, wk_ref, wv_ref, wq_ref, wu_ref, vec_ref,
+                  tok_out, k_out, v_out, q_out, w_out, vec_out, wu_out, query_doc, key_doc,
+                  tok, kbuf, vbuf, qbuf, wbuf, vecs, wu, kdoc,
                   sem_in, sem_out, sem_w, sem_l, sem_o):
     n_ctx = lax.axis_size("ctx")
     zs = n_ctx // 2
@@ -949,11 +982,11 @@
     def shard(m, owner):
         if m == 3:
             return vecs.at[owner]
-        return (wbuf.at[0], wbuf.at[1], wbuf.at[2], None, wo, wu)[m].at[weight_rows(owner), :]
+        return (wbuf.at[0], wbuf.at[1], wbuf.at[2], None, wu)[m].at[weight_rows(owner), :]
 
     vecs[w, 0 : vec_ref.shape[0], :] = vec_ref[...]
-    shards = (wk_ref, wv_ref, wq_ref, vecs.at[w], wo_ref, wu_ref)
-    for m in (3, 0, 1, 2, 4, 5):
+    shards = (wk_ref, wv_ref, wq_ref, vecs.at[w], wu_ref)
+    for m in (3, 0, 1, 2, 4):
         remote(shards[m], shard(m, w), sem_w.at[0, 1, m], sem_w.at[1, 1, m], y_peer).start()
         remote(shards[m], shard(m, w), sem_w.at[0, 0, m], sem_w.at[1, 0, m], core_peer).start()
         if m != 3:
@@ -1077,12 +1110,10 @@
 
     pltpu.make_async_copy(wbuf, w_out, sem_l.at[6]).start()
 
-    for m in (4, 5):
-        weight_forward(m)
-    for m, full, target in ((4, wo, wo_out), (5, wu, wu_out)):
-        weight_end(m)
-        pltpu.make_async_copy(full, target, sem_l.at[m - 4]).start()
-    for m in range(6):
+    weight_forward(4)
+    weight_end(4)
+    pltpu.make_async_copy(wu, wu_out, sem_l.at[1]).start()
+    for m in range(5):
         for kind in range(3):
             weight_arrival(m, kind).wait_send()
 
@@ -1102,12 +1133,11 @@
             pltpu.make_async_copy(src.at[j], dst.at[j], sem_o.at[i, j]).wait()
     pltpu.make_async_copy(qbuf, q_out, sem_l.at[5]).wait()
     pltpu.make_async_copy(wbuf, w_out, sem_l.at[6]).wait()
-    pltpu.make_async_copy(wo, wo_out, sem_l.at[0]).wait()
     pltpu.make_async_copy(wu, wu_out, sem_l.at[1]).wait()
     pltpu.make_async_copy(kdoc, key_doc, sem_l.at[3]).wait()
 
 
-def gather_project(inputs, doc_starts, vectors, key_weight, value_weight, query_weight, out_weight, up_weight):
+def gather_project(inputs, doc_starts, vectors, key_weight, value_weight, query_weight, up_weight):
     n_ctx, n_wsh = lax.axis_size("ctx"), lax.axis_size("wsh")
     tall = inputs.shape[0]
     n_slices = 8
@@ -1120,18 +1150,18 @@
     return pl.pallas_call(
         functools.partial(gather_kernel, 5),
         out_shape=(shape(runs, BF), shape(runs, BF), shape(runs, BF), shape((tall, D), BF), shape((3, D, D), BF),
-                   shape((16, D), F32), shape((D, D), BF), shape((D, up_weight.shape[1]), BF), shape((tall, 128), BF),
+                   shape((16, D), F32), shape((D, up_weight.shape[1]), BF), shape((tall, 128), BF),
                    shape((n_ctx * tall, 128), BF)),
-        in_specs=[any_spec, pl.BlockSpec(memory_space=pltpu.SMEM)] + [any_spec] * 5 + [vm_spec],
-        out_specs=(any_spec,) * 5 + (vm_spec,) + (any_spec,) * 2 + (vm_spec, any_spec),
+        in_specs=[any_spec, pl.BlockSpec(memory_space=pltpu.SMEM)] + [any_spec] * 4 + [vm_spec],
+        out_specs=(any_spec,) * 5 + (vm_spec,) + (any_spec,) + (vm_spec, any_spec),
         scratch_shapes=[
             vm(runs, BF), vm(runs, BF), vm(runs, BF), vm((tall, D), BF), vm((3, D, D), BF), vm((n_wsh, 16, D // n_wsh), F32),
-            vm((D, D), BF), vm((D, up_weight.shape[1]), BF), vm((n_ctx * tall, 128), BF),
-            dma((n_ctx, n_slices)), dma((3, far, n_slices)), dma((2, 4, 6)), dma((7,)), dma((3, n_ctx)),
+            vm((D, up_weight.shape[1]), BF), vm((n_ctx * tall, 128), BF),
+            dma((n_ctx, n_slices)), dma((3, far, n_slices)), dma((2, 4, 5)), dma((7,)), dma((3, n_ctx)),
         ],
         compiler_params=pltpu.CompilerParams(collective_id=1, has_side_effects=True, vmem_limit_bytes=63 * 2**20),
         name="gather_project",
-    )(inputs, doc_starts, key_weight, value_weight, query_weight, out_weight, up_weight, vectors)
+    )(inputs, doc_starts, key_weight, value_weight, query_weight, up_weight, vectors)
 
 
 def local(
@@ -1174,11 +1204,13 @@
             vectors = vectors + lax.pad(v.astype(F32), jnp.zeros((), F32), (ends,))
             place += v.shape[0]
         vectors = vectors.reshape(8 + n_wsh, own)
-        all_tokens, keys, values, queries, kvq_w, vec, out_w, up_w, query_doc, key_doc = gather_project(
-            inputs, doc_starts, vectors, key_weight, value_weight, query_weight, out_weight, up_weight
+        all_tokens, keys, values, queries, kvq_w, vec, up_w, query_doc, key_doc = gather_project(
+            inputs, doc_starts, vectors, key_weight, value_weight, query_weight, up_weight
         )
-        down_own, _unused = lax.optimization_barrier((down_weight, vec))
-        down_far = lax.ppermute(down_own, "wsh", [(i, i ^ 2) for i in range(n_wsh)])
+        out_own, down_own, _unused = lax.optimization_barrier((out_weight, down_weight, vec))
+        across = [(i, i ^ 2) for i in range(n_wsh)]
+        out_far = lax.ppermute(out_own, "wsh", across)
+        down_far = lax.ppermute(down_own, "wsh", across)
         all_tokens, keys, values = [r.reshape(stream_rows, D) for r in (all_tokens, keys, values)]
     else:
         first_row = lax.axis_index("ctx") * tok_rows
@@ -1198,7 +1230,7 @@
     mixed_t, log_rows = attn_fwd(doc_start, queries, query_doc, keys, key_doc, values, tq=tile)
     if fast:
         layer_out, grad_sum1, grad_attn, vec_grads, grad_up_w, grad_down_w, grad_out_w = middle(
-            mixed_t, inputs, cotangent[0], vec, out_w, up_w, down_own, down_far
+            mixed_t, inputs, cotangent[0], vec, out_own, out_far, up_w, down_own, down_far
         )
         grad_q, grad_k, grad_v = attn_bwd(
             doc_start, queries, query_doc, grad_attn, log_rows, mixed_t, keys, key_doc, values, tq=tile

time: 360 us -> 366 us (1.017); the launches traced: 355 us -> 366 us
  waiting for transfers between devices: 8.55 us -> 16.4 us
    pallas_call x1, Pallas kernels: 184 us -> 194 us  [finish(): pl.pallas_call(functools.partial(finish_kernel, sources, len(parts)), out...]
    ppermute x1 -> x2, waiting for transfers between devices: 8.55 us -> 16.4 us  [the longest x1 16.4 us: local(): out_far = lax.ppermute(out_own, 'wsh', across)]
    pallas_call x1, Pallas kernels: 69.2 us -> 62.7 us  [gather_project(): pl.pallas_call(functools.partial(gather_kernel, 5), out_shape=(shape(runs...]
    pallas_call x2, Pallas kernels: 43.4 us -> 39.6 us  [the longest x1 23.1 us: attn_bwd(): pl.pallas_call(functools.partial(bwd_kernel, tq, tk), out_shape=(jax.Shap...]
  transfers between devices with their start and end apart: 1 -> 2, of which waited for: 1 -> 1; matrix products, arithmetic and copies ran while one was open for 0% -> 0% of each run, Pallas kernels for 6% -> 5%
where the time goes in v9:
time: 366 us
  Pallas kernels  341 us (93%)
  waiting for transfers between devices  16.4 us (4%)
  local copies, waits for them, and re-layouts  4.75 us (1%)
    pallas_call x1, Pallas kernels, finish(): pl.pallas_call(functools.partial(finish_kernel, sources, len(parts)), out...  194 us
    pallas_call x1, Pallas kernels, gather_project(): pl.pallas_call(functools.partial(gather_kernel, 5), out_shape=(shape(runs...  62.7 us
    pallas_call x1, Pallas kernels, middle(): pl.pallas_call(middle_kernel, out_shape=(shape((rows, D), BF), shape((row...  38.6 us
    pallas_call x1, Pallas kernels, attn_bwd(): pl.pallas_call(functools.partial(bwd_kernel, tq, tk), out_shape=(jax.Shap...  23.1 us
    pallas_call x1, Pallas kernels, attn_fwd(): pl.pallas_call(functools.partial(fwd_kernel, tq, tk), out_shape=(jax.Shap...  16.6 us
    ppermute x1, waiting for transfers between devices, local(): out_far = lax.ppermute(out_own, 'wsh', across)  16.4 us
  transfers between devices with their start and end apart: 2, of which 1 were waited for; matrix products, arithmetic and copies ran while one was open for 0% of the time, Pallas kernels for 5%

profile of v9, /device:TPU:0, one launch (start us, length us, event | category | flops | bytes accessed | tf_op | source)
XLA Modules:
  0.0 366.0 jit_solution(3023605325527338875)
XLA Ops:
  0.7 0.9 convert_add_fusion
  1.5 0.7 reshape.82.vec_ref
  2.2 62.7 %gather_project.1 = (bf16[8,512,768]{2,1,0:T(8,128)(2,1)}, bf16[8,512,768]{2,1,0:T(8,128)(2,1)}, bf16[8,512,768]{2,1,0:T(8,128)(2,1)}, bf16[512,768]{1,0:T(8,128...) custom-call(bf16[512,768]{1,0:T(8,128)(2,1)} %bitcast.30, ...), custom_call_target="tpu_custom_call" | custom-call | tf_op jit(solution)/shard_map/gather_project/pallas_call | solution.py:1150
  64.9 0.6 collective-permute-start.1
  65.5 1.5 collective-permute-start
  67.0 16.6 %attend.1 = (f32[768,512]{1,0:T(8,128)}, f32[6,2,512]{2,1,0:T(2,128)}) custom-call(s32[8]{0:T(128)} %bitcast.41, bf16[512,768]{1,0:T(8,128)(2,1)} %get-tuple-element.50.q_ref, bf16[512,128]{1,0:T(8,128)(2,1)} %get-tuple-element.51.qaug_ref, bf16[4096,768]{1,0:T(8,128)(2,1)} %bitcast.26, bf16[4096,128]{1,0:T(8,128)(2,1)} %get-tuple-element.53.kaug_ref, ...), custom_call_target="tpu_custom_call" | custom-call | tf_op jit(solution)/shard_map/attend/pallas_call | solution.py:121
  83.6 16.4 %collective-permute-done.out_far = bf16[192,768]{1,0:T(8,128)(2,1)S(1)} collective-permute-done((bf16[192,768]{1,0:T(8,128)(2,1)}, bf16[192,768]{1,0:T(8,128)(2,1)S(1)}, u32[]{:S(2)}, u32[]{:S(2)}) %collective-permute-start) | collective-permute-done | bytes 294944 | tf_op jit(solution)/shard_map/ppermute | solution.py:1212
  100.0 0.0 copy-start.2
  100.0 0.0 collective-permute-done.1.down_far
  100.0 0.7 copy-done.2
  100.7 38.6 %middle.1 = (bf16[512,768]{1,0:T(8,128)(2,1)}, f32[512,768]{1,0:T(8,128)}, bf16[512,768]{1,0:T(8,128)(2,1)}, f32[16,768]{1,0:T(8,128)}, bf16[768,3072]{1,0:T(8,1...) custom-call(f32[768,512]{1,0:T(8,128)} %get-tuple-element.55.attn_ref.ot_ref, bf16[512,768]{1,0:T(8,128)(2,1)} %bitcast.31, ...), custom_call_target="tpu_custom_call" | custom-call | tf_op jit(solution)/shard_map/middle/pallas_call | solution.py:394
  139.3 23.1 %attend_back.1 = (bf16[512,768]{1,0:T(8,128)(2,1)}, bf16[4096,768]{1,0:T(8,128)(2,1)}, bf16[4096,768]{1,0:T(8,128)(2,1)}) custom-call(s32[8]{0:T(128)} %bitcast.42, bf16[512,768]{1,0:T(8,128)(2,1)} %get-tuple-element.50.q_ref, bf16[512,128]{1,0:T(8,128)(2,1)} %get-tuple-element.51.qaug_ref, bf16[512,768]{1,0:T(8,128)(2,1)} %get-tuple-element.65.do_ref, ...), custom_call_target="tpu_custom_call" | custom-call | tf_op jit(solution)/shard_map/attend_back/pallas_call | solution.py:206
  162.4 194.3 %finish.1 = (bf16[12,192,768]{2,1,0:T(8,128)(2,1)}, f32[8,192]{1,0:T(8,128)}, f32[1,768]{1,0:T(1,128)}, bf16[512,768]{1,0:T(8,128)(2,1)}) custom-call(bf16[4,192,3072]{2,1,0:T(8,128)(2,1)} %bitcast.35, bf16[4,192,768]{2,1,0:T(8,128)(2,1)} %bitcast.37, bf16[4,768,768]{2,1,0:T(8,128)(2,1)} %bitcast.36, f32[16,768]{1,0:T(8,128)} %get-tuple-element.64.refs_3_, ...), custom_call_target="tpu_custom_call" | custom-call | tf_op jit(solution)/shard_map/finish/pallas_call | solution.py:888
  356.7 0.0 copy-start.3
  356.7 0.0 copy-start
  356.8 0.0 copy-start.1
  356.8 1.6 fusion
  358.4 5.3 %widen.1 = (f32[1,192,3072]{2,1,0:T(8,128)}, f32[1,192,768]{2,1,0:T(8,128)}, f32[4,192,768]{2,1,0:T(8,128)}, f32[1,192,768]{2,1,0:T(8,128)}, f32[1,192,768]{2,1,0:T(8,128)}, /*index=5*/f32[1,192,768]{2,1,0:T(8,128)}) custom-call(bf16[12,192,768]{2,1,0:T(8,128)(2,1)} %get-tuple-element.74.in_ref), custom_call_target="tpu_custom_call" | custom-call | tf_op jit(solution)/shard_map/widen/pallas_call | solution.py:860
  363.7 0.0 copy-done.3
  363.7 0.6 reduce
  364.3 0.0 copy-done
  364.3 0.9 copy.37
  365.1 0.0 copy-done.1
  365.1 0.9 copy.38
Async XLA Ops:
  64.9 35.1 %collective-permute-start.1 = (bf16[768,768]{1,0:T(8,128)(2,1)}, bf16[768,768]{1,0:T(8,128)(2,1)}, u32[]{:S(2)}, u32[]{:S(2)}) collective-permute-start(bf16[768,768]{1,0:T(8,128)(2,1)} %down_own), channel_id=1, source_target_pairs={{0,2},{1,3},{2,0},{3,1},{4,6},{5,7},{6,4},{7,5},{8,10},{9,11},{10,... | collective-permute-start | bytes 3538952 | tf_op jit(solution)/shard_map/ppermute | solution.py:1213
  65.5 34.5 %collective-permute-start = (bf16[192,768]{1,0:T(8,128)(2,1)}, bf16[192,768]{1,0:T(8,128)(2,1)S(1)}, u32[]{:S(2)}, u32[]{:S(2)}) collective-permute-start(bf16[192,768]{1,0:T(8,128)(2,1)} %out_own), channel_id=1, source_target_pairs={{0,2},{1,3},{2,0},{3,1},{4,6},{5,7},{6,4},{7,5},{8,10},{9,11},{10,... | collective-permute-start | bytes 884744 | tf_op jit(solution)/shard_map/ppermute | solution.py:1212
  100.0 0.7 copy-start.2
  356.7 6.9 %copy-start.3 = (f32[1,768]{1,0:T(1,128)S(1)}, f32[1,768]{1,0:T(1,128)}, u32[]{:S(2)}) copy-start(f32[1,768]{1,0:T(1,128)} %get-tuple-element.82) | copy-start | bytes 9220
  356.7 7.5 %copy-start = (bf16[512,768]{1,0:T(8,128)(2,1)S(1)}, bf16[512,768]{1,0:T(8,128)(2,1)}, u32[]{:S(2)}) copy-start(bf16[512,768]{1,0:T(8,128)(2,1)} %get-tuple-element.60) | copy-start | bytes 2359300
  356.8 8.4 %copy-start.1 = (bf16[512,768]{1,0:T(8,128)(2,1)S(1)}, bf16[512,768]{1,0:T(8,128)(2,1)}, u32[]{:S(2)}) copy-start(bf16[512,768]{1,0:T(8,128)(2,1)} %get-tuple-element.73) | copy-start | bytes 2359300

commit v10 on v9

--- a/solution.py
+++ b/solution.py
@@ -270,7 +270,7 @@
     attn_b[...] = attn_ref[...].astype(BF)
     out_b, attn_g, attn_s, down_bias, final_g, final_s = [vec_ref[i : i + 1, :] for i in range(2, 8)]
     arrived(0)
-    block = 128
+    block = 256
 
     def over_rows(fn):
         def one(i, carry):
@@ -451,8 +451,6 @@
     barrier = pltpu.get_barrier_semaphore()
     for dev in [core_peer, y_peer, x_peer] + [z_peer(d) for d in range(1, zs)]:
         pl.semaphore_signal(barrier, inc=1, device_id=dev, device_id_type=MESH)
-    pl.semaphore_wait(barrier, zs + 2)
-
     def send(src, dst, sems, idx, dev):
         return pltpu.make_async_remote_copy(
             src_ref=src, dst_ref=dst, send_sem=sems.at[(0,) + idx], recv_sem=sems.at[(1,) + idx],
@@ -509,12 +507,13 @@
              pltpu.make_async_copy(own_in_ref, own, sem_in.at[2])]
     for copy in fetch:
         copy.start()
+    for k in range(4):
+        share_load(k)
+    acc[...] = jnp.zeros_like(acc)
+    bias[...] = jnp.zeros_like(bias)
+    pl.semaphore_wait(barrier, zs + 2)
     for k in range(n_ready):
         share_send(k)
-        if k < 4:
-            share_load(k)
-    acc[...] = jnp.zeros_like(acc)
-    bias[...] = jnp.zeros_like(bias)
     fetch[0].wait()
 
     near_rows, far_rows = pl.ds(0, cut), pl.ds(cut, tall - cut)
@@ -530,14 +529,14 @@
                 copy.wait()
 
             def tokens_part(r, carry):
-                rs = pl.ds(pl.multiple_of(r * 128, 128), 128)
+                rs = pl.ds(pl.multiple_of(r * 256, 256), 256)
                 g = lax.dot_general(loads[at, 0, rs, :], weights[0], NT, preferred_element_type=F32)
                 g = g + lax.dot_general(loads[at, 1, rs, :], weights[1], NT, preferred_element_type=F32)
                 run_part[i, rs, :] = g.astype(BF)
-                bias[0:8, :] += jnp.sum(loads[at, 1, rs, :].astype(F32).reshape(16, 8, 2 * half), axis=0)
+                bias[0:8, :] += jnp.sum(loads[at, 1, rs, :].astype(F32).reshape(32, 8, 2 * half), axis=0)
                 return carry
 
-            lax.fori_loop(0, tall // 128, tokens_part, 0)
+            lax.fori_loop(0, tall // 256, tokens_part, 0)
 
             @pl.when(mine_too == 0)
             def _():
@@ -696,7 +695,7 @@
 
     def chunk_step(m):
         for lag, stage in enumerate((stage_c, stage_d, stage_d2, stage_e, stage_e2, stage_f)):
-            guarded(stage, m - (lag and lag + 5), 0, n_chunks)
+            guarded(stage, m - (lag and lag + 1), 0, n_chunks)
 
     def first_step(t, carry):
         guarded(unit, t, 0, n_pos)
@@ -746,12 +745,12 @@
     to_bf(0, 2)
 
     def query_tokens(r, carry):
-        rs = pl.ds(pl.multiple_of(r * 128, 128), 128)
+        rs = pl.ds(pl.multiple_of(r * 256, 256), 256)
         own[rs, :] += lax.dot_general(dq[rs, :], weights[2], NT, preferred_element_type=F32)
-        bias[8:16, :] += jnp.sum(dq[rs, :].astype(F32).reshape(16, 8, 2 * half), axis=0)
+        bias[8:16, :] += jnp.sum(dq[rs, :].astype(F32).reshape(32, 8, 2 * half), axis=0)
         return carry
 
-    lax.fori_loop(0, tall // 128, query_tokens, 0)
+    lax.fori_loop(0, tall // 256, query_tokens, 0)
 
     sums[0] = vec_ref[...]
     sums[0, 0:1, :] = jnp.sum(bias[8:16, :], axis=0, keepdims=True)
@@ -797,7 +796,7 @@
         guarded(lambda k: vec_last(), m - done - 5, 0, 1)
         return carry
 
-    lax.fori_loop(done, n_chunks + 10, second_step, 0)
+    lax.fori_loop(done, n_chunks + 6, second_step, 0)
     wait_in(last_x, sem_x, (n_pos // 2,))
     own[far_rows, :] += last_x[...].astype(F32)
     grad_ref[...] = own[...].astype(BF)
@@ -881,7 +880,7 @@
     n = len(sources) + 3
     spans += [(len(sources) + j, 1, 1) for j in range(3)]
     half, piece, tall = D // 2, rows // zs, inputs.shape[0]
-    n_pos, cut = 4 * hops + 2, tall // 2
+    n_pos, cut = 4 * hops + 2, tall * 5 // 8
     vm, dma, shape = pltpu.VMEM, pltpu.SemaphoreType.DMA, jax.ShapeDtypeStruct
     any_spec = pl.BlockSpec(memory_space=pltpu.HBM)
     vm_spec = pl.BlockSpec(memory_space=pltpu.VMEM)
@@ -1055,7 +1054,7 @@
     weight_end(0)
     weight_end(1)
 
-    step_rows = 128
+    step_rows = 256
     steps = tok.shape[1] // step_rows
 
     def query_part(i, carry):

time: 366 us -> 346 us (0.945)
  Pallas kernels: 341 us -> 319 us
    pallas_call x1, Pallas kernels: 194 us -> 180 us  [finish(): pl.pallas_call(functools.partial(finish_kernel, sources, len(parts)), out...]
    pallas_call x1, Pallas kernels: 38.6 us -> 32.1 us  [middle(): pl.pallas_call(middle_kernel, out_shape=(shape((rows, D), BF), shape((row...]
where the time goes in v10:
time: 346 us; the launch traced here: 345 us
  Pallas kernels  319 us (92%)
  waiting for transfers between devices  16.4 us (5%)
  local copies, waits for them, and re-layouts  4.75 us (1%)
    pallas_call x1, Pallas kernels, finish(): pl.pallas_call(functools.partial(finish_kernel, sources, len(parts)), out...  180 us
    pallas_call x1, Pallas kernels, gather_project(): pl.pallas_call(functools.partial(gather_kernel, 5), out_shape=(shape(runs...  62.7 us
    pallas_call x1, Pallas kernels, middle(): pl.pallas_call(middle_kernel, out_shape=(shape((rows, D), BF), shape((row...  32.1 us
    pallas_call x1, Pallas kernels, attn_bwd(): pl.pallas_call(functools.partial(bwd_kernel, tq, tk), out_shape=(jax.Shap...  23.1 us
    pallas_call x1, Pallas kernels, attn_fwd(): pl.pallas_call(functools.partial(fwd_kernel, tq, tk), out_shape=(jax.Shap...  16.6 us
    ppermute x1, waiting for transfers between devices, local(): out_far = lax.ppermute(out_own, 'wsh', across)  16.4 us
  transfers between devices with their start and end apart: 2, of which 1 were waited for; matrix products, arithmetic and copies ran while one was open for 0% of the time, Pallas kernels for 5%

profile of v10, /device:TPU:0, one launch (start us, length us, event | category | flops | bytes accessed | tf_op | source)
XLA Modules:
  0.0 344.9 jit_solution(6268910622708131139)
XLA Ops:
  0.7 0.9 convert_add_fusion
  1.5 0.7 reshape.82.vec_ref
  2.2 62.7 %gather_project.1 = (bf16[8,512,768]{2,1,0:T(8,128)(2,1)}, bf16[8,512,768]{2,1,0:T(8,128)(2,1)}, bf16[8,512,768]{2,1,0:T(8,128)(2,1)}, bf16[512,768]{1,0:T(8,128...) custom-call(bf16[512,768]{1,0:T(8,128)(2,1)} %bitcast.30, ...), custom_call_target="tpu_custom_call" | custom-call | tf_op jit(solution)/shard_map/gather_project/pallas_call | solution.py:1149
  64.9 0.6 collective-permute-start.1
  65.5 1.5 collective-permute-start
  67.0 16.6 %attend.1 = (f32[768,512]{1,0:T(8,128)}, f32[6,2,512]{2,1,0:T(2,128)}) custom-call(s32[8]{0:T(128)} %bitcast.41, bf16[512,768]{1,0:T(8,128)(2,1)} %get-tuple-element.50.q_ref, bf16[512,128]{1,0:T(8,128)(2,1)} %get-tuple-element.51.qaug_ref, bf16[4096,768]{1,0:T(8,128)(2,1)} %bitcast.26, bf16[4096,128]{1,0:T(8,128)(2,1)} %get-tuple-element.53.kaug_ref, ...), custom_call_target="tpu_custom_call" | custom-call | tf_op jit(solution)/shard_map/attend/pallas_call | solution.py:121
  83.6 16.4 %collective-permute-done.out_far = bf16[192,768]{1,0:T(8,128)(2,1)S(1)} collective-permute-done((bf16[192,768]{1,0:T(8,128)(2,1)}, bf16[192,768]{1,0:T(8,128)(2,1)S(1)}, u32[]{:S(2)}, u32[]{:S(2)}) %collective-permute-start) | collective-permute-done | bytes 294944 | tf_op jit(solution)/shard_map/ppermute | solution.py:1211
  100.0 0.0 copy-start.2
  100.0 0.0 collective-permute-done.1.down_far
  100.0 0.7 copy-done.2
  100.7 32.1 %middle.1 = (bf16[512,768]{1,0:T(8,128)(2,1)}, f32[512,768]{1,0:T(8,128)}, bf16[512,768]{1,0:T(8,128)(2,1)}, f32[16,768]{1,0:T(8,128)}, bf16[768,3072]{1,0:T(8,1...) custom-call(f32[768,512]{1,0:T(8,128)} %get-tuple-element.55.attn_ref.ot_ref, bf16[512,768]{1,0:T(8,128)(2,1)} %bitcast.31, ...), custom_call_target="tpu_custom_call" | custom-call | tf_op jit(solution)/shard_map/middle/pallas_call | solution.py:394
  132.8 23.1 %attend_back.1 = (bf16[512,768]{1,0:T(8,128)(2,1)}, bf16[4096,768]{1,0:T(8,128)(2,1)}, bf16[4096,768]{1,0:T(8,128)(2,1)}) custom-call(s32[8]{0:T(128)} %bitcast.42, bf16[512,768]{1,0:T(8,128)(2,1)} %get-tuple-element.50.q_ref, bf16[512,128]{1,0:T(8,128)(2,1)} %get-tuple-element.51.qaug_ref, bf16[512,768]{1,0:T(8,128)(2,1)} %get-tuple-element.65.do_ref, ...), custom_call_target="tpu_custom_call" | custom-call | tf_op jit(solution)/shard_map/attend_back/pallas_call | solution.py:206
  155.9 179.7 %finish.1 = (bf16[12,192,768]{2,1,0:T(8,128)(2,1)}, f32[8,192]{1,0:T(8,128)}, f32[1,768]{1,0:T(1,128)}, bf16[512,768]{1,0:T(8,128)(2,1)}) custom-call(bf16[4,192,3072]{2,1,0:T(8,128)(2,1)} %bitcast.35, bf16[4,192,768]{2,1,0:T(8,128)(2,1)} %bitcast.37, bf16[4,768,768]{2,1,0:T(8,128)(2,1)} %bitcast.36, f32[16,768]{1,0:T(8,128)} %get-tuple-element.64.refs_3_, ...), custom_call_target="tpu_custom_call" | custom-call | tf_op jit(solution)/shard_map/finish/pallas_call | solution.py:887
  335.6 0.0 copy-start.3
  335.6 0.0 copy-start
  335.6 0.0 copy-start.1
  335.6 1.6 fusion
  337.2 5.3 %widen.1 = (f32[1,192,3072]{2,1,0:T(8,128)}, f32[1,192,768]{2,1,0:T(8,128)}, f32[4,192,768]{2,1,0:T(8,128)}, f32[1,192,768]{2,1,0:T(8,128)}, f32[1,192,768]{2,1,0:T(8,128)}, /*index=5*/f32[1,192,768]{2,1,0:T(8,128)}) custom-call(bf16[12,192,768]{2,1,0:T(8,128)(2,1)} %get-tuple-element.74.in_ref), custom_call_target="tpu_custom_call" | custom-call | tf_op jit(solution)/shard_map/widen/pallas_call | solution.py:859
  342.5 0.0 copy-done.3
  342.5 0.6 reduce
  343.1 0.0 copy-done
  343.1 0.9 copy.37
  344.0 0.0 copy-done.1
  344.0 0.9 copy.38
Async XLA Ops:
  64.9 35.1 %collective-permute-start.1 = (bf16[768,768]{1,0:T(8,128)(2,1)}, bf16[768,768]{1,0:T(8,128)(2,1)}, u32[]{:S(2)}, u32[]{:S(2)}) collective-permute-start(bf16[768,768]{1,0:T(8,128)(2,1)} %down_own), channel_id=1, source_target_pairs={{0,2},{1,3},{2,0},{3,1},{4,6},{5,7},{6,4},{7,5},{8,10},{9,11},{10,... | collective-permute-start | bytes 3538952 | tf_op jit(solution)/shard_map/ppermute | solution.py:1212
  65.5 34.5 %collective-permute-start = (bf16[192,768]{1,0:T(8,128)(2,1)}, bf16[192,768]{1,0:T(8,128)(2,1)S(1)}, u32[]{:S(2)}, u32[]{:S(2)}) collective-permute-start(bf16[192,768]{1,0:T(8,128)(2,1)} %out_own), channel_id=1, source_target_pairs={{0,2},{1,3},{2,0},{3,1},{4,6},{5,7},{6,4},{7,5},{8,10},{9,11},{10,... | collective-permute-start | bytes 884744 | tf_op jit(solution)/shard_map/ppermute | solution.py:1211
  100.0 0.7 copy-start.2
  335.6 6.9 %copy-start.3 = (f32[1,768]{1,0:T(1,128)S(1)}, f32[1,768]{1,0:T(1,128)}, u32[]{:S(2)}) copy-start(f32[1,768]{1,0:T(1,128)} %get-tuple-element.82) | copy-start | bytes 9220
  335.6 7.5 %copy-start = (bf16[512,768]{1,0:T(8,128)(2,1)S(1)}, bf16[512,768]{1,0:T(8,128)(2,1)}, u32[]{:S(2)}) copy-start(bf16[512,768]{1,0:T(8,128)(2,1)} %get-tuple-element.60) | copy-start | bytes 2359300
  335.6 8.4 %copy-start.1 = (bf16[512,768]{1,0:T(8,128)(2,1)S(1)}, bf16[512,768]{1,0:T(8,128)(2,1)}, u32[]{:S(2)}) copy-start(bf16[512,768]{1,0:T(8,128)(2,1)} %get-tuple-element.73) | copy-start | bytes 2359300

commit v11 on v10

--- a/solution.py
+++ b/solution.py
@@ -225,7 +225,7 @@
     )(docs, q, qaug, do, lse, ot, k, kaug, v)
 
 
-def middle_kernel(attn_ref, in_ref, cot_ref, vec_ref, out_own, out_far, wu_ref, down_own, down_far,
+def middle_kernel(attn_ref, in_ref, cot_ref, vec_ref, wo_ref, wu_ref, down_own, down_far,
                   out_ref, sum1_ref, do_ref, grads_ref, up_out, down_out, attn_out,
                   wo, wu, wd, attn_b, first, hat1, scale1, first_b, act, slope, sum2, down_b, up_b, first_b2, first_t,
                   g_up, g_down, g_out, sem_w, sem_d, sem_o):
@@ -233,38 +233,31 @@
     a, w = lax.axis_index("ctx"), lax.axis_index("wsh")
     y, c = w // 2, lax.rem(w, 2)
     core_peer = (a, y * 2 + (1 - c))
+    tall = down_own.shape[0]
     MESH = pl.DeviceIdType.MESH
-    owners = (w, (1 - y) * 2 + c)
     barrier = pltpu.get_barrier_semaphore()
     pl.semaphore_signal(barrier, inc=1, device_id=core_peer, device_id_type=MESH)
     pl.semaphore_wait(barrier, 1)
-
-    def share(j, s, full, ref):
-        tall = ref.shape[0]
-        there = full.at[pl.ds(pl.multiple_of(owners[s] * tall, 16), tall), :]
-        return (
-            pltpu.make_async_copy(ref, there, sem_w.at[j, s]),
-            pltpu.make_async_remote_copy(
-                src_ref=ref, dst_ref=there, send_sem=sem_d.at[0, j, s], recv_sem=sem_d.at[1, j, s],
-                device_id=core_peer, device_id_type=MESH),
-        )
-
-    shares = [[share(j, s, full, ref) for s, ref in enumerate(pair)]
-              for j, (full, pair) in enumerate(((wo, (out_own, out_far)), (wd, (down_own, down_far))))]
-    up_load = pltpu.make_async_copy(wu_ref, wu, sem_w.at[2, 0])
-    for pair in shares:
-        for kept, passed in pair:
-            passed.start()
-            kept.start()
-    up_load.start()
+    passed = []
+    for s, (ref, owner) in enumerate(((down_own, w), (down_far, (1 - y) * 2 + c))):
+        there = wd.at[pl.ds(pl.multiple_of(owner * tall, 16), tall), :]
+        passed.append(pltpu.make_async_remote_copy(
+            src_ref=ref, dst_ref=there, send_sem=sem_d.at[0, s], recv_sem=sem_d.at[1, s],
+            device_id=core_peer, device_id_type=MESH))
+        passed[-1].start()
+        pltpu.make_async_copy(ref, there, sem_w.at[2 + s]).start()
+    loading = [pltpu.make_async_copy(wo_ref, wo, sem_w.at[0]), pltpu.make_async_copy(wu_ref, wu, sem_w.at[1])]
+    for copy in loading:
+        copy.start()
 
     def arrived(j):
-        if j == 1:
-            up_load.wait()
+        if j < 2:
+            loading[j].wait()
         else:
-            for kept, passed in shares[j // 2]:
-                kept.wait()
-                passed.wait_recv()
+            for s, owner in enumerate((w, (1 - y) * 2 + c)):
+                there = wd.at[pl.ds(pl.multiple_of(owner * tall, 16), tall), :]
+                pltpu.make_async_copy(there, there, sem_w.at[2 + s]).wait()
+                passed[s].wait_recv()
 
     grads_ref[...] = jnp.zeros_like(grads_ref)
     attn_b[...] = attn_ref[...].astype(BF)
@@ -380,12 +373,11 @@
 
     over_wide(wide_end)
     pltpu.make_async_copy(g_out, attn_out, sem_o.at[2, 0]).wait()
-    for pair in shares:
-        for _kept, passed in pair:
-            passed.wait_send()
-
-
-def middle(attn_t, inputs, cotangent, vec, out_own, out_far, up_w, down_own, down_far):
+    for copy in passed:
+        copy.wait_send()
+
+
+def middle(attn_t, inputs, cotangent, vec, out_w, up_w, down_own, down_far):
     rows = inputs.shape[0]
     wide = up_w.shape[1]
     vm, dma, shape = pltpu.VMEM, pltpu.SemaphoreType.DMA, jax.ShapeDtypeStruct
@@ -395,17 +387,17 @@
         middle_kernel,
         out_shape=(shape((rows, D), BF), shape((rows, D), F32), shape((rows, D), BF), shape((16, D), F32),
                    shape((D, wide), BF), shape((wide, D), BF), shape((D, D), BF)),
-        in_specs=[vm_spec] * 4 + [any_spec] * 5,
+        in_specs=[vm_spec] * 4 + [any_spec] * 4,
         out_specs=(vm_spec,) * 4 + (any_spec,) * 3,
         scratch_shapes=[
             vm((D, D), BF), vm((D, wide), BF), vm((wide, D), BF), vm((D, rows), BF), vm((rows, D), F32),
             vm((rows, D), F32), vm((rows, 1), F32), vm((rows, D), BF), vm((rows, wide), BF), vm((rows, wide), F32),
             vm((rows, D), F32), vm((rows, D), BF), vm((rows, wide), BF), vm((rows, D), BF), vm((D, rows), BF),
-            vm((D, wide), BF), vm((wide, D), BF), vm((D, D), BF), dma((3, 2)), dma((2, 2, 2)), dma((3, wide // D)),
+            vm((D, wide), BF), vm((wide, D), BF), vm((D, D), BF), dma((4,)), dma((2, 2)), dma((3, wide // D)),
         ],
         compiler_params=pltpu.CompilerParams(collective_id=3, has_side_effects=True, vmem_limit_bytes=63 * 2**20),
         name="middle",
-    )(attn_t, inputs, cotangent, vec, out_own, out_far, up_w, down_own, down_far)
+    )(attn_t, inputs, cotangent, vec, out_w, up_w, down_own, down_far)
 
 
 def reach(n_ctx):
@@ -855,10 +847,10 @@
 
 def widen(summed, spans):
     n, rows, _width = summed.shape
-    part = rows // 4
+    part = rows // 2
     outs = pl.pallas_call(
         functools.partial(widen_kernel, spans),
-        grid=(4,),
+        grid=(2,),
         out_shape=[jax.ShapeDtypeStruct((down, rows, across * D), F32) for _first, down, across in spans],
         in_specs=[pl.BlockSpec((n, part, D), lambda i: (0, i, 0))],
         out_specs=[pl.BlockSpec((down, part, across * D), lambda i: (0, i, 0)) for _first, down, across in spans],
@@ -907,9 +899,9 @@
     return widen(summed, spans), small, wide, grad_own
 
 
-def gather_kernel(cut, tok_ref, docs_ref, wk_ref, wv_ref, wq_ref, wu_ref, vec_ref,
-                  tok_out, k_out, v_out, q_out, w_out, vec_out, wu_out, query_doc, key_doc,
-                  tok, kbuf, vbuf, qbuf, wbuf, vecs, wu, kdoc,
+def gather_kernel(cut, tok_ref, docs_ref, wk_ref, wv_ref, wq_ref, wo_ref, wu_ref, vec_ref,
+                  tok_out, k_out, v_out, q_out, w_out, vec_out, wo_out, wu_out, query_doc, key_doc,
+                  tok, kbuf, vbuf, qbuf, wbuf, vecs, wo, wu, kdoc,
                   sem_in, sem_out, sem_w, sem_l, sem_o):
     n_ctx = lax.axis_size("ctx")
     zs = n_ctx // 2
@@ -981,11 +973,11 @@
     def shard(m, owner):
         if m == 3:
             return vecs.at[owner]
-        return (wbuf.at[0], wbuf.at[1], wbuf.at[2], None, wu)[m].at[weight_rows(owner), :]
+        return (wbuf.at[0], wbuf.at[1], wbuf.at[2], None, wo, wu)[m].at[weight_rows(owner), :]
 
     vecs[w, 0 : vec_ref.shape[0], :] = vec_ref[...]
-    shards = (wk_ref, wv_ref, wq_ref, vecs.at[w], wu_ref)
-    for m in (3, 0, 1, 2, 4):
+    shards = (wk_ref, wv_ref, wq_ref, vecs.at[w], wo_ref, wu_ref)
+    for m in (3, 0, 1, 2, 4, 5):
         remote(shards[m], shard(m, w), sem_w.at[0, 1, m], sem_w.at[1, 1, m], y_peer).start()
         remote(shards[m], shard(m, w), sem_w.at[0, 0, m], sem_w.at[1, 0, m], core_peer).start()
         if m != 3:
@@ -1109,10 +1101,12 @@
 
     pltpu.make_async_copy(wbuf, w_out, sem_l.at[6]).start()
 
-    weight_forward(4)
-    weight_end(4)
-    pltpu.make_async_copy(wu, wu_out, sem_l.at[1]).start()
-    for m in range(5):
+    for m in (4, 5):
+        weight_forward(m)
+    for m, full, target in ((4, wo, wo_out), (5, wu, wu_out)):
+        weight_end(m)
+        pltpu.make_async_copy(full, target, sem_l.at[m - 4]).start()
+    for m in range(6):
         for kind in range(3):
             weight_arrival(m, kind).wait_send()
 
@@ -1132,11 +1126,12 @@
             pltpu.make_async_copy(src.at[j], dst.at[j], sem_o.at[i, j]).wait()
     pltpu.make_async_copy(qbuf, q_out, sem_l.at[5]).wait()
     pltpu.make_async_copy(wbuf, w_out, sem_l.at[6]).wait()
+    pltpu.make_async_copy(wo, wo_out, sem_l.at[0]).wait()
     pltpu.make_async_copy(wu, wu_out, sem_l.at[1]).wait()
     pltpu.make_async_copy(kdoc, key_doc, sem_l.at[3]).wait()
 
 
-def gather_project(inputs, doc_starts, vectors, key_weight, value_weight, query_weight, up_weight):
+def gather_project(inputs, doc_starts, vectors, key_weight, value_weight, query_weight, out_weight, up_weight):
     n_ctx, n_wsh = lax.axis_size("ctx"), lax.axis_size("wsh")
     tall = inputs.shape[0]
     n_slices = 8
@@ -1149,18 +1144,18 @@
     return pl.pallas_call(
         functools.partial(gather_kernel, 5),
         out_shape=(shape(runs, BF), shape(runs, BF), shape(runs, BF), shape((tall, D), BF), shape((3, D, D), BF),
-                   shape((16, D), F32), shape((D, up_weight.shape[1]), BF), shape((tall, 128), BF),
+                   shape((16, D), F32), shape((D, D), BF), shape((D, up_weight.shape[1]), BF), shape((tall, 128), BF),
                    shape((n_ctx * tall, 128), BF)),
-        in_specs=[any_spec, pl.BlockSpec(memory_space=pltpu.SMEM)] + [any_spec] * 4 + [vm_spec],
-        out_specs=(any_spec,) * 5 + (vm_spec,) + (any_spec,) + (vm_spec, any_spec),
+        in_specs=[any_spec, pl.BlockSpec(memory_space=pltpu.SMEM)] + [any_spec] * 5 + [vm_spec],
+        out_specs=(any_spec,) * 5 + (vm_spec,) + (any_spec,) * 2 + (vm_spec, any_spec),
         scratch_shapes=[
             vm(runs, BF), vm(runs, BF), vm(runs, BF), vm((tall, D), BF), vm((3, D, D), BF), vm((n_wsh, 16, D // n_wsh), F32),
-            vm((D, up_weight.shape[1]), BF), vm((n_ctx * tall, 128), BF),
-            dma((n_ctx, n_slices)), dma((3, far, n_slices)), dma((2, 4, 5)), dma((7,)), dma((3, n_ctx)),
+            vm((D, D), BF), vm((D, up_weight.shape[1]), BF), vm((n_ctx * tall, 128), BF),
+            dma((n_ctx, n_slices)), dma((3, far, n_slices)), dma((2, 4, 6)), dma((7,)), dma((3, n_ctx)),
         ],
         compiler_params=pltpu.CompilerParams(collective_id=1, has_side_effects=True, vmem_limit_bytes=63 * 2**20),
         name="gather_project",
-    )(inputs, doc_starts, key_weight, value_weight, query_weight, up_weight, vectors)
+    )(inputs, doc_starts, key_weight, value_weight, query_weight, out_weight, up_weight, vectors)
 
 
 def local(
@@ -1203,13 +1198,11 @@
             vectors = vectors + lax.pad(v.astype(F32), jnp.zeros((), F32), (ends,))
             place += v.shape[0]
         vectors = vectors.reshape(8 + n_wsh, own)
-        all_tokens, keys, values, queries, kvq_w, vec, up_w, query_doc, key_doc = gather_project(
-            inputs, doc_starts, vectors, key_weight, value_weight, query_weight, up_weight
+        all_tokens, keys, values, queries, kvq_w, vec, out_w, up_w, query_doc, key_doc = gather_project(
+            inputs, doc_starts, vectors, key_weight, value_weight, query_weight, out_weight, up_weight
         )
-        out_own, down_own, _unused = lax.optimization_barrier((out_weight, down_weight, vec))
-        across = [(i, i ^ 2) for i in range(n_wsh)]
-        out_far = lax.ppermute(out_own, "wsh", across)
-        down_far = lax.ppermute(down_own, "wsh", across)
+        down_own, _unused = lax.optimization_barrier((down_weight, vec))
+        down_far = lax.ppermute(down_own, "wsh", [(i, i ^ 2) for i in range(n_wsh)])
         all_tokens, keys, values = [r.reshape(stream_rows, D) for r in (all_tokens, keys, values)]
     else:
         first_row = lax.axis_index("ctx") * tok_rows
@@ -1229,7 +1222,7 @@
     mixed_t, log_rows = attn_fwd(doc_start, queries, query_doc, keys, key_doc, values, tq=tile)
     if fast:
         layer_out, grad_sum1, grad_attn, vec_grads, grad_up_w, grad_down_w, grad_out_w = middle(
-            mixed_t, inputs, cotangent[0], vec, out_own, out_far, up_w, down_own, down_far
+            mixed_t, inputs, cotangent[0], vec, out_w, up_w, down_own, down_far
         )
         grad_q, grad_k, grad_v = attn_bwd(
             doc_start, queries, query_doc, grad_attn, log_rows, mixed_t, keys, key_doc, values, tq=tile

time: 346 us -> 343 us (level); the launches traced: 345 us -> 346 us
  Pallas kernels: 319 us -> 330 us
  waiting for transfers between devices: 16.4 us -> 8.59 us
    ppermute x2 -> x1, waiting for transfers between devices: 16.4 us -> 8.59 us  [local(): down_far = lax.ppermute(down_own, 'wsh', [(i, i ^ 2) for i in range(n_wsh)])]
    pallas_call x1, Pallas kernels: 62.7 us -> 69.2 us  [gather_project(): pl.pallas_call(functools.partial(gather_kernel, 5), out_shape=(shape(runs...]
  transfers between devices with their start and end apart: 2 -> 1, of which waited for: 1 -> 1; matrix products, arithmetic and copies ran while one was open for 0% -> 0% of each run, Pallas kernels for 5% -> 6%
where the time goes in v11:
time: 343 us; the launch traced here: 346 us
  Pallas kernels  330 us (96%)
  waiting for transfers between devices  8.59 us (3%)
  local copies, waits for them, and re-layouts  4.26 us (1%)
    pallas_call x1, Pallas kernels, finish(): pl.pallas_call(functools.partial(finish_kernel, sources, len(parts)), out...  178 us
    pallas_call x1, Pallas kernels, gather_project(): pl.pallas_call(functools.partial(gather_kernel, 5), out_shape=(shape(runs...  69.2 us
    pallas_call x1, Pallas kernels, middle(): pl.pallas_call(middle_kernel, out_shape=(shape((rows, D), BF), shape((row...  31.9 us
    pallas_call x1, Pallas kernels, attn_bwd(): pl.pallas_call(functools.partial(bwd_kernel, tq, tk), out_shape=(jax.Shap...  26.4 us
    pallas_call x1, Pallas kernels, attn_fwd(): pl.pallas_call(functools.partial(fwd_kernel, tq, tk), out_shape=(jax.Shap...  19.7 us
    ppermute x1, waiting for transfers between devices, local(): down_far = lax.ppermute(down_own, 'wsh', [(i, i ^ 2) for i in range(n_wsh)])  8.59 us
  transfers between devices with their start and end apart: 1, of which 1 were waited for; matrix products, arithmetic and copies ran while one was open for 0% of the time, Pallas kernels for 6%

profile of v11, /device:TPU:0, one launch (start us, length us, event | category | flops | bytes accessed | tf_op | source)
XLA Modules:
  0.0 345.6 jit_solution(17963281246364639977)
XLA Ops:
  0.7 0.9 convert_add_fusion
  1.5 0.7 reshape.82.vec_ref
  2.2 69.2 %gather_project.1 = (bf16[8,512,768]{2,1,0:T(8,128)(2,1)}, bf16[8,512,768]{2,1,0:T(8,128)(2,1)}, bf16[8,512,768]{2,1,0:T(8,128)(2,1)}, bf16[512,768]{1,0:T(8,128...) custom-call(bf16[512,768]{1,0:T(8,128)(2,1)} %bitcast.30, ...), custom_call_target="tpu_custom_call" | custom-call | tf_op jit(solution)/shard_map/gather_project/pallas_call | solution.py:1144
  71.4 0.6 collective-permute-start
  72.0 19.7 %attend.1 = (f32[768,512]{1,0:T(8,128)}, f32[6,2,512]{2,1,0:T(2,128)}) custom-call(s32[8]{0:T(128)} %bitcast.41, bf16[512,768]{1,0:T(8,128)(2,1)} %get-tuple-element.50.q_ref, bf16[512,128]{1,0:T(8,128)(2,1)} %get-tuple-element.51.qaug_ref, bf16[4096,768]{1,0:T(8,128)(2,1)} %bitcast.26, bf16[4096,128]{1,0:T(8,128)(2,1)} %get-tuple-element.53.kaug_ref, ...), custom_call_target="tpu_custom_call" | custom-call | tf_op jit(solution)/shard_map/attend/pallas_call | solution.py:121
  91.7 8.6 %collective-permute-done.down_far = bf16[768,768]{1,0:T(8,128)(2,1)} collective-permute-done((bf16[768,768]{1,0:T(8,128)(2,1)}, bf16[768,768]{1,0:T(8,128)(2,1)}, u32[]{:S(2)}, u32[]{:S(2)}) %collective-permute-start) | collective-permute-done | bytes 1179680 | tf_op jit(solution)/shard_map/ppermute | solution.py:1205
  100.3 31.9 %middle.1 = (bf16[512,768]{1,0:T(8,128)(2,1)}, f32[512,768]{1,0:T(8,128)}, bf16[512,768]{1,0:T(8,128)(2,1)}, f32[16,768]{1,0:T(8,128)}, bf16[768,3072]{1,0:T(8,1...) custom-call(f32[768,512]{1,0:T(8,128)} %get-tuple-element.55.attn_ref.ot_ref, bf16[512,768]{1,0:T(8,128)(2,1)} %bitcast.31, ...), custom_call_target="tpu_custom_call" | custom-call | tf_op jit(solution)/shard_map/middle/pallas_call | solution.py:386
  132.2 26.4 %attend_back.1 = (bf16[512,768]{1,0:T(8,128)(2,1)}, bf16[4096,768]{1,0:T(8,128)(2,1)}, bf16[4096,768]{1,0:T(8,128)(2,1)}) custom-call(s32[8]{0:T(128)} %bitcast.42, bf16[512,768]{1,0:T(8,128)(2,1)} %get-tuple-element.50.q_ref, bf16[512,128]{1,0:T(8,128)(2,1)} %get-tuple-element.51.qaug_ref, bf16[512,768]{1,0:T(8,128)(2,1)} %get-tuple-element.65.do_ref, ...), custom_call_target="tpu_custom_call" | custom-call | tf_op jit(solution)/shard_map/attend_back/pallas_call | solution.py:206
  158.7 178.2 %finish.1 = (bf16[12,192,768]{2,1,0:T(8,128)(2,1)}, f32[8,192]{1,0:T(8,128)}, f32[1,768]{1,0:T(1,128)}, bf16[512,768]{1,0:T(8,128)(2,1)}) custom-call(bf16[4,192,3072]{2,1,0:T(8,128)(2,1)} %bitcast.35, bf16[4,192,768]{2,1,0:T(8,128)(2,1)} %bitcast.37, bf16[4,768,768]{2,1,0:T(8,128)(2,1)} %bitcast.36, f32[16,768]{1,0:T(8,128)} %get-tuple-element.64.refs_3_, ...), custom_call_target="tpu_custom_call" | custom-call | tf_op jit(solution)/shard_map/finish/pallas_call | solution.py:879
  336.9 0.0 copy-start.2
  336.9 0.0 copy-start
  336.9 0.0 copy-start.1
  336.9 1.8 fusion
  338.7 4.5 %widen.1 = (f32[1,192,3072]{2,1,0:T(8,128)}, f32[1,192,768]{2,1,0:T(8,128)}, f32[4,192,768]{2,1,0:T(8,128)}, f32[1,192,768]{2,1,0:T(8,128)}, f32[1,192,768]{2,1,0:T(8,128)}, /*index=5*/f32[1,192,768]{2,1,0:T(8,128)}) custom-call(bf16[12,192,768]{2,1,0:T(8,128)(2,1)} %get-tuple-element.74.in_ref), custom_call_target="tpu_custom_call" | custom-call | tf_op jit(solution)/shard_map/widen/pallas_call | solution.py:851
  343.2 0.0 copy-done.2
  343.2 0.6 reduce
  343.8 0.0 copy-done
  343.8 0.9 copy.37
  344.7 0.0 copy-done.1
  344.7 0.9 copy.38
Async XLA Ops:
  71.4 28.9 %collective-permute-start = (bf16[768,768]{1,0:T(8,128)(2,1)}, bf16[768,768]{1,0:T(8,128)(2,1)}, u32[]{:S(2)}, u32[]{:S(2)}) collective-permute-start(bf16[768,768]{1,0:T(8,128)(2,1)} %down_own), channel_id=1, source_target_pairs={{0,2},{1,3},{2,0},{3,1},{4,6},{5,7},{6,4},{7,5},{8,10},{9,11},{10,... | collective-permute-start | bytes 3538952 | tf_op jit(solution)/shard_map/ppermute | solution.py:1205
  336.9 6.4 %copy-start.2 = (f32[1,768]{1,0:T(1,128)S(1)}, f32[1,768]{1,0:T(1,128)}, u32[]{:S(2)}) copy-start(f32[1,768]{1,0:T(1,128)} %get-tuple-element.82) | copy-start | bytes 9220
  336.9 7.0 %copy-start = (bf16[512,768]{1,0:T(8,128)(2,1)S(1)}, bf16[512,768]{1,0:T(8,128)(2,1)}, u32[]{:S(2)}) copy-start(bf16[512,768]{1,0:T(8,128)(2,1)} %get-tuple-element.60) | copy-start | bytes 2359300
  336.9 7.8 %copy-start.1 = (bf16[512,768]{1,0:T(8,128)(2,1)S(1)}, bf16[512,768]{1,0:T(8,128)(2,1)}, u32[]{:S(2)}) copy-start(bf16[512,768]{1,0:T(8,128)(2,1)} %get-tuple-element.73) | copy-start | bytes 2359300

commit v12 on v11

--- a/solution.py
+++ b/solution.py
@@ -838,28 +838,42 @@
     lax.fori_loop(0, n_pos // 2, drain_x, 0)
 
 
-def widen_kernel(spans, in_ref, *outs):
+def widen_kernel(spans, in_ref, small_ref, wide_ref, grad_ref, layer_ref, grad_out, layer_out, *outs):
+    grad_out[...] = grad_ref[...]
+    layer_out[...] = layer_ref[...]
     for (first, down, across), out in zip(spans, outs):
         for r in range(down):
             for col in range(across):
                 out[r, :, col * D : (col + 1) * D] = in_ref[first + r * across + col].astype(F32)
-
-
-def widen(summed, spans):
+    vectors = outs[len(spans) :]
+    for i, out in enumerate(vectors[:-1]):
+        out[...] = small_ref[i : i + 1, :]
+    vectors[-1][...] = wide_ref[...]
+
+
+def widen(summed, spans, small, wide, grad_inputs, layer_out):
     n, rows, _width = summed.shape
     part = rows // 2
+    tokens = pl.BlockSpec((grad_inputs.shape[0] // 2, D), lambda i: (i, 0))
+    shape = jax.ShapeDtypeStruct
+    vectors = [(1, small.shape[1])] * small.shape[0] + [wide.shape]
     outs = pl.pallas_call(
         functools.partial(widen_kernel, spans),
         grid=(2,),
-        out_shape=[jax.ShapeDtypeStruct((down, rows, across * D), F32) for _first, down, across in spans],
-        in_specs=[pl.BlockSpec((n, part, D), lambda i: (0, i, 0))],
-        out_specs=[pl.BlockSpec((down, part, across * D), lambda i: (0, i, 0)) for _first, down, across in spans],
+        out_shape=[shape(grad_inputs.shape, BF)] * 2
+        + [shape((down, rows, across * D), F32) for _first, down, across in spans]
+        + [shape(v, F32) for v in vectors],
+        in_specs=[pl.BlockSpec((n, part, D), lambda i: (0, i, 0)), pl.BlockSpec(small.shape, lambda i: (0, 0)),
+                  pl.BlockSpec(wide.shape, lambda i: (0, 0)), tokens, tokens],
+        out_specs=[tokens] * 2 + [pl.BlockSpec((down, part, across * D), lambda i: (0, i, 0)) for _first, down, across in spans]
+        + [pl.BlockSpec(v, lambda i: (0, 0)) for v in vectors],
         name="widen",
-    )(summed)
-    return [o.reshape(-1, o.shape[2]) for o in outs]
-
-
-def finish(matrices, vec, grad_k, grad_v, all_tokens, grad_q, kvq_w, own_grad, inputs):
+    )(summed, small, wide, grad_inputs, layer_out)
+    grad_inputs, layer_out, mats, vectors = outs[0], outs[1], outs[2 : len(spans) + 2], outs[len(spans) + 2 :]
+    return grad_inputs, layer_out, [o.reshape(-1, o.shape[2]) for o in mats], [v.reshape(-1) for v in vectors[:-1]], vectors[-1].reshape(-1)
+
+
+def finish(matrices, vec, grad_k, grad_v, all_tokens, grad_q, kvq_w, own_grad, inputs, layer_out):
     n_ctx, n_wsh = lax.axis_size("ctx"), lax.axis_size("wsh")
     zs, hops = n_ctx // 2, reach(n_ctx) // 2
     rows = D // n_wsh
@@ -896,7 +910,7 @@
         compiler_params=pltpu.CompilerParams(collective_id=2, has_side_effects=True, vmem_limit_bytes=63 * 2**20),
         name="finish",
     )(*parts, vec, grad_k, grad_v, all_tokens, grad_q, kvq_w, own_grad, inputs)
-    return widen(summed, spans), small, wide, grad_own
+    return widen(summed, spans, small, wide, grad_own, layer_out)
 
 
 def gather_kernel(cut, tok_ref, docs_ref, wk_ref, wv_ref, wq_ref, wo_ref, wu_ref, vec_ref,
@@ -1227,14 +1241,14 @@
         grad_q, grad_k, grad_v = attn_bwd(
             doc_start, queries, query_doc, grad_attn, log_rows, mixed_t, keys, key_doc, values, tq=tile
         )
-        mats, small, wide, grad_inputs = finish(
+        grad_inputs, layer_out, mats, small, wide = finish(
             (grad_up_w, grad_out_w, grad_down_w), vec_grads, grad_k.reshape(n_ctx, tok_rows, D),
-            grad_v.reshape(n_ctx, tok_rows, D), all_tokens.reshape(n_ctx, tok_rows, D), grad_q, kvq_w, grad_sum1, inputs,
+            grad_v.reshape(n_ctx, tok_rows, D), all_tokens.reshape(n_ctx, tok_rows, D), grad_q, kvq_w, grad_sum1, inputs, layer_out,
         )
         up_sum, out_sum, down_sum, key_sum, value_sum, query_sum = mats
         return (
             layer_out.reshape(1, tok_rows, D), grad_inputs.reshape(1, tok_rows, D), query_sum, key_sum, value_sum,
-            out_sum, up_sum, down_sum, small[0], small[1], small[2], small[3], small[4], wide[0],
+            out_sum, up_sum, down_sum, small[0], small[1], small[2], small[3], small[4], wide,
             small[5], small[6], small[7],
         )
 

time: 343 us -> 342 us (level)
  local copies, waits for them, and re-layouts: 4.26 us -> 0.68 us
  transfers between devices with their start and end apart: 1 -> 1, of which waited for: 1 -> 1; matrix products, arithmetic and copies ran while one was open for 0% -> 0% of each run, Pallas kernels for 6% -> 5%
where the time goes in v12:
time: 342 us; the launch traced here: 343 us
  Pallas kernels  327 us (96%)
  waiting for transfers between devices  11.7 us (3%)
    pallas_call x1, Pallas kernels, finish(): pl.pallas_call(functools.partial(finish_kernel, sources, len(parts)), out...  181 us
    pallas_call x1, Pallas kernels, gather_project(): pl.pallas_call(functools.partial(gather_kernel, 5), out_shape=(shape(runs...  69.2 us
    pallas_call x1, Pallas kernels, middle(): pl.pallas_call(middle_kernel, out_shape=(shape((rows, D), BF), shape((row...  31.9 us
    pallas_call x1, Pallas kernels, attn_bwd(): pl.pallas_call(functools.partial(bwd_kernel, tq, tk), out_shape=(jax.Shap...  23.1 us
    pallas_call x1, Pallas kernels, attn_fwd(): pl.pallas_call(functools.partial(fwd_kernel, tq, tk), out_shape=(jax.Shap...  16.6 us
    ppermute x1, waiting for transfers between devices, local(): down_far = lax.ppermute(down_own, 'wsh', [(i, i ^ 2) for i in range(n_wsh)])  11.7 us
  transfers between devices with their start and end apart: 1, of which 1 were waited for; matrix products, arithmetic and copies ran while one was open for 0% of the time, Pallas kernels for 5%

profile of v12, /device:TPU:0, one launch (start us, length us, event | category | flops | bytes accessed | tf_op | source)
XLA Modules:
  0.0 343.0 jit_solution(10449680285040741716)
XLA Ops:
  0.7 0.9 convert_add_fusion
  1.5 0.7 reshape.109.vec_ref
  2.2 69.2 %gather_project.1 = (bf16[8,512,768]{2,1,0:T(8,128)(2,1)}, bf16[8,512,768]{2,1,0:T(8,128)(2,1)}, bf16[8,512,768]{2,1,0:T(8,128)(2,1)}, bf16[512,768]{1,0:T(8,128...) custom-call(bf16[512,768]{1,0:T(8,128)(2,1)} %bitcast.30, ...), custom_call_target="tpu_custom_call" | custom-call | tf_op jit(solution)/shard_map/gather_project/pallas_call | solution.py:1158
  71.4 0.6 collective-permute-start
  72.0 16.6 %attend.1 = (f32[768,512]{1,0:T(8,128)}, f32[6,2,512]{2,1,0:T(2,128)}) custom-call(s32[8]{0:T(128)} %bitcast.39, bf16[512,768]{1,0:T(8,128)(2,1)} %get-tuple-element.61.q_ref, bf16[512,128]{1,0:T(8,128)(2,1)} %get-tuple-element.62.qaug_ref, bf16[4096,768]{1,0:T(8,128)(2,1)} %bitcast.26, bf16[4096,128]{1,0:T(8,128)(2,1)} %get-tuple-element.64.kaug_ref, ...), custom_call_target="tpu_custom_call" | custom-call | tf_op jit(solution)/shard_map/attend/pallas_call | solution.py:121
  88.5 11.7 %collective-permute-done.down_far = bf16[768,768]{1,0:T(8,128)(2,1)} collective-permute-done((bf16[768,768]{1,0:T(8,128)(2,1)}, bf16[768,768]{1,0:T(8,128)(2,1)}, u32[]{:S(2)}, u32[]{:S(2)}) %collective-permute-start) | collective-permute-done | bytes 1179680 | tf_op jit(solution)/shard_map/ppermute | solution.py:1219
  100.3 31.9 %middle.1 = (bf16[512,768]{1,0:T(8,128)(2,1)}, f32[512,768]{1,0:T(8,128)}, bf16[512,768]{1,0:T(8,128)(2,1)}, f32[16,768]{1,0:T(8,128)}, bf16[768,3072]{1,0:T(8,1...) custom-call(f32[768,512]{1,0:T(8,128)} %get-tuple-element.66.attn_ref.ot_ref, bf16[512,768]{1,0:T(8,128)(2,1)} %bitcast.31, ...), custom_call_target="tpu_custom_call" | custom-call | tf_op jit(solution)/shard_map/middle/pallas_call | solution.py:386
  132.2 23.1 %attend_back.1 = (bf16[512,768]{1,0:T(8,128)(2,1)}, bf16[4096,768]{1,0:T(8,128)(2,1)}, bf16[4096,768]{1,0:T(8,128)(2,1)}) custom-call(s32[8]{0:T(128)} %bitcast.40, bf16[512,768]{1,0:T(8,128)(2,1)} %get-tuple-element.61.q_ref, bf16[512,128]{1,0:T(8,128)(2,1)} %get-tuple-element.62.qaug_ref, bf16[512,768]{1,0:T(8,128)(2,1)} %get-tuple-element.75.do_ref, ...), custom_call_target="tpu_custom_call" | custom-call | tf_op jit(solution)/shard_map/attend_back/pallas_call | solution.py:206
  155.3 181.2 %finish.1 = (bf16[12,192,768]{2,1,0:T(8,128)(2,1)}, f32[8,192]{1,0:T(8,128)}, f32[1,768]{1,0:T(1,128)}, bf16[512,768]{1,0:T(8,128)(2,1)}) custom-call(bf16[4,192,3072]{2,1,0:T(8,128)(2,1)} %bitcast.35, bf16[4,192,768]{2,1,0:T(8,128)(2,1)} %bitcast.37, bf16[4,768,768]{2,1,0:T(8,128)(2,1)} %bitcast.36, f32[16,768]{1,0:T(8,128)} %get-tuple-element.74.refs_3_, ...), custom_call_target="tpu_custom_call" | custom-call | tf_op jit(solution)/shard_map/finish/pallas_call | solution.py:893
  336.6 5.2 %widen.1 = (bf16[512,768]{1,0:T(8,128)(2,1)}, bf16[512,768]{1,0:T(8,128)(2,1)}, f32[1,192,3072]{2,1,0:T(8,128)}, f32[1,192,768]{2,1,0:T(8,128)}, f32[4,192,768]{...) custom-call(bf16[12,192,768]{2,1,0:T(8,128)(2,1)} %get-tuple-element, ...), custom_call_target="tpu_custom_call" | custom-call | tf_op jit(solution)/shard_map/widen/pallas_call | solution.py:860
  341.8 1.3 reduce
Async XLA Ops:
  71.4 28.9 %collective-permute-start = (bf16[768,768]{1,0:T(8,128)(2,1)}, bf16[768,768]{1,0:T(8,128)(2,1)}, u32[]{:S(2)}, u32[]{:S(2)}) collective-permute-start(bf16[768,768]{1,0:T(8,128)(2,1)} %down_own), channel_id=1, source_target_pairs={{0,2},{1,3},{2,0},{3,1},{4,6},{5,7},{6,4},{7,5},{8,10},{9,11},{10,... | collective-permute-start | bytes 3538952 | tf_op jit(solution)/shard_map/ppermute | solution.py:1219
